TPU v7x, 32 devices: a whole 2x2x4 slice. The times are simulated.
32 devices in a mesh: ctx: 16 (over z, x, core), wsh: 2 (over y).
Axes of the slice: x: 2, y: 2, z: 4, core: 2. Of those that a mesh axis runs over, the one named last changes fastest.
Arguments:
- tokens: bfloat16 [2, 4096, 1024], P('wsh', 'ctx'), may hold values from -6 to 6
- ln1_gain: bfloat16 [1024], P('wsh'), may hold values from 0.5 to 1.5
- ln1_bias: bfloat16 [1024], P('wsh'), may hold values from -1.25 to 1.25
- ln2_gain: bfloat16 [1024], P('wsh'), may hold values from 0.5 to 1.5
- ln2_bias: bfloat16 [1024], P('wsh'), may hold values from -1.25 to 1.25
- w_qkv: bfloat16 [1024, 3072], P('wsh'), may hold values from -0.1875 to 0.1875
- b_qkv: bfloat16 [3072], P('wsh'), may hold values from -0.625 to 0.625
- w_out: bfloat16 [1024, 1024], P('wsh'), may hold values from -2 to 2
- b_out: bfloat16 [1024], P('wsh'), may hold values from -3 to 3
- w_up: bfloat16 [1024, 4096], P('wsh'), may hold values from -0.1875 to 0.1875
- b_up: bfloat16 [4096], P('wsh'), may hold values from -3 to 3
- w_down: bfloat16 [4096, 1024], P('wsh'), may hold values from -0.09375 to 0.09375
- b_down: bfloat16 [1024], P('wsh'), may hold values from -3 to 3
- lengths: int32 [2], P('wsh'), may hold values from 1024 to 4096, as said below
- block_map: int32 [32], replicated, may hold values from 0 to 31, as said below
- cotangent: bfloat16 [2, 4096, 1024], P('wsh', 'ctx'), may hold values from -6 to 6
Outputs:
- output: bfloat16 [2, 4096, 1024], P('wsh', 'ctx')
- grad_tokens: float32 [2, 4096, 1024], P('wsh', 'ctx')
- grad_ln1_gain: float32 [1024], P('wsh')
- grad_ln1_bias: float32 [1024], P('wsh')
- grad_ln2_gain: float32 [1024], P('wsh')
- grad_ln2_bias: float32 [1024], P('wsh')
- grad_w_qkv: float32 [1024, 3072], P('wsh')
- grad_b_qkv: float32 [3072], P('wsh')
- grad_w_out: float32 [1024, 1024], P('wsh')
- grad_b_out: float32 [1024], P('wsh')
- grad_w_up: float32 [1024, 4096], P('wsh')
- grad_b_up: float32 [4096], P('wsh')
- grad_w_down: float32 [4096, 1024], P('wsh')
- grad_b_down: float32 [1024], P('wsh')
Inputs may be any that keep to these rules, and one draw needn't show every extreme that they name: `lengths`: some slot is full (4096 valid tokens) in every draw; tokens at positions from a slot's length on are padding. `block_map`: A permutation of the 32 position blocks; stored blocks 2c and 2c + 1 hold two blocks whose indices sum to 31.
All inputs are finite; a program needn't handle non-finite values.
Results may differ from a plain program's by a relative error of at most 0.019.
Values may be sent and summed in bfloat16 or wider, within the bound.
No kernel may reach another device: no remote copies, remote signals or barrier semaphores. Data moves between devices by JAX's collectives and lax.ppermute only.
A program may use at most 320 MiB of HBM per device.

v0:
```python
from functools import partial
import math

import jax
import jax.numpy as jnp
from jax import lax
from jax.sharding import PartitionSpec as P

H = 16
HD = 64
ROT = 16


epsilon = 1e-05


def norm_forward(values, norm_gain, norm_shift):
    average = jnp.mean(values, axis=-1, keepdims=True)
    centred = values - average
    variance = jnp.mean(centred * centred, axis=-1, keepdims=True)
    inverse = lax.rsqrt(variance + epsilon)
    normed = centred * inverse
    return (normed * norm_gain + norm_shift, normed, inverse)


def norm_backward(grad_out, normed, inverse, norm_gain):
    scaled = grad_out * norm_gain
    adjusted = (
        scaled
        - jnp.mean(scaled, axis=-1, keepdims=True)
        - normed * jnp.mean(scaled * normed, axis=-1, keepdims=True)
    )
    return (adjusted * inverse, jnp.sum(grad_out * normed, axis=0), jnp.sum(grad_out, axis=0))


def rotary_tables(positions):
    half_rot = ROT // 2
    frequency = 10000.0 ** (-jnp.arange(half_rot, dtype=jnp.float32) * 2.0 / ROT)
    angles = positions.astype(jnp.float32)[:, None] * frequency[None, :]
    return (jnp.cos(angles)[:, None, :], jnp.sin(angles)[:, None, :])


def rotate_forward(values, cosine_table, sine_table):
    half_rot = ROT // 2
    leading = values[..., :half_rot]
    trailing = values[..., half_rot:ROT]
    return jnp.concatenate(
        [
            leading * cosine_table - trailing * sine_table,
            trailing * cosine_table + leading * sine_table,
            values[..., ROT:],
        ],
        axis=-1,
    )


def rotate_backward(grads, cosine_table, sine_table):
    half_rot = ROT // 2
    leading = grads[..., :half_rot]
    trailing = grads[..., half_rot:ROT]
    return jnp.concatenate(
        [
            leading * cosine_table + trailing * sine_table,
            trailing * cosine_table - leading * sine_table,
            grads[..., ROT:],
        ],
        axis=-1,
    )


def masked_scores(query_rows, key_rows, query_pos, key_pos, key_live):
    raw_scores = jnp.einsum(
        "qhd,khd->hqk", query_rows, key_rows, preferred_element_type=jnp.float32
    )
    allowed = (key_pos[None, :] <= query_pos[:, None]) & key_live[None, :]
    return (jnp.where(allowed[None], raw_scores * (1.0 / math.sqrt(HD)), -1e30), allowed)


def score_grads(
    query_rows, key_rows, value_rows, grad_rows, query_pos, key_pos, key_live, log_total, row_dots
):
    scores = masked_scores(query_rows, key_rows, query_pos, key_pos, key_live)[0]
    probability = jnp.exp(scores - log_total[..., None])
    grad_prob = jnp.einsum(
        "qhd,khd->hqk", grad_rows, value_rows, preferred_element_type=jnp.float32
    )
    grad_score = (probability * (grad_prob - row_dots[..., None]) * (1.0 / math.sqrt(HD))).astype(
        jnp.bfloat16
    )
    return (probability.astype(jnp.bfloat16), grad_score)


def shards(
    tokens,
    ln1_gain,
    ln1_bias,
    ln2_gain,
    ln2_bias,
    w_qkv,
    b_qkv,
    w_out,
    b_out,
    w_up,
    b_up,
    w_down,
    b_down,
    lengths,
    block_map,
    cotangent,
):
    gathered = (
        lax.all_gather(ln1_gain, "wsh", axis=0, tiled=True),
        lax.all_gather(ln1_bias, "wsh", axis=0, tiled=True),
        lax.all_gather(ln2_gain, "wsh", axis=0, tiled=True),
        lax.all_gather(ln2_bias, "wsh", axis=0, tiled=True),
        lax.all_gather(w_qkv, "wsh", axis=0, tiled=True),
        lax.all_gather(b_qkv, "wsh", axis=0, tiled=True),
        lax.all_gather(w_out, "wsh", axis=0, tiled=True),
        lax.all_gather(b_out, "wsh", axis=0, tiled=True),
        lax.all_gather(w_up, "wsh", axis=0, tiled=True),
        lax.all_gather(b_up, "wsh", axis=0, tiled=True),
        lax.all_gather(w_down, "wsh", axis=0, tiled=True),
        lax.all_gather(b_down, "wsh", axis=0, tiled=True),
    )
    (
        norm1_gain,
        norm1_shift,
        norm2_gain,
        norm2_shift,
        qkv_weight,
        qkv_bias,
        out_weight,
        out_bias,
        up_weight,
        up_bias,
        down_weight,
        down_bias,
    ) = gathered
    tok_rows = tokens.shape[1]
    model_width = tokens.shape[2]
    half_rows = tok_rows // 2
    seq_rows = tok_rows * lax.axis_size("ctx")
    head_count = H
    head_size = HD
    ctx_index = lax.axis_index("ctx")
    own_blocks = lax.dynamic_slice_in_dim(block_map, 2 * ctx_index, 2)
    local_offsets = jnp.arange(half_rows, dtype=jnp.int32)
    positions = (own_blocks[:, None] * half_rows + local_offsets[None, :]).reshape(tok_rows)
    key_pos = (block_map[:, None] * half_rows + local_offsets[None, :]).reshape(seq_rows)
    length = lengths[0]
    own_live = positions < length
    live_rows = own_live.astype(jnp.float32)
    key_live = key_pos < length
    gain_first = norm1_gain.astype(jnp.float32)
    gain_second = norm2_gain.astype(jnp.float32)
    token_rows = tokens[0].astype(jnp.float32)
    normal_first, normed_first, inverse_first = norm_forward(
        token_rows, gain_first, norm1_shift.astype(jnp.float32)
    )
    normal_second, normed_second, inverse_second = norm_forward(
        token_rows, gain_second, norm2_shift.astype(jnp.float32)
    )
    attn_in = normal_first.astype(jnp.bfloat16)
    mlp_in = normal_second.astype(jnp.bfloat16)
    projected = (
        jnp.dot(attn_in, qkv_weight, preferred_element_type=jnp.float32)
        + qkv_bias.astype(jnp.float32)
    ).reshape(tok_rows, 3, head_count, head_size)
    cosine_table, sine_table = rotary_tables(positions)
    queries = rotate_forward(projected[:, 0], cosine_table, sine_table).astype(jnp.bfloat16)
    key_own = (
        rotate_forward(projected[:, 1], cosine_table, sine_table)
        .astype(jnp.bfloat16)
        .reshape(tok_rows, model_width)
    )
    value_own = projected[:, 2].astype(jnp.bfloat16).reshape(tok_rows, model_width)
    keys_all, values_all = (
        lax.all_gather(key_own, "ctx", axis=0, tiled=True),
        lax.all_gather(value_own, "ctx", axis=0, tiled=True),
    )
    block_len = math.gcd(seq_rows, 1024)
    block_count = seq_rows // block_len
    key_stack = keys_all.reshape(block_count, block_len, head_count, head_size)
    value_stack = values_all.reshape(block_count, block_len, head_count, head_size)
    pos_stack = key_pos.reshape(block_count, block_len)
    live_stack = key_live.reshape(block_count, block_len)

    def stats_step(running, key_part):
        key_block, pos_block, live_block = key_part
        scores, allowed = masked_scores(queries, key_block, positions, pos_block, live_block)
        peak_score = jnp.maximum(running[0], jnp.max(scores, axis=-1))
        exp_total = running[1] * jnp.exp(running[0] - peak_score) + jnp.sum(
            jnp.where(allowed[None], jnp.exp(scores - peak_score[..., None]), 0.0), axis=-1
        )
        return ((peak_score, exp_total), None)

    start_peak = jnp.full((head_count, tok_rows), -1e30, jnp.float32)
    final_state = lax.scan(
        stats_step, (start_peak, jnp.zeros_like(start_peak)), (key_stack, pos_stack, live_stack)
    )[0]
    log_total = final_state[0] + jnp.log(final_state[1])

    def value_step(running, key_part):
        key_block, value_block, pos_block, live_block = key_part
        scores = masked_scores(queries, key_block, positions, pos_block, live_block)[0]
        probability = jnp.exp(scores - log_total[..., None]).astype(jnp.bfloat16)
        return (
            running
            + jnp.einsum(
                "hqk,khd->qhd", probability, value_block, preferred_element_type=jnp.float32
            ),
            None,
        )

    zero_heads = jnp.zeros((tok_rows, head_count, head_size), jnp.float32)
    attended = lax.scan(value_step, zero_heads, (key_stack, value_stack, pos_stack, live_stack))[0]
    context_low = attended.reshape(tok_rows, model_width).astype(jnp.bfloat16)
    hidden = jnp.dot(mlp_in, up_weight, preferred_element_type=jnp.float32) + up_bias.astype(
        jnp.float32
    )
    activated, gelu_pull = jax.vjp(partial(jax.nn.gelu, approximate=False), hidden)
    act_low = activated.astype(jnp.bfloat16)
    branch = (
        jnp.dot(context_low, out_weight, preferred_element_type=jnp.float32)
        + out_bias.astype(jnp.float32)
        + jnp.dot(act_low, down_weight, preferred_element_type=jnp.float32)
        + down_bias.astype(jnp.float32)
    )
    output_rows = (live_rows[:, None] * (token_rows + branch)).astype(jnp.bfloat16)
    cot_rows = cotangent[0].astype(jnp.float32)
    grad_branch = (live_rows[:, None] * cot_rows).astype(jnp.bfloat16)
    grad_w_out = jnp.einsum(
        "tc,td->cd", context_low, grad_branch, preferred_element_type=jnp.float32
    )
    grad_w_down = jnp.einsum("tc,td->cd", act_low, grad_branch, preferred_element_type=jnp.float32)
    grad_branch_sum = jnp.sum(grad_branch.astype(jnp.float32), axis=0)
    grad_act = jnp.einsum("td,cd->tc", grad_branch, down_weight, preferred_element_type=jnp.float32)
    grad_hidden = gelu_pull(grad_act)[0].astype(jnp.bfloat16)
    grad_w_up = jnp.einsum("tc,td->cd", mlp_in, grad_hidden, preferred_element_type=jnp.float32)
    grad_b_up = jnp.sum(grad_hidden.astype(jnp.float32), axis=0)
    grad_mlp_in = jnp.einsum(
        "td,cd->tc", grad_hidden, up_weight, preferred_element_type=jnp.float32
    )
    grad_context = jnp.einsum(
        "td,cd->tc", grad_branch, out_weight, preferred_element_type=jnp.float32
    ).astype(jnp.bfloat16)
    grad_heads = grad_context.reshape(tok_rows, head_count, head_size)
    row_dots = jnp.sum(grad_heads.astype(jnp.float32) * attended, axis=-1).T

    def grad_step(running, key_part):
        key_block, value_block, pos_block, live_block = key_part
        prob_low, grad_score = score_grads(
            queries,
            key_block,
            value_block,
            grad_heads,
            positions,
            pos_block,
            live_block,
            log_total,
            row_dots,
        )
        query_sum = running + jnp.einsum(
            "hqk,khd->qhd", grad_score, key_block, preferred_element_type=jnp.float32
        )
        key_term = jnp.einsum(
            "hqk,qhd->khd", grad_score, queries, preferred_element_type=jnp.float32
        )
        value_term = jnp.einsum(
            "hqk,qhd->khd", prob_low, grad_heads, preferred_element_type=jnp.float32
        )
        return (query_sum, (key_term, value_term))

    query_grad, term_stacks = lax.scan(
        grad_step, zero_heads, (key_stack, value_stack, pos_stack, live_stack)
    )
    key_grad, value_grad = (
        lax.psum_scatter(
            term_stacks[0].reshape(seq_rows, model_width).astype(jnp.bfloat16),
            "ctx",
            scatter_dimension=0,
            tiled=True,
        ).astype(jnp.float32),
        lax.psum_scatter(
            term_stacks[1].reshape(seq_rows, model_width).astype(jnp.bfloat16),
            "ctx",
            scatter_dimension=0,
            tiled=True,
        ).astype(jnp.float32),
    )
    key_grad = key_grad.reshape(tok_rows, head_count, head_size)
    value_grad = value_grad.reshape(tok_rows, head_count, head_size)
    grad_projected = (
        jnp.stack(
            [
                rotate_backward(query_grad, cosine_table, sine_table),
                rotate_backward(key_grad, cosine_table, sine_table),
                value_grad,
            ],
            axis=1,
        )
        .reshape(tok_rows, 3 * model_width)
        .astype(jnp.bfloat16)
    )
    grad_w_qkv = jnp.einsum(
        "tc,td->cd", attn_in, grad_projected, preferred_element_type=jnp.float32
    )
    grad_b_qkv = jnp.sum(grad_projected.astype(jnp.float32), axis=0)
    grad_attn_in = jnp.einsum(
        "td,cd->tc", grad_projected, qkv_weight, preferred_element_type=jnp.float32
    )
    grad_input_first, grad_gain_first, grad_shift_first = norm_backward(
        grad_attn_in, normed_first, inverse_first, gain_first
    )
    grad_input_second, grad_gain_second, grad_shift_second = norm_backward(
        grad_mlp_in, normed_second, inverse_second, gain_second
    )
    grad_input = live_rows[:, None] * cot_rows + grad_input_first + grad_input_second
    shares = (
        lax.psum_scatter(
            grad_gain_first.astype(jnp.bfloat16), "wsh", scatter_dimension=0, tiled=True
        ).astype(jnp.float32),
        lax.psum_scatter(
            grad_shift_first.astype(jnp.bfloat16), "wsh", scatter_dimension=0, tiled=True
        ).astype(jnp.float32),
        lax.psum_scatter(
            grad_gain_second.astype(jnp.bfloat16), "wsh", scatter_dimension=0, tiled=True
        ).astype(jnp.float32),
        lax.psum_scatter(
            grad_shift_second.astype(jnp.bfloat16), "wsh", scatter_dimension=0, tiled=True
        ).astype(jnp.float32),
        lax.psum_scatter(
            grad_w_qkv.astype(jnp.bfloat16), "wsh", scatter_dimension=0, tiled=True
        ).astype(jnp.float32),
        lax.psum_scatter(
            grad_b_qkv.astype(jnp.bfloat16), "wsh", scatter_dimension=0, tiled=True
        ).astype(jnp.float32),
        lax.psum_scatter(
            grad_w_out.astype(jnp.bfloat16), "wsh", scatter_dimension=0, tiled=True
        ).astype(jnp.float32),
        lax.psum_scatter(
            grad_branch_sum.astype(jnp.bfloat16), "wsh", scatter_dimension=0, tiled=True
        ).astype(jnp.float32),
        lax.psum_scatter(
            grad_w_up.astype(jnp.bfloat16), "wsh", scatter_dimension=0, tiled=True
        ).astype(jnp.float32),
        lax.psum_scatter(
            grad_b_up.astype(jnp.bfloat16), "wsh", scatter_dimension=0, tiled=True
        ).astype(jnp.float32),
        lax.psum_scatter(
            grad_w_down.astype(jnp.bfloat16), "wsh", scatter_dimension=0, tiled=True
        ).astype(jnp.float32),
        lax.psum_scatter(
            grad_branch_sum.astype(jnp.bfloat16), "wsh", scatter_dimension=0, tiled=True
        ).astype(jnp.float32),
    )
    totals = (
        lax.psum(shares[0].astype(jnp.bfloat16), "ctx").astype(jnp.float32),
        lax.psum(shares[1].astype(jnp.bfloat16), "ctx").astype(jnp.float32),
        lax.psum(shares[2].astype(jnp.bfloat16), "ctx").astype(jnp.float32),
        lax.psum(shares[3].astype(jnp.bfloat16), "ctx").astype(jnp.float32),
        lax.psum(shares[4].astype(jnp.bfloat16), "ctx").astype(jnp.float32),
        lax.psum(shares[5].astype(jnp.bfloat16), "ctx").astype(jnp.float32),
        lax.psum(shares[6].astype(jnp.bfloat16), "ctx").astype(jnp.float32),
        lax.psum(shares[7].astype(jnp.bfloat16), "ctx").astype(jnp.float32),
        lax.psum(shares[8].astype(jnp.bfloat16), "ctx").astype(jnp.float32),
        lax.psum(shares[9].astype(jnp.bfloat16), "ctx").astype(jnp.float32),
        lax.psum(shares[10].astype(jnp.bfloat16), "ctx").astype(jnp.float32),
        lax.psum(shares[11].astype(jnp.bfloat16), "ctx").astype(jnp.float32),
    )
    return (
        output_rows[None],
        grad_input[None],
        totals[0],
        totals[1],
        totals[2],
        totals[3],
        totals[4],
        totals[5],
        totals[6],
        totals[7],
        totals[8],
        totals[9],
        totals[10],
        totals[11],
    )


def solution(mesh):
    placed = (
        P("wsh", "ctx", None),
        P("wsh"),
        P("wsh"),
        P("wsh"),
        P("wsh"),
        P("wsh", None),
        P("wsh"),
        P("wsh", None),
        P("wsh"),
        P("wsh", None),
        P("wsh"),
        P("wsh", None),
        P("wsh"),
        P("wsh"),
        P(),
        P("wsh", "ctx", None),
    )
    return jax.shard_map(
        shards,
        mesh=mesh,
        in_specs=placed,
        out_specs=(
            P("wsh", "ctx", None),
            P("wsh", "ctx", None),
            P("wsh"),
            P("wsh"),
            P("wsh"),
            P("wsh"),
            P("wsh", None),
            P("wsh"),
            P("wsh", None),
            P("wsh"),
            P("wsh", None),
            P("wsh"),
            P("wsh", None),
            P("wsh"),
        ),
        check_vma=False,
    )
```

profile of v0, /device:TPU:0, one launch (start us, length us, event | category | flops | bytes accessed | tf_op | source)
XLA Modules:
  0.0 1370.9 jit_solution(6145052709611915597)
XLA Ops:
  9.0 5.3 all-gather
  23.6 69.1 %all-gather.14.cloned.1.call-done = bf16[1024,3072]{1,0:T(8,128)(2,1)} async-done(((bf16[512,3072]{1,0:T(8,128)(2,1)}), bf16[1024,3072]{1,0:T(8,128)(2,1)}) %all-gather.14.cloned.1.call-update) | async-done | bytes 6291472 | tf_op jit(solution)/shard_map/all_gather | solution.py:116
  92.7 6.4 convolution_add_fusion.1
  107.6 19.8 %all-gather.20.cloned.1.call-done = bf16[1024,1024]{1,0:T(8,128)(2,1)} async-done(((bf16[512,1024]{1,0:T(8,128)(2,1)}), bf16[1024,1024]{1,0:T(8,128)(2,1)}) %all-gather.20.cloned.1.call-update) | async-done | bytes 2097168 | tf_op jit(solution)/shard_map/all_gather | solution.py:118
  133.1 75.2 %all-gather.18.cloned.1.call-done = bf16[4096,1024]{0,1:T(8,128)(2,1)} async-done(((bf16[256,1024]{0,1:T(8,128)(2,1)}), bf16[4096,1024]{0,1:T(8,128)(2,1)}) %all-gather.18.cloned.1.call-update) | async-done | bytes 8388624 | tf_op jit(solution)/shard_map/all_gather | solution.py:178
  208.3 14.7 %reshape.388 = bf16[4,1024,16,64]{1,0,3,2:T(4,128)(2,1)} reshape(bf16[4096,1024]{0,1:T(8,128)(2,1)} %all-gather.18.cloned.1.call-done) | data formatting | bytes 16777216 | tf_op jit(solution)/shard_map/reshape | solution.py:183
  223.0 9.4 copy.59
  232.5 78.5 %while.39 = (s32[]{:T(128)}, f32[16,256]{1,0:T(8,128)S(1)}, f32[16,256]{1,0:T(8,128)S(1)}, s32[4,1024]{1,0:T(4,128)S(1)}, pred[4,1024]{1,0:T(4,128)(4,1)S(1)}, /...) while((s32[]{:T(128)}, f32[16,256]{1,0:T(8,128)S(1)}, ...), condition=%wide.region_5.6_spmd.clone, body=%wide.region_2.5_spmd.clone.sunk | while | flops 570970368 | bytes 37193340 | solution.py:198
  232.9 10.1 fusion.185
  243.0 8.9 select_reduce_fusion.2
  252.4 10.1 fusion.185
  262.5 8.0 select_reduce_fusion.2
  271.1 10.2 fusion.185
  281.3 8.2 select_reduce_fusion.2
  290.0 12.3 fusion.185
  302.2 8.7 select_reduce_fusion.2
  311.0 14.5 %reshape.387 = bf16[4,1024,16,64]{1,0,3,2:T(4,128)(2,1)} reshape(bf16[4096,1024]{0,1:T(8,128)(2,1)} %all-gather.16.cloned.1.call-done) | data formatting | bytes 16777216 | tf_op jit(solution)/shard_map/reshape | solution.py:184
  325.5 9.6 copy.58
  335.1 33.7 %while.40 = (s32[]{:T(128)}, f32[256,16,64]{0,2,1:T(8,128)S(1)}, bf16[4,1024,16,64]{1,3,2,0:T(8,128)(2,1)}, s32[4,1024]{1,0:T(4,128)S(1)}, pred[4,1024]{1,0:T(4,...) while((s32[]{:T(128)}, f32[256,16,64]{0,2,1:T(8,128)S(1)}, ...), condition=%wide.region_7.8_spmd.clone, body=%wide.region_6.7_spmd.clone.sunk | while | flops 1091567872 | bytes 7374983 | solution.py:216
  336.0 7.8 fusion.190
  344.3 7.8 fusion.190
  352.6 7.8 fusion.190
  361.0 7.8 fusion.190
  369.7 184.2 %while.41 = (s32[]{:T(128)}, f32[256,16,64]{0,2,1:T(8,128)S(1)}, bf16[4,1024,16,64]{1,3,2,0:T(8,128)(2,1)}, bf16[4,1024,16,64]{1,3,2,0:T(8,128)(2,1)}, bf16[4,10...) while((s32[]{:T(128)}, f32[256,16,64]{0,2,1:T(8,128)S(1)}, ...), condition=%wide.region_10.11_spmd.clone, body=%wide.region_9.10_spmd.clone.sunk | while | flops 2731540736 | bytes 128782016 | solution.py:274
  370.2 9.7 fusion.201
  379.9 10.9 fusion.202
  398.2 7.4 fusion.203
  405.6 12.5 bitcast_dynamic-update-slice_fusion.5
  418.6 9.7 fusion.201
  428.3 10.9 fusion.202
  446.5 5.6 fusion.203
  452.1 11.2 bitcast_dynamic-update-slice_fusion.5
  463.8 9.7 fusion.201
  473.5 10.9 fusion.202
  491.8 5.6 fusion.203
  497.4 11.2 bitcast_dynamic-update-slice_fusion.5
  509.0 9.7 fusion.201
  518.8 10.9 fusion.202
  537.0 5.6 fusion.203
  542.6 11.2 bitcast_dynamic-update-slice_fusion.5
  553.9 11.1 copy.63
  565.0 12.1 copy.70
  577.2 11.1 copy.64
  588.3 13.1 copy.71
  615.2 16.3 %multiply_convert_fusion = (bf16[256,4096]{1,0:T(8,128)(2,1)}, f32[256,4096]{1,0:T(8,128)}, f32[256,4096]{1,0:T(8,128)}) fusion(f32[4096]{0:T(1024)S(1)} %convert_element_type.256, bf16[1024,4096]{1,0:T(8,128)(2,1)} %all-gather.22.cloned.1.call-done, bf16[1,256,1024]{2,1,0:T(8,128)(2,1)S(1)} %copy-done.2, f32[1024]{0:T(1024)S(1)} %bitcast.361, ...), kind=kOutput, calls=%fused_computation.72 | convolution fusion | flops 2218262528 | bytes 19425280 | tf_op jit(solution)/shard_map/dot_general | solution.py:218
  631.4 11.5 fusion.137
  644.3 5.9 convolution_convert_fusion.1
  650.7 7.3 convolution_convert_fusion
  661.3 19.2 %reduce-scatter.7.cloned.1.call-done = bf16[256,1024]{0,1:T(8,128)(2,1)} async-done(((bf16[4096,1024]{0,1:T(8,128)(2,1)}), bf16[256,1024]{0,1:T(8,128)(2,1)}) %reduce-scatter.7.cloned.1.call-update) | async-done | bytes 524304 | tf_op jit(solution)/shard_map/reduce_scatter | solution.py:278
  682.9 106.9 %reduce-scatter.9.cloned.1.call-done = bf16[256,1024]{0,1:T(8,128)(2,1)} async-done(((bf16[4096,1024]{0,1:T(8,128)(2,1)}), bf16[256,1024]{0,1:T(8,128)(2,1)}) %reduce-scatter.9.cloned.1.call-update) | async-done | bytes 524304 | tf_op jit(solution)/shard_map/reduce_scatter | solution.py:284
  792.4 4.8 convolution_convert_fusion.2
  797.3 94.4 %reduce-scatter.15.cloned.1.call-done = bf16[512,4096]{1,0:T(8,128)(2,1)} async-done(((bf16[1024,4096]{1,0:T(8,128)(2,1)}), bf16[512,4096]{1,0:T(8,128)(2,1)}) %reduce-scatter.15.cloned.1.call-update) | async-done | bytes 4194320 | tf_op jit(solution)/shard_map/reduce_scatter | solution.py:344
  891.7 101.5 %reduce-scatter.17.cloned.1.call-done = bf16[2048,1024]{1,0:T(8,128)(2,1)} async-done(((bf16[4096,1024]{1,0:T(8,128)(2,1)}), bf16[2048,1024]{1,0:T(8,128)(2,1)}) %reduce-scatter.17.cloned.1.call-update) | async-done | bytes 4194320 | tf_op jit(solution)/shard_map/reduce_scatter | solution.py:350
  993.2 34.1 %reduce-scatter.13.cloned.1.call-done = bf16[512,1024]{1,0:T(8,128)(2,1)} async-done(((bf16[1024,1024]{1,0:T(8,128)(2,1)}), bf16[512,1024]{1,0:T(8,128)(2,1)}) %reduce-scatter.13.cloned.1.call-update) | async-done | bytes 1048592 | tf_op jit(solution)/shard_map/reduce_scatter | solution.py:338
  1027.3 79.9 %reduce-scatter.11.cloned.1.call-done = bf16[512,3072]{1,0:T(8,128)(2,1)} async-done(((bf16[1024,3072]{1,0:T(8,128)(2,1)}), bf16[512,3072]{1,0:T(8,128)(2,1)}) %reduce-scatter.11.cloned.1.call-update) | async-done | bytes 3145744 | tf_op jit(solution)/shard_map/reduce_scatter | solution.py:332
  1114.8 4.5 all-gather.6
  1119.5 6.6 fusion.139
  1126.2 6.0 fusion.138
  1133.8 5.8 fusion.101
  1139.7 7.1 all-reduce.9
  1147.2 61.8 %all-reduce.7 = (bf16[512]{0:T(512)(128)(2,1)S(1)}, bf16[512]{0:T(512)(128)(2,1)S(1)}, bf16[512]{0:T(512)(128)(2,1)S(1)}, bf16[512]{0:T(512)(128)(2,1)S(1)}, bf1...) all-reduce(bf16[512]{0:T(512)(128)(2,1)S(1)} %dynamic-slice.1, ...), channel_id=1, replica_groups=mesh['ctx'=16,'wsh'=2] {'ctx'}, use_global_device_ids=true, to_apply=%region_19.20 | all-reduce | flops 6144 | bytes 24576 | tf_op jit(solution)/shard_map/psum | solution.py:358
  1214.3 133.0 %all-reduce.12.cloned.1.call-done = (bf16[512,3072]{1,0:T(8,128)(2,1)}, bf16[512,1024]{1,0:T(8,128)(2,1)}, bf16[512,4096]{1,0:T(8,128)(2,1)}, bf16[2048,1024]{1,0:T(8,128)(2,1)}) async-done(((bf16[512,3072]{1,0:T(8,128)(2,1)}, bf16[512,1024]{1,0:T(8,128)(2,1)}, bf16[512,4096]{1,0:T(8,128)(2,1)}, bf16[2048,1024]{1,0:T(8,128)(2,1)}), (bf16[512,3072]{1,0:T(8,128)(2,1)}, bf16[512,1024]{1,0:T(8,128)(2,1)}, ...) | async-done | bytes 12582928 | tf_op jit(solution)/shard_map/psum | solution.py:362
  1347.2 6.8 convert_element_type.292
  1354.1 4.4 convert_element_type.295
  (265 shorter events, 102.9 us)
Async XLA Ops:
  7.2 1.6 copy-start.1
  7.2 1.8 copy-start.32
  7.2 7.0 copy-start.33
  7.2 11.4 copy-start.31
  7.2 15.8 %copy-start.38 = (s32[32]{0:T(128)S(1)}, s32[32]{0:T(128)}, u32[]{:S(2)}) copy-start(s32[32]{0:T(128)} %param.36) | copy-start | bytes 388
  7.2 85.5 %all-gather.14.cloned.1.call-start = ((), (), s32[]{:S(2)}) async-start(), calls=%async_computation.6 | async-start | bytes 9437184 | tf_op jit(solution)/shard_map/all_gather | solution.py:116
  8.0 119.5 %all-gather.20.cloned.1.call-start = ((), (), s32[]{:S(2)}) async-start(), calls=%async_computation.9 | async-start | bytes 3145728 | tf_op jit(solution)/shard_map/all_gather | solution.py:118
  8.7 199.6 %all-gather.18.cloned.1.call-start = ((), (), s32[]{:S(2)}) async-start(), calls=%async_computation.8 | async-start | bytes 8912896 | tf_op jit(solution)/shard_map/all_gather | solution.py:178
  9.0 83.8 %copy-start.25 = (f32[256]{0:T(256)}, f32[256]{0:T(256)S(1)}, u32[]{:S(2)}) copy-start(f32[256]{0:T(256)S(1)} %broadcast_multiply_fusion.4) | copy-start | bytes 3076
  14.2 78.5 %copy-start.15 = (f32[2,1,512]{2,1,0:T(1,128)}, f32[2,1,512]{2,1,0:T(1,128)S(1)}, u32[]{:S(2)}) copy-start(f32[2,1,512]{2,1,0:T(1,128)S(1)} %convert_element_type.298) | copy-start | bytes 12292
  18.6 74.1 %copy-start.17 = (f32[2,1,512]{2,1,0:T(1,128)}, f32[2,1,512]{2,1,0:T(1,128)S(1)}, u32[]{:S(2)}) copy-start(f32[2,1,512]{2,1,0:T(1,128)S(1)} %convert_element_type.299) | copy-start | bytes 12292
  23.5 69.3 %copy-start.27 = (f32[256]{0:T(256)}, f32[256]{0:T(256)S(1)}, u32[]{:S(2)}) copy-start(f32[256]{0:T(256)S(1)} %add_rsqrt_fusion) | copy-start | bytes 3076
  23.6 78.4 %copy-start.21 = (f32[256,8]{0,1:T(8,128)}, f32[256,8]{0,1:T(8,128)S(1)}, u32[]{:S(2)}) copy-start(f32[256,8]{0,1:T(8,128)S(1)} %get-tuple-element.483) | copy-start | bytes 24580
  23.6 78.4 %copy-start.23 = (f32[256,8]{0,1:T(8,128)}, f32[256,8]{0,1:T(8,128)S(1)}, u32[]{:S(2)}) copy-start(f32[256,8]{0,1:T(8,128)S(1)} %get-tuple-element.484) | copy-start | bytes 24580
  101.9 1.0 copy-start.10
  104.4 206.5 %all-gather.16.cloned.1.call-start = ((), (), s32[]{:S(2)}) async-start(), calls=%async_computation.7 | async-start | bytes 8912896 | tf_op jit(solution)/shard_map/all_gather | solution.py:179
  105.4 22.0 %copy-start.3 = (bf16[1,256,1024]{2,1,0:T(8,128)(2,1)S(1)}, bf16[1,256,1024]{2,1,0:T(8,128)(2,1)}, u32[]{:S(2)}) copy-start(bf16[1,256,1024]{2,1,0:T(8,128)(2,1)} %param.37) | copy-start | bytes 1572868
  105.4 509.7 %all-gather.22.cloned.1.call-start = ((), (), s32[]{:S(2)}) async-start(), calls=%async_computation.10 | async-start | bytes 12582912 | tf_op jit(solution)/shard_map/all_gather | solution.py:120
  106.0 27.0 %copy-start.14 = (bf16[256,16,8]{0,2,1:T(8,128)(2,1)S(1)}, bf16[256,16,8]{0,2,1:T(8,128)(2,1)}, u32[]{:S(2)}) copy-start(bf16[256,16,8]{0,2,1:T(8,128)(2,1)} %get-tuple-element.474) | copy-start | bytes 196612
  106.0 525.4 %all-gather.24.cloned.1.call-start = ((), (), s32[]{:S(2)}) async-start(), calls=%async_computation.11 | async-start | bytes 12582912 | tf_op jit(solution)/shard_map/all_gather | solution.py:122
  106.6 573.9 %reduce-scatter.7.cloned.1.call-start = ((), (), s32[]{:S(2)}) async-start(), calls=%async_computation.12 | async-start | bytes 8912896 | tf_op jit(solution)/shard_map/reduce_scatter | solution.py:278
  107.6 115.5 %copy-start.19 = (f32[256]{0:T(256)}, f32[256]{0:T(256)S(1)}, u32[]{:S(2)}) copy-start(f32[256]{0:T(256)S(1)} %fusion.125) | copy-start | bytes 3076
  390.8 3.4 copy-start
  439.1 3.4 copy-start
  484.4 3.4 copy-start
  529.6 3.4 copy-start
  577.1 212.6 %reduce-scatter.9.cloned.1.call-start = ((), (), s32[]{:S(2)}) async-start(), calls=%async_computation.13 | async-start | bytes 8912896 | tf_op jit(solution)/shard_map/reduce_scatter | solution.py:284
  601.4 0.7 copy-start.34
  601.4 5.0 copy-start.35
  601.4 9.4 copy-start.30
  601.4 13.7 %copy-start.2 = (bf16[1,256,1024]{2,1,0:T(8,128)(2,1)S(1)}, bf16[1,256,1024]{2,1,0:T(8,128)(2,1)}, u32[]{:S(2)}) copy-start(bf16[1,256,1024]{2,1,0:T(8,128)(2,1)} %param.22) | copy-start | bytes 1572868
  601.4 13.7 %copy-start.26 = (f32[256]{0:T(256)S(1)}, f32[256]{0:T(256)}, u32[]{:S(2)}) copy-start(f32[256]{0:T(256)} %copy-done.25) | copy-start | bytes 3076
  601.4 13.7 %copy-start.28 = (f32[256]{0:T(256)S(1)}, f32[256]{0:T(256)}, u32[]{:S(2)}) copy-start(f32[256]{0:T(256)} %copy-done.27) | copy-start | bytes 3076
  601.4 290.3 %reduce-scatter.15.cloned.1.call-start = ((), (), s32[]{:S(2)}) async-start(), calls=%async_computation.16 | async-start | bytes 12582912 | tf_op jit(solution)/shard_map/reduce_scatter | solution.py:344
  615.1 16.3 %copy-start.4 = (bf16[1,256,1024]{2,1,0:T(8,128)(2,1)S(1)}, bf16[1,256,1024]{2,1,0:T(8,128)(2,1)}, u32[]{:S(2)}) copy-start(bf16[1,256,1024]{2,1,0:T(8,128)(2,1)} %param.37) | copy-start | bytes 1572868
  615.1 16.3 %copy-start.20 = (f32[256]{0:T(256)S(1)}, f32[256]{0:T(256)}, u32[]{:S(2)}) copy-start(f32[256]{0:T(256)} %copy-done.19) | copy-start | bytes 3076
  642.9 1.4 copy-start.12
  650.2 343.0 %reduce-scatter.17.cloned.1.call-start = ((), (), s32[]{:S(2)}) async-start(), calls=%async_computation.17 | async-start | bytes 12582912 | tf_op jit(solution)/shard_map/reduce_scatter | solution.py:350
  658.0 1.0 copy-start.6
  658.1 369.3 %reduce-scatter.13.cloned.1.call-start = ((), (), s32[]{:S(2)}) async-start(), calls=%async_computation.15 | async-start | bytes 3145728 | tf_op jit(solution)/shard_map/reduce_scatter | solution.py:338
  659.1 23.6 %copy-start.22 = (f32[256,8]{0,1:T(8,128)S(1)}, f32[256,8]{0,1:T(8,128)}, u32[]{:S(2)}) copy-start(f32[256,8]{0,1:T(8,128)} %copy-done.21) | copy-start | bytes 24580
  659.1 23.6 %copy-start.24 = (f32[256,8]{0,1:T(8,128)S(1)}, f32[256,8]{0,1:T(8,128)}, u32[]{:S(2)}) copy-start(f32[256,8]{0,1:T(8,128)} %copy-done.23) | copy-start | bytes 24580
  661.2 446.0 %reduce-scatter.11.cloned.1.call-start = ((), (), s32[]{:S(2)}) async-start(), calls=%async_computation.14 | async-start | bytes 9437184 | tf_op jit(solution)/shard_map/reduce_scatter | solution.py:332
  680.5 112.0 %copy-start.16 = (f32[2,1,512]{2,1,0:T(1,128)S(1)}, f32[2,1,512]{2,1,0:T(1,128)}, u32[]{:S(2)}) copy-start(f32[2,1,512]{2,1,0:T(1,128)} %copy-done.15) | copy-start | bytes 12292
  680.5 112.0 %copy-start.18 = (f32[2,1,512]{2,1,0:T(1,128)S(1)}, f32[2,1,512]{2,1,0:T(1,128)}, u32[]{:S(2)}) copy-start(f32[2,1,512]{2,1,0:T(1,128)} %copy-done.17) | copy-start | bytes 12292
  791.3 1.1 copy-start.5
  797.3 550.0 %all-reduce.12.cloned.1.call-start = ((), (), s32[]{:S(2)}) async-start(), calls=%async_computation.18 | async-start | bytes 25165824 | tf_op jit(solution)/shard_map/psum | solution.py:362
  1107.2 0.7 copy-start.39
  1107.2 3.2 copy-start.36
  1107.2 7.5 copy-start.37
  1119.5 6.6 copy-start.8
  1126.1 6.0 copy-start.11
  1210.3 153.3 %copy-start.29 = (f32[512]{0:T(512)}, f32[512]{0:T(512)S(1)}, u32[]{:S(2)}) copy-start(f32[512]{0:T(512)S(1)} %convert_element_type.290) | copy-start | bytes 6148
  1347.2 6.8 copy-start.7
  1354.1 4.4 copy-start.9
  1358.5 3.5 copy-start.13
Sparse Core Ops, SparseCore 0:
  9.6 83.0 all-gather.13
  94.3 33.1 all-gather.19
  130.2 78.0 all-gather.17
  210.9 76.2 all-gather.15
  288.6 102.1 all-gather.21
  392.2 103.9 all-gather.23
  577.3 103.1 reduce-scatter.6
  685.1 104.5 reduce-scatter.8
  792.6 99.0 reduce-scatter.14
  893.9 99.2 reduce-scatter.16
  995.5 31.8 reduce-scatter.12
  1030.1 77.0 reduce-scatter.10
  1111.8 235.4 all-reduce.11
where the time goes:
time: 1380 us; the launch traced here: 1370 us
  waiting for transfers between devices  736 us (53%)
  matrix products  320 us (23%)
  local copies, waits for them, and re-layouts  125 us (9%)
  blocking collectives  105 us (8%)
  other arithmetic  66.7 us (5%)
  between operations  17.3 us (1%)
    psum x1, waiting for transfers between devices, shards(): lax.psum(shares[4].astype(jnp.bfloat16), 'ctx').astype(jnp.float32)  133 us
    reduce_scatter x1, waiting for transfers between devices, shards(): lax.psum_scatter(term_stacks[1].reshape(seq_rows, model_width).astype(jnp...  107 us
    reduce_scatter x1, waiting for transfers between devices, shards(): lax.psum_scatter(grad_w_down.astype(jnp.bfloat16), 'wsh', scatter_dimensi...  102 us
    reduce_scatter x1, waiting for transfers between devices, shards(): lax.psum_scatter(grad_w_up.astype(jnp.bfloat16), 'wsh', scatter_dimension...  94.4 us
    dot_general x8, matrix products, masked_scores(): jnp.einsum('qhd,khd->hqk', query_rows, key_rows, preferred_element_type=j...  81.5 us
    reduce_scatter x1, waiting for transfers between devices, shards(): lax.psum_scatter(grad_w_qkv.astype(jnp.bfloat16), 'wsh', scatter_dimensio...  79.9 us
    all_gather x1, waiting for transfers between devices, shards(): lax.all_gather(key_own, 'ctx', axis=0, tiled=True)  75.2 us
    all_gather x1, waiting for transfers between devices, shards(): lax.all_gather(w_qkv, 'wsh', axis=0, tiled=True)  69.1 us
  transfers between devices with their start and end apart: 13, of which 10 were waited for; matrix products, arithmetic and copies ran while one was open for 35% of the time, Pallas kernels for 0%

commit v1 on v0

--- a/solution.py
+++ b/solution.py
@@ -4,6 +4,8 @@
 import jax
 import jax.numpy as jnp
 from jax import lax
+from jax.experimental import pallas as pl
+from jax.experimental.pallas import tpu as pltpu
 from jax.sharding import PartitionSpec as P
 
 H = 16
@@ -386,6 +388,387 @@
     )
 
 
+HB = 128
+NEG=-1e30
+f32=jnp.float32; bf16=jnp.bfloat16
+
+def _nn(a,b): return lax.dot_general(a,b,(((1,),(0,)),((),())),preferred_element_type=f32)
+def _nt(a,b): return lax.dot_general(a,b,(((1,),(1,)),((),())),preferred_element_type=f32)
+
+def attn_fwd_kernel(bm, x_ref, o_ref, lse_ref, q_s, kt_s, v_s, *, nblk, bq, bk):
+    def perm(i,_):
+        p=bm[i]; c=i//2; l=pl.multiple_of((i%2)*HB,HB); d=pl.multiple_of(p*HB,HB)
+        q_s[:,pl.ds(d,HB)]=x_ref[c,0:64,pl.ds(l,HB)]*bf16(0.125)
+        kt_s[pl.ds(d,HB),:]=x_ref[c,64:128,pl.ds(l,HB)].astype(f32).T.astype(bf16)
+        v_s[:,pl.ds(d,HB)]=x_ref[c,128:192,pl.ds(l,HB)]
+        return 0
+    lax.fori_loop(0,nblk,perm,0)
+    S=nblk*HB; nq=S//bq; r=bq//bk
+    def step(q,qo,ko,carry,mask):
+        m,l,acc=carry
+        s=_nn(kt_s[pl.ds(ko,bk),:],q)
+        if mask is not None: s=jnp.where(mask,s,NEG)
+        mn=jnp.maximum(m,jnp.max(s,axis=0,keepdims=True))
+        a=jnp.exp(m-mn); p=jnp.exp(s-mn)
+        l=l*a+jnp.sum(p,axis=0,keepdims=True)
+        acc=acc*a+_nn(v_s[:,pl.ds(ko,bk)],p.astype(bf16))
+        return mn,l,acc
+    ki=lax.broadcasted_iota(jnp.int32,(bk,bq),0); qi_=lax.broadcasted_iota(jnp.int32,(bk,bq),1)
+    def qloop(i,_):
+        qo=pl.multiple_of(i*bq,bq)
+        q=q_s[:,pl.ds(qo,bq)]
+        c=(jnp.full((1,bq),NEG,f32),jnp.zeros((1,bq),f32),jnp.zeros((64,bq),f32))
+        c=lax.fori_loop(0,i*r,lambda j,c: step(q,qo,pl.multiple_of(j*bk,bk),c,None),c)
+        for t in range(r):
+            c=step(q,qo,pl.multiple_of(qo+t*bk,bk),c,ki+t*bk<=qi_)
+        m,l,acc=c
+        q_s[:,pl.ds(qo,bq)]=(acc*(1.0/l)).astype(bf16)
+        lse_ref[:,pl.ds(qo,bq)]=m+jnp.log(l)
+        return 0
+    lax.fori_loop(0,nq,qloop,0)
+    def unperm(i,_):
+        p=bm[i]; c=i//2; l=pl.multiple_of((i%2)*HB,HB); d=pl.multiple_of(p*HB,HB)
+        o_ref[c,:,pl.ds(l,HB)]=q_s[:,pl.ds(d,HB)]
+        return 0
+    lax.fori_loop(0,nblk,unperm,0)
+
+def attn_fwd(bm,x,*,bq=512,bk=512):
+    n=x.shape[0]; S=n*256; nblk=2*n
+    bq=math.gcd(S,bq); bk=math.gcd(bq,bk)
+    return pl.pallas_call(
+        lambda *a: attn_fwd_kernel(*a,nblk=nblk,bq=bq,bk=bk),
+        out_shape=(jax.ShapeDtypeStruct((n,64,256),bf16),jax.ShapeDtypeStruct((1,S),f32)),
+        in_specs=[pl.BlockSpec(memory_space=pltpu.SMEM),pl.BlockSpec(memory_space=pltpu.VMEM)],
+        out_specs=(pl.BlockSpec(memory_space=pltpu.VMEM),pl.BlockSpec(memory_space=pltpu.VMEM)),
+        scratch_shapes=[pltpu.VMEM((64,S),bf16),pltpu.VMEM((S,64),bf16),pltpu.VMEM((64,S),bf16)],
+        compiler_params=pltpu.CompilerParams(vmem_limit_bytes=56<<20),name="attn_fwd")(bm,x)
+
+def attn_bwd_kernel(bm, x_ref, o_ref, do_ref, lse_ref, cs_ref, g_ref, q_s, kt_s, k_s, vt_s, do_s, dl_s, dq_s, dk_s, dv_s, *, nblk, bq, bk):
+    def perm(i,_):
+        p=bm[i]; c=i//2; l=pl.multiple_of((i%2)*HB,HB); d=pl.multiple_of(p*HB,HB)
+        q_s[:,pl.ds(d,HB)]=x_ref[c,0:64,pl.ds(l,HB)]*bf16(0.125)
+        k=x_ref[c,64:128,pl.ds(l,HB)]
+        k_s[:,pl.ds(d,HB)]=k*bf16(0.125)
+        kt_s[pl.ds(d,HB),:]=k.astype(f32).T.astype(bf16)
+        vt_s[pl.ds(d,HB),:]=x_ref[c,128:192,pl.ds(l,HB)].astype(f32).T.astype(bf16)
+        do=do_ref[c,:,pl.ds(l,HB)]
+        do_s[:,pl.ds(d,HB)]=do
+        dl_s[:,pl.ds(d,HB)]=jnp.sum(do.astype(f32)*o_ref[c,:,pl.ds(l,HB)].astype(f32),axis=0,keepdims=True)
+        return 0
+    lax.fori_loop(0,nblk,perm,0)
+    S=nblk*HB; nq=S//bq; r=bq//bk
+    dk_s[...]=jnp.zeros_like(dk_s); dv_s[...]=jnp.zeros_like(dv_s)
+    def step(q,do,lse,dl,ko,dq,mask):
+        s=_nn(kt_s[pl.ds(ko,bk),:],q)
+        p=jnp.exp(s-lse)
+        if mask is not None: p=jnp.where(mask,p,0.0)
+        dp=_nn(vt_s[pl.ds(ko,bk),:],do)
+        ds=(p*(dp-dl)).astype(bf16)
+        pb=p.astype(bf16)
+        dv_s[:,pl.ds(ko,bk)]+=_nt(do,pb)
+        dk_s[:,pl.ds(ko,bk)]+=_nt(q,ds)
+        return dq+_nn(k_s[:,pl.ds(ko,bk)],ds)
+    ki=lax.broadcasted_iota(jnp.int32,(bk,bq),0); qi_=lax.broadcasted_iota(jnp.int32,(bk,bq),1)
+    def qloop(i,_):
+        qo=pl.multiple_of(i*bq,bq)
+        q=q_s[:,pl.ds(qo,bq)]; do=do_s[:,pl.ds(qo,bq)]; lse=lse_ref[:,pl.ds(qo,bq)]; dl=dl_s[:,pl.ds(qo,bq)]
+        dq=jnp.zeros((64,bq),f32)
+        dq=lax.fori_loop(0,i*r,lambda j,c: step(q,do,lse,dl,pl.multiple_of(j*bk,bk),c,None),dq)
+        for t in range(r):
+            dq=step(q,do,lse,dl,pl.multiple_of(qo+t*bk,bk),dq,ki+t*bk<=qi_)
+        dq_s[:,pl.ds(qo,bq)]=dq
+        return 0
+    lax.fori_loop(0,nq,qloop,0)
+    def unperm(i,_):
+        p=bm[i]; c=i//2; l=pl.multiple_of((i%2)*HB,HB); d=pl.multiple_of(p*HB,HB)
+        cos=cs_ref[0:8,pl.ds(d,HB)]; sin=cs_ref[8:16,pl.ds(d,HB)]
+        for n_,src in ((0,dq_s),(1,dk_s)):
+            g=src[:,pl.ds(d,HB)]
+            a=g[0:8]; b=g[8:16]
+            full=jnp.concatenate([a*cos+b*sin,b*cos-a*sin,g[16:64]],axis=0)
+            g_ref[c,64*n_:64*n_+64,pl.ds(l,HB)]=full.astype(bf16)
+        g_ref[c,128:192,pl.ds(l,HB)]=dv_s[:,pl.ds(d,HB)].astype(bf16)
+        return 0
+    lax.fori_loop(0,nblk,unperm,0)
+
+def attn_bwd(bm,x,o,do,lse,cs,*,bq=512,bk=512):
+    n=x.shape[0]; S=n*256; nblk=2*n
+    bq=math.gcd(S,bq); bk=math.gcd(bq,bk)
+    vm=pl.BlockSpec(memory_space=pltpu.VMEM)
+    return pl.pallas_call(
+        lambda *a: attn_bwd_kernel(*a,nblk=nblk,bq=bq,bk=bk),
+        out_shape=jax.ShapeDtypeStruct((n,192,256),bf16),
+        in_specs=[pl.BlockSpec(memory_space=pltpu.SMEM)]+[vm]*5,
+        out_specs=vm,
+        scratch_shapes=[pltpu.VMEM((64,S),bf16),pltpu.VMEM((S,64),bf16),pltpu.VMEM((64,S),bf16),pltpu.VMEM((S,64),bf16),pltpu.VMEM((64,S),bf16),
+                        pltpu.VMEM((1,S),f32),pltpu.VMEM((64,S),f32),pltpu.VMEM((64,S),f32),pltpu.VMEM((64,S),f32)],
+        compiler_params=pltpu.CompilerParams(vmem_limit_bytes=56<<20),name="attn_bwd")(bm,x,o,do,lse,cs)
+
+
+SWAP = [(0, 1), (1, 0)]
+
+
+def fast_fits(mesh):
+    return mesh.shape["wsh"] == 2 and mesh.shape["ctx"] == H
+
+
+def mlp_kernel(x_ref, dy_ref, wu_ref, wd_ref, bu_ref, y_ref, dx_ref, gu_ref, gd_ref, gb_ref, xt_s):
+    first = pl.program_id(0) == 0
+
+    @pl.when(first)
+    def _():
+        xt_s[...] = x_ref[...].astype(f32).T.astype(bf16)
+
+    x = x_ref[...]
+    dy = dy_ref[...]
+    wu = wu_ref[...]
+    wd = wd_ref[...]
+    u = _nn(x, wu) + bu_ref[...]
+    cdf = 0.5 * (1.0 + lax.erf(u * (1.0 / math.sqrt(2.0))))
+    pdf = jnp.exp(-0.5 * u * u) * (1.0 / math.sqrt(2.0 * math.pi))
+    act = (u * cdf).astype(bf16)
+    du = (_nt(dy, wd) * (cdf + u * pdf)).astype(bf16)
+    y = _nn(act, wd)
+    dx = _nt(du, wu)
+
+    @pl.when(first)
+    def _():
+        y_ref[...] = y
+        dx_ref[...] = dx
+
+    @pl.when(jnp.logical_not(first))
+    def _():
+        y_ref[...] += y
+        dx_ref[...] += dx
+
+    gd_ref[...] = lax.dot_general(
+        act, dy, (((0,), (0,)), ((), ())), preferred_element_type=f32
+    ).astype(bf16)
+    gu_ref[...] = _nn(xt_s[...], du).astype(bf16)
+    gb_ref[...] = jnp.sum(du.astype(f32), axis=0, keepdims=True)
+
+
+def mlp(x, dy, wu, wd, bu, tile=256):
+    rows, width = x.shape
+    hidden = wu.shape[1]
+    whole = pl.BlockSpec((rows, width), lambda i: (0, 0))
+    cols = pl.BlockSpec((width, tile), lambda i: (0, i))
+    down = pl.BlockSpec((tile, width), lambda i: (i, 0))
+    vec = pl.BlockSpec((1, tile), lambda i: (0, i))
+    return pl.pallas_call(
+        mlp_kernel,
+        grid=(hidden // tile,),
+        in_specs=[whole, whole, cols, down, vec],
+        out_specs=(whole, whole, cols, down, vec),
+        out_shape=(
+            jax.ShapeDtypeStruct((rows, width), f32),
+            jax.ShapeDtypeStruct((rows, width), f32),
+            jax.ShapeDtypeStruct((width, hidden), bf16),
+            jax.ShapeDtypeStruct((hidden, width), bf16),
+            jax.ShapeDtypeStruct((1, hidden), f32),
+        ),
+        scratch_shapes=[pltpu.VMEM((width, rows), bf16)],
+        compiler_params=pltpu.CompilerParams(vmem_limit_bytes=56 << 20),
+        name="mlp",
+    )(x, dy, wu, wd, bu)
+
+
+def fast_shards(
+    tokens,
+    ln1_gain,
+    ln1_bias,
+    ln2_gain,
+    ln2_bias,
+    w_qkv,
+    b_qkv,
+    w_out,
+    b_out,
+    w_up,
+    b_up,
+    w_down,
+    b_down,
+    lengths,
+    block_map,
+    cotangent,
+):
+    ctx = lax.axis_index("ctx")
+    me = lax.axis_index("wsh")
+    core = ctx % 2
+    n_ctx = lax.axis_size("ctx")
+    rows, width = tokens.shape[1:]
+    half = width // 2
+    seq = rows * n_ctx
+    heads = H // 2
+    hid = w_up.shape[1] // 2
+    pair_perm = [(i, i ^ 1) for i in range(n_ctx)]
+
+    def swap(v):
+        return lax.ppermute(v, "wsh", SWAP)
+
+    def fetch_rows(mine, other):
+        q = half // 2
+        got = swap(lax.dynamic_slice_in_dim(other, core * q, q))
+        sib = lax.ppermute(got, "ctx", pair_perm)
+        out = jnp.zeros((width, mine.shape[1]), mine.dtype)
+        out = lax.dynamic_update_slice_in_dim(out, mine, me * half, 0)
+        base = (1 - me) * half
+        out = lax.dynamic_update_slice_in_dim(out, got, base + core * q, 0)
+        return lax.dynamic_update_slice_in_dim(out, sib, base + (1 - core) * q, 0)
+
+    len_parts = jnp.stack([lengths[0] // 64, lengths[0] % 64]).astype(bf16)
+    small = jnp.concatenate(
+        [ln1_gain, ln1_bias, ln2_gain, ln2_bias, b_out, b_down, b_qkv, len_parts, jnp.zeros((126,), bf16)]
+    )
+    small = lax.all_gather(small, "wsh", axis=0, tiled=False)
+    vec = lambda i: small[:, i * half : (i + 1) * half].reshape(width).astype(f32)
+    g1, s1, g2, s2, bo, bd = [vec(i) for i in range(6)]
+    qkv_bias = small[:, 6 * half : 9 * half].reshape(3, 2, half).astype(f32)
+    qkv_bias = lax.dynamic_index_in_dim(qkv_bias, me, 1, keepdims=False).reshape(3 * half)
+    lens = small[:, 9 * half : 9 * half + 2].astype(jnp.int32)
+    lens = lens[:, 0] * 64 + lens[:, 1]
+    other_len = lens[1 - me]
+
+    x2 = jnp.stack([tokens[0], swap(tokens[0])])
+    cot2 = jnp.stack([cotangent[0], swap(cotangent[0])])
+    wq4 = w_qkv.reshape(half, 3, 2, half)
+    wq_mine = lax.dynamic_index_in_dim(wq4, me, 2, keepdims=False).reshape(half, 3 * half)
+    wq_send = lax.dynamic_index_in_dim(wq4, 1 - me, 2, keepdims=False).reshape(half, 3 * half)
+    wq = fetch_rows(wq_mine, wq_send)
+    wu_mine = lax.dynamic_slice_in_dim(w_up, me * hid, hid, 1)
+    wu_send = lax.dynamic_slice_in_dim(w_up, (1 - me) * hid, hid, 1)
+    wu = fetch_rows(wu_mine, wu_send)
+
+    own_blocks = lax.dynamic_slice_in_dim(block_map, 2 * ctx, 2)
+    offs = jnp.arange(HB, dtype=jnp.int32)
+    positions = (own_blocks[:, None] * HB + offs[None, :]).reshape(rows)
+    live2 = jnp.stack([positions < lengths[0], positions < other_len]).astype(f32)[..., None]
+    freq = 10000.0 ** (-jnp.arange(ROT // 2, dtype=f32) * 2.0 / ROT)
+    ang = freq[:, None] * jnp.arange(seq, dtype=jnp.int32).astype(f32)[None, :]
+    table = jnp.concatenate([jnp.cos(ang), jnp.sin(ang)])
+    own_ang = freq[:, None] * positions.astype(f32)[None, :]
+    cos = jnp.cos(own_ang)[None, :, None, :]
+    sin = jnp.sin(own_ang)[None, :, None, :]
+
+    xf = x2.astype(f32)
+    mean = jnp.mean(xf, axis=-1, keepdims=True)
+    cen = xf - mean
+    inv = lax.rsqrt(jnp.mean(cen * cen, axis=-1, keepdims=True) + epsilon)
+    xhat = cen * inv
+    attn_in = (xhat * g1 + s1).astype(bf16)
+    mlp_in = (xhat * g2 + s2).astype(bf16)
+    dy2 = (live2 * cot2.astype(f32)).astype(bf16)
+
+    qkv = lax.dot_general(
+        wq, attn_in.reshape(2 * rows, width), (((0,), (1,)), ((), ())), preferred_element_type=f32
+    )
+    qkv = (qkv + qkv_bias[:, None]).reshape(3, heads, HD, 2, rows)
+
+    def rope(v):
+        a = v[:, :8]
+        b = v[:, 8:16]
+        return jnp.concatenate([a * cos - b * sin, b * cos + a * sin, v[:, 16:]], axis=1)
+
+    parts = jnp.stack([rope(qkv[0]), rope(qkv[1]), qkv[2]]).astype(bf16)
+    send = parts.transpose(3, 1, 0, 2, 4).reshape(2 * heads, 3 * HD, rows)
+    dctx = jnp.einsum("ed,std->set", w_out, dy2, preferred_element_type=f32).astype(bf16)
+    dctx = dctx.reshape(2 * heads, HD, rows)
+
+    def exchange(v):
+        return lax.all_to_all(v, "ctx", 0, 0, tiled=False)
+
+    qkv_head = exchange(send)
+    do_head = exchange(dctx)
+
+    y_mlp, d_mlp, g_up, g_down, gb_up = mlp(
+        mlp_in.reshape(2 * rows, width),
+        dy2.reshape(2 * rows, width),
+        wu,
+        w_down,
+        b_up.astype(f32)[None, :],
+    )
+    up_keep = lax.dynamic_slice_in_dim(g_up, me * half, half, 0)
+    up_send = lax.dynamic_slice_in_dim(g_up, (1 - me) * half, half, 0)
+    up_got = swap(up_send)
+
+    def join_cols(keep, got, n):
+        a = keep.reshape(half, -1, n)
+        b = got.reshape(half, -1, n)
+        pair = jnp.where(me == 0, jnp.stack([a, b], axis=2), jnp.stack([b, a], axis=2))
+        return pair.reshape(half, -1)
+
+    tot_down, tot_up = lax.psum((g_down, join_cols(up_keep, up_got, hid)), "ctx")
+
+    o_head, lse = attn_fwd(block_map, qkv_head, bq=1024, bk=1024)
+    ob = exchange(o_head).reshape(2, half, rows)
+    g_head = attn_bwd(block_map, qkv_head, o_head, do_head, lse, table)
+    d_qkv = exchange(g_head).reshape(2, heads, 3, HD, rows)
+    d_qkv = d_qkv.transpose(0, 2, 1, 3, 4).reshape(2, 3 * half, rows)
+
+    part = jnp.einsum("sct,cd->std", ob, w_out, preferred_element_type=f32) + y_mlp.reshape(
+        2, rows, width
+    )
+    y_got = swap(part[1].astype(bf16)).astype(f32)
+    output = (live2[0] * (xf[0] + part[0] + y_got + bo + bd)).astype(bf16)
+    g_out = jnp.einsum("sct,std->cd", ob, dy2, preferred_element_type=f32).astype(bf16)
+
+    g_qkv = jnp.einsum("stf,sct->fc", attn_in, d_qkv, preferred_element_type=f32).astype(bf16)
+    d_attn = jnp.einsum("sct,fc->stf", d_qkv, wq, preferred_element_type=f32)
+    q_keep = lax.dynamic_slice_in_dim(g_qkv, me * half, half, 0)
+    q_send = lax.dynamic_slice_in_dim(g_qkv, (1 - me) * half, half, 0)
+    q_tot = join_cols(q_keep, swap(q_send), half)
+    q_tot, g_out, tot_down, tot_up = lax.optimization_barrier((q_tot, g_out, tot_down, tot_up))
+    tot_out, tot_qkv = lax.psum((g_out, q_tot), "ctx")
+
+    d_mlp = d_mlp.reshape(2, rows, width)
+    e = d_attn * g1 + d_mlp * g2
+    e_own = e[0] + swap(e[1].astype(bf16)).astype(f32)
+    dx = inv[0] * (
+        e_own
+        - jnp.mean(e_own, axis=-1, keepdims=True)
+        - xhat[0] * jnp.mean(e_own * xhat[0], axis=-1, keepdims=True)
+    )
+    grad_tokens = live2[0] * cot2[0].astype(f32) + dx
+
+    both = (0, 1)
+    gb_qkv = jnp.sum(d_qkv.astype(f32), axis=(0, 2)).reshape(3, 1, half)
+    mine = (jnp.arange(2) == me).astype(f32)
+    gb_qkv = (gb_qkv * mine[None, :, None]).reshape(3 * width)
+    gb_hid = (gb_up * mine[:, None]).reshape(2 * hid)
+    flat = jnp.concatenate(
+        [
+            jnp.sum(d_attn * xhat, axis=both),
+            jnp.sum(d_attn, axis=both),
+            jnp.sum(d_mlp * xhat, axis=both),
+            jnp.sum(d_mlp, axis=both),
+            jnp.sum(dy2[0].astype(f32), axis=0),
+            gb_qkv,
+            gb_hid,
+        ]
+    )
+    flat = lax.psum(flat, ("ctx", "wsh"))
+
+    def own(start, size):
+        return lax.dynamic_slice_in_dim(flat, start + me * size, size)
+
+    gb_out = own(4 * width, half)
+    return (
+        output[None],
+        grad_tokens[None],
+        own(0, half),
+        own(width, half),
+        own(2 * width, half),
+        own(3 * width, half),
+        tot_qkv.astype(f32),
+        own(5 * width, 3 * half),
+        tot_out.astype(f32),
+        gb_out,
+        tot_up.astype(f32),
+        own(8 * width, hid),
+        tot_down.astype(f32),
+        gb_out,
+    )
+
+
 def solution(mesh):
     placed = (
         P("wsh", "ctx", None),
@@ -405,8 +788,9 @@
         P(),
         P("wsh", "ctx", None),
     )
+    body = fast_shards if fast_fits(mesh) else shards
     return jax.shard_map(
-        shards,
+        body,
         mesh=mesh,
         in_specs=placed,
         out_specs=(

time: 1380 us -> 600 us (0.43)
  waiting for transfers between devices: 736 us -> 232 us
  matrix products: 320 us -> 11.9 us
  Pallas kernels: 0 us -> 80.9 us
  local copies, waits for them, and re-layouts: 125 us -> 88.7 us
  starting transfers between devices: 0.93 us -> 37 us
  other arithmetic: 66.7 us -> 41.2 us
  blocking collectives: 105 us -> 90.8 us
    reduce_scatter x6 -> x0, waiting for transfers between devices: 436 us -> none  [the longest x1 107 us: shards(): lax.psum_scatter(term_stacks[1].reshape(seq_rows, model_width).astype(jnp...]
    dot_general x40 -> x6, matrix products: 320 us -> 11.9 us  [the longest x1 3.59 us: fast_shards(): d_attn = jnp.einsum('sct,fc->stf', d_qkv, wq, preferred_element_type=f32)]
    all_gather x6 -> x0, waiting for transfers between devices: 164 us -> none  [the longest x1 75.2 us: shards(): lax.all_gather(key_own, 'ctx', axis=0, tiled=True)]
    pallas_call x0 -> x3, Pallas kernels: none -> 80.9 us  [the longest x1 35 us: attn_bwd(): pl.pallas_call(lambda *a: attn_bwd_kernel(*a, nblk=nblk, bq=bq, bk=bk), o...]
    all_to_all x0 -> x4, waiting for transfers between devices: none -> 46.2 us  [exchange(): return lax.all_to_all(v, 'ctx', 0, 0, tiled=False)]
    reduce_sum x9 -> x6, other arithmetic: 36.8 us -> 6.89 us  [the longest x1 2.99 us: fast_shards(): jnp.sum(d_mlp, axis=both)]
    psum x1 -> x2, waiting for transfers between devices: 133 us -> 162 us  [the longest x1 109 us: fast_shards(): lax.psum((g_down, join_cols(up_keep, up_got, hid)), 'ctx')]
    all_to_all x0 -> x4, starting transfers between devices: none -> 27.4 us  [exchange(): return lax.all_to_all(v, 'ctx', 0, 0, tiled=False)]
  transfers between devices with their start and end apart: 13 -> 16, of which waited for: 10 -> 5; matrix products, arithmetic and copies ran while one was open for 35% -> 17% of each run, Pallas kernels for 0% -> 9%
where the time goes in v1:
time: 600 us; the launch traced here: 598 us
  waiting for transfers between devices  232 us (39%)
  blocking collectives  90.8 us (15%)
  local copies, waits for them, and re-layouts  88.7 us (15%)
  Pallas kernels  80.9 us (13%)
  other arithmetic  41.2 us (7%)
  starting transfers between devices  37 us (6%)
  between operations  15.6 us (3%)
  matrix products  11.9 us (2%)
    psum x1, waiting for transfers between devices, fast_shards(): lax.psum((g_down, join_cols(up_keep, up_got, hid)), 'ctx')  109 us
    psum x1, waiting for transfers between devices, fast_shards(): tot_out, tot_qkv = lax.psum((g_out, q_tot), 'ctx')  53.4 us
    all_gather x1, blocking collectives, fast_shards(): small = lax.all_gather(small, 'wsh', axis=0, tiled=False)  49.3 us
    all_to_all x4, waiting for transfers between devices, exchange(): return lax.all_to_all(v, 'ctx', 0, 0, tiled=False)  46.2 us
    psum x1, blocking collectives, fast_shards(): flat = lax.psum(flat, ('ctx', 'wsh'))  41.5 us
    pallas_call x1, Pallas kernels, attn_bwd(): pl.pallas_call(lambda *a: attn_bwd_kernel(*a, nblk=nblk, bq=bq, bk=bk), o...  35 us
    all_to_all x4, starting transfers between devices, exchange(): return lax.all_to_all(v, 'ctx', 0, 0, tiled=False)  27.4 us
    unnamed x142, local copies, waits for them, and re-layouts  26.6 us
  transfers between devices with their start and end apart: 16, of which 5 were waited for; matrix products, arithmetic and copies ran while one was open for 17% of the time, Pallas kernels for 9%

profile of v1, /device:TPU:0, one launch (start us, length us, event | category | flops | bytes accessed | tf_op | source)
XLA Modules:
  0.0 598.4 jit_solution(4941927910537968324)
XLA Ops:
  7.2 3.0 collective-permute-start
  10.3 2.7 dynamic_slice.67
  13.1 2.0 collective-permute-start.4
  15.0 4.6 copy.84
  19.7 3.3 constant_dynamic-slice_fusion.4
  24.1 49.3 %all-gather.1 = bf16[2,1,4736]{2,1,0:T(2,128)(2,1)S(1)} all-gather(bf16[1,1,4736]{2,1,0:T(2,128)(2,1)S(1)} %reshape.426), channel_id=2, replica_groups=mesh['ctx'=16,'wsh'=2] {'wsh'}, dimensions={0}, use_global_device_ids=true | all-gather | bytes 28416 | tf_op jit(solution)/shard_map/all_gather | solution.py:622
  75.5 2.7 broadcast_in_dim.16
  79.2 1.5 dynamic-slice_dynamic-update-slice_fusion
  81.3 2.6 copy.85
  87.9 1.4 add_convert_fusion.1.x_ref
  89.8 1.2 fusion.2.dy_ref
  91.0 1.4 copy.86
  93.4 2.3 constant_dynamic-update-slice_fusion.8
  95.7 1.4 copy.87
  98.0 2.3 constant_dynamic-update-slice_fusion.7.wu_ref
  100.4 24.2 %mlp.1 = (f32[512,1024]{1,0:T(8,128)}, f32[512,1024]{1,0:T(8,128)}, bf16[1024,2048]{1,0:T(8,128)(2,1)}, bf16[2048,1024]{1,0:T(8,128)(2,1)}, f32[1,2048]{1,0:T(1,128)}) custom-call(bf16[512,1024]{1,0:T(8,128)(2,1)} %add_convert_fusion.1.x_ref, bf16[512,1024]{1,0:T(8,128)(2,1)} %fusion.2.dy_ref, bf16[1024,2048]{1,0:T(8,128)(2,1)} %constant_dynamic-update-slice_fusion.7.wu_ref, ...), custom_call_target="tpu_custom_call" | custom-call | tf_op jit(solution)/shard_map/mlp/pallas_call | solution.py:558
  124.6 3.0 fusion.26
  127.6 2.1 convolution_add_fusion
  131.0 2.8 squeeze.24
  133.8 1.4 slice.136
  135.2 1.7 fusion.29
  136.9 1.6 squeeze.46
  138.5 1.7 fusion.30
  140.2 1.4 slice.140
  143.0 1.3 pad_maximum_fusion
  144.3 6.3 %all-to-all-start = ((bf16[16,192,256]{2,1,0:T(8,128)(2,1)}), bf16[16,192,256]{2,1,0:T(8,128)(2,1)S(1)}, u32[]{:S(2)}, u32[]{:S(2)}) async-start(bf16[16,192,256]{2,1,0:T(8,128)(2,1)} %bitcast.177), calls=%async_computation | async-start | bytes 3145728 | tf_op jit(solution)/shard_map/all_to_all | solution.py:677
  150.7 1.4 multiply_convert_fusion
  153.1 1.6 fusion.4
  154.7 2.0 copy.96
  156.7 25.9 %all-to-all-done.a_1_ = bf16[16,192,256]{2,1,0:T(8,128)(2,1)S(1)} async-done(((bf16[16,192,256]{2,1,0:T(8,128)(2,1)}), bf16[16,192,256]{2,1,0:T(8,128)(2,1)S(1)}, u32[]{:S(2)}, u32[]{:S(2)}) %all-to-all-start) | async-done | bytes 1572896 | tf_op jit(solution)/shard_map/all_to_all | solution.py:677
  182.6 9.2 %all-to-all-start.2 = ((bf16[16,64,256]{2,1,0:T(8,128)(2,1)}), bf16[16,64,256]{2,1,0:T(8,128)(2,1)}, u32[]{:S(2)}, u32[]{:S(2)}) async-start(bf16[16,64,256]{2,1,0:T(8,128)(2,1)} %bitcast.189), calls=%async_computation.2 | async-start | bytes 1048576 | tf_op jit(solution)/shard_map/all_to_all | solution.py:677
  191.8 4.8 dynamic-slice_bitcast_fusion
  196.6 1.5 collective-permute-start.9
  198.1 21.7 %attn_fwd.1 = (bf16[16,64,256]{2,1,0:T(8,128)(2,1)}, f32[1,4096]{1,0:T(1,128)}) custom-call(s32[32]{0:T(128)} %a_0_.3, bf16[16,192,256]{2,1,0:T(8,128)(2,1)} %copy-done.2), custom_call_target="tpu_custom_call" | custom-call | tf_op jit(solution)/shard_map/attn_fwd/pallas_call | solution.py:438
  219.8 6.0 all-to-all-start.1
  227.0 35.0 %attn_bwd.1 = bf16[16,192,256]{2,1,0:T(8,128)(2,1)} custom-call(s32[32]{0:T(128)} %a_0_.3, bf16[16,192,256]{2,1,0:T(8,128)(2,1)} %copy-done.2, bf16[16,64,256]{2,1,0:T(8,128)(2,1)} %get-tuple-element.25.a_2_, bf16[16,64,256]{2,1,0:T(8,128)(2,1)} %all-to-all-done.2.a_3_, f32[1,4096]{1,0:T(1,128)} %get-tuple-element.27.a_4_, f32[16,4096]{1,0:T(8,128)} %pad_maximum_fusion.2.a_5_), custom_call_target="tpu_custom_call" | custom-call | tf_op jit(solution)/shard_map/attn_bwd/pallas_call | solution.py:498
  262.9 6.0 %all-to-all-start.3 = ((bf16[16,192,256]{2,1,0:T(8,128)(2,1)}), bf16[16,192,256]{2,1,0:T(8,128)(2,1)S(1)}, u32[]{:S(2)}, u32[]{:S(2)}) async-start(bf16[16,192,256]{2,1,0:T(8,128)(2,1)} %attn_bwd.1), calls=%async_computation.3 | async-start | bytes 3145728 | tf_op jit(solution)/shard_map/all_to_all | solution.py:677
  269.0 5.8 maximum_select_fusion
  274.8 6.2 %copy.103 = bf16[512,1,2,2048]{0,3,2,1:T(8,128)(2,1)} copy(bf16[512,1,2,2048]{3,0,2,1:T(8,128)(2,1)} %maximum_select_fusion) | data formatting | bytes 8388608 | tf_op jit(solution)/shard_map/jit(_where)/select_n | solution.py:696
  281.7 1.2 convert_reduce_fusion.2
  282.9 2.5 fusion.25
  287.0 1.7 add.275
  288.7 20.3 %all-to-all-done.3 = bf16[16,192,256]{2,1,0:T(8,128)(2,1)S(1)} async-done(((bf16[16,192,256]{2,1,0:T(8,128)(2,1)}), bf16[16,192,256]{2,1,0:T(8,128)(2,1)S(1)}, u32[]{:S(2)}, u32[]{:S(2)}) %all-to-all-start.3) | async-done | bytes 1572896 | tf_op jit(solution)/shard_map/all_to_all | solution.py:677
  309.3 2.1 bitcast_convert_fusion
  311.4 1.9 constant_dynamic-slice_fusion.2
  313.3 2.4 fusion.18
  315.8 1.7 collective-permute-start.6
  317.5 1.7 bitcast_convert_fusion.1
  319.2 3.6 fusion.27
  322.8 1.3 copy-done.10
  325.7 1.7 copy.100
  327.4 23.6 %collective-permute-done.8 = bf16[512,1536]{1,0:T(8,128)(2,1)} collective-permute-done((bf16[512,1536]{1,0:T(8,128)(2,1)}, bf16[512,1536]{1,0:T(8,128)(2,1)}, u32[]{:S(2)}, u32[]{:S(2)}) %collective-permute-start.8) | collective-permute-done | bytes 1572896 | tf_op jit(solution)/shard_map/ppermute | solution.py:606
  351.0 2.6 copy.101
  353.6 2.2 maximum_select_fusion.1
  355.7 2.1 copy.102
  357.8 109.1 %all-reduce.7.cloned.1.call-done = (bf16[2048,1024]{1,0:T(8,128)(2,1)}, bf16[512,4096]{0,1:T(8,128)(2,1)}) async-done(((bf16[2048,1024]{1,0:T(8,128)(2,1)}, bf16[512,4096]{0,1:T(8,128)(2,1)}), (bf16[2048,1024]{1,0:T(8,128)(2,1)}, bf16[512,4096]{0,1:T(8,128)(2,1)})) %all-reduce.7.cloned.1.call-update) | async-done | bytes 8388624 | tf_op jit(solution)/shard_map/psum | solution.py:699
  467.6 41.5 %psum.35 = f32[12288]{0:T(1024)S(1)} all-reduce(f32[12288]{0:T(1024)S(1)} %constant_dynamic-update-slice_fusion), channel_id=1, replica_groups=mesh['ctx'=16,'wsh'=2] {'ctx','wsh'}, use_global_device_ids=true, to_apply=%region_10.11 | all-reduce | flops 12288 | bytes 98304 | tf_op jit(solution)/shard_map/psum | solution.py:748
  511.1 1.8 fusion.20
  513.0 3.8 add_bitcast_fusion
  516.8 7.0 %copy.105 = f32[512,4096]{1,0:T(8,128)} copy(bf16[512,4096]{0,1:T(8,128)(2,1)} %get-tuple-element.34) | data formatting | bytes 12582912
  523.8 6.7 %convert_element_type.251 = f32[2048,1024]{1,0:T(8,128)} convert(bf16[2048,1024]{1,0:T(8,128)(2,1)} %get-tuple-element.35) | non-fusion elementwise | flops 2097152 | bytes 12582912 | tf_op jit(solution)/shard_map/convert_element_type | solution.py:767
  530.5 53.4 %all-reduce.5.cloned.1.call-done = (bf16[512,3072]{0,1:T(8,128)(2,1)}, bf16[512,1024]{1,0:T(8,128)(2,1)}) async-done(((bf16[512,3072]{0,1:T(8,128)(2,1)}, bf16[512,1024]{1,0:T(8,128)(2,1)}), (bf16[512,3072]{0,1:T(8,128)(2,1)}, bf16[512,1024]{1,0:T(8,128)(2,1)})) %all-reduce.5.cloned.1.call-update) | async-done | bytes 4194320 | tf_op jit(solution)/shard_map/psum | solution.py:720
  583.9 5.5 copy.104
  589.4 1.6 convert_element_type.249
  (216 shorter events, 23.3 us)
Async XLA Ops:
  7.2 145.9 %copy-start = (bf16[512,1024]{1,0:T(8,128)(2,1)S(1)}, bf16[512,1024]{1,0:T(8,128)(2,1)}, u32[]{:S(2)}) copy-start(bf16[512,1024]{1,0:T(8,128)(2,1)} %param.23) | copy-start | bytes 3145732
  7.2 78.4 %collective-permute-start = (bf16[256,1024]{1,0:T(8,128)(2,1)}, bf16[256,1024]{1,0:T(8,128)(2,1)S(1)}, u32[]{:S(2)}, u32[]{:S(2)}) collective-permute-start(bf16[256,1024]{1,0:T(8,128)(2,1)} %bitcast.167), channel_id=1, source_target_pairs={{0,1},{1,0},{2,3},{3,2},{4,5},{5,4},{6,7},{7,6},{8,9},{9,8},{10,11... | collective-permute-start | bytes 1572872 | tf_op jit(solution)/shard_map/ppermute | solution.py:606
  10.2 77.5 %collective-permute-start.3 = (bf16[256,1024]{1,0:T(8,128)(2,1)}, bf16[256,1024]{1,0:T(8,128)(2,1)S(1)}, u32[]{:S(2)}, u32[]{:S(2)}) collective-permute-start(bf16[256,1024]{1,0:T(8,128)(2,1)} %bitcast.181), channel_id=1, source_target_pairs={{0,1},{1,0},{2,3},{3,2},{4,5},{5,4},{6,7},{7,6},{8,9},{9,8},{10,11... | collective-permute-start | bytes 1572872 | tf_op jit(solution)/shard_map/ppermute | solution.py:606
  13.1 76.3 %collective-permute-start.4 = (bf16[256,2048]{1,0:T(8,128)(2,1)}, bf16[256,2048]{1,0:T(8,128)(2,1)}, u32[]{:S(2)}, u32[]{:S(2)}) collective-permute-start(bf16[256,2048]{1,0:T(8,128)(2,1)} %dynamic_slice.67), channel_id=1, source_target_pairs={{0,1},{1,0},{2,3},{3,2},{4,5},{5,4},{6,7},{7,6},{8,9},{9,8},{10,11... | collective-permute-start | bytes 3145736 | tf_op jit(solution)/shard_map/ppermute | solution.py:606
  19.7 4.2 copy-start.45
  19.7 4.2 copy-start.53
  19.7 4.3 copy-start.54
  19.7 4.3 copy-start.55
  19.7 4.3 copy-start.56
  19.7 4.3 copy-start.57
  19.7 4.3 copy-start.58
  19.7 54.9 %copy-start.46 = (s32[32]{0:T(128)S(1)}, s32[32]{0:T(128)}, u32[]{:S(2)}) copy-start(s32[32]{0:T(128)} %a_0_.3) | copy-start | bytes 388
  23.1 66.3 %collective-permute-start.1 = (bf16[256,1536]{0,1:T(8,128)(2,1)S(1)}, bf16[256,1536]{0,1:T(8,128)(2,1)}, u32[]{:S(2)}, u32[]{:S(2)}) collective-permute-start(bf16[256,1536]{0,1:T(8,128)(2,1)S(1)} %constant_dynamic-slice_fusion.3), channel_id=1, source_target_pairs={{0,1},{1,0},{2,3},{3,2},{4,5},{5,4},{6,7},{7,6},{8,9},{9,8},{10,11... | collective-permute-start | bytes 2359304 | tf_op jit(solution)/shard_map/ppermute | solution.py:606
  75.5 2.7 copy-start.49
  75.5 2.7 copy-start.51
  75.5 3.7 copy-start.14
  79.2 1.5 copy-start.44
  80.7 3.7 copy-start.47
  80.7 7.2 %copy-start.28 = (f32[1,4,2,128]{3,1,2,0:T(4,128)}, f32[1,4,2,128]{3,1,2,0:T(4,128)S(1)}, u32[]{:S(2)}) copy-start(f32[1,4,2,128]{3,1,2,0:T(4,128)S(1)} %copy.122) | copy-start | bytes 12292
  81.3 43.2 %copy-start.30 = (f32[1,4,2,128]{3,1,2,0:T(4,128)}, f32[1,4,2,128]{3,1,2,0:T(4,128)S(1)}, u32[]{:S(2)}) copy-start(f32[1,4,2,128]{3,1,2,0:T(4,128)S(1)} %copy.118) | copy-start | bytes 12292
  83.9 40.7 %copy-start.32 = (f32[1,4,2,128]{3,1,2,0:T(4,128)}, f32[1,4,2,128]{3,1,2,0:T(4,128)S(1)}, u32[]{:S(2)}) copy-start(f32[1,4,2,128]{3,1,2,0:T(4,128)S(1)} %copy.119) | copy-start | bytes 12292
  84.0 1.4 copy-start.7
  85.4 2.3 copy-start.8
  85.6 2.3 copy-start.11
  85.6 39.0 %copy-start.4 = (bf16[256,1024]{1,0:T(8,128)(2,1)}, bf16[256,1024]{1,0:T(8,128)(2,1)S(1)}, u32[]{:S(2)}) copy-start(bf16[256,1024]{1,0:T(8,128)(2,1)S(1)} %collective-permute-done) | copy-start | bytes 1572868
  87.7 1.6 copy-start.22
  89.3 6.3 %collective-permute-start.2 = (bf16[256,1536]{0,1:T(8,128)(2,1)}, bf16[256,1536]{0,1:T(8,128)(2,1)}, u32[]{:S(2)}, u32[]{:S(2)}) collective-permute-start(bf16[256,1536]{0,1:T(8,128)(2,1)} %collective-permute-done.1), channel_id=1, source_target_pairs={{0,2},{2,0},{4,6},{6,4},{8,10},{10,8},{12,14},{14,12},{16,18},{18,... | collective-permute-start | bytes 2359304 | tf_op jit(solution)/shard_map/ppermute | solution.py:611
  89.3 8.7 %collective-permute-start.5 = (bf16[256,2048]{1,0:T(8,128)(2,1)}, bf16[256,2048]{1,0:T(8,128)(2,1)}, u32[]{:S(2)}, u32[]{:S(2)}) collective-permute-start(bf16[256,2048]{1,0:T(8,128)(2,1)} %collective-permute-done.4), channel_id=1, source_target_pairs={{0,2},{2,0},{4,6},{6,4},{8,10},{10,8},{12,14},{14,12},{16,18},{18,... | collective-permute-start | bytes 3145736 | tf_op jit(solution)/shard_map/ppermute | solution.py:611
  124.6 3.0 copy-start.12
  140.2 1.8 copy-start.24
  144.3 6.3 %copy-start.50 = (pred[2,128]{1,0:T(4,128)(4,1)S(1)}, pred[2,128]{1,0:T(4,128)(4,1)}, u32[]{:S(2)}) copy-start(pred[2,128]{1,0:T(4,128)(4,1)} %copy-done.49) | copy-start | bytes 772
  144.3 6.3 %copy-start.52 = (pred[2,128]{1,0:T(4,128)(4,1)S(1)}, pred[2,128]{1,0:T(4,128)(4,1)}, u32[]{:S(2)}) copy-start(pred[2,128]{1,0:T(4,128)(4,1)} %copy-done.51) | copy-start | bytes 772
  144.3 38.3 %all-to-all-start = ((bf16[16,192,256]{2,1,0:T(8,128)(2,1)}), bf16[16,192,256]{2,1,0:T(8,128)(2,1)S(1)}, u32[]{:S(2)}, u32[]{:S(2)}) async-start(bf16[16,192,256]{2,1,0:T(8,128)(2,1)} %bitcast.177), calls=%async_computation | async-start | bytes 3145728 | tf_op jit(solution)/shard_map/all_to_all | solution.py:677
  150.7 130.6 %copy-start.38 = (f32[2,256]{1,0:T(2,128)}, f32[2,256]{1,0:T(2,128)S(1)}, u32[]{:S(2)}) copy-start(f32[2,256]{1,0:T(2,128)S(1)} %add_convert_fusion.7) | copy-start | bytes 6148
  182.6 14.0 %copy-start.2 = (bf16[16,192,256]{2,1,0:T(8,128)(2,1)}, bf16[16,192,256]{2,1,0:T(8,128)(2,1)S(1)}, u32[]{:S(2)}) copy-start(bf16[16,192,256]{2,1,0:T(8,128)(2,1)S(1)} %all-to-all-done.a_1_) | copy-start | bytes 4718596
  182.6 37.2 %all-to-all-start.2 = ((bf16[16,64,256]{2,1,0:T(8,128)(2,1)}), bf16[16,64,256]{2,1,0:T(8,128)(2,1)}, u32[]{:S(2)}, u32[]{:S(2)}) async-start(bf16[16,64,256]{2,1,0:T(8,128)(2,1)} %bitcast.189), calls=%async_computation.2 | async-start | bytes 1048576 | tf_op jit(solution)/shard_map/all_to_all | solution.py:677
  196.6 29.2 %copy-start.48 = (f32[8]{0:T(128)S(1)}, f32[8]{0:T(128)}, u32[]{:S(2)}) copy-start(f32[8]{0:T(128)} %copy-done.47) | copy-start | bytes 100
  196.6 72.3 %collective-permute-start.9 = (bf16[512,2048]{1,0:T(8,128)(2,1)}, bf16[512,2048]{1,0:T(8,128)(2,1)}, u32[]{:S(2)}, u32[]{:S(2)}) collective-permute-start(bf16[512,2048]{1,0:T(8,128)(2,1)} %get-tuple-element.89), channel_id=1, source_target_pairs={{0,1},{1,0},{2,3},{3,2},{4,5},{5,4},{6,7},{7,6},{8,9},{9,8},{10,11... | collective-permute-start | bytes 6291464 | tf_op jit(solution)/shard_map/ppermute | solution.py:606
  219.8 42.3 %all-to-all-start.1 = ((bf16[16,64,256]{2,1,0:T(8,128)(2,1)}), bf16[16,64,256]{2,1,0:T(8,128)(2,1)S(1)}, u32[]{:S(2)}, u32[]{:S(2)}) async-start(bf16[16,64,256]{2,1,0:T(8,128)(2,1)} %get-tuple-element.25.a_2_), calls=%async_computation.1 | async-start | bytes 1048576 | tf_op jit(solution)/shard_map/all_to_all | solution.py:677
  262.9 46.2 %all-to-all-start.3 = ((bf16[16,192,256]{2,1,0:T(8,128)(2,1)}), bf16[16,192,256]{2,1,0:T(8,128)(2,1)S(1)}, u32[]{:S(2)}, u32[]{:S(2)}) async-start(bf16[16,192,256]{2,1,0:T(8,128)(2,1)} %attn_bwd.1), calls=%async_computation.3 | async-start | bytes 3145728 | tf_op jit(solution)/shard_map/all_to_all | solution.py:677
  268.9 198.0 %all-reduce.7.cloned.1.call-start = ((), (), s32[]{:S(2)}) async-start(), calls=%async_computation.5 | async-start | bytes 16777216 | tf_op jit(solution)/shard_map/psum | solution.py:699
  281.0 4.4 copy-start.41
  281.0 302.8 %all-reduce.5.cloned.1.call-start = ((), (), s32[]{:S(2)}) async-start(), calls=%async_computation.4 | async-start | bytes 8388608 | tf_op jit(solution)/shard_map/psum | solution.py:720
  281.7 3.8 copy-start.20
  285.4 1.6 copy-start.17
  288.7 20.5 %copy-start.5 = (bf16[256,1024]{1,0:T(8,128)(2,1)S(1)}, bf16[256,1024]{1,0:T(8,128)(2,1)}, u32[]{:S(2)}) copy-start(bf16[256,1024]{1,0:T(8,128)(2,1)} %copy-done.4) | copy-start | bytes 1572868
  288.7 20.5 %copy-start.31 = (f32[1,4,2,128]{3,1,2,0:T(4,128)S(1)}, f32[1,4,2,128]{3,1,2,0:T(4,128)}, u32[]{:S(2)}) copy-start(f32[1,4,2,128]{3,1,2,0:T(4,128)} %copy-done.30) | copy-start | bytes 12292
  288.7 20.5 %copy-start.33 = (f32[1,4,2,128]{3,1,2,0:T(4,128)S(1)}, f32[1,4,2,128]{3,1,2,0:T(4,128)}, u32[]{:S(2)}) copy-start(f32[1,4,2,128]{3,1,2,0:T(4,128)} %copy-done.32) | copy-start | bytes 12292
  288.7 20.5 %copy-start.40 = (f32[2,256]{1,0:T(2,128)S(1)}, f32[2,256]{1,0:T(2,128)}, u32[]{:S(2)}) copy-start(f32[2,256]{1,0:T(2,128)} %copy-done.39) | copy-start | bytes 6148
  311.4 6.1 %copy-start.16 = (bf16[2,256,1024]{2,1,0:T(8,128)(2,1)S(1)}, bf16[2,256,1024]{2,1,0:T(8,128)(2,1)}, u32[]{:S(2)}) copy-start(bf16[2,256,1024]{2,1,0:T(8,128)(2,1)} %copy-done.15) | copy-start | bytes 3145732
  311.4 6.1 %copy-start.21 = (bf16[16,64,256]{2,1,0:T(8,128)(2,1)S(1)}, bf16[16,64,256]{2,1,0:T(8,128)(2,1)}, u32[]{:S(2)}) copy-start(bf16[16,64,256]{2,1,0:T(8,128)(2,1)} %copy-done.19) | copy-start | bytes 1572868
  311.4 7.8 %copy-start.18 = (f32[512,1024]{1,0:T(8,128)S(1)}, f32[512,1024]{1,0:T(8,128)}, u32[]{:S(2)}) copy-start(f32[512,1024]{1,0:T(8,128)} %get-tuple-element.28) | copy-start | bytes 6291460
  313.3 5.9 copy-start.13
  313.3 5.9 copy-start.29
  313.3 37.6 %collective-permute-start.8 = (bf16[512,1536]{1,0:T(8,128)(2,1)}, bf16[512,1536]{1,0:T(8,128)(2,1)}, u32[]{:S(2)}, u32[]{:S(2)}) collective-permute-start(bf16[512,1536]{1,0:T(8,128)(2,1)} %get-tuple-element.91), channel_id=1, source_target_pairs={{0,1},{1,0},{2,3},{3,2},{4,5},{5,4},{6,7},{7,6},{8,9},{9,8},{10,11... | collective-permute-start | bytes 4718600 | tf_op jit(solution)/shard_map/ppermute | solution.py:606
  315.8 197.2 %collective-permute-start.6 = (bf16[256,1024]{1,0:T(8,128)(2,1)}, bf16[256,1024]{1,0:T(8,128)(2,1)}, u32[]{:S(2)}, u32[]{:S(2)}) collective-permute-start(bf16[256,1024]{1,0:T(8,128)(2,1)} %fusion.18), channel_id=1, source_target_pairs={{0,1},{1,0},{2,3},{3,2},{4,5},{5,4},{6,7},{7,6},{8,9},{9,8},{10,11... | collective-permute-start | bytes 1572872 | tf_op jit(solution)/shard_map/ppermute | solution.py:606
  322.8 1.3 copy-start.10
  325.0 186.1 %collective-permute-start.7 = (bf16[256,1024]{1,0:T(8,128)(2,1)}, bf16[256,1024]{1,0:T(8,128)(2,1)S(1)}, u32[]{:S(2)}, u32[]{:S(2)}) collective-permute-start(bf16[256,1024]{1,0:T(8,128)(2,1)} %fusion.19), channel_id=1, source_target_pairs={{0,1},{1,0},{2,3},{3,2},{4,5},{5,4},{6,7},{7,6},{8,9},{9,8},{10,11... | collective-permute-start | bytes 1572872 | tf_op jit(solution)/shard_map/ppermute | solution.py:606
  466.9 46.0 %copy-start.6 = (f32[2,256,1024]{2,1,0:T(8,128)S(1)}, f32[2,256,1024]{2,1,0:T(8,128)}, u32[]{:S(2)}) copy-start(f32[2,256,1024]{2,1,0:T(8,128)} %add.275) | copy-start | bytes 6291460
  466.9 46.0 %copy-start.9 = (bf16[1,256,1024]{2,1,0:T(8,128)(2,1)S(1)}, bf16[1,256,1024]{2,1,0:T(8,128)(2,1)}, u32[]{:S(2)}) copy-start(bf16[1,256,1024]{2,1,0:T(8,128)(2,1)} %param.31) | copy-start | bytes 1572868
  466.9 46.0 %slice-start = ((f32[2,256]{1,0:T(2,128)}), f32[1,256]{1,0:T(1,128)S(1)}, s32[]{:S(2)}) async-start(f32[2,256]{1,0:T(2,128)} %copy-done.38), calls=%async_computation.6 | async-start | bytes 2048 | tf_op jit(solution)/shard_map/slice | solution.py:711
  511.1 79.9 %copy-start.42 = (f32[512]{0:T(512)}, f32[512]{0:T(512)S(1)}, u32[]{:S(2)}) copy-start(f32[512]{0:T(512)S(1)} %get-tuple-element.163) | copy-start | bytes 6148
  583.9 5.5 copy-start.23
  583.9 7.7 %copy-start.1 = (bf16[512,1024]{1,0:T(8,128)(2,1)S(1)}, bf16[512,1024]{1,0:T(8,128)(2,1)}, u32[]{:S(2)}) copy-start(bf16[512,1024]{1,0:T(8,128)(2,1)} %param.23) | copy-start | bytes 3145732
  (12 other events, 10.2 us)
Sparse Core Ops, SparseCore 0:
  281.1 185.7 all-reduce.6
  471.7 112.0 all-reduce.4

commit v2 on v1

--- a/solution.py
+++ b/solution.py
@@ -512,65 +512,396 @@
     return mesh.shape["wsh"] == 2 and mesh.shape["ctx"] == H
 
 
-def mlp_kernel(x_ref, dy_ref, wu_ref, wd_ref, bu_ref, y_ref, dx_ref, gu_ref, gd_ref, gb_ref, xt_s):
+def _params(mb=56):
+    return pltpu.CompilerParams(vmem_limit_bytes=mb << 20)
+
+
+def _norm(x):
+    xf = x.astype(f32)
+    cen = xf - jnp.mean(xf, axis=-1, keepdims=True)
+    inv = lax.rsqrt(jnp.mean(cen * cen, axis=-1, keepdims=True) + epsilon)
+    return cen * inv, inv
+
+
+def _pieces(ids):
+    me, core = ids[0], ids[1]
+    return me, core
+
+
+def qkv_kernel(
+    ids, xo_ref, xg_ref, n_ref, wq_ref, wk_ref, wv_ref, gq_ref, gk_ref, gv_ref, sq_ref, sk_ref, sv_ref,
+    bq_ref, bk_ref, bv_ref, cs_ref, send_ref, ain_ref, min_ref
+):
+    rows, width = xo_ref.shape
+    half = width // 2
+    q4 = half // 2
+
+    @pl.when(pl.program_id(0) == 0)
+    def _():
+        for s in range(2):
+            x = xo_ref[...] if s == 0 else jnp.concatenate([xg_ref[0:rows, :], xg_ref[rows:, :]], axis=1)
+            xhat, _ = _norm(x)
+            ain_ref[s * rows : (s + 1) * rows, :] = (xhat * n_ref[0:1, :] + n_ref[1:2, :]).astype(bf16)
+            min_ref[s * rows : (s + 1) * rows, :] = (xhat * n_ref[2:3, :] + n_ref[3:4, :]).astype(bf16)
+
+    me = ids[0]
+    core = ids[1]
+    base = (1 - me) * half
+    a_own = ain_ref[:, pl.ds(pl.multiple_of(me * half, half), half)]
+    a_got = ain_ref[:, pl.ds(pl.multiple_of(base + core * q4, q4), q4)]
+    a_sib = ain_ref[:, pl.ds(pl.multiple_of(base + (1 - core) * q4, q4), q4)]
+    cos = cs_ref[0:8, :]
+    sin = cs_ref[8:16, :]
+    for n, (w, g, sb, b) in enumerate(
+        (
+            (wq_ref, gq_ref, sq_ref, bq_ref),
+            (wk_ref, gk_ref, sk_ref, bk_ref),
+            (wv_ref, gv_ref, sv_ref, bv_ref),
+        )
+    ):
+        t = _nn(a_own, w[...]) + _nn(a_got, g[...]) + _nn(a_sib, sb[...]) + b[...]
+        t = t.T
+        for s in range(2):
+            for k in range(2):
+                v = t[k * HD : (k + 1) * HD, s * rows : (s + 1) * rows]
+                if n < 2:
+                    lead = v[0:8]
+                    trail = v[8:16]
+                    v = jnp.concatenate([lead * cos - trail * sin, trail * cos + lead * sin, v[16:]], axis=0)
+                send_ref[s, k, n * HD : (n + 1) * HD, :] = v.astype(bf16)
+
+
+def _wq_specs(half, width, rows):
+    own = lambda p: pl.BlockSpec((half, 128), lambda i, ids: (0, p * (width // 128) + ids[0] * (half // 128) + i))
+    got = lambda p: pl.BlockSpec((half // 2, 128), lambda i, ids: (2 * rows // (half // 2) + p, i))
+    sib = lambda p: pl.BlockSpec((half // 2, 128), lambda i, ids: (p, i))
+    return [own(p) for p in range(3)] + [got(p) for p in range(3)] + [sib(p) for p in range(3)]
+
+
+def _x_got_spec(rows, half):
+    return pl.BlockSpec((2 * rows, half), lambda i, ids: (0, 0))
+
+
+def qkv_forward(ids, xo, got, norms, w_own, w_sib, bias, cs):
+    rows, width = xo.shape
+    half = width // 2
+    full = lambda a: pl.BlockSpec(a.shape, lambda i, ids: (0,) * a.ndim)
+    bsp = lambda p: pl.BlockSpec((1, 128), lambda i, ids: (0, p * (half // 128) + i))
+    heads = half // HD
+    res = lambda: pl.BlockSpec((2 * rows, width), lambda i, ids: (0, 0))
+    return pl.pallas_call(
+        qkv_kernel,
+        grid_spec=pltpu.PrefetchScalarGridSpec(
+            num_scalar_prefetch=1,
+            grid=(half // 128,),
+            in_specs=[full(xo), _x_got_spec(rows, half), full(norms)]
+            + _wq_specs(half, width, rows)
+            + [bsp(p) for p in range(3)]
+            + [full(cs)],
+            out_specs=(pl.BlockSpec((2, 2, 3 * HD, rows), lambda i, ids: (0, i, 0, 0)), res(), res()),
+        ),
+        out_shape=(
+            jax.ShapeDtypeStruct((2, heads, 3 * HD, rows), bf16),
+            jax.ShapeDtypeStruct((2 * rows, width), bf16),
+            jax.ShapeDtypeStruct((2 * rows, width), bf16),
+        ),
+        compiler_params=_params(),
+        name="qkv_forward",
+    )(ids, xo, got, norms, w_own, w_own, w_own, got, got, got, w_sib, w_sib, w_sib, bias, bias, bias, cs)
+
+
+def mlp_kernel(
+    ids, x_ref, dy_ref, wo_ref, wg_ref, ws_ref, wd_ref, bu_ref, y_ref, dx_ref, gu_ref, gd_ref, gb_ref, xt_s
+):
     first = pl.program_id(0) == 0
+    rows, width = x_ref.shape
+    half = width // 2
+    q4 = half // 2
+    me = ids[0]
+    core = ids[1]
+    base = (1 - me) * half
+    spans = (
+        (pl.multiple_of(me * half, half), half, wo_ref),
+        (pl.multiple_of(base + core * q4, q4), q4, wg_ref),
+        (pl.multiple_of(base + (1 - core) * q4, q4), q4, ws_ref),
+    )
 
     @pl.when(first)
     def _():
         xt_s[...] = x_ref[...].astype(f32).T.astype(bf16)
-
-    x = x_ref[...]
+        y_ref[...] = jnp.zeros_like(y_ref)
+        dx_ref[...] = jnp.zeros_like(dx_ref)
+
     dy = dy_ref[...]
-    wu = wu_ref[...]
     wd = wd_ref[...]
-    u = _nn(x, wu) + bu_ref[...]
+    u = bu_ref[...] + sum(_nn(x_ref[:, pl.ds(o, n)], w[...]) for o, n, w in spans)
     cdf = 0.5 * (1.0 + lax.erf(u * (1.0 / math.sqrt(2.0))))
     pdf = jnp.exp(-0.5 * u * u) * (1.0 / math.sqrt(2.0 * math.pi))
     act = (u * cdf).astype(bf16)
     du = (_nt(dy, wd) * (cdf + u * pdf)).astype(bf16)
-    y = _nn(act, wd)
-    dx = _nt(du, wu)
-
-    @pl.when(first)
-    def _():
-        y_ref[...] = y
-        dx_ref[...] = dx
-
-    @pl.when(jnp.logical_not(first))
-    def _():
-        y_ref[...] += y
-        dx_ref[...] += dx
-
+    y_ref[...] += _nn(act, wd)
+    for o, n, w in spans:
+        dx_ref[:, pl.ds(o, n)] += _nt(du, w[...])
     gd_ref[...] = lax.dot_general(
         act, dy, (((0,), (0,)), ((), ())), preferred_element_type=f32
     ).astype(bf16)
-    gu_ref[...] = _nn(xt_s[...], du).astype(bf16)
+    gu = _nn(xt_s[...], du).astype(bf16)
+    n = gu_ref.shape[0]
+    r = half // n
+    for h in range(2):
+        for c in range(n):
+            gu_ref[c, h * r : (h + 1) * r, :] = gu[h * half + c * r : h * half + (c + 1) * r, :]
     gb_ref[...] = jnp.sum(du.astype(f32), axis=0, keepdims=True)
 
 
-def mlp(x, dy, wu, wd, bu, tile=256):
+def mlp(ids, x, dy, w_own, w_got, w_sib, wd, bu, n, tile=256):
     rows, width = x.shape
-    hidden = wu.shape[1]
-    whole = pl.BlockSpec((rows, width), lambda i: (0, 0))
-    cols = pl.BlockSpec((width, tile), lambda i: (0, i))
-    down = pl.BlockSpec((tile, width), lambda i: (i, 0))
-    vec = pl.BlockSpec((1, tile), lambda i: (0, i))
+    half = width // 2
+    hidden = w_got.shape[1]
+    steps = hidden // tile
+    whole = pl.BlockSpec((rows, width), lambda i, ids: (0, 0))
+    down = pl.BlockSpec((tile, width), lambda i, ids: (i, 0))
+    vec = pl.BlockSpec((1, tile), lambda i, ids: (0, i))
     return pl.pallas_call(
         mlp_kernel,
-        grid=(hidden // tile,),
-        in_specs=[whole, whole, cols, down, vec],
-        out_specs=(whole, whole, cols, down, vec),
+        grid_spec=pltpu.PrefetchScalarGridSpec(
+            num_scalar_prefetch=1,
+            grid=(steps,),
+            in_specs=[
+                whole,
+                whole,
+                pl.BlockSpec((half, tile), lambda i, ids: (0, ids[0] * steps + i)),
+                pl.BlockSpec((half // 2, tile), lambda i, ids: (0, i)),
+                pl.BlockSpec((half // 2, tile), lambda i, ids: (0, i)),
+                down,
+                vec,
+            ],
+            out_specs=(whole, whole, pl.BlockSpec((n, width // n, tile), lambda i, ids: (0, 0, i)), down, vec),
+            scratch_shapes=[pltpu.VMEM((width, rows), bf16)],
+        ),
         out_shape=(
             jax.ShapeDtypeStruct((rows, width), f32),
             jax.ShapeDtypeStruct((rows, width), f32),
-            jax.ShapeDtypeStruct((width, hidden), bf16),
+            jax.ShapeDtypeStruct((n, width // n, hidden), bf16),
             jax.ShapeDtypeStruct((hidden, width), bf16),
             jax.ShapeDtypeStruct((1, hidden), f32),
         ),
-        scratch_shapes=[pltpu.VMEM((width, rows), bf16)],
-        compiler_params=pltpu.CompilerParams(vmem_limit_bytes=56 << 20),
+        compiler_params=_params(),
+        cost_estimate=pl.CostEstimate(
+            flops=12 * rows * width * hidden, transcendentals=2 * rows * hidden, bytes_accessed=24 << 20
+        ),
         name="mlp",
-    )(x, dy, wu, wd, bu)
+    )(ids, x, dy, w_own, w_got, w_sib, wd, bu)
+
+
+def qkv_back_kernel(
+    ids, d_ref, a_ref, xo_ref, xg_ref, n_ref, wq_ref, wk_ref, wv_ref, gq_ref, gk_ref, gv_ref, sq_ref, sk_ref,
+    sv_ref, dm_ref, ob_ref, dy_ref, gb_ref, ga_ref, gb2_ref, eo_ref, ex_ref, at_s, da_s, bs_s
+):
+    rows, width = xo_ref.shape
+    half = width // 2
+    q4 = half // 2
+    me = ids[0]
+    core = ids[1]
+    base = (1 - me) * half
+    i = pl.program_id(0)
+    outs = (ga_ref, gb2_ref)
+    n = ga_ref.shape[0]
+    r = half // (2 * n)
+    lanes = pl.ds(pl.multiple_of(i * 128, 128), 128)
+
+    @pl.when(i == 0)
+    def _():
+        at_s[...] = a_ref[...].astype(f32).T.astype(bf16)
+        da_s[...] = jnp.zeros_like(da_s)
+
+    ones = jnp.ones((8, rows), bf16)
+    for p, (w, gw, sw) in enumerate(
+        ((wq_ref, gq_ref, sq_ref), (wk_ref, gk_ref, sk_ref), (wv_ref, gv_ref, sv_ref))
+    ):
+        g = jnp.zeros((width, 128), f32)
+        b = jnp.zeros((8, 128), f32)
+        for s in range(2):
+            dp = jnp.concatenate([d_ref[s, k, p * HD : (p + 1) * HD, :] for k in range(2)], axis=0)
+            g = g + _nt(at_s[:, s * rows : (s + 1) * rows], dp)
+            b = b + _nt(ones, dp)
+            dt = dp.astype(f32).T.astype(bf16)
+            for o, m, ref in (
+                (pl.multiple_of(me * half, half), half, w),
+                (pl.multiple_of(base + core * q4, q4), q4, gw),
+                (pl.multiple_of(base + (1 - core) * q4, q4), q4, sw),
+            ):
+                da_s[s * rows : (s + 1) * rows, pl.ds(o, m)] += _nt(dt, ref[...])
+        bs_s[p * 8 : (p + 1) * 8, lanes] = b
+        g16 = g.astype(bf16)
+        for h in range(2):
+            for c in range(n):
+                for a in range(2):
+                    at = h * half + (c * 2 + a) * r
+                    u = (h * 3 + p) * r
+                    outs[a][c, u : u + r, lanes] = g16[at : at + r, :]
+
+    go = sum(_nn(ob_ref[s], dy_ref[s * rows : (s + 1) * rows, :]) for s in range(2)).astype(bf16)
+    per = 128 // (2 * r)
+    for k in range(per):
+        for a in range(2):
+            at = (k * 2 + a) * r
+            for h in range(2):
+                u = (6 + h) * r
+                outs[a][i * per + k, u : u + r, :] = go[at : at + r, h * half : (h + 1) * half]
+
+    @pl.when(i == pl.num_programs(0) - 1)
+    def _():
+        sums = [jnp.zeros((1, width), f32) for _ in range(4)]
+        for s in range(2):
+            x = xo_ref[...] if s == 0 else jnp.concatenate([xg_ref[0:rows, :], xg_ref[rows:, :]], axis=1)
+            xhat, _ = _norm(x)
+            da = da_s[s * rows : (s + 1) * rows, :]
+            dm = dm_ref[s * rows : (s + 1) * rows, :]
+            e = da * n_ref[0:1, :] + dm * n_ref[2:3, :]
+            if s == 0:
+                eo_ref[...] = e
+            else:
+                ex_ref[...] = e.astype(bf16)
+            for k, v in enumerate((da * xhat, da, dm * xhat, dm)):
+                sums[k] = sums[k] + jnp.sum(v, axis=0, keepdims=True)
+        sums.append(jnp.sum(dy_ref[0:rows, :].astype(f32), axis=0, keepdims=True))
+        flat = [v[:, h * half : (h + 1) * half] for v in sums for h in range(2)]
+        zero = jnp.zeros((1, half), f32)
+        for p in range(3):
+            flat += [jnp.where(me == k, bs_s[p * 8 : p * 8 + 1, :], zero) for k in range(2)]
+        hid = gb_ref.shape[1] // half
+        flat += [
+            jnp.where(me == k, gb_ref[:, t * half : (t + 1) * half], zero) for k in range(2) for t in range(hid)
+        ]
+        flat += [zero] * (2 * n - len(flat))
+        pad = jnp.zeros((6, half), f32)
+        top = 8 * r
+        for c in range(n):
+            gb2_ref[c, top : top + 8, :] = jnp.concatenate([flat[2 * c], flat[2 * c + 1], pad], axis=0).astype(bf16)
+
+
+def qkv_backward(ids, d, a, xo, got, norms, w_own, w_sib, d_mlp, ob, dy, gb_up, n):
+    rows, width = xo.shape
+    half = width // 2
+    r = half // (2 * n)
+    full = lambda v: pl.BlockSpec(v.shape, lambda i, ids: (0,) * v.ndim)
+    out = [
+        jax.ShapeDtypeStruct((n, 8 * r, half), bf16),
+        jax.ShapeDtypeStruct((n, 8 * r + 8, half), bf16),
+        jax.ShapeDtypeStruct((rows, width), f32),
+        jax.ShapeDtypeStruct((rows, width), bf16),
+    ]
+    return pl.pallas_call(
+        qkv_back_kernel,
+        grid_spec=pltpu.PrefetchScalarGridSpec(
+            num_scalar_prefetch=1,
+            grid=(half // 128,),
+            in_specs=[pl.BlockSpec((2, 2, 3 * HD, rows), lambda i, ids: (0, i, 0, 0))]
+            + [full(a), full(xo), _x_got_spec(rows, half), full(norms)]
+            + _wq_specs(half, width, rows)
+            + [full(d_mlp), pl.BlockSpec((2, 128, rows), lambda i, ids: (0, i, 0)), full(dy), full(gb_up)],
+            out_specs=tuple(full(v) for v in out),
+            scratch_shapes=[
+                pltpu.VMEM((width, 2 * rows), bf16),
+                pltpu.VMEM((2 * rows, width), f32),
+                pltpu.VMEM((24, half), f32),
+            ],
+        ),
+        out_shape=tuple(out),
+        compiler_params=_params(),
+        name="qkv_backward",
+    )(ids, d, a, xo, got, norms, w_own, w_own, w_own, got, got, got, w_sib, w_sib, w_sib, d_mlp, ob, dy, gb_up)
+
+
+def join_kernel(ids, own_ref, got_ref, o_ref):
+    mine = (pl.program_id(0) // (pl.num_programs(0) // 2)) == ids[1]
+
+    @pl.when(mine)
+    def _():
+        o_ref[...] = own_ref[...].astype(f32)
+
+    @pl.when(jnp.logical_not(mine))
+    def _():
+        o_ref[...] = got_ref[...].astype(f32)
+
+
+def join(ids, own, got):
+    n, r, w = own.shape
+    src = pl.BlockSpec((1, r, w), lambda i, ids: (i % n, 0, 0))
+    return pl.pallas_call(
+        join_kernel,
+        grid_spec=pltpu.PrefetchScalarGridSpec(
+            num_scalar_prefetch=1,
+            grid=(2 * n,),
+            in_specs=[src, src],
+            out_specs=pl.BlockSpec((1, r, w), lambda i, ids: (i, 0, 0)),
+        ),
+        out_shape=jax.ShapeDtypeStruct((2 * n, r, w), f32),
+        compiler_params=_params(),
+        name="join",
+    )(ids, own, got)
+
+
+def unpack_kernel(ids, ao_ref, ag_ref, bo_ref, bg_ref, q_ref, o_ref, s_ref):
+    mine = (pl.program_id(0) // (pl.num_programs(0) // 2)) == ids[1]
+    r = ao_ref.shape[1] // 8
+    half = ao_ref.shape[2]
+    for a, (own, got) in enumerate(((ao_ref, ag_ref), (bo_ref, bg_ref))):
+        v = jnp.where(mine, own[0].astype(f32), got[0].astype(f32))
+        for w in range(2):
+            for p in range(3):
+                u = (w * 3 + p) * r
+                at = (p * 2 + w) * half
+                q_ref[a * r : (a + 1) * r, at : at + half] = v[u : u + r, :]
+            u = (6 + w) * r
+            o_ref[a * r : (a + 1) * r, w * half : (w + 1) * half] = v[u : u + r, :]
+        if a == 1:
+            s_ref[0] = v[8 * r : 8 * r + 8, :]
+
+
+def unpack(ids, a_own, a_got, b_own, b_got):
+    n, ra, half = a_own.shape
+    r = ra // 8
+    spec = lambda v: pl.BlockSpec((1,) + v.shape[1:], lambda i, ids: (i % n, 0, 0))
+    return pl.pallas_call(
+        unpack_kernel,
+        grid_spec=pltpu.PrefetchScalarGridSpec(
+            num_scalar_prefetch=1,
+            grid=(2 * n,),
+            in_specs=[spec(v) for v in (a_own, a_got, b_own, b_got)],
+            out_specs=(
+                pl.BlockSpec((2 * r, 6 * half), lambda i, ids: (i, 0)),
+                pl.BlockSpec((2 * r, 2 * half), lambda i, ids: (i, 0)),
+                pl.BlockSpec((1, 8, half), lambda i, ids: (i, 0, 0)),
+            ),
+        ),
+        out_shape=(
+            jax.ShapeDtypeStruct((4 * n * r, 6 * half), f32),
+            jax.ShapeDtypeStruct((4 * n * r, 2 * half), f32),
+            jax.ShapeDtypeStruct((2 * n, 8, half), f32),
+        ),
+        compiler_params=_params(),
+        name="unpack",
+    )(ids, a_own, a_got, b_own, b_got)
+
+
+def last_kernel(eo_ref, er_ref, x_ref, c_ref, live_ref, o_ref):
+    xhat, inv = _norm(x_ref[...])
+    e = eo_ref[...] + er_ref[...].astype(f32)
+    dx = inv * (
+        e - jnp.mean(e, axis=-1, keepdims=True) - xhat * jnp.mean(e * xhat, axis=-1, keepdims=True)
+    )
+    o_ref[...] = live_ref[...] * c_ref[...].astype(f32) + dx
+
+
+def last(e_own, e_got, x, cot, live):
+    return pl.pallas_call(
+        last_kernel,
+        out_shape=jax.ShapeDtypeStruct(x.shape, f32),
+        compiler_params=_params(),
+        name="token_grad",
+    )(e_own, e_got, x, cot, live)
 
 
 def fast_shards(
@@ -600,152 +931,148 @@
     seq = rows * n_ctx
     heads = H // 2
     hid = w_up.shape[1] // 2
-    pair_perm = [(i, i ^ 1) for i in range(n_ctx)]
+    ids = jnp.stack([me, core]).astype(jnp.int32)
+    CORE, X, ZN, ZF = 0, 1, 2, 3
 
     def swap(v):
         return lax.ppermute(v, "wsh", SWAP)
 
-    def fetch_rows(mine, other):
-        q = half // 2
-        got = swap(lax.dynamic_slice_in_dim(other, core * q, q))
-        sib = lax.ppermute(got, "ctx", pair_perm)
-        out = jnp.zeros((width, mine.shape[1]), mine.dtype)
-        out = lax.dynamic_update_slice_in_dim(out, mine, me * half, 0)
-        base = (1 - me) * half
-        out = lax.dynamic_update_slice_in_dim(out, got, base + core * q, 0)
-        return lax.dynamic_update_slice_in_dim(out, sib, base + (1 - core) * q, 0)
+    def flip(v, bit):
+        return lax.ppermute(v, "ctx", [(i, i ^ (1 << bit)) for i in range(n_ctx)])
+
+    def bit_of(bit):
+        return (ctx >> bit) & 1
+
+    def halve(v, bit):
+        b = bit_of(bit)
+        v = v.reshape((2, v.shape[0] // 2) + v.shape[1:])
+        got = flip(lax.dynamic_index_in_dim(v, 1 - b, 0, keepdims=False), bit)
+        keep = lax.dynamic_index_in_dim(v, b, 0, keepdims=False)
+        return (keep.astype(f32) + got.astype(f32)).astype(bf16)
+
+    def ordered(first, a, b, axis=0):
+        return jnp.where(first == 0, jnp.concatenate([a, b], axis), jnp.concatenate([b, a], axis))
+
+    def double(v, bit):
+        return ordered(bit_of(bit), v, flip(v, bit))
+
+    half_core = lambda v: lax.dynamic_slice_in_dim(v, core * (half // 2), half // 2, 0)
 
     len_parts = jnp.stack([lengths[0] // 64, lengths[0] % 64]).astype(bf16)
     small = jnp.concatenate(
         [ln1_gain, ln1_bias, ln2_gain, ln2_bias, b_out, b_down, b_qkv, len_parts, jnp.zeros((126,), bf16)]
-    )
-    small = lax.all_gather(small, "wsh", axis=0, tiled=False)
+    )[None]
+    small = ordered(me, small, swap(small))
+    cot_own = cotangent[0]
+    cot_got = swap(cot_own)
+    other = (1 - me) * half
+    cols = [lax.dynamic_slice_in_dim(half_core(w_qkv), p * width + other, half, 1) for p in range(3)]
+    wu_send = lax.dynamic_slice_in_dim(half_core(w_up), (1 - me) * hid, hid, 1)
+    x_own = tokens[0]
+    pack = jnp.concatenate([x_own[:, :half], x_own[:, half:]] + cols)
+    cot_got, pack = lax.optimization_barrier((cot_got, pack))
+    got = swap(pack)
+    wq_sib = flip(got[2 * rows :], CORE)
+    got, wu_send = lax.optimization_barrier((got, wu_send))
+    wu_got = swap(wu_send)
+    wu_sib = flip(wu_got, CORE)
+
     vec = lambda i: small[:, i * half : (i + 1) * half].reshape(width).astype(f32)
-    g1, s1, g2, s2, bo, bd = [vec(i) for i in range(6)]
-    qkv_bias = small[:, 6 * half : 9 * half].reshape(3, 2, half).astype(f32)
-    qkv_bias = lax.dynamic_index_in_dim(qkv_bias, me, 1, keepdims=False).reshape(3 * half)
+    norms = jnp.stack([vec(i) for i in range(4)])
+    bias_out = vec(4) + vec(5)
+    qkv_bias = small[:, 6 * half : 9 * half].astype(f32).reshape(3, width)
+    qkv_bias = lax.dynamic_slice_in_dim(qkv_bias, me * half, half, 1).reshape(1, 3 * half)
     lens = small[:, 9 * half : 9 * half + 2].astype(jnp.int32)
     lens = lens[:, 0] * 64 + lens[:, 1]
     other_len = lens[1 - me]
 
-    x2 = jnp.stack([tokens[0], swap(tokens[0])])
-    cot2 = jnp.stack([cotangent[0], swap(cotangent[0])])
-    wq4 = w_qkv.reshape(half, 3, 2, half)
-    wq_mine = lax.dynamic_index_in_dim(wq4, me, 2, keepdims=False).reshape(half, 3 * half)
-    wq_send = lax.dynamic_index_in_dim(wq4, 1 - me, 2, keepdims=False).reshape(half, 3 * half)
-    wq = fetch_rows(wq_mine, wq_send)
-    wu_mine = lax.dynamic_slice_in_dim(w_up, me * hid, hid, 1)
-    wu_send = lax.dynamic_slice_in_dim(w_up, (1 - me) * hid, hid, 1)
-    wu = fetch_rows(wu_mine, wu_send)
-
     own_blocks = lax.dynamic_slice_in_dim(block_map, 2 * ctx, 2)
     offs = jnp.arange(HB, dtype=jnp.int32)
     positions = (own_blocks[:, None] * HB + offs[None, :]).reshape(rows)
-    live2 = jnp.stack([positions < lengths[0], positions < other_len]).astype(f32)[..., None]
+    live_own = (positions < lengths[0]).astype(f32)[:, None]
+    live_got = (positions < other_len).astype(f32)[:, None]
     freq = 10000.0 ** (-jnp.arange(ROT // 2, dtype=f32) * 2.0 / ROT)
     ang = freq[:, None] * jnp.arange(seq, dtype=jnp.int32).astype(f32)[None, :]
     table = jnp.concatenate([jnp.cos(ang), jnp.sin(ang)])
     own_ang = freq[:, None] * positions.astype(f32)[None, :]
-    cos = jnp.cos(own_ang)[None, :, None, :]
-    sin = jnp.sin(own_ang)[None, :, None, :]
-
-    xf = x2.astype(f32)
-    mean = jnp.mean(xf, axis=-1, keepdims=True)
-    cen = xf - mean
-    inv = lax.rsqrt(jnp.mean(cen * cen, axis=-1, keepdims=True) + epsilon)
-    xhat = cen * inv
-    attn_in = (xhat * g1 + s1).astype(bf16)
-    mlp_in = (xhat * g2 + s2).astype(bf16)
-    dy2 = (live2 * cot2.astype(f32)).astype(bf16)
-
-    qkv = lax.dot_general(
-        wq, attn_in.reshape(2 * rows, width), (((0,), (1,)), ((), ())), preferred_element_type=f32
-    )
-    qkv = (qkv + qkv_bias[:, None]).reshape(3, heads, HD, 2, rows)
-
-    def rope(v):
-        a = v[:, :8]
-        b = v[:, 8:16]
-        return jnp.concatenate([a * cos - b * sin, b * cos + a * sin, v[:, 16:]], axis=1)
-
-    parts = jnp.stack([rope(qkv[0]), rope(qkv[1]), qkv[2]]).astype(bf16)
-    send = parts.transpose(3, 1, 0, 2, 4).reshape(2 * heads, 3 * HD, rows)
-    dctx = jnp.einsum("ed,std->set", w_out, dy2, preferred_element_type=f32).astype(bf16)
-    dctx = dctx.reshape(2 * heads, HD, rows)
+    own_table = jnp.concatenate([jnp.cos(own_ang), jnp.sin(own_ang)])
 
     def exchange(v):
         return lax.all_to_all(v, "ctx", 0, 0, tiled=False)
 
-    qkv_head = exchange(send)
-    do_head = exchange(dctx)
+    dy = jnp.concatenate(
+        [(live_own * cot_own.astype(f32)).astype(bf16), (live_got * cot_got.astype(f32)).astype(bf16)]
+    )
+    dctx = jnp.einsum("ed,std->set", w_out, dy.reshape(2, rows, width), preferred_element_type=f32).astype(bf16)
+    do_head = exchange(dctx.reshape(2 * heads, HD, rows))
+
+    send, attn_in, mlp_in = qkv_forward(ids, x_own, got, norms, w_qkv, wq_sib, qkv_bias, own_table)
+    qkv_head = exchange(send.reshape(2 * heads, 3 * HD, rows))
+
+    mlp_in, do_head = lax.optimization_barrier((mlp_in, do_head))
 
     y_mlp, d_mlp, g_up, g_down, gb_up = mlp(
-        mlp_in.reshape(2 * rows, width),
-        dy2.reshape(2 * rows, width),
-        wu,
-        w_down,
-        b_up.astype(f32)[None, :],
-    )
-    up_keep = lax.dynamic_slice_in_dim(g_up, me * half, half, 0)
-    up_send = lax.dynamic_slice_in_dim(g_up, (1 - me) * half, half, 0)
-    up_got = swap(up_send)
-
-    def join_cols(keep, got, n):
-        a = keep.reshape(half, -1, n)
-        b = got.reshape(half, -1, n)
-        pair = jnp.where(me == 0, jnp.stack([a, b], axis=2), jnp.stack([b, a], axis=2))
-        return pair.reshape(half, -1)
-
-    tot_down, tot_up = lax.psum((g_down, join_cols(up_keep, up_got, hid)), "ctx")
+        ids, mlp_in, dy, w_up, wu_got, wu_sib, w_down, b_up.astype(f32)[None, :], n_ctx
+    )
+
+    chain_a = (CORE, X, ZN, ZF)
+    chain_b = (CORE, ZN, ZF, X)
+    v_down = g_down.reshape(n_ctx, hid // n_ctx, width)
+    v_up = g_up
+    qkv_head, v_down, v_up = lax.optimization_barrier((qkv_head, v_down, v_up))
+    v_down = halve(v_down, chain_a[0])
+    v_up = halve(v_up, chain_b[0])
+    qkv_head, v_down, v_up = lax.optimization_barrier((qkv_head, v_down, v_up))
+    v_down = halve(v_down, chain_a[1])
+    v_up = halve(v_up, chain_b[1])
 
     o_head, lse = attn_fwd(block_map, qkv_head, bq=1024, bk=1024)
     ob = exchange(o_head).reshape(2, half, rows)
+    qkv_head, v_down, v_up = lax.optimization_barrier((qkv_head, v_down, v_up))
     g_head = attn_bwd(block_map, qkv_head, o_head, do_head, lse, table)
-    d_qkv = exchange(g_head).reshape(2, heads, 3, HD, rows)
-    d_qkv = d_qkv.transpose(0, 2, 1, 3, 4).reshape(2, 3 * half, rows)
+    d_qkv = exchange(g_head).reshape(2, heads, 3 * HD, rows)
+
+    for a, b in zip(chain_a[2:], chain_b[2:]):
+        v_down = halve(v_down, a)
+        v_up = halve(v_up, b)
+    v_up = v_up.reshape(1, 2, half // n_ctx, hid)
+    up_keep = lax.dynamic_index_in_dim(v_up, me, 1, keepdims=False)
+    up_got = swap(lax.dynamic_index_in_dim(v_up, 1 - me, 1, keepdims=False))
+    v_up = ordered(me, up_keep, up_got, axis=2)
+    for a, b in zip(chain_a[:0:-1], chain_b[:0:-1]):
+        v_down = double(v_down, a)
+        v_up = double(v_up, b)
+    tot_down = join(ids, v_down, flip(v_down, CORE)).reshape(hid, width)
+    tot_up = join(ids, v_up, flip(v_up, CORE)).reshape(half, 2 * hid)
 
     part = jnp.einsum("sct,cd->std", ob, w_out, preferred_element_type=f32) + y_mlp.reshape(
         2, rows, width
     )
     y_got = swap(part[1].astype(bf16)).astype(f32)
-    output = (live2[0] * (xf[0] + part[0] + y_got + bo + bd)).astype(bf16)
-    g_out = jnp.einsum("sct,std->cd", ob, dy2, preferred_element_type=f32).astype(bf16)
-
-    g_qkv = jnp.einsum("stf,sct->fc", attn_in, d_qkv, preferred_element_type=f32).astype(bf16)
-    d_attn = jnp.einsum("sct,fc->stf", d_qkv, wq, preferred_element_type=f32)
-    q_keep = lax.dynamic_slice_in_dim(g_qkv, me * half, half, 0)
-    q_send = lax.dynamic_slice_in_dim(g_qkv, (1 - me) * half, half, 0)
-    q_tot = join_cols(q_keep, swap(q_send), half)
-    q_tot, g_out, tot_down, tot_up = lax.optimization_barrier((q_tot, g_out, tot_down, tot_up))
-    tot_out, tot_qkv = lax.psum((g_out, q_tot), "ctx")
-
-    d_mlp = d_mlp.reshape(2, rows, width)
-    e = d_attn * g1 + d_mlp * g2
-    e_own = e[0] + swap(e[1].astype(bf16)).astype(f32)
-    dx = inv[0] * (
-        e_own
-        - jnp.mean(e_own, axis=-1, keepdims=True)
-        - xhat[0] * jnp.mean(e_own * xhat[0], axis=-1, keepdims=True)
-    )
-    grad_tokens = live2[0] * cot2[0].astype(f32) + dx
-
-    both = (0, 1)
-    gb_qkv = jnp.sum(d_qkv.astype(f32), axis=(0, 2)).reshape(3, 1, half)
-    mine = (jnp.arange(2) == me).astype(f32)
-    gb_qkv = (gb_qkv * mine[None, :, None]).reshape(3 * width)
-    gb_hid = (gb_up * mine[:, None]).reshape(2 * hid)
-    flat = jnp.concatenate(
-        [
-            jnp.sum(d_attn * xhat, axis=both),
-            jnp.sum(d_attn, axis=both),
-            jnp.sum(d_mlp * xhat, axis=both),
-            jnp.sum(d_mlp, axis=both),
-            jnp.sum(dy2[0].astype(f32), axis=0),
-            gb_qkv,
-            gb_hid,
-        ]
-    )
-    flat = lax.psum(flat, ("ctx", "wsh"))
+    output = (live_own * (x_own.astype(f32) + part[0] + y_got + bias_out)).astype(bf16)
+
+    v_a, v_b, e_own, e_send = qkv_backward(
+        ids, d_qkv, attn_in, x_own, got, norms, w_qkv, wq_sib, d_mlp, ob, dy, gb_up, n_ctx
+    )
+    for a, b in zip(chain_a, chain_b):
+        v_a = halve(v_a, a)
+        v_b = halve(v_b, b)
+    e_got = swap(e_send)
+    n3 = 3 * half // (2 * n_ctx)
+    mixed = []
+    for v, chain in ((v_a[0], chain_a), (v_b[0], chain_b)):
+        extra = v[8 * n3 // 3 :]
+        keep = lax.dynamic_slice_in_dim(v, me * n3, n3, 0)
+        give = lax.dynamic_slice_in_dim(v, (1 - me) * n3, n3, 0)
+        got = swap(jnp.concatenate([give, extra]))
+        extra = (extra.astype(f32) + got[n3:].astype(f32)).astype(bf16)
+        v = jnp.concatenate([ordered(me, keep, got[:n3]), v[2 * n3 : 8 * n3 // 3], extra])[None]
+        for a in chain[:0:-1]:
+            v = double(v, a)
+        mixed += [v, flip(v, CORE)]
+    tot_qkv, tot_out, flat = unpack(ids, *mixed)
+    grad_tokens = last(e_own, e_got, x_own, cot_own, live_own)
+    flat = flat[:, :2].reshape(2 * n_ctx * half)
 
     def own(start, size):
         return lax.dynamic_slice_in_dim(flat, start + me * size, size)
@@ -758,13 +1085,13 @@
         own(width, half),
         own(2 * width, half),
         own(3 * width, half),
-        tot_qkv.astype(f32),
+        tot_qkv,
         own(5 * width, 3 * half),
-        tot_out.astype(f32),
+        tot_out,
         gb_out,
-        tot_up.astype(f32),
+        tot_up,
         own(8 * width, hid),
-        tot_down.astype(f32),
+        tot_down,
         gb_out,
     )
 

time: 600 us -> 499 us (0.83)
  blocking collectives: 90.8 us -> 0 us
  Pallas kernels: 80.9 us -> 147 us
  local copies, waits for them, and re-layouts: 88.7 us -> 42.8 us
  waiting for transfers between devices: 232 us -> 195 us
  starting transfers between devices: 37 us -> 70.2 us
  between operations: 15.6 us -> 2.03 us
  matrix products: 11.9 us -> 2.64 us
    psum x2 -> x0, waiting for transfers between devices: 162 us -> none  [the longest x1 109 us: fast_shards(): lax.psum((g_down, join_cols(up_keep, up_got, hid)), 'ctx')]
    ppermute x2 -> x34, waiting for transfers between devices: 0.01 us -> 156 us  [flip(): return lax.ppermute(v, 'ctx', [(i, i ^ 1 << bit) for i in range(n_ctx)])]
    pallas_call x1 -> x7, Pallas kernels: 24.2 us -> 90.1 us  [the longest x2 24.9 us: join(): pl.pallas_call(join_kernel, grid_spec=pltpu.PrefetchScalarGridSpec(num_sc...]
    all_gather x1 -> x0, blocking collectives: 49.3 us -> none  [fast_shards(): small = lax.all_gather(small, 'wsh', axis=0, tiled=False)]
    all_to_all x4, waiting for transfers between devices: 46.2 us -> 0.3 us  [exchange(): return lax.all_to_all(v, 'ctx', 0, 0, tiled=False)]
    psum x1 -> x0, blocking collectives: 41.5 us -> none  [fast_shards(): flat = lax.psum(flat, ('ctx', 'wsh'))]
    ppermute x2 -> x34, starting transfers between devices: 0.5 us -> 35.5 us  [flip(): return lax.ppermute(v, 'ctx', [(i, i ^ 1 << bit) for i in range(n_ctx)])]
    ppermute x8 -> x9, waiting for transfers between devices: 23.6 us -> 39.4 us  [swap(): return lax.ppermute(v, 'wsh', SWAP)]
  transfers between devices with their start and end apart: 16 -> 47, of which waited for: 5 -> 22; matrix products, arithmetic and copies ran while one was open for 17% -> 14% of each run, Pallas kernels for 9% -> 27%
where the time goes in v2:
time: 499 us; the launch traced here: 497 us
  waiting for transfers between devices  195 us (39%)
  Pallas kernels  147 us (29%)
  starting transfers between devices  70.2 us (14%)
  local copies, waits for them, and re-layouts  42.8 us (9%)
  other arithmetic  37.3 us (7%)
    ppermute x34, waiting for transfers between devices, flip(): return lax.ppermute(v, 'ctx', [(i, i ^ 1 << bit) for i in range(n_ctx)])  156 us
    ppermute x9, waiting for transfers between devices, swap(): return lax.ppermute(v, 'wsh', SWAP)  39.4 us
    ppermute x34, starting transfers between devices, flip(): return lax.ppermute(v, 'ctx', [(i, i ^ 1 << bit) for i in range(n_ctx)])  35.5 us
    pallas_call x1, Pallas kernels, attn_bwd(): pl.pallas_call(lambda *a: attn_bwd_kernel(*a, nblk=nblk, bq=bq, bk=bk), o...  35 us
    pallas_call x2, Pallas kernels, join(): pl.pallas_call(join_kernel, grid_spec=pltpu.PrefetchScalarGridSpec(num_sc...  24.9 us
    pallas_call x1, Pallas kernels, mlp(): pl.pallas_call(mlp_kernel, grid_spec=pltpu.PrefetchScalarGridSpec(num_sca...  22.2 us
    all_to_all x4, starting transfers between devices, exchange(): return lax.all_to_all(v, 'ctx', 0, 0, tiled=False)  22.1 us
    pallas_call x1, Pallas kernels, attn_fwd(): pl.pallas_call(lambda *a: attn_fwd_kernel(*a, nblk=nblk, bq=bq, bk=bk), o...  21.7 us
  transfers between devices with their start and end apart: 47, of which 22 were waited for; matrix products, arithmetic and copies ran while one was open for 14% of the time, Pallas kernels for 27%

profile of v2, /device:TPU:0, one launch (start us, length us, event | category | flops | bytes accessed | tf_op | source)
XLA Modules:
  0.0 497.0 jit_solution(6700715114617727081)
XLA Ops:
  0.7 3.0 collective-permute-start
  4.4 4.9 concatenate.140
  9.5 1.7 slice_dynamic-update-slice_fusion.1
  11.2 1.7 slice_dynamic-update-slice_fusion
  13.7 1.8 dynamic-slice_dynamic-update-slice_fusion.2
  15.5 1.8 dynamic-slice_dynamic-update-slice_fusion.1
  17.4 1.8 dynamic-slice_dynamic-update-slice_fusion
  19.9 2.7 dynamic_slice.173
  22.8 2.1 collective-permute-start.1
  29.4 6.0 %all-to-all-start.1 = ((bf16[16,64,256]{2,1,0:T(8,128)(2,1)}), bf16[16,64,256]{2,1,0:T(8,128)(2,1)}, u32[]{:S(2)}, u32[]{:S(2)}) async-start(bf16[16,64,256]{2,1,0:T(8,128)(2,1)} %bitcast.15), calls=%async_computation.1 | async-start | bytes 1048576 | tf_op jit(solution)/shard_map/all_to_all | solution.py:1001
  35.9 17.4 %collective-permute-done.1.xg_ref.gq_ref.gk_ref.gv_ref = bf16[1280,512]{1,0:T(8,128)(2,1)S(1)} collective-permute-done((bf16[1280,512]{1,0:T(8,128)(2,1)}, bf16[1280,512]{1,0:T(8,128)(2,1)S(1)}, u32[]{:S(2)}, u32[]{:S(2)}) %collective-permute-start.1) | collective-permute-done | bytes 1310752 | tf_op jit(solution)/shard_map/ppermute | solution.py:938
  54.3 1.8 collective-permute-start.4
  58.3 9.4 %qkv_forward.1 = (bf16[2,8,192,256]{3,2,1,0:T(8,128)(2,1)}, bf16[512,1024]{1,0:T(8,128)(2,1)}, bf16[512,1024]{1,0:T(8,128)(2,1)}) custom-call(s32[2]{0:T(128)} %pad_add_fusion.ids, bf16[256,1024]{1,0:T(8,128)(2,1)} %bitcast.185, bf16[1280,512]{1,0:T(8,128)(2,1)} %copy-done.1, f32[4,1024]{1,0:T(4,128)} %maximum_convert_fusion.n_ref, ...), custom_call_target="tpu_custom_call" | custom-call | tf_op jit(solution)/shard_map/qkv_forward/pallas_call | solution.py:592
  67.7 5.9 %all-to-all-start = ((bf16[16,192,256]{2,1,0:T(8,128)(2,1)}), bf16[16,192,256]{2,1,0:T(8,128)(2,1)S(1)}, u32[]{:S(2)}, u32[]{:S(2)}) async-start(bf16[16,192,256]{2,1,0:T(8,128)(2,1)} %bitcast.219), calls=%async_computation | async-start | bytes 3145728 | tf_op jit(solution)/shard_map/all_to_all | solution.py:1001
  73.7 6.5 %collective-permute-done.4.wg_ref = bf16[256,2048]{1,0:T(8,128)(2,1)} collective-permute-done((bf16[256,2048]{1,0:T(8,128)(2,1)}, bf16[256,2048]{1,0:T(8,128)(2,1)}, u32[]{:S(2)}, u32[]{:S(2)}) %collective-permute-start.4) | collective-permute-done | bytes 1048608 | tf_op jit(solution)/shard_map/ppermute | solution.py:938
  80.8 2.4 collective-permute-done.5.ws_ref
  83.2 22.2 %mlp.1 = (f32[512,1024]{1,0:T(8,128)}, f32[512,1024]{1,0:T(8,128)}, bf16[16,64,2048]{2,1,0:T(8,128)(2,1)}, bf16[2048,1024]{1,0:T(8,128)(2,1)}, f32[1,2048]{1,0:T(1,128)}) custom-call(s32[2]{0:T(128)} %pad_add_fusion.ids, bf16[512,1024]{1,0:T(8,128)(2,1)} %get-tuple-element.51.x_ref, bf16[512,1024]{1,0:T(8,128)(2,1)} %copy-done.12, bf16[512,4096]{1,0:T(8,128)(2,1)} %wo_ref.1, ...), custom_call_target="tpu_custom_call" | custom-call | flops 12884901888 | bytes 25165824 | tf_op jit(solution)/shard_map/mlp/pallas_call | solution.py:665
  105.6 3.7 dynamic-slice_bitcast_fusion.1
  111.6 2.7 collective-permute-done.6
  114.3 3.2 fusion.1
  117.5 2.4 fusion
  121.1 2.7 collective-permute-start.9
  124.8 4.4 collective-permute-start.10
  129.7 21.7 %attn_fwd.1 = (bf16[16,64,256]{2,1,0:T(8,128)(2,1)}, f32[1,4096]{1,0:T(1,128)}) custom-call(s32[32]{0:T(128)} %a_0_.3, bf16[16,192,256]{2,1,0:T(8,128)(2,1)} %copy-done.3), custom_call_target="tpu_custom_call" | custom-call | tf_op jit(solution)/shard_map/attn_fwd/pallas_call | solution.py:438
  151.4 4.3 all-to-all-start.2
  156.4 2.7 fusion.5
  159.1 2.6 fusion.4
  161.7 35.0 %attn_bwd.1 = bf16[16,192,256]{2,1,0:T(8,128)(2,1)} custom-call(s32[32]{0:T(128)} %a_0_.3, bf16[16,192,256]{2,1,0:T(8,128)(2,1)} %copy-done.3, bf16[16,64,256]{2,1,0:T(8,128)(2,1)} %get-tuple-element.59.a_2_, bf16[16,64,256]{2,1,0:T(8,128)(2,1)} %all-to-all-done.1.a_3_, f32[1,4096]{1,0:T(1,128)} %get-tuple-element.65.a_4_, f32[16,4096]{1,0:T(8,128)} %pad_maximum_fusion.1.a_5_), custom_call_target="tpu_custom_call" | custom-call | tf_op jit(solution)/shard_map/attn_bwd/pallas_call | solution.py:498
  196.7 5.9 %all-to-all-start.3 = ((bf16[16,192,256]{2,1,0:T(8,128)(2,1)}), bf16[16,192,256]{2,1,0:T(8,128)(2,1)S(1)}, u32[]{:S(2)}, u32[]{:S(2)}) async-start(bf16[16,192,256]{2,1,0:T(8,128)(2,1)} %attn_bwd.1), calls=%async_computation.3 | async-start | bytes 3145728 | tf_op jit(solution)/shard_map/all_to_all | solution.py:1001
  202.7 1.9 dynamic-slice_bitcast_fusion.8
  204.6 2.8 collective-permute-start.30
  210.1 52.9 %collective-permute-done.30 = bf16[2,64,2048]{2,1,0:T(8,128)(2,1)S(1)} collective-permute-done((bf16[2,64,2048]{2,1,0:T(8,128)(2,1)}, bf16[2,64,2048]{2,1,0:T(8,128)(2,1)S(1)}, u32[]{:S(2)}, u32[]{:S(2)}) %collective-permute-start.30) | collective-permute-done | bytes 524320 | tf_op jit(solution)/shard_map/ppermute | solution.py:941
  266.1 6.0 %collective-permute-done.31 = bf16[1,64,2048]{2,1,0:T(8,128)(2,1)S(1)} collective-permute-done((bf16[1,64,2048]{2,1,0:T(8,128)(2,1)S(1)}, bf16[1,64,2048]{2,1,0:T(8,128)(2,1)S(1)}, u32[]{:S(2)}, u32[]{:S(2)}) %collective-permute-start.31) | collective-permute-done | bytes 262176 | tf_op jit(solution)/shard_map/ppermute | solution.py:941
  273.9 5.0 %collective-permute-done.38 = bf16[1,128,1024]{2,1,0:T(8,128)(2,1)S(1)} collective-permute-done((bf16[1,128,1024]{2,1,0:T(8,128)(2,1)S(1)}, bf16[1,128,1024]{2,1,0:T(8,128)(2,1)S(1)}, u32[]{:S(2)}, u32[]{:S(2)}) %collective-permute-start.38) | collective-permute-done | bytes 262176 | tf_op jit(solution)/shard_map/ppermute | solution.py:941
  280.8 17.6 %qkv_backward.1 = (bf16[16,128,512]{2,1,0:T(8,128)(2,1)}, bf16[16,136,512]{2,1,0:T(8,128)(2,1)}, f32[256,1024]{1,0:T(8,128)}, bf16[256,1024]{1,0:T(8,128)(2,1)}) custom-call(s32[2]{0:T(128)} %pad_add_fusion.ids, bf16[2,8,192,256]{3,2,1,0:T(8,128)(2,1)} %bitcast.194, bf16[512,1024]{1,0:T(8,128)(2,1)} %get-tuple-element.66.a_ref, bf16[256,1024]{1,0:T(8,128)(2,1)} %bitcast.186, ...), custom_call_target="tpu_custom_call" | custom-call | tf_op jit(solution)/shard_map/qkv_backward/pallas_call | solution.py:795
  298.4 2.4 dynamic-slice_bitcast_fusion.3
  304.5 2.1 maximum_select_fusion.9
  306.6 2.9 collective-permute-start.40
  309.5 1.9 collective-permute-done.33
  312.6 3.0 collective-permute-start.34
  315.6 13.8 %collective-permute-done.40 = bf16[2,128,1024]{2,1,0:T(8,128)(2,1)} collective-permute-done((bf16[2,128,1024]{2,1,0:T(8,128)(2,1)}, bf16[2,128,1024]{2,1,0:T(8,128)(2,1)}, u32[]{:S(2)}, u32[]{:S(2)}) %collective-permute-start.40) | collective-permute-done | bytes 524320 | tf_op jit(solution)/shard_map/ppermute | solution.py:941
  329.4 1.7 maximum_select_fusion.5
  331.1 2.4 collective-permute-start.41
  336.9 1.8 collective-permute-done.34
  339.1 28.7 %collective-permute-done.13 = bf16[4,128,512]{2,1,0:T(8,128)(2,1)S(1)} collective-permute-done((bf16[4,128,512]{2,1,0:T(8,128)(2,1)S(1)}, bf16[4,128,512]{2,1,0:T(8,128)(2,1)S(1)}, u32[]{:S(2)}, u32[]{:S(2)}) %collective-permute-start.13) | collective-permute-done | bytes 524320 | tf_op jit(solution)/shard_map/ppermute | solution.py:941
  368.3 2.0 collective-permute-start.23
  370.3 14.7 %collective-permute-done.14 = bf16[2,128,512]{2,1,0:T(8,128)(2,1)S(1)} collective-permute-done((bf16[2,128,512]{2,1,0:T(8,128)(2,1)S(1)}, bf16[2,128,512]{2,1,0:T(8,128)(2,1)S(1)}, u32[]{:S(2)}, u32[]{:S(2)}) %collective-permute-start.14) | collective-permute-done | bytes 262176 | tf_op jit(solution)/shard_map/ppermute | solution.py:941
  387.1 5.8 %collective-permute-done.15 = bf16[1,128,512]{2,1,0:T(8,128)(2,1)S(1)} collective-permute-done((bf16[1,128,512]{2,1,0:T(8,128)(2,1)S(1)}, bf16[1,128,512]{2,1,0:T(8,128)(2,1)S(1)}, u32[]{:S(2)}, u32[]{:S(2)}) %collective-permute-start.15) | collective-permute-done | bytes 131104 | tf_op jit(solution)/shard_map/ppermute | solution.py:941
  394.1 3.0 collective-permute-done.16
  398.5 3.1 collective-permute-done.25
  404.2 2.3 collective-permute-start.18
  406.8 3.0 collective-permute-start.27
  409.7 1.6 maximum_select_fusion.own_ref
  411.4 6.7 %collective-permute-done.18 = bf16[2,128,512]{2,1,0:T(8,128)(2,1)S(1)} collective-permute-done((bf16[2,128,512]{2,1,0:T(8,128)(2,1)S(1)}, bf16[2,128,512]{2,1,0:T(8,128)(2,1)S(1)}, u32[]{:S(2)}, u32[]{:S(2)}) %collective-permute-start.18) | collective-permute-done | bytes 262176 | tf_op jit(solution)/shard_map/ppermute | solution.py:941
  418.2 1.7 collective-permute-start.19
  419.9 2.5 collective-permute-done.27
  422.6 1.9 fusion.16
  426.3 10.0 %collective-permute-done.28 = bf16[4,136,512]{2,1,0:T(8,128)(2,1)S(1)} collective-permute-done((bf16[4,136,512]{2,1,0:T(8,128)(2,1)S(1)}, bf16[4,136,512]{2,1,0:T(8,128)(2,1)S(1)}, u32[]{:S(2)}, u32[]{:S(2)}) %collective-permute-start.28) | collective-permute-done | bytes 557088 | tf_op jit(solution)/shard_map/ppermute | solution.py:941
  440.9 2.2 fusion.20
  443.1 9.4 %collective-permute-done.11.er_ref = bf16[256,1024]{1,0:T(8,128)(2,1)} collective-permute-done((bf16[256,1024]{1,0:T(8,128)(2,1)}, bf16[256,1024]{1,0:T(8,128)(2,1)}, u32[]{:S(2)}, u32[]{:S(2)}) %collective-permute-start.11) | collective-permute-done | bytes 524320 | tf_op jit(solution)/shard_map/ppermute | solution.py:938
  452.6 3.4 token_grad.1
  456.0 12.5 %join.3 = f32[16,128,1024]{2,1,0:T(8,128)} custom-call(s32[2]{0:T(128)} %pad_add_fusion.ids, bf16[8,128,1024]{2,1,0:T(8,128)(2,1)} %maximum_select_fusion.1.own_ref, bf16[8,128,1024]{2,1,0:T(8,128)(2,1)} %collective-permute-done.42.got_ref), custom_call_target="tpu_custom_call" | custom-call | tf_op jit(solution)/shard_map/join/pallas_call | solution.py:832
  468.5 12.5 %join.2 = f32[16,32,4096]{2,1,0:T(8,128)} custom-call(s32[2]{0:T(128)} %pad_add_fusion.ids, bf16[8,32,4096]{2,1,0:T(8,128)(2,1)} %maximum_select_fusion.own_ref, bf16[8,32,4096]{2,1,0:T(8,128)(2,1)} %collective-permute-done.36.got_ref), custom_call_target="tpu_custom_call" | custom-call | tf_op jit(solution)/shard_map/join/pallas_call | solution.py:832
  481.0 12.5 %unpack.1 = (f32[512,3072]{1,0:T(8,128)}, f32[512,1024]{1,0:T(8,128)}, f32[16,8,512]{2,1,0:T(8,128)}) custom-call(s32[2]{0:T(128)} %pad_add_fusion.ids, bf16[8,128,512]{2,1,0:T(8,128)(2,1)} %maximum_select_fusion.3.ao_ref, bf16[8,128,512]{2,1,0:T(8,128)(2,1)} %collective-permute-done.20.ag_ref, bf16[8,136,512]{2,1,0:T(8,128)(2,1)} %copy-done.9, ...), custom_call_target="tpu_custom_call" | custom-call | tf_op jit(solution)/shard_map/unpack/pallas_call | solution.py:867
  (196 shorter events, 52.8 us)
Async XLA Ops:
  0.6 27.0 %copy-start = (bf16[512,1024]{1,0:T(8,128)(2,1)S(1)}, bf16[512,1024]{1,0:T(8,128)(2,1)}, u32[]{:S(2)}) copy-start(bf16[512,1024]{1,0:T(8,128)(2,1)} %param.23) | copy-start | bytes 3145732
  0.7 22.1 %collective-permute-start = (bf16[256,1024]{1,0:T(8,128)(2,1)}, bf16[256,1024]{1,0:T(8,128)(2,1)S(1)}, u32[]{:S(2)}, u32[]{:S(2)}) collective-permute-start(bf16[256,1024]{1,0:T(8,128)(2,1)} %bitcast.217), channel_id=1, source_target_pairs={{0,1},{1,0},{2,3},{3,2},{4,5},{5,4},{6,7},{7,6},{8,9},{9,8},{10,11... | collective-permute-start | bytes 1572872 | tf_op jit(solution)/shard_map/ppermute | solution.py:938
  9.3 13.3 %collective-permute-start.2 = (bf16[1,4736]{1,0:T(2,128)(2,1)S(1)}, bf16[1,4736]{1,0:T(2,128)(2,1)S(1)}, u32[]{:S(2)}, u32[]{:S(2)}) collective-permute-start(bf16[1,4736]{1,0:T(2,128)(2,1)S(1)} %broadcast_in_dim.33), channel_id=1, source_target_pairs={{0,1},{1,0},{2,3},{3,2},{4,5},{5,4},{6,7},{7,6},{8,9},{9,8},{10,11... | collective-permute-start | bytes 28424 | tf_op jit(solution)/shard_map/ppermute | solution.py:938
  11.2 15.0 %copy-start.17 = (bf16[1,256,1024]{2,1,0:T(8,128)(2,1)S(1)}, bf16[1,256,1024]{2,1,0:T(8,128)(2,1)}, u32[]{:S(2)}) copy-start(bf16[1,256,1024]{2,1,0:T(8,128)(2,1)} %param.31) | copy-start | bytes 1572868
  22.8 33.3 %copy-start.20 = (bf16[2,4736]{1,0:T(2,128)(2,1)}, bf16[2,4736]{1,0:T(2,128)(2,1)S(1)}, u32[]{:S(2)}) copy-start(bf16[2,4736]{1,0:T(2,128)(2,1)S(1)} %broadcast_select_fusion) | copy-start | bytes 56836
  22.8 30.5 %collective-permute-start.1 = (bf16[1280,512]{1,0:T(8,128)(2,1)}, bf16[1280,512]{1,0:T(8,128)(2,1)S(1)}, u32[]{:S(2)}, u32[]{:S(2)}) collective-permute-start(bf16[1280,512]{1,0:T(8,128)(2,1)} %dynamic-slice_dynamic-update-slice_fusion), channel_id=1, source_target_pairs={{0,1},{1,0},{2,3},{3,2},{4,5},{5,4},{6,7},{7,6},{8,9},{9,8},{10,11... | collective-permute-start | bytes 3932168 | tf_op jit(solution)/shard_map/ppermute | solution.py:938
  29.4 38.4 %all-to-all-start.1 = ((bf16[16,64,256]{2,1,0:T(8,128)(2,1)}), bf16[16,64,256]{2,1,0:T(8,128)(2,1)}, u32[]{:S(2)}, u32[]{:S(2)}) async-start(bf16[16,64,256]{2,1,0:T(8,128)(2,1)} %bitcast.15), calls=%async_computation.1 | async-start | bytes 1048576 | tf_op jit(solution)/shard_map/all_to_all | solution.py:1001
  53.3 4.1 copy-start.1
  54.3 3.1 collective-permute-start.3
  54.3 25.9 %collective-permute-start.4 = (bf16[256,2048]{1,0:T(8,128)(2,1)}, bf16[256,2048]{1,0:T(8,128)(2,1)}, u32[]{:S(2)}, u32[]{:S(2)}) collective-permute-start(bf16[256,2048]{1,0:T(8,128)(2,1)} %dynamic_slice.173), channel_id=1, source_target_pairs={{0,1},{1,0},{2,3},{3,2},{4,5},{5,4},{6,7},{7,6},{8,9},{9,8},{10,11... | collective-permute-start | bytes 3145736 | tf_op jit(solution)/shard_map/ppermute | solution.py:938
  67.7 12.5 %copy-start.22 = (bf16[2048]{0:T(1024)(128)(2,1)S(1)}, bf16[2048]{0:T(1024)(128)(2,1)}, u32[]{:S(2)}) copy-start(bf16[2048]{0:T(1024)(128)(2,1)} %param.26) | copy-start | bytes 12292
  67.7 37.9 %all-to-all-start = ((bf16[16,192,256]{2,1,0:T(8,128)(2,1)}), bf16[16,192,256]{2,1,0:T(8,128)(2,1)S(1)}, u32[]{:S(2)}, u32[]{:S(2)}) async-start(bf16[16,192,256]{2,1,0:T(8,128)(2,1)} %bitcast.219), calls=%async_computation | async-start | bytes 3145728 | tf_op jit(solution)/shard_map/all_to_all | solution.py:1001
  80.2 3.0 collective-permute-start.5
  105.6 3.7 copy-start.3
  105.6 4.5 copy-start.10
  109.4 4.9 collective-permute-start.6
  111.6 5.9 %collective-permute-start.7 = (bf16[8,64,2048]{2,1,0:T(8,128)(2,1)}, bf16[8,64,2048]{2,1,0:T(8,128)(2,1)}, u32[]{:S(2)}, u32[]{:S(2)}) collective-permute-start(bf16[8,64,2048]{2,1,0:T(8,128)(2,1)} %dynamic-slice_bitcast_fusion), channel_id=1, source_target_pairs={{0,2},{2,0},{4,6},{6,4},{8,10},{10,8},{12,14},{14,12},{16,18},{18,... | collective-permute-start | bytes 6291464 | tf_op jit(solution)/shard_map/ppermute | solution.py:941
  111.6 5.9 %copy-start.11 = (bf16[16,64,2048]{2,1,0:T(8,128)(2,1)S(1)}, bf16[16,64,2048]{2,1,0:T(8,128)(2,1)}, u32[]{:S(2)}) copy-start(bf16[16,64,2048]{2,1,0:T(8,128)(2,1)} %get-tuple-element.57) | copy-start | bytes 12582916
  119.9 4.9 copy-start.5
  121.1 35.3 %collective-permute-start.9 = (bf16[4,128,1024]{2,1,0:T(8,128)(2,1)}, bf16[4,128,1024]{2,1,0:T(8,128)(2,1)}, u32[]{:S(2)}, u32[]{:S(2)}) collective-permute-start(bf16[4,128,1024]{2,1,0:T(8,128)(2,1)} %dynamic-slice_bitcast_fusion.5), channel_id=1, source_target_pairs={{0,4},{2,6},{4,0},{6,2},{8,12},{10,14},{12,8},{14,10},{16,20},{18,... | collective-permute-start | bytes 3145736 | tf_op jit(solution)/shard_map/ppermute | solution.py:941
  124.8 34.3 %collective-permute-start.10 = (bf16[4,64,2048]{2,1,0:T(8,128)(2,1)}, bf16[4,64,2048]{2,1,0:T(8,128)(2,1)}, u32[]{:S(2)}, u32[]{:S(2)}) collective-permute-start(bf16[4,64,2048]{2,1,0:T(8,128)(2,1)} %dynamic-slice_bitcast_fusion.4), channel_id=1, source_target_pairs={{0,8},{2,10},{4,12},{6,14},{8,0},{10,2},{12,4},{14,6},{16,24},{18,... | collective-permute-start | bytes 3145736 | tf_op jit(solution)/shard_map/ppermute | solution.py:941
  151.4 45.3 %all-to-all-start.2 = ((bf16[16,64,256]{2,1,0:T(8,128)(2,1)}), bf16[16,64,256]{2,1,0:T(8,128)(2,1)}, u32[]{:S(2)}, u32[]{:S(2)}) async-start(bf16[16,64,256]{2,1,0:T(8,128)(2,1)} %get-tuple-element.59.a_2_), calls=%async_computation.2 | async-start | bytes 1048576 | tf_op jit(solution)/shard_map/all_to_all | solution.py:1001
  156.4 2.8 copy-start.6
  196.7 82.9 %all-to-all-start.3 = ((bf16[16,192,256]{2,1,0:T(8,128)(2,1)}), bf16[16,192,256]{2,1,0:T(8,128)(2,1)S(1)}, u32[]{:S(2)}, u32[]{:S(2)}) async-start(bf16[16,192,256]{2,1,0:T(8,128)(2,1)} %attn_bwd.1), calls=%async_computation.3 | async-start | bytes 3145728 | tf_op jit(solution)/shard_map/all_to_all | solution.py:1001
  204.6 58.4 %collective-permute-start.30 = (bf16[2,64,2048]{2,1,0:T(8,128)(2,1)}, bf16[2,64,2048]{2,1,0:T(8,128)(2,1)S(1)}, u32[]{:S(2)}, u32[]{:S(2)}) collective-permute-start(bf16[2,64,2048]{2,1,0:T(8,128)(2,1)} %dynamic-slice_bitcast_fusion.8), channel_id=1, source_target_pairs={{0,16},{2,18},{4,20},{6,22},{8,24},{10,26},{12,28},{14,30},{16,0},... | collective-permute-start | bytes 1572872 | tf_op jit(solution)/shard_map/ppermute | solution.py:941
  207.4 58.4 %copy-start.13 = (bf16[4,128,1024]{2,1,0:T(8,128)(2,1)S(1)}, bf16[4,128,1024]{2,1,0:T(8,128)(2,1)}, u32[]{:S(2)}) copy-start(bf16[4,128,1024]{2,1,0:T(8,128)(2,1)} %fusion.5) | copy-start | bytes 3145732
  208.5 57.2 %collective-permute-start.37 = (bf16[2,128,1024]{2,1,0:T(8,128)(2,1)S(1)}, bf16[2,128,1024]{2,1,0:T(8,128)(2,1)S(1)}, u32[]{:S(2)}, u32[]{:S(2)}) collective-permute-start(bf16[2,128,1024]{2,1,0:T(8,128)(2,1)S(1)} %dynamic-slice_bitcast_fusion.7), channel_id=1, source_target_pairs={{0,8},{2,10},{4,12},{6,14},{8,0},{10,2},{12,4},{14,6},{16,24},{18,... | collective-permute-start | bytes 1572872 | tf_op jit(solution)/shard_map/ppermute | solution.py:941
  264.2 7.9 %collective-permute-start.31 = (bf16[1,64,2048]{2,1,0:T(8,128)(2,1)S(1)}, bf16[1,64,2048]{2,1,0:T(8,128)(2,1)S(1)}, u32[]{:S(2)}, u32[]{:S(2)}) collective-permute-start(bf16[1,64,2048]{2,1,0:T(8,128)(2,1)S(1)} %constant_dynamic-slice_fusion.1), channel_id=1, source_target_pairs={{0,4},{2,6},{4,0},{6,2},{8,12},{10,14},{12,8},{14,10},{16,20},{18,... | collective-permute-start | bytes 786440 | tf_op jit(solution)/shard_map/ppermute | solution.py:941
  266.0 12.9 %collective-permute-start.38 = (bf16[1,128,1024]{2,1,0:T(8,128)(2,1)S(1)}, bf16[1,128,1024]{2,1,0:T(8,128)(2,1)S(1)}, u32[]{:S(2)}, u32[]{:S(2)}) collective-permute-start(bf16[1,128,1024]{2,1,0:T(8,128)(2,1)S(1)} %constant_dynamic-slice_fusion), channel_id=1, source_target_pairs={{0,16},{2,18},{4,20},{6,22},{8,24},{10,26},{12,28},{14,30},{16,0},... | collective-permute-start | bytes 786440 | tf_op jit(solution)/shard_map/ppermute | solution.py:941
  272.8 28.0 %collective-permute-start.32 = (bf16[1,32,2048]{2,1,0:T(8,128)(2,1)S(1)}, bf16[1,32,2048]{2,1,0:T(8,128)(2,1)S(1)}, u32[]{:S(2)}, u32[]{:S(2)}) collective-permute-start(bf16[1,32,2048]{2,1,0:T(8,128)(2,1)S(1)} %get-tuple-element.79), channel_id=1, source_target_pairs={{0,1},{1,0},{2,3},{3,2},{4,5},{5,4},{6,7},{7,6},{8,9},{9,8},{10,11... | collective-permute-start | bytes 393224 | tf_op jit(solution)/shard_map/ppermute | solution.py:938
  279.7 24.9 %collective-permute-start.39 = (bf16[1,128,1024]{2,1,0:T(8,128)(2,1)}, bf16[1,128,1024]{2,1,0:T(8,128)(2,1)}, u32[]{:S(2)}, u32[]{:S(2)}) collective-permute-start(bf16[1,128,1024]{2,1,0:T(8,128)(2,1)} %add_convert_fusion), channel_id=1, source_target_pairs={{0,16},{2,18},{4,20},{6,22},{8,24},{10,26},{12,28},{14,30},{16,0},... | collective-permute-start | bytes 786440 | tf_op jit(solution)/shard_map/ppermute | solution.py:941
  280.8 20.7 %copy-start.18 = (bf16[1,32,2048]{2,1,0:T(8,128)(2,1)S(1)}, bf16[1,32,2048]{2,1,0:T(8,128)(2,1)}, u32[]{:S(2)}) copy-start(bf16[1,32,2048]{2,1,0:T(8,128)(2,1)} %get-tuple-element.78) | copy-start | bytes 393220
  298.4 4.8 copy-start.14
  300.9 32.6 %collective-permute-start.12 = (bf16[8,128,512]{2,1,0:T(8,128)(2,1)}, bf16[8,128,512]{2,1,0:T(8,128)(2,1)}, u32[]{:S(2)}, u32[]{:S(2)}) collective-permute-start(bf16[8,128,512]{2,1,0:T(8,128)(2,1)} %dynamic-slice_bitcast_fusion.3), channel_id=1, source_target_pairs={{0,2},{2,0},{4,6},{6,4},{8,10},{10,8},{12,14},{14,12},{16,18},{18,... | collective-permute-start | bytes 3145736 | tf_op jit(solution)/shard_map/ppermute | solution.py:941
  302.6 8.9 %collective-permute-start.33 = (bf16[1,32,4096]{2,1,0:T(8,128)(2,1)S(1)}, bf16[1,32,4096]{2,1,0:T(8,128)(2,1)}, u32[]{:S(2)}, u32[]{:S(2)}) collective-permute-start(bf16[1,32,4096]{2,1,0:T(8,128)(2,1)S(1)} %maximum_select_fusion.12), channel_id=1, source_target_pairs={{0,4},{2,6},{4,0},{6,2},{8,12},{10,14},{12,8},{14,10},{16,20},{18,... | collective-permute-start | bytes 786440 | tf_op jit(solution)/shard_map/ppermute | solution.py:941
  304.3 30.9 %collective-permute-start.21 = (bf16[8,136,512]{2,1,0:T(8,128)(2,1)}, bf16[8,136,512]{2,1,0:T(8,128)(2,1)}, u32[]{:S(2)}, u32[]{:S(2)}) collective-permute-start(bf16[8,136,512]{2,1,0:T(8,128)(2,1)} %dynamic-slice_bitcast_fusion.2), channel_id=1, source_target_pairs={{0,2},{2,0},{4,6},{6,4},{8,10},{10,8},{12,14},{14,12},{16,18},{18,... | collective-permute-start | bytes 3342344 | tf_op jit(solution)/shard_map/ppermute | solution.py:941
  306.6 22.8 %collective-permute-start.40 = (bf16[2,128,1024]{2,1,0:T(8,128)(2,1)}, bf16[2,128,1024]{2,1,0:T(8,128)(2,1)}, u32[]{:S(2)}, u32[]{:S(2)}) collective-permute-start(bf16[2,128,1024]{2,1,0:T(8,128)(2,1)} %maximum_select_fusion.9), channel_id=1, source_target_pairs={{0,8},{2,10},{4,12},{6,14},{8,0},{10,2},{12,4},{14,6},{16,24},{18,... | collective-permute-start | bytes 1572872 | tf_op jit(solution)/shard_map/ppermute | solution.py:941
  309.5 24.0 %copy-start.16 = (bf16[16,128,512]{2,1,0:T(8,128)(2,1)S(1)}, bf16[16,128,512]{2,1,0:T(8,128)(2,1)}, u32[]{:S(2)}) copy-start(bf16[16,128,512]{2,1,0:T(8,128)(2,1)} %get-tuple-element.71) | copy-start | bytes 6291460
  312.6 26.1 %collective-permute-start.34 = (bf16[2,32,4096]{2,1,0:T(8,128)(2,1)S(1)}, bf16[2,32,4096]{2,1,0:T(8,128)(2,1)S(1)}, u32[]{:S(2)}, u32[]{:S(2)}) collective-permute-start(bf16[2,32,4096]{2,1,0:T(8,128)(2,1)S(1)} %maximum_select_fusion.8), channel_id=1, source_target_pairs={{0,16},{2,18},{4,20},{6,22},{8,24},{10,26},{12,28},{14,30},{16,0},... | collective-permute-start | bytes 1572872 | tf_op jit(solution)/shard_map/ppermute | solution.py:941
  331.1 71.0 %collective-permute-start.41 = (bf16[4,128,1024]{2,1,0:T(8,128)(2,1)S(1)}, bf16[4,128,1024]{2,1,0:T(8,128)(2,1)S(1)}, u32[]{:S(2)}, u32[]{:S(2)}) collective-permute-start(bf16[4,128,1024]{2,1,0:T(8,128)(2,1)S(1)} %maximum_select_fusion.5), channel_id=1, source_target_pairs={{0,4},{2,6},{4,0},{6,2},{8,12},{10,14},{12,8},{14,10},{16,20},{18,... | collective-permute-start | bytes 3145736 | tf_op jit(solution)/shard_map/ppermute | solution.py:941
  335.1 32.8 %collective-permute-start.13 = (bf16[4,128,512]{2,1,0:T(8,128)(2,1)S(1)}, bf16[4,128,512]{2,1,0:T(8,128)(2,1)S(1)}, u32[]{:S(2)}, u32[]{:S(2)}) collective-permute-start(bf16[4,128,512]{2,1,0:T(8,128)(2,1)S(1)} %dynamic-slice_bitcast_fusion.9), channel_id=1, source_target_pairs={{0,4},{2,6},{4,0},{6,2},{8,12},{10,14},{12,8},{14,10},{16,20},{18,... | collective-permute-start | bytes 1572872 | tf_op jit(solution)/shard_map/ppermute | solution.py:941
  336.8 31.3 %collective-permute-start.22 = (bf16[4,136,512]{2,1,0:T(8,128)(2,1)S(1)}, bf16[4,136,512]{2,1,0:T(8,128)(2,1)S(1)}, u32[]{:S(2)}, u32[]{:S(2)}) collective-permute-start(bf16[4,136,512]{2,1,0:T(8,128)(2,1)S(1)} %dynamic-slice_bitcast_fusion.6), channel_id=1, source_target_pairs={{0,8},{2,10},{4,12},{6,14},{8,0},{10,2},{12,4},{14,6},{16,24},{18,... | collective-permute-start | bytes 1671176 | tf_op jit(solution)/shard_map/ppermute | solution.py:941
  338.9 70.9 %collective-permute-start.35 = (bf16[4,32,4096]{2,1,0:T(8,128)(2,1)S(1)}, bf16[4,32,4096]{2,1,0:T(8,128)(2,1)S(1)}, u32[]{:S(2)}, u32[]{:S(2)}) collective-permute-start(bf16[4,32,4096]{2,1,0:T(8,128)(2,1)S(1)} %maximum_select_fusion.4), channel_id=1, source_target_pairs={{0,8},{2,10},{4,12},{6,14},{8,0},{10,2},{12,4},{14,6},{16,24},{18,... | collective-permute-start | bytes 3145736 | tf_op jit(solution)/shard_map/ppermute | solution.py:941
  368.0 16.9 %collective-permute-start.14 = (bf16[2,128,512]{2,1,0:T(8,128)(2,1)S(1)}, bf16[2,128,512]{2,1,0:T(8,128)(2,1)S(1)}, u32[]{:S(2)}, u32[]{:S(2)}) collective-permute-start(bf16[2,128,512]{2,1,0:T(8,128)(2,1)S(1)} %dynamic-slice_bitcast_fusion.11), channel_id=1, source_target_pairs={{0,8},{2,10},{4,12},{6,14},{8,0},{10,2},{12,4},{14,6},{16,24},{18,... | collective-permute-start | bytes 786440 | tf_op jit(solution)/shard_map/ppermute | solution.py:941
  368.3 17.1 %collective-permute-start.23 = (bf16[2,136,512]{2,1,0:T(8,128)(2,1)S(1)}, bf16[2,136,512]{2,1,0:T(8,128)(2,1)S(1)}, u32[]{:S(2)}, u32[]{:S(2)}) collective-permute-start(bf16[2,136,512]{2,1,0:T(8,128)(2,1)S(1)} %dynamic-slice_bitcast_fusion.10), channel_id=1, source_target_pairs={{0,16},{2,18},{4,20},{6,22},{8,24},{10,26},{12,28},{14,30},{16,0},... | collective-permute-start | bytes 835592 | tf_op jit(solution)/shard_map/ppermute | solution.py:941
  385.1 7.8 %collective-permute-start.15 = (bf16[1,128,512]{2,1,0:T(8,128)(2,1)S(1)}, bf16[1,128,512]{2,1,0:T(8,128)(2,1)S(1)}, u32[]{:S(2)}, u32[]{:S(2)}) collective-permute-start(bf16[1,128,512]{2,1,0:T(8,128)(2,1)S(1)} %constant_dynamic-slice_fusion.3), channel_id=1, source_target_pairs={{0,16},{2,18},{4,20},{6,22},{8,24},{10,26},{12,28},{14,30},{16,0},... | collective-permute-start | bytes 393224 | tf_op jit(solution)/shard_map/ppermute | solution.py:941
  385.5 11.7 %collective-permute-start.24 = (bf16[1,136,512]{2,1,0:T(8,128)(2,1)S(1)}, bf16[1,136,512]{2,1,0:T(8,128)(2,1)S(1)}, u32[]{:S(2)}, u32[]{:S(2)}) collective-permute-start(bf16[1,136,512]{2,1,0:T(8,128)(2,1)S(1)} %constant_dynamic-slice_fusion.2), channel_id=1, source_target_pairs={{0,4},{2,6},{4,0},{6,2},{8,12},{10,14},{12,8},{14,10},{16,20},{18,... | collective-permute-start | bytes 417800 | tf_op jit(solution)/shard_map/ppermute | solution.py:941
  392.9 4.2 collective-permute-start.16
  397.1 7.1 %collective-permute-start.17 = (bf16[1,128,512]{2,1,0:T(8,128)(2,1)S(1)}, bf16[1,128,512]{2,1,0:T(8,128)(2,1)S(1)}, u32[]{:S(2)}, u32[]{:S(2)}) collective-permute-start(bf16[1,128,512]{2,1,0:T(8,128)(2,1)S(1)} %maximum_bitcast_fusion.1), channel_id=1, source_target_pairs={{0,16},{2,18},{4,20},{6,22},{8,24},{10,26},{12,28},{14,30},{16,0},... | collective-permute-start | bytes 393224 | tf_op jit(solution)/shard_map/ppermute | solution.py:941
  397.3 4.2 collective-permute-start.25
  401.6 5.1 %collective-permute-start.26 = (bf16[1,136,512]{2,1,0:T(8,128)(2,1)S(1)}, bf16[1,136,512]{2,1,0:T(8,128)(2,1)S(1)}, u32[]{:S(2)}, u32[]{:S(2)}) collective-permute-start(bf16[1,136,512]{2,1,0:T(8,128)(2,1)S(1)} %maximum_bitcast_fusion), channel_id=1, source_target_pairs={{0,4},{2,6},{4,0},{6,2},{8,12},{10,14},{12,8},{14,10},{16,20},{18,... | collective-permute-start | bytes 417800 | tf_op jit(solution)/shard_map/ppermute | solution.py:941
  403.7 52.3 %collective-permute-start.42 = (bf16[8,128,1024]{2,1,0:T(8,128)(2,1)}, bf16[8,128,1024]{2,1,0:T(8,128)(2,1)}, u32[]{:S(2)}, u32[]{:S(2)}) collective-permute-start(bf16[8,128,1024]{2,1,0:T(8,128)(2,1)} %maximum_select_fusion.1.own_ref), channel_id=1, source_target_pairs={{0,2},{2,0},{4,6},{6,4},{8,10},{10,8},{12,14},{14,12},{16,18},{18,... | collective-permute-start | bytes 6291464 | tf_op jit(solution)/shard_map/ppermute | solution.py:941
  404.2 13.9 %collective-permute-start.18 = (bf16[2,128,512]{2,1,0:T(8,128)(2,1)S(1)}, bf16[2,128,512]{2,1,0:T(8,128)(2,1)S(1)}, u32[]{:S(2)}, u32[]{:S(2)}) collective-permute-start(bf16[2,128,512]{2,1,0:T(8,128)(2,1)S(1)} %maximum_select_fusion.11), channel_id=1, source_target_pairs={{0,8},{2,10},{4,12},{6,14},{8,0},{10,2},{12,4},{14,6},{16,24},{18,... | collective-permute-start | bytes 786440 | tf_op jit(solution)/shard_map/ppermute | solution.py:941
  406.8 15.6 %collective-permute-start.27 = (bf16[2,136,512]{2,1,0:T(8,128)(2,1)S(1)}, bf16[2,136,512]{2,1,0:T(8,128)(2,1)S(1)}, u32[]{:S(2)}, u32[]{:S(2)}) collective-permute-start(bf16[2,136,512]{2,1,0:T(8,128)(2,1)S(1)} %maximum_select_fusion.10), channel_id=1, source_target_pairs={{0,16},{2,18},{4,20},{6,22},{8,24},{10,26},{12,28},{14,30},{16,0},... | collective-permute-start | bytes 835592 | tf_op jit(solution)/shard_map/ppermute | solution.py:941
  411.4 57.1 %collective-permute-start.36 = (bf16[8,32,4096]{2,1,0:T(8,128)(2,1)}, bf16[8,32,4096]{2,1,0:T(8,128)(2,1)}, u32[]{:S(2)}, u32[]{:S(2)}) collective-permute-start(bf16[8,32,4096]{2,1,0:T(8,128)(2,1)} %maximum_select_fusion.own_ref), channel_id=1, source_target_pairs={{0,2},{2,0},{4,6},{6,4},{8,10},{10,8},{12,14},{14,12},{16,18},{18,... | collective-permute-start | bytes 6291464 | tf_op jit(solution)/shard_map/ppermute | solution.py:941
  418.2 18.4 %collective-permute-start.19 = (bf16[4,128,512]{2,1,0:T(8,128)(2,1)S(1)}, bf16[4,128,512]{2,1,0:T(8,128)(2,1)S(1)}, u32[]{:S(2)}, u32[]{:S(2)}) collective-permute-start(bf16[4,128,512]{2,1,0:T(8,128)(2,1)S(1)} %maximum_select_fusion.7), channel_id=1, source_target_pairs={{0,4},{2,6},{4,0},{6,2},{8,12},{10,14},{12,8},{14,10},{16,20},{18,... | collective-permute-start | bytes 1572872 | tf_op jit(solution)/shard_map/ppermute | solution.py:941
  422.5 13.8 %collective-permute-start.28 = (bf16[4,136,512]{2,1,0:T(8,128)(2,1)S(1)}, bf16[4,136,512]{2,1,0:T(8,128)(2,1)S(1)}, u32[]{:S(2)}, u32[]{:S(2)}) collective-permute-start(bf16[4,136,512]{2,1,0:T(8,128)(2,1)S(1)} %maximum_select_fusion.6), channel_id=1, source_target_pairs={{0,8},{2,10},{4,12},{6,14},{8,0},{10,2},{12,4},{14,6},{16,24},{18,... | collective-permute-start | bytes 1671176 | tf_op jit(solution)/shard_map/ppermute | solution.py:941
  425.0 12.9 %copy-start.7 = (f32[2,256,1024]{2,1,0:T(8,128)}, f32[2,256,1024]{2,1,0:T(8,128)S(1)}, u32[]{:S(2)}) copy-start(f32[2,256,1024]{2,1,0:T(8,128)S(1)} %add.315) | copy-start | bytes 6291460
  425.1 15.8 %copy-start.4 = (bf16[1,256,1024]{2,1,0:T(8,128)(2,1)S(1)}, bf16[1,256,1024]{2,1,0:T(8,128)(2,1)}, u32[]{:S(2)}) copy-start(bf16[1,256,1024]{2,1,0:T(8,128)(2,1)} %param.16) | copy-start | bytes 1572868
  425.1 13.2 %collective-permute-start.8 = (bf16[256,1024]{1,0:T(8,128)(2,1)S(1)}, bf16[256,1024]{1,0:T(8,128)(2,1)S(1)}, u32[]{:S(2)}, u32[]{:S(2)}) collective-permute-start(bf16[256,1024]{1,0:T(8,128)(2,1)S(1)} %fusion.21), channel_id=1, source_target_pairs={{0,1},{1,0},{2,3},{3,2},{4,5},{5,4},{6,7},{7,6},{8,9},{9,8},{10,11... | collective-permute-start | bytes 1572872 | tf_op jit(solution)/shard_map/ppermute | solution.py:938
  436.5 6.6 %copy-start.9 = (bf16[8,136,512]{2,1,0:T(8,128)(2,1)}, bf16[8,136,512]{2,1,0:T(8,128)(2,1)S(1)}, u32[]{:S(2)}) copy-start(bf16[8,136,512]{2,1,0:T(8,128)(2,1)S(1)} %maximum_select_fusion.2.bo_ref) | copy-start | bytes 3342340
  436.5 44.4 %collective-permute-start.29 = (bf16[8,136,512]{2,1,0:T(8,128)(2,1)S(1)}, bf16[8,136,512]{2,1,0:T(8,128)(2,1)}, u32[]{:S(2)}, u32[]{:S(2)}) collective-permute-start(bf16[8,136,512]{2,1,0:T(8,128)(2,1)S(1)} %maximum_select_fusion.2.bo_ref), channel_id=1, source_target_pairs={{0,2},{2,0},{4,6},{6,4},{8,10},{10,8},{12,14},{14,12},{16,18},{18,... | collective-permute-start | bytes 3342344 | tf_op jit(solution)/shard_map/ppermute | solution.py:941
  437.9 43.1 %collective-permute-start.20 = (bf16[8,128,512]{2,1,0:T(8,128)(2,1)}, bf16[8,128,512]{2,1,0:T(8,128)(2,1)}, u32[]{:S(2)}, u32[]{:S(2)}) collective-permute-start(bf16[8,128,512]{2,1,0:T(8,128)(2,1)} %maximum_select_fusion.3.ao_ref), channel_id=1, source_target_pairs={{0,2},{2,0},{4,6},{6,4},{8,10},{10,8},{12,14},{14,12},{16,18},{18,... | collective-permute-start | bytes 3145736 | tf_op jit(solution)/shard_map/ppermute | solution.py:941
  438.3 14.2 %collective-permute-start.11 = (bf16[256,1024]{1,0:T(8,128)(2,1)}, bf16[256,1024]{1,0:T(8,128)(2,1)}, u32[]{:S(2)}, u32[]{:S(2)}) collective-permute-start(bf16[256,1024]{1,0:T(8,128)(2,1)} %get-tuple-element.70), channel_id=1, source_target_pairs={{0,1},{1,0},{2,3},{3,2},{4,5},{5,4},{6,7},{7,6},{8,9},{9,8},{10,11... | collective-permute-start | bytes 1572872 | tf_op jit(solution)/shard_map/ppermute | solution.py:938
  (6 other events, 6.3 us)

commit v3 on v2

--- a/solution.py
+++ b/solution.py
@@ -529,37 +529,27 @@
 
 
 def qkv_kernel(
-    ids, xo_ref, xg_ref, n_ref, wq_ref, wk_ref, wv_ref, gq_ref, gk_ref, gv_ref, sq_ref, sk_ref, sv_ref,
-    bq_ref, bk_ref, bv_ref, cs_ref, send_ref, ain_ref, min_ref
+    ids, xo_ref, xg_ref, n_ref, wq_ref, wk_ref, wv_ref, gq_ref, gk_ref, gv_ref, bq_ref, bk_ref, bv_ref, cs_ref,
+    send_ref, ain_ref, min_ref
 ):
     rows, width = xo_ref.shape
     half = width // 2
-    q4 = half // 2
 
     @pl.when(pl.program_id(0) == 0)
     def _():
         for s in range(2):
-            x = xo_ref[...] if s == 0 else jnp.concatenate([xg_ref[0:rows, :], xg_ref[rows:, :]], axis=1)
+            x = xo_ref[...] if s == 0 else xg_ref[...]
             xhat, _ = _norm(x)
             ain_ref[s * rows : (s + 1) * rows, :] = (xhat * n_ref[0:1, :] + n_ref[1:2, :]).astype(bf16)
             min_ref[s * rows : (s + 1) * rows, :] = (xhat * n_ref[2:3, :] + n_ref[3:4, :]).astype(bf16)
 
     me = ids[0]
-    core = ids[1]
-    base = (1 - me) * half
     a_own = ain_ref[:, pl.ds(pl.multiple_of(me * half, half), half)]
-    a_got = ain_ref[:, pl.ds(pl.multiple_of(base + core * q4, q4), q4)]
-    a_sib = ain_ref[:, pl.ds(pl.multiple_of(base + (1 - core) * q4, q4), q4)]
+    a_got = ain_ref[:, pl.ds(pl.multiple_of((1 - me) * half, half), half)]
     cos = cs_ref[0:8, :]
     sin = cs_ref[8:16, :]
-    for n, (w, g, sb, b) in enumerate(
-        (
-            (wq_ref, gq_ref, sq_ref, bq_ref),
-            (wk_ref, gk_ref, sk_ref, bk_ref),
-            (wv_ref, gv_ref, sv_ref, bv_ref),
-        )
-    ):
-        t = _nn(a_own, w[...]) + _nn(a_got, g[...]) + _nn(a_sib, sb[...]) + b[...]
+    for n, (w, g, b) in enumerate(((wq_ref, gq_ref, bq_ref), (wk_ref, gk_ref, bk_ref), (wv_ref, gv_ref, bv_ref))):
+        t = _nn(a_own, w[...]) + _nn(a_got, g[...]) + b[...]
         t = t.T
         for s in range(2):
             for k in range(2):
@@ -571,18 +561,13 @@
                 send_ref[s, k, n * HD : (n + 1) * HD, :] = v.astype(bf16)
 
 
-def _wq_specs(half, width, rows):
-    own = lambda p: pl.BlockSpec((half, 128), lambda i, ids: (0, p * (width // 128) + ids[0] * (half // 128) + i))
-    got = lambda p: pl.BlockSpec((half // 2, 128), lambda i, ids: (2 * rows // (half // 2) + p, i))
-    sib = lambda p: pl.BlockSpec((half // 2, 128), lambda i, ids: (p, i))
-    return [own(p) for p in range(3)] + [got(p) for p in range(3)] + [sib(p) for p in range(3)]
-
-
-def _x_got_spec(rows, half):
-    return pl.BlockSpec((2 * rows, half), lambda i, ids: (0, 0))
-
-
-def qkv_forward(ids, xo, got, norms, w_own, w_sib, bias, cs):
+def _wq_specs(half, width, cols):
+    own = lambda p: pl.BlockSpec((half, cols), lambda i, ids: (0, p * (width // cols) + ids[0] * (half // cols) + i))
+    got = lambda p: pl.BlockSpec((half, cols), lambda i, ids: (0, p * (half // cols) + i))
+    return [own(p) for p in range(3)] + [got(p) for p in range(3)]
+
+
+def qkv_forward(ids, xo, xg, norms, w_own, w_got, bias, cs):
     rows, width = xo.shape
     half = width // 2
     full = lambda a: pl.BlockSpec(a.shape, lambda i, ids: (0,) * a.ndim)
@@ -594,8 +579,8 @@
         grid_spec=pltpu.PrefetchScalarGridSpec(
             num_scalar_prefetch=1,
             grid=(half // 128,),
-            in_specs=[full(xo), _x_got_spec(rows, half), full(norms)]
-            + _wq_specs(half, width, rows)
+            in_specs=[full(xo), full(xg), full(norms)]
+            + _wq_specs(half, width, 128)
             + [bsp(p) for p in range(3)]
             + [full(cs)],
             out_specs=(pl.BlockSpec((2, 2, 3 * HD, rows), lambda i, ids: (0, i, 0, 0)), res(), res()),
@@ -606,31 +591,27 @@
             jax.ShapeDtypeStruct((2 * rows, width), bf16),
         ),
         compiler_params=_params(),
+        cost_estimate=pl.CostEstimate(flops=1 << 20, transcendentals=0, bytes_accessed=1 << 20),
         name="qkv_forward",
-    )(ids, xo, got, norms, w_own, w_own, w_own, got, got, got, w_sib, w_sib, w_sib, bias, bias, bias, cs)
+    )(ids, xo, xg, norms, w_own, w_own, w_own, w_got, w_got, w_got, bias, bias, bias, cs)
 
 
 def mlp_kernel(
-    ids, x_ref, dy_ref, wo_ref, wg_ref, ws_ref, wd_ref, bu_ref, y_ref, dx_ref, gu_ref, gd_ref, gb_ref, xt_s
+    ids, x_ref, xt_ref, dy_ref, wo_ref, wg_ref, wd_ref, bu_ref, y0_ref, dx0_ref, y_ref, dx_ref, gu_ref,
+    gd_ref, gb_ref, *, resume
 ):
-    first = pl.program_id(0) == 0
     rows, width = x_ref.shape
     half = width // 2
-    q4 = half // 2
     me = ids[0]
-    core = ids[1]
-    base = (1 - me) * half
     spans = (
         (pl.multiple_of(me * half, half), half, wo_ref),
-        (pl.multiple_of(base + core * q4, q4), q4, wg_ref),
-        (pl.multiple_of(base + (1 - core) * q4, q4), q4, ws_ref),
-    )
-
-    @pl.when(first)
+        (pl.multiple_of((1 - me) * half, half), half, wg_ref),
+    )
+
+    @pl.when(pl.program_id(0) == 0)
     def _():
-        xt_s[...] = x_ref[...].astype(f32).T.astype(bf16)
-        y_ref[...] = jnp.zeros_like(y_ref)
-        dx_ref[...] = jnp.zeros_like(dx_ref)
+        y_ref[...] = y0_ref[...] if resume else jnp.zeros_like(y_ref)
+        dx_ref[...] = dx0_ref[...] if resume else jnp.zeros_like(dx_ref)
 
     dy = dy_ref[...]
     wd = wd_ref[...]
@@ -642,10 +623,11 @@
     y_ref[...] += _nn(act, wd)
     for o, n, w in spans:
         dx_ref[:, pl.ds(o, n)] += _nt(du, w[...])
-    gd_ref[...] = lax.dot_general(
-        act, dy, (((0,), (0,)), ((), ())), preferred_element_type=f32
-    ).astype(bf16)
-    gu = _nn(xt_s[...], du).astype(bf16)
+    gd = lax.dot_general(act, dy, (((0,), (0,)), ((), ())), preferred_element_type=f32).astype(bf16)
+    k, r, _ = gd_ref.shape
+    for c in range(k):
+        gd_ref[c] = gd[c * r : (c + 1) * r, :]
+    gu = _nn(xt_ref[...], du).astype(bf16)
     n = gu_ref.shape[0]
     r = half // n
     for h in range(2):
@@ -654,36 +636,48 @@
     gb_ref[...] = jnp.sum(du.astype(f32), axis=0, keepdims=True)
 
 
-def mlp(ids, x, dy, w_own, w_got, w_sib, wd, bu, n, tile=256):
+def mlp(ids, x, xt, dy, w_own, w_got, wd, bu, n, sibling, before=None, tile=256):
     rows, width = x.shape
     half = width // 2
-    hidden = w_got.shape[1]
-    steps = hidden // tile
+    steps = w_got.shape[1] // (2 * tile)
+    hidden = steps * tile
+    part = lambda i, ids: (1 - ids[1] if sibling else ids[1]) * steps + i
     whole = pl.BlockSpec((rows, width), lambda i, ids: (0, 0))
-    down = pl.BlockSpec((tile, width), lambda i, ids: (i, 0))
-    vec = pl.BlockSpec((1, tile), lambda i, ids: (0, i))
+    sums = [jax.ShapeDtypeStruct((rows, width), f32)] * 2
+    if before is None:
+        before = (jnp.zeros((8, 128), f32),) * 2
+        start = pl.BlockSpec((8, 128), lambda i, ids: (0, 0))
+    else:
+        start = whole
+    per = hidden // n
     return pl.pallas_call(
-        mlp_kernel,
+        partial(mlp_kernel, resume=start is whole),
         grid_spec=pltpu.PrefetchScalarGridSpec(
             num_scalar_prefetch=1,
             grid=(steps,),
             in_specs=[
                 whole,
+                pl.BlockSpec((width, rows), lambda i, ids: (0, 0)),
                 whole,
-                pl.BlockSpec((half, tile), lambda i, ids: (0, ids[0] * steps + i)),
-                pl.BlockSpec((half // 2, tile), lambda i, ids: (0, i)),
-                pl.BlockSpec((half // 2, tile), lambda i, ids: (0, i)),
-                down,
-                vec,
+                pl.BlockSpec((half, tile), lambda i, ids: (0, ids[0] * 2 * steps + part(i, ids))),
+                pl.BlockSpec((half, tile), lambda i, ids: (0, part(i, ids))),
+                pl.BlockSpec((tile, width), lambda i, ids: (part(i, ids), 0)),
+                pl.BlockSpec((1, tile), lambda i, ids: (0, part(i, ids))),
+                start,
+                start,
             ],
-            out_specs=(whole, whole, pl.BlockSpec((n, width // n, tile), lambda i, ids: (0, 0, i)), down, vec),
-            scratch_shapes=[pltpu.VMEM((width, rows), bf16)],
+            out_specs=(
+                whole,
+                whole,
+                pl.BlockSpec((n, width // n, tile), lambda i, ids: (0, 0, i)),
+                pl.BlockSpec((tile // per, per, width), lambda i, ids: (i, 0, 0)),
+                pl.BlockSpec((1, tile), lambda i, ids: (0, i)),
+            ),
         ),
         out_shape=(
-            jax.ShapeDtypeStruct((rows, width), f32),
-            jax.ShapeDtypeStruct((rows, width), f32),
+            *sums,
             jax.ShapeDtypeStruct((n, width // n, hidden), bf16),
-            jax.ShapeDtypeStruct((hidden, width), bf16),
+            jax.ShapeDtypeStruct((n, per, width), bf16),
             jax.ShapeDtypeStruct((1, hidden), f32),
         ),
         compiler_params=_params(),
@@ -691,70 +685,67 @@
             flops=12 * rows * width * hidden, transcendentals=2 * rows * hidden, bytes_accessed=24 << 20
         ),
         name="mlp",
-    )(ids, x, dy, w_own, w_got, w_sib, wd, bu)
+    )(ids, x, xt, dy, w_own, w_got, wd, bu, *before)
 
 
 def qkv_back_kernel(
-    ids, d_ref, a_ref, xo_ref, xg_ref, n_ref, wq_ref, wk_ref, wv_ref, gq_ref, gk_ref, gv_ref, sq_ref, sk_ref,
-    sv_ref, dm_ref, ob_ref, dy_ref, gb_ref, ga_ref, gb2_ref, eo_ref, ex_ref, at_s, da_s, bs_s
+    ids, d_ref, at_ref, xo_ref, xg_ref, n_ref, wq_ref, wk_ref, wv_ref, gq_ref, gk_ref, gv_ref, dm_ref,
+    ob_ref, dy_ref, gb_ref, ak_ref, as_ref, bk_ref, bs_ref, eo_ref, ex_ref, da_s, sum_s, g_s
 ):
     rows, width = xo_ref.shape
     half = width // 2
     q4 = half // 2
     me = ids[0]
     core = ids[1]
-    base = (1 - me) * half
     i = pl.program_id(0)
-    outs = (ga_ref, gb2_ref)
-    n = ga_ref.shape[0]
-    r = half // (2 * n)
-    lanes = pl.ds(pl.multiple_of(i * 128, 128), 128)
-
-    @pl.when(i == 0)
-    def _():
-        at_s[...] = a_ref[...].astype(f32).T.astype(bf16)
-        da_s[...] = jnp.zeros_like(da_s)
-
+    outs = ((ak_ref, bk_ref), (as_ref, bs_ref))
+    n = ak_ref.shape[0]
+    r = half // (4 * n)
+    nh = d_ref.shape[1]
+    cols = nh * HD
+    lanes = pl.ds(pl.multiple_of(i * cols, cols), cols)
     ones = jnp.ones((8, rows), bf16)
-    for p, (w, gw, sw) in enumerate(
-        ((wq_ref, gq_ref, sq_ref), (wk_ref, gk_ref, sk_ref), (wv_ref, gv_ref, sv_ref))
+    dts = [[], []]
+    for p in range(3):
+        g = jnp.zeros((width, cols), f32)
+        b = jnp.zeros((8, cols), f32)
+        for s in range(2):
+            dp = jnp.concatenate([d_ref[s, k, p * HD : (p + 1) * HD, :] for k in range(nh)], axis=0)
+            g = g + _nt(at_ref[:, s * rows : (s + 1) * rows], dp)
+            b = b + _nt(ones, dp)
+            dts[s].append(dp.astype(f32).T.astype(bf16))
+        sum_s[p * 8 : (p + 1) * 8, lanes] = b
+        g_s[...] = g.astype(bf16)
+        for side in range(2):
+            which = core if side == 0 else 1 - core
+            for h in range(2):
+                for c in range(n):
+                    for a in range(2):
+                        at = pl.multiple_of(h * half + which * q4 + (c * 2 + a) * r, r)
+                        u = (h * 3 + p) * r
+                        outs[side][a][c, u : u + r, lanes] = g_s[pl.ds(at, r), :]
+    for o, m, refs in (
+        (pl.multiple_of(me * half, half), half, (wq_ref, wk_ref, wv_ref)),
+        (pl.multiple_of((1 - me) * half, half), half, (gq_ref, gk_ref, gv_ref)),
     ):
-        g = jnp.zeros((width, 128), f32)
-        b = jnp.zeros((8, 128), f32)
+        w = jnp.concatenate([v[...] for v in refs], axis=1)
         for s in range(2):
-            dp = jnp.concatenate([d_ref[s, k, p * HD : (p + 1) * HD, :] for k in range(2)], axis=0)
-            g = g + _nt(at_s[:, s * rows : (s + 1) * rows], dp)
-            b = b + _nt(ones, dp)
-            dt = dp.astype(f32).T.astype(bf16)
-            for o, m, ref in (
-                (pl.multiple_of(me * half, half), half, w),
-                (pl.multiple_of(base + core * q4, q4), q4, gw),
-                (pl.multiple_of(base + (1 - core) * q4, q4), q4, sw),
-            ):
-                da_s[s * rows : (s + 1) * rows, pl.ds(o, m)] += _nt(dt, ref[...])
-        bs_s[p * 8 : (p + 1) * 8, lanes] = b
-        g16 = g.astype(bf16)
-        for h in range(2):
-            for c in range(n):
-                for a in range(2):
-                    at = h * half + (c * 2 + a) * r
-                    u = (h * 3 + p) * r
-                    outs[a][c, u : u + r, lanes] = g16[at : at + r, :]
-
-    go = sum(_nn(ob_ref[s], dy_ref[s * rows : (s + 1) * rows, :]) for s in range(2)).astype(bf16)
-    per = 128 // (2 * r)
-    for k in range(per):
-        for a in range(2):
-            at = (k * 2 + a) * r
-            for h in range(2):
-                u = (6 + h) * r
-                outs[a][i * per + k, u : u + r, :] = go[at : at + r, h * half : (h + 1) * half]
+            v = _nt(jnp.concatenate(dts[s], axis=1), w)
+            at = slice(s * rows, (s + 1) * rows)
+
+            @pl.when(i == 0)
+            def _(v=v, at=at, o=o, m=m):
+                da_s[at, pl.ds(o, m)] = v
+
+            @pl.when(i > 0)
+            def _(v=v, at=at, o=o, m=m):
+                da_s[at, pl.ds(o, m)] += v
 
     @pl.when(i == pl.num_programs(0) - 1)
     def _():
         sums = [jnp.zeros((1, width), f32) for _ in range(4)]
         for s in range(2):
-            x = xo_ref[...] if s == 0 else jnp.concatenate([xg_ref[0:rows, :], xg_ref[rows:, :]], axis=1)
+            x = xo_ref[...] if s == 0 else xg_ref[...]
             xhat, _ = _norm(x)
             da = da_s[s * rows : (s + 1) * rows, :]
             dm = dm_ref[s * rows : (s + 1) * rows, :]
@@ -769,25 +760,52 @@
         flat = [v[:, h * half : (h + 1) * half] for v in sums for h in range(2)]
         zero = jnp.zeros((1, half), f32)
         for p in range(3):
-            flat += [jnp.where(me == k, bs_s[p * 8 : p * 8 + 1, :], zero) for k in range(2)]
+            flat += [jnp.where(me == k, sum_s[p * 8 : p * 8 + 1, :], zero) for k in range(2)]
         hid = gb_ref.shape[1] // half
         flat += [
             jnp.where(me == k, gb_ref[:, t * half : (t + 1) * half], zero) for k in range(2) for t in range(hid)
         ]
-        flat += [zero] * (2 * n - len(flat))
+        flat += [zero] * (4 * n - len(flat))
         pad = jnp.zeros((6, half), f32)
         top = 8 * r
+        first = core == 0
         for c in range(n):
-            gb2_ref[c, top : top + 8, :] = jnp.concatenate([flat[2 * c], flat[2 * c + 1], pad], axis=0).astype(bf16)
-
-
-def qkv_backward(ids, d, a, xo, got, norms, w_own, w_sib, d_mlp, ob, dy, gb_up, n):
+            low = jnp.concatenate([flat[2 * c], flat[2 * c + 1], pad], axis=0).astype(bf16)
+            d = c + n
+            high = jnp.concatenate([flat[2 * d], flat[2 * d + 1], pad], axis=0).astype(bf16)
+            bk_ref[c, top : top + 8, :] = jnp.where(first, low, high)
+            bs_ref[c, top : top + 8, :] = jnp.where(first, high, low)
+
+    rows_o = ob_ref.shape[1]
+    go = sum(_nn(ob_ref[s], dy_ref[s * rows : (s + 1) * rows, :]) for s in range(2)).astype(bf16)
+    same = core == i
+    for k in range(rows_o // (2 * r)):
+        for a in range(2):
+            at = (k * 2 + a) * r
+            for h in range(2):
+                u = (6 + h) * r
+                v = go[at : at + r, h * half : (h + 1) * half]
+
+                @pl.when(same)
+                def _(v=v, a=a, k=k, u=u):
+                    outs[0][a][k, u : u + r, :] = v
+
+                @pl.when(jnp.logical_not(same))
+                def _(v=v, a=a, k=k, u=u):
+                    outs[1][a][k, u : u + r, :] = v
+
+
+def qkv_backward(ids, d, at, xo, xg, norms, w_own, w_got, d_mlp, ob, dy, gb_up, n):
     rows, width = xo.shape
     half = width // 2
-    r = half // (2 * n)
+    r = half // (4 * n)
     full = lambda v: pl.BlockSpec(v.shape, lambda i, ids: (0,) * v.ndim)
+    steps = 2
+    cols = half // steps
     out = [
         jax.ShapeDtypeStruct((n, 8 * r, half), bf16),
+        jax.ShapeDtypeStruct((n, 8 * r, half), bf16),
+        jax.ShapeDtypeStruct((n, 8 * r + 8, half), bf16),
         jax.ShapeDtypeStruct((n, 8 * r + 8, half), bf16),
         jax.ShapeDtypeStruct((rows, width), f32),
         jax.ShapeDtypeStruct((rows, width), bf16),
@@ -796,84 +814,118 @@
         qkv_back_kernel,
         grid_spec=pltpu.PrefetchScalarGridSpec(
             num_scalar_prefetch=1,
-            grid=(half // 128,),
-            in_specs=[pl.BlockSpec((2, 2, 3 * HD, rows), lambda i, ids: (0, i, 0, 0))]
-            + [full(a), full(xo), _x_got_spec(rows, half), full(norms)]
-            + _wq_specs(half, width, rows)
-            + [full(d_mlp), pl.BlockSpec((2, 128, rows), lambda i, ids: (0, i, 0)), full(dy), full(gb_up)],
+            grid=(steps,),
+            in_specs=[pl.BlockSpec((2, cols // HD, 3 * HD, rows), lambda i, ids: (0, i, 0, 0))]
+            + [full(at), full(xo), full(xg), full(norms)]
+            + _wq_specs(half, width, cols)
+            + [full(d_mlp), pl.BlockSpec((2, cols, rows), lambda i, ids: (0, i, 0)), full(dy), full(gb_up)],
             out_specs=tuple(full(v) for v in out),
             scratch_shapes=[
-                pltpu.VMEM((width, 2 * rows), bf16),
                 pltpu.VMEM((2 * rows, width), f32),
                 pltpu.VMEM((24, half), f32),
+                pltpu.VMEM((width, cols), bf16),
             ],
         ),
         out_shape=tuple(out),
         compiler_params=_params(),
         name="qkv_backward",
-    )(ids, d, a, xo, got, norms, w_own, w_own, w_own, got, got, got, w_sib, w_sib, w_sib, d_mlp, ob, dy, gb_up)
+    )(ids, d, at, xo, xg, norms, w_own, w_own, w_own, w_got, w_got, w_got, d_mlp, ob, dy, gb_up)
+
+
+def _mine(ids):
+    return (pl.program_id(0) // 2) == ids[1]
+
+
+def _own_block(i, ids):
+    return jnp.clip(i - 2 * ids[1], 0, 1)
+
+
+def _got_block(i, ids):
+    return jnp.clip(i - 2 * (1 - ids[1]), 0, 1)
 
 
 def join_kernel(ids, own_ref, got_ref, o_ref):
-    mine = (pl.program_id(0) // (pl.num_programs(0) // 2)) == ids[1]
+    mine = _mine(ids)
+    shape = o_ref.shape
 
     @pl.when(mine)
     def _():
-        o_ref[...] = own_ref[...].astype(f32)
+        o_ref[...] = own_ref[...].astype(f32).reshape(shape)
 
     @pl.when(jnp.logical_not(mine))
     def _():
-        o_ref[...] = got_ref[...].astype(f32)
-
-
-def join(ids, own, got):
+        o_ref[...] = got_ref[...].astype(f32).reshape(shape)
+
+
+def join_rows(ids, own, got):
     n, r, w = own.shape
-    src = pl.BlockSpec((1, r, w), lambda i, ids: (i % n, 0, 0))
+    src = lambda f: pl.BlockSpec((n // 2, r, w), lambda i, ids: (f(i, ids), 0, 0))
     return pl.pallas_call(
         join_kernel,
         grid_spec=pltpu.PrefetchScalarGridSpec(
             num_scalar_prefetch=1,
-            grid=(2 * n,),
-            in_specs=[src, src],
-            out_specs=pl.BlockSpec((1, r, w), lambda i, ids: (i, 0, 0)),
+            grid=(4,),
+            in_specs=[src(_own_block), src(_got_block)],
+            out_specs=pl.BlockSpec((n * r // 2, w), lambda i, ids: (i, 0)),
         ),
-        out_shape=jax.ShapeDtypeStruct((2 * n, r, w), f32),
+        out_shape=jax.ShapeDtypeStruct((2 * n * r, w), f32),
         compiler_params=_params(),
-        name="join",
+        name="join_rows",
     )(ids, own, got)
 
 
+def join_cols(ids, own, got):
+    n, _, r, w = own.shape
+    src = lambda f: pl.BlockSpec((n, 1, r, w), lambda i, ids: (0, f(i, ids), 0, 0))
+    return pl.pallas_call(
+        join_kernel,
+        grid_spec=pltpu.PrefetchScalarGridSpec(
+            num_scalar_prefetch=1,
+            grid=(4,),
+            in_specs=[src(_own_block), src(_got_block)],
+            out_specs=pl.BlockSpec((n * r, w), lambda i, ids: (0, (i % 2) * 2 + i // 2)),
+        ),
+        out_shape=jax.ShapeDtypeStruct((n * r, 4 * w), f32),
+        compiler_params=_params(),
+        name="join_cols",
+    )(ids, own, got)
+
+
 def unpack_kernel(ids, ao_ref, ag_ref, bo_ref, bg_ref, q_ref, o_ref, s_ref):
-    mine = (pl.program_id(0) // (pl.num_programs(0) // 2)) == ids[1]
+    mine = _mine(ids)
+    k = ao_ref.shape[0]
     r = ao_ref.shape[1] // 8
     half = ao_ref.shape[2]
     for a, (own, got) in enumerate(((ao_ref, ag_ref), (bo_ref, bg_ref))):
-        v = jnp.where(mine, own[0].astype(f32), got[0].astype(f32))
-        for w in range(2):
-            for p in range(3):
-                u = (w * 3 + p) * r
-                at = (p * 2 + w) * half
-                q_ref[a * r : (a + 1) * r, at : at + half] = v[u : u + r, :]
-            u = (6 + w) * r
-            o_ref[a * r : (a + 1) * r, w * half : (w + 1) * half] = v[u : u + r, :]
-        if a == 1:
-            s_ref[0] = v[8 * r : 8 * r + 8, :]
+        for c in range(k):
+            v = jnp.where(mine, own[c].astype(f32), got[c].astype(f32))
+            to = slice((c * 2 + a) * r, (c * 2 + a + 1) * r)
+            for w in range(2):
+                for p in range(3):
+                    u = (w * 3 + p) * r
+                    at = (p * 2 + w) * half
+                    q_ref[to, at : at + half] = v[u : u + r, :]
+                u = (6 + w) * r
+                o_ref[to, w * half : (w + 1) * half] = v[u : u + r, :]
+            if a == 1:
+                s_ref[c] = v[8 * r : 8 * r + 8, :]
 
 
 def unpack(ids, a_own, a_got, b_own, b_got):
     n, ra, half = a_own.shape
     r = ra // 8
-    spec = lambda v: pl.BlockSpec((1,) + v.shape[1:], lambda i, ids: (i % n, 0, 0))
+    k = n // 2
+    spec = lambda v, f: pl.BlockSpec((k,) + v.shape[1:], lambda i, ids: (f(i, ids), 0, 0))
     return pl.pallas_call(
         unpack_kernel,
         grid_spec=pltpu.PrefetchScalarGridSpec(
             num_scalar_prefetch=1,
-            grid=(2 * n,),
-            in_specs=[spec(v) for v in (a_own, a_got, b_own, b_got)],
+            grid=(4,),
+            in_specs=[spec(a_own, _own_block), spec(a_got, _got_block), spec(b_own, _own_block), spec(b_got, _got_block)],
             out_specs=(
-                pl.BlockSpec((2 * r, 6 * half), lambda i, ids: (i, 0)),
-                pl.BlockSpec((2 * r, 2 * half), lambda i, ids: (i, 0)),
-                pl.BlockSpec((1, 8, half), lambda i, ids: (i, 0, 0)),
+                pl.BlockSpec((2 * k * r, 6 * half), lambda i, ids: (i, 0)),
+                pl.BlockSpec((2 * k * r, 2 * half), lambda i, ids: (i, 0)),
+                pl.BlockSpec((k, 8, half), lambda i, ids: (i, 0, 0)),
             ),
         ),
         out_shape=(
@@ -943,39 +995,41 @@
     def bit_of(bit):
         return (ctx >> bit) & 1
 
-    def halve(v, bit):
+    def add(a, b):
+        return (a.astype(f32) + b.astype(f32)).astype(bf16)
+
+    def halve(pair, bit):
         b = bit_of(bit)
-        v = v.reshape((2, v.shape[0] // 2) + v.shape[1:])
-        got = flip(lax.dynamic_index_in_dim(v, 1 - b, 0, keepdims=False), bit)
-        keep = lax.dynamic_index_in_dim(v, b, 0, keepdims=False)
-        return (keep.astype(f32) + got.astype(f32)).astype(bf16)
+
+        def part(k):
+            terms = [v.reshape((2, v.shape[0] // 2) + v.shape[1:]) for v in pair]
+            return add(*[lax.dynamic_index_in_dim(v, k, 0, keepdims=False) for v in terms])
+
+        return part(b), flip(part(1 - b), bit)
 
     def ordered(first, a, b, axis=0):
         return jnp.where(first == 0, jnp.concatenate([a, b], axis), jnp.concatenate([b, a], axis))
 
     def double(v, bit):
         return ordered(bit_of(bit), v, flip(v, bit))
-
-    half_core = lambda v: lax.dynamic_slice_in_dim(v, core * (half // 2), half // 2, 0)
 
     len_parts = jnp.stack([lengths[0] // 64, lengths[0] % 64]).astype(bf16)
     small = jnp.concatenate(
         [ln1_gain, ln1_bias, ln2_gain, ln2_bias, b_out, b_down, b_qkv, len_parts, jnp.zeros((126,), bf16)]
     )[None]
     small = ordered(me, small, swap(small))
+    x_own = tokens[0]
+    x_got = swap(x_own)
+    q4 = half // 4
+    rows_of = lambda v, at, n: lax.dynamic_slice_in_dim(v, at, n, 0)
+    wq_rows = rows_of(w_qkv, (2 * core + bit_of(X)) * q4, q4)
+    cols = [lax.dynamic_slice_in_dim(wq_rows, p * width + (1 - me) * half, half, 1) for p in range(3)]
+    wq_got = swap(jnp.concatenate(cols, axis=1))
+    wu_send = lax.dynamic_slice_in_dim(rows_of(w_up, core * 2 * q4, 2 * q4), (1 - me) * hid, hid, 1)
+    wq_got, wu_send = lax.optimization_barrier((wq_got, wu_send))
+    wq_got = double(double(wq_got, X), CORE)
+    wu_got = swap(wu_send)
     cot_own = cotangent[0]
-    cot_got = swap(cot_own)
-    other = (1 - me) * half
-    cols = [lax.dynamic_slice_in_dim(half_core(w_qkv), p * width + other, half, 1) for p in range(3)]
-    wu_send = lax.dynamic_slice_in_dim(half_core(w_up), (1 - me) * hid, hid, 1)
-    x_own = tokens[0]
-    pack = jnp.concatenate([x_own[:, :half], x_own[:, half:]] + cols)
-    cot_got, pack = lax.optimization_barrier((cot_got, pack))
-    got = swap(pack)
-    wq_sib = flip(got[2 * rows :], CORE)
-    got, wu_send = lax.optimization_barrier((got, wu_send))
-    wu_got = swap(wu_send)
-    wu_sib = flip(wu_got, CORE)
 
     vec = lambda i: small[:, i * half : (i + 1) * half].reshape(width).astype(f32)
     norms = jnp.stack([vec(i) for i in range(4)])
@@ -1000,50 +1054,55 @@
     def exchange(v):
         return lax.all_to_all(v, "ctx", 0, 0, tiled=False)
 
+    send, attn_in, mlp_in = qkv_forward(ids, x_own, x_got, norms, w_qkv, wq_got, qkv_bias, own_table)
+    qkv_head = exchange(send.reshape(2 * heads, 3 * HD, rows))
+    mlp_in, wu_got, cot_send = lax.optimization_barrier((mlp_in, wu_got, cot_own))
+    cot_got = swap(cot_send)
+    wu_got = double(wu_got, CORE)
     dy = jnp.concatenate(
         [(live_own * cot_own.astype(f32)).astype(bf16), (live_got * cot_got.astype(f32)).astype(bf16)]
     )
     dctx = jnp.einsum("ed,std->set", w_out, dy.reshape(2, rows, width), preferred_element_type=f32).astype(bf16)
     do_head = exchange(dctx.reshape(2 * heads, HD, rows))
 
-    send, attn_in, mlp_in = qkv_forward(ids, x_own, got, norms, w_qkv, wq_sib, qkv_bias, own_table)
-    qkv_head = exchange(send.reshape(2 * heads, 3 * HD, rows))
-
-    mlp_in, do_head = lax.optimization_barrier((mlp_in, do_head))
-
-    y_mlp, d_mlp, g_up, g_down, gb_up = mlp(
-        ids, mlp_in, dy, w_up, wu_got, wu_sib, w_down, b_up.astype(f32)[None, :], n_ctx
-    )
-
-    chain_a = (CORE, X, ZN, ZF)
-    chain_b = (CORE, ZN, ZF, X)
-    v_down = g_down.reshape(n_ctx, hid // n_ctx, width)
-    v_up = g_up
-    qkv_head, v_down, v_up = lax.optimization_barrier((qkv_head, v_down, v_up))
-    v_down = halve(v_down, chain_a[0])
-    v_up = halve(v_up, chain_b[0])
-    qkv_head, v_down, v_up = lax.optimization_barrier((qkv_head, v_down, v_up))
-    v_down = halve(v_down, chain_a[1])
-    v_up = halve(v_up, chain_b[1])
+    mlp_t = mlp_in.T
+    attn_t = attn_in.T
+    run = partial(mlp, ids, mlp_in, mlp_t, dy, w_up, wu_got, w_down, b_up.astype(f32)[None, :], n_ctx // 2)
+    y_mlp, d_mlp, u_send, v_send, gb_send = run(True)
+    u_got = flip(u_send, CORE)
+    v_got = flip(v_send, CORE)
+    y_mlp, d_mlp, u_keep, v_keep, gb_keep = run(False, (y_mlp, d_mlp))
+    gb_up = ordered(core, gb_keep, gb_send, axis=1)
+
+    chain_a = (X, ZN, ZF)
+    chain_b = (ZN, ZF, X)
+    qkv_head, u_keep, v_keep, u_got, v_got = lax.optimization_barrier((qkv_head, u_keep, v_keep, u_got, v_got))
+    down = halve((v_keep, v_got), chain_a[0])
+    up = halve((u_keep, u_got), chain_b[0])
 
     o_head, lse = attn_fwd(block_map, qkv_head, bq=1024, bk=1024)
+    qkv_head, o_head, do_head, down, up = lax.optimization_barrier((qkv_head, o_head, do_head, down, up))
     ob = exchange(o_head).reshape(2, half, rows)
-    qkv_head, v_down, v_up = lax.optimization_barrier((qkv_head, v_down, v_up))
+    down = halve(down, chain_a[1])
+    up = halve(up, chain_b[1])
     g_head = attn_bwd(block_map, qkv_head, o_head, do_head, lse, table)
+    g_head, ob, down, up = lax.optimization_barrier((g_head, ob, down, up))
     d_qkv = exchange(g_head).reshape(2, heads, 3 * HD, rows)
 
-    for a, b in zip(chain_a[2:], chain_b[2:]):
-        v_down = halve(v_down, a)
-        v_up = halve(v_up, b)
-    v_up = v_up.reshape(1, 2, half // n_ctx, hid)
-    up_keep = lax.dynamic_index_in_dim(v_up, me, 1, keepdims=False)
-    up_got = swap(lax.dynamic_index_in_dim(v_up, 1 - me, 1, keepdims=False))
-    v_up = ordered(me, up_keep, up_got, axis=2)
-    for a, b in zip(chain_a[:0:-1], chain_b[:0:-1]):
-        v_down = double(v_down, a)
-        v_up = double(v_up, b)
-    tot_down = join(ids, v_down, flip(v_down, CORE)).reshape(hid, width)
-    tot_up = join(ids, v_up, flip(v_up, CORE)).reshape(half, 2 * hid)
+    down = add(*halve(down, chain_a[2]))
+    up = add(*halve(up, chain_b[2]))
+    up = up.reshape(1, 2, up.shape[1] // 2, up.shape[2])
+    up_keep = lax.dynamic_slice_in_dim(up, me, 1, 1)
+    up_got = swap(lax.dynamic_slice_in_dim(up, 1 - me, 1, 1))
+    up = ordered(me, up_keep, up_got, axis=1)
+    down = double(down, chain_a[2])
+    up = double(up, chain_b[2])
+    d_qkv, down, up = lax.optimization_barrier((d_qkv, down, up))
+    for a, b in zip(chain_a[1::-1], chain_b[1::-1]):
+        down = double(down, a)
+        up = double(up, b)
+    tot_down = join_rows(ids, down, flip(down, CORE))
+    tot_up = join_cols(ids, up, flip(up, CORE))
 
     part = jnp.einsum("sct,cd->std", ob, w_out, preferred_element_type=f32) + y_mlp.reshape(
         2, rows, width
@@ -1051,27 +1110,32 @@
     y_got = swap(part[1].astype(bf16)).astype(f32)
     output = (live_own * (x_own.astype(f32) + part[0] + y_got + bias_out)).astype(bf16)
 
-    v_a, v_b, e_own, e_send = qkv_backward(
-        ids, d_qkv, attn_in, x_own, got, norms, w_qkv, wq_sib, d_mlp, ob, dy, gb_up, n_ctx
-    )
+    a_keep, a_send, b_keep, b_send, e_own, e_send = qkv_backward(
+        ids, d_qkv, attn_t, x_own, x_got, norms, w_qkv, wq_got, d_mlp, ob, dy, gb_up, n_ctx // 2
+    )
+    v_a = (a_keep, flip(a_send, CORE))
+    v_b = (b_keep, flip(b_send, CORE))
     for a, b in zip(chain_a, chain_b):
         v_a = halve(v_a, a)
         v_b = halve(v_b, b)
     e_got = swap(e_send)
     n3 = 3 * half // (2 * n_ctx)
     mixed = []
-    for v, chain in ((v_a[0], chain_a), (v_b[0], chain_b)):
+    for v, chain in ((add(*v_a)[0], chain_a), (add(*v_b)[0], chain_b)):
         extra = v[8 * n3 // 3 :]
         keep = lax.dynamic_slice_in_dim(v, me * n3, n3, 0)
         give = lax.dynamic_slice_in_dim(v, (1 - me) * n3, n3, 0)
-        got = swap(jnp.concatenate([give, extra]))
-        extra = (extra.astype(f32) + got[n3:].astype(f32)).astype(bf16)
-        v = jnp.concatenate([ordered(me, keep, got[:n3]), v[2 * n3 : 8 * n3 // 3], extra])[None]
-        for a in chain[:0:-1]:
+        back = swap(jnp.concatenate([give, extra]))
+        extra = add(extra, back[n3:])
+        v = jnp.concatenate([ordered(me, keep, back[:n3]), v[2 * n3 : 8 * n3 // 3], extra])[None]
+        for a in chain[::-1]:
             v = double(v, a)
-        mixed += [v, flip(v, CORE)]
-    tot_qkv, tot_out, flat = unpack(ids, *mixed)
+        mixed.append(v)
     grad_tokens = last(e_own, e_got, x_own, cot_own, live_own)
+    mixed[0], mixed[1], grad_tokens, output, tot_down, tot_up = lax.optimization_barrier(
+        (mixed[0], mixed[1], grad_tokens, output, tot_down, tot_up)
+    )
+    tot_qkv, tot_out, flat = unpack(ids, mixed[0], flip(mixed[0], CORE), mixed[1], flip(mixed[1], CORE))
     flat = flat[:, :2].reshape(2 * n_ctx * half)
 
     def own(start, size):

time: 499 us -> 445 us (0.89)
  waiting for transfers between devices: 195 us -> 156 us
  other arithmetic: 37.3 us -> 56.8 us
  local copies, waits for them, and re-layouts: 42.8 us -> 26.2 us
  Pallas kernels: 147 us -> 135 us
    ppermute x9 -> x10, waiting for transfers between devices: 39.4 us -> 14.9 us  [swap(): return lax.ppermute(v, 'wsh', SWAP)]
    ppermute x34 -> x35, waiting for transfers between devices: 156 us -> 135 us  [flip(): return lax.ppermute(v, 'ctx', [(i, i ^ 1 << bit) for i in range(n_ctx)])]
    squeeze x16 -> x0, local copies, waits for them, and re-layouts: 14.1 us -> none  [halve(): got = flip(lax.dynamic_index_in_dim(v, 1 - b, 0, keepdims=False), bit)]
    select_n x16 -> x20, other arithmetic: 11.2 us -> 22.5 us  [ordered(): jnp.where(first == 0, jnp.concatenate([a, b], axis), jnp.concatenate([b,...]
    convert_element_type x17 -> x18, other arithmetic: 16.8 us -> 24.7 us  [the longest x17 22.4 us: add(): return (a.astype(f32) + b.astype(f32)).astype(bf16)]
    all_to_all x4, waiting for transfers between devices: 0.3 us -> 6.32 us  [exchange(): return lax.all_to_all(v, 'ctx', 0, 0, tiled=False)]
    pallas_call x1, Pallas kernels: 12.5 us -> 7.12 us  [unpack(): pl.pallas_call(unpack_kernel, grid_spec=pltpu.PrefetchScalarGridSpec(num_...]
    unnamed x61 -> x67, local copies, waits for them, and re-layouts: 13.1 us -> 7.82 us
  transfers between devices with their start and end apart: 47 -> 49, of which waited for: 22 -> 19; matrix products, arithmetic and copies ran while one was open for 14% -> 16% of each run, Pallas kernels for 27% -> 24%
where the time goes in v3:
time: 445 us; the launch traced here: 443 us
  waiting for transfers between devices  156 us (35%)
  Pallas kernels  135 us (30%)
  starting transfers between devices  65.7 us (15%)
  other arithmetic  56.8 us (13%)
  local copies, waits for them, and re-layouts  26.2 us (6%)
    ppermute x35, waiting for transfers between devices, flip(): return lax.ppermute(v, 'ctx', [(i, i ^ 1 << bit) for i in range(n_ctx)])  135 us
    pallas_call x1, Pallas kernels, attn_bwd(): pl.pallas_call(lambda *a: attn_bwd_kernel(*a, nblk=nblk, bq=bq, bk=bk), o...  35 us
    ppermute x35, starting transfers between devices, flip(): return lax.ppermute(v, 'ctx', [(i, i ^ 1 << bit) for i in range(n_ctx)])  33.2 us
    pallas_call x2, Pallas kernels, mlp(): pl.pallas_call(partial(mlp_kernel, resume=start is whole), grid_spec=pltp...  28.7 us
    select_n x20, other arithmetic, ordered(): jnp.where(first == 0, jnp.concatenate([a, b], axis), jnp.concatenate([b,...  22.5 us
    convert_element_type x17, other arithmetic, add(): return (a.astype(f32) + b.astype(f32)).astype(bf16)  22.4 us
    pallas_call x1, Pallas kernels, attn_fwd(): pl.pallas_call(lambda *a: attn_fwd_kernel(*a, nblk=nblk, bq=bq, bk=bk), o...  21.7 us
    all_to_all x4, starting transfers between devices, exchange(): return lax.all_to_all(v, 'ctx', 0, 0, tiled=False)  17.7 us
  transfers between devices with their start and end apart: 49, of which 19 were waited for; matrix products, arithmetic and copies ran while one was open for 16% of the time, Pallas kernels for 24%

profile of v3, /device:TPU:0, one launch (start us, length us, event | category | flops | bytes accessed | tf_op | source)
XLA Modules:
  0.0 443.3 jit_solution(11393729278637851310)
XLA Ops:
  0.7 3.0 collective-permute-start
  4.4 4.9 %concatenate.177 = bf16[4736]{0:T(1024)(128)(2,1)S(1)} concatenate(bf16[512]{0:T(512)(128)(2,1)} %param.17, bf16[512]{0:T(512)(128)(2,1)} %param.18, bf16[512]{0:T(512)(128)(2,1)} %param.19, bf16[512]{0:T(512)(128)(2,1)} %param.20, bf16[512]{0:T(512)(128)(2,1)} %param.24, bf16[512]{0:T(512)(128)(2,1)} %param.28, bf16[1536]{0:T(1024)(128)(2,1)} %param.22, bf16[1]{0:T(256)(128)(2,1)} %bitcast.4, ...), dimensions={0} | concatenate | bytes 18944 | tf_op jit(solution)/shard_map/concatenate | solution.py:1017
  10.8 2.0 collective-permute-start.2
  16.3 1.8 dynamic_slice.194
  18.1 6.6 %collective-permute-done.2 = bf16[128,1536]{1,0:T(8,128)(2,1)S(1)} collective-permute-done((bf16[128,1536]{1,0:T(8,128)(2,1)S(1)}, bf16[128,1536]{1,0:T(8,128)(2,1)S(1)}, u32[]{:S(2)}, u32[]{:S(2)}) %collective-permute-start.2) | collective-permute-done | bytes 393248 | tf_op jit(solution)/shard_map/ppermute | solution.py:990
  24.7 1.7 collective-permute-start.3
  26.5 1.6 collective-permute-start.5
  28.1 6.8 %collective-permute-done.3 = bf16[128,1536]{1,0:T(8,128)(2,1)S(1)} collective-permute-done((bf16[128,1536]{1,0:T(8,128)(2,1)S(1)}, bf16[128,1536]{1,0:T(8,128)(2,1)S(1)}, u32[]{:S(2)}, u32[]{:S(2)}) %collective-permute-start.3) | collective-permute-done | bytes 393248 | tf_op jit(solution)/shard_map/ppermute | solution.py:993
  38.8 2.9 maximum_select_fusion.3.gq_ref.gk_ref.gv_ref
  42.5 9.6 %qkv_forward.1 = (bf16[2,8,192,256]{3,2,1,0:T(8,128)(2,1)}, bf16[512,1024]{1,0:T(8,128)(2,1)}, bf16[512,1024]{1,0:T(8,128)(2,1)}) custom-call(s32[2]{0:T(128)} %pad_add_fusion.ids, bf16[256,1024]{1,0:T(8,128)(2,1)} %bitcast.156, bf16[256,1024]{1,0:T(8,128)(2,1)} %copy-done.13, f32[4,1024]{1,0:T(4,128)} %maximum_convert_fusion.n_ref, ...), custom_call_target="tpu_custom_call" | custom-call | flops 1048576 | bytes 1048576 | tf_op jit(solution)/shard_map/qkv_forward/pallas_call | solution.py:577
  56.1 6.0 %all-to-all-start = ((bf16[16,192,256]{2,1,0:T(8,128)(2,1)}), bf16[16,192,256]{2,1,0:T(8,128)(2,1)S(1)}, u32[]{:S(2)}, u32[]{:S(2)}) async-start(bf16[16,192,256]{2,1,0:T(8,128)(2,1)} %bitcast.171), calls=%async_computation | async-start | bytes 3145728 | tf_op jit(solution)/shard_map/all_to_all | solution.py:1055
  62.2 2.3 copy.34
  64.5 2.0 collective-permute-done.6
  68.7 4.6 %maximum_select_fusion.wg_ref = bf16[512,2048]{1,0:T(8,128)(2,1)} fusion(bf16[256,2048]{1,0:T(8,128)(2,1)} %collective-permute-done.7, bf16[256,2048]{1,0:T(8,128)(2,1)} %collective-permute-done.5, pred[]{:T(512)S(6)} %eq.19), kind=kLoop, calls=%fused_computation | loop fusion | flops 9437184 | bytes 4194305 | tf_op jit(solution)/shard_map/jit(_where)/select_n | solution.py:1011
  73.9 13.7 %mlp.2 = (f32[512,1024]{1,0:T(8,128)}, f32[512,1024]{1,0:T(8,128)}, bf16[8,128,1024]{2,1,0:T(8,128)(2,1)}, bf16[8,128,1024]{2,1,0:T(8,128)(2,1)}, f32[1,1024]{1,0:T(1,128)}) custom-call(s32[2]{0:T(128)} %pad_add_fusion.ids, bf16[512,1024]{1,0:T(8,128)(2,1)} %get-tuple-element.74.x_ref, bf16[1024,512]{1,0:T(8,128)(2,1)} %bitcast.174, ...), custom_call_target="tpu_custom_call" | custom-call | flops 6442450944 | bytes 25165824 | tf_op jit(solution)/shard_map/mlp/pallas_call | solution.py:653
  88.2 14.9 %mlp.3 = (f32[512,1024]{1,0:T(8,128)}, f32[512,1024]{1,0:T(8,128)}, bf16[8,128,1024]{2,1,0:T(8,128)(2,1)}, bf16[8,128,1024]{2,1,0:T(8,128)(2,1)}, f32[1,1024]{1,0:T(1,128)}) custom-call(s32[2]{0:T(128)} %pad_add_fusion.ids, bf16[512,1024]{1,0:T(8,128)(2,1)} %get-tuple-element.74.x_ref, bf16[1024,512]{1,0:T(8,128)(2,1)} %bitcast.175, ...), custom_call_target="tpu_custom_call" | custom-call | flops 6442450944 | bytes 25165824 | tf_op jit(solution)/shard_map/mlp/pallas_call | solution.py:653
  103.2 5.2 %fusion.2 = (bf16[4,128,1024]{2,1,0:T(8,128)(2,1)}, bf16[4,128,1024]{2,1,0:T(8,128)(2,1)}) fusion(bf16[2,4,128,1024]{3,2,1,0:T(8,128)(2,1)} %bitcast.19, s32[]{:T(128)S(6)} %select_n.355, bf16[2,4,128,1024]{3,2,1,0:T(8,128)(2,1)} %bitcast.168, s32[]{:T(128)S(6)} %select_n.354), kind=kLoop, calls=%fused_computation.15 | loop fusion | flops 4194304 | bytes 6291464 | tf_op jit(solution)/shard_map/convert_element_type | solution.py:999
  109.8 3.9 fusion.4
  113.7 1.6 collective-permute-start.11
  117.1 4.1 all-to-all-start.1
  121.2 21.7 %attn_fwd.1 = (bf16[16,64,256]{2,1,0:T(8,128)(2,1)}, f32[1,4096]{1,0:T(1,128)}) custom-call(s32[32]{0:T(128)} %a_0_.3, bf16[16,192,256]{2,1,0:T(8,128)(2,1)} %copy-done.1), custom_call_target="tpu_custom_call" | custom-call | tf_op jit(solution)/shard_map/attn_fwd/pallas_call | solution.py:438
  142.9 6.3 %all-to-all-done.1.a_3_ = bf16[16,64,256]{2,1,0:T(8,128)(2,1)S(1)} async-done(((bf16[16,64,256]{2,1,0:T(8,128)(2,1)}), bf16[16,64,256]{2,1,0:T(8,128)(2,1)S(1)}, u32[]{:S(2)}, u32[]{:S(2)}) %all-to-all-start.1) | async-done | bytes 524320 | tf_op jit(solution)/shard_map/all_to_all | solution.py:1055
  149.2 3.6 all-to-all-start.2
  152.8 2.5 fusion.14
  155.3 1.8 collective-permute-start.12
  157.1 2.4 fusion.16
  159.5 2.4 collective-permute-start.13
  163.2 35.0 %attn_bwd.1 = bf16[16,192,256]{2,1,0:T(8,128)(2,1)} custom-call(s32[32]{0:T(128)} %a_0_.3, bf16[16,192,256]{2,1,0:T(8,128)(2,1)} %copy-done.1, bf16[16,64,256]{2,1,0:T(8,128)(2,1)} %get-tuple-element.90.a_2_, bf16[16,64,256]{2,1,0:T(8,128)(2,1)} %copy-done.14, f32[1,4096]{1,0:T(1,128)} %get-tuple-element.92.a_4_, f32[16,4096]{1,0:T(8,128)} %pad_maximum_fusion.2.a_5_), custom_call_target="tpu_custom_call" | custom-call | tf_op jit(solution)/shard_map/attn_bwd/pallas_call | solution.py:498
  199.0 4.0 all-to-all-start.3
  203.0 1.8 add_convert_fusion.17
  204.8 1.5 collective-permute-start.16
  206.4 2.3 copy.36
  209.9 2.5 collective-permute-start.14
  212.4 11.7 %collective-permute-done.16 = bf16[1,128,1024]{2,1,0:T(8,128)(2,1)S(1)} collective-permute-done((bf16[1,128,1024]{2,1,0:T(8,128)(2,1)}, bf16[1,128,1024]{2,1,0:T(8,128)(2,1)S(1)}, u32[]{:S(2)}, u32[]{:S(2)}) %collective-permute-start.16) | collective-permute-done | bytes 262176 | tf_op jit(solution)/shard_map/ppermute | solution.py:993
  225.2 1.6 collective-permute-start.17
  226.8 24.9 %collective-permute-done.14 = bf16[1,128,1024]{2,1,0:T(8,128)(2,1)S(1)} collective-permute-done((bf16[1,128,1024]{2,1,0:T(8,128)(2,1)S(1)}, bf16[1,128,1024]{2,1,0:T(8,128)(2,1)S(1)}, u32[]{:S(2)}, u32[]{:S(2)}) %collective-permute-start.14) | collective-permute-done | bytes 262176 | tf_op jit(solution)/shard_map/ppermute | solution.py:993
  252.0 1.7 collective-permute-start.18
  254.3 10.9 %collective-permute-done.15 = bf16[1,128,1024]{2,1,0:T(8,128)(2,1)S(1)} collective-permute-done((bf16[1,128,1024]{2,1,0:T(8,128)(2,1)S(1)}, bf16[1,128,1024]{2,1,0:T(8,128)(2,1)S(1)}, u32[]{:S(2)}, u32[]{:S(2)}) %collective-permute-start.15) | collective-permute-done | bytes 262176 | tf_op jit(solution)/shard_map/ppermute | solution.py:993
  267.2 15.6 %qkv_backward.1 = (bf16[8,128,512]{2,1,0:T(8,128)(2,1)}, bf16[8,128,512]{2,1,0:T(8,128)(2,1)}, bf16[8,136,512]{2,1,0:T(8,128)(2,1)}, bf16[8,136,512]{2,1,0:T(8,1...) custom-call(s32[2]{0:T(128)} %pad_add_fusion.ids, bf16[2,8,192,256]{3,2,1,0:T(8,128)(2,1)} %bitcast.159, ...), custom_call_target="tpu_custom_call" | custom-call | tf_op jit(solution)/shard_map/qkv_backward/pallas_call | solution.py:813
  283.4 2.9 collective-permute-start.40
  286.3 22.4 %collective-permute-done.37 = bf16[2,128,1024]{2,1,0:T(8,128)(2,1)S(1)} collective-permute-done((bf16[2,128,1024]{2,1,0:T(8,128)(2,1)}, bf16[2,128,1024]{2,1,0:T(8,128)(2,1)S(1)}, u32[]{:S(2)}, u32[]{:S(2)}) %collective-permute-start.37) | collective-permute-done | bytes 524320 | tf_op jit(solution)/shard_map/ppermute | solution.py:993
  311.7 1.9 add_convert_fusion.7
  315.8 1.7 add_convert_fusion.5
  317.5 1.9 collective-permute-start.28
  320.2 25.8 %collective-permute-done.20 = bf16[4,128,512]{2,1,0:T(8,128)(2,1)S(1)} collective-permute-done((bf16[4,128,512]{2,1,0:T(8,128)(2,1)S(1)}, bf16[4,128,512]{2,1,0:T(8,128)(2,1)S(1)}, u32[]{:S(2)}, u32[]{:S(2)}) %collective-permute-start.20) | collective-permute-done | bytes 524320 | tf_op jit(solution)/shard_map/ppermute | solution.py:993
  346.3 1.9 maximum_select_fusion.1.own_ref
  348.3 7.8 %collective-permute-done.28 = bf16[4,136,512]{2,1,0:T(8,128)(2,1)S(1)} collective-permute-done((bf16[4,136,512]{2,1,0:T(8,128)(2,1)S(1)}, bf16[4,136,512]{2,1,0:T(8,128)(2,1)S(1)}, u32[]{:S(2)}, u32[]{:S(2)}) %collective-permute-start.28) | collective-permute-done | bytes 557088 | tf_op jit(solution)/shard_map/ppermute | solution.py:993
  356.2 4.0 collective-permute-done.21
  360.4 1.6 maximum_select_fusion.2.own_ref
  362.0 8.2 %collective-permute-done.29 = bf16[2,136,512]{2,1,0:T(8,128)(2,1)S(1)} collective-permute-done((bf16[2,136,512]{2,1,0:T(8,128)(2,1)S(1)}, bf16[2,136,512]{2,1,0:T(8,128)(2,1)S(1)}, u32[]{:S(2)}, u32[]{:S(2)}) %collective-permute-start.29) | collective-permute-done | bytes 278560 | tf_op jit(solution)/shard_map/ppermute | solution.py:993
  371.8 1.6 collective-permute-start.23
  373.4 2.6 collective-permute-done.23
  376.3 1.6 collective-permute-start.31
  377.9 2.6 collective-permute-done.31
  380.6 1.9 collective-permute-start.32
  383.4 1.6 collective-permute-start.36
  385.7 2.8 collective-permute-start.25
  390.1 5.9 %collective-permute-done.25 = bf16[2,128,512]{2,1,0:T(8,128)(2,1)} collective-permute-done((bf16[2,128,512]{2,1,0:T(8,128)(2,1)}, bf16[2,128,512]{2,1,0:T(8,128)(2,1)}, u32[]{:S(2)}, u32[]{:S(2)}) %collective-permute-start.25) | collective-permute-done | bytes 262176 | tf_op jit(solution)/shard_map/ppermute | solution.py:993
  402.0 2.4 fusion.9
  406.3 3.4 token_grad.1
  412.1 7.0 %join_rows.1 = f32[2048,1024]{1,0:T(8,128)} custom-call(s32[2]{0:T(128)} %pad_add_fusion.ids, bf16[8,128,1024]{2,1,0:T(8,128)(2,1)} %copy-done.2, bf16[8,128,1024]{2,1,0:T(8,128)(2,1)} %collective-permute-done.39.got_ref), custom_call_target="tpu_custom_call" | custom-call | tf_op jit(solution)/shard_map/join_rows/pallas_call | solution.py:863
  419.1 7.1 %join_cols.1 = f32[512,4096]{1,0:T(8,128)} custom-call(s32[2]{0:T(128)} %pad_add_fusion.ids, bf16[8,2,64,1024]{3,2,1,0:T(8,128)(2,1)} %maximum_select_fusion.2.own_ref, bf16[8,2,64,1024]{3,2,1,0:T(8,128)(2,1)} %collective-permute-done.42.got_ref), custom_call_target="tpu_custom_call" | custom-call | tf_op jit(solution)/shard_map/join_cols/pallas_call | solution.py:880
  426.7 4.0 collective-permute-done.43.ag_ref
  432.6 7.1 %unpack.1 = (f32[512,3072]{1,0:T(8,128)}, f32[512,1024]{1,0:T(8,128)}, f32[16,8,512]{2,1,0:T(8,128)}) custom-call(s32[2]{0:T(128)} %pad_add_fusion.ids, bf16[8,128,512]{2,1,0:T(8,128)(2,1)} %maximum_select_fusion.5.ao_ref, bf16[8,128,512]{2,1,0:T(8,128)(2,1)} %copy-done.20, bf16[8,136,512]{2,1,0:T(8,128)(2,1)} %maximum_select_fusion.4.bo_ref, ...), custom_call_target="tpu_custom_call" | custom-call | tf_op jit(solution)/shard_map/unpack/pallas_call | solution.py:919
  (197 shorter events, 55.9 us)
Async XLA Ops:
  0.6 114.6 %copy-start = (bf16[512,1024]{1,0:T(8,128)(2,1)S(1)}, bf16[512,1024]{1,0:T(8,128)(2,1)}, u32[]{:S(2)}) copy-start(bf16[512,1024]{1,0:T(8,128)(2,1)} %param.23) | copy-start | bytes 3145732
  0.7 41.1 %collective-permute-start = (bf16[256,1024]{1,0:T(8,128)(2,1)}, bf16[256,1024]{1,0:T(8,128)(2,1)S(1)}, u32[]{:S(2)}, u32[]{:S(2)}) collective-permute-start(bf16[256,1024]{1,0:T(8,128)(2,1)} %bitcast.155), channel_id=1, source_target_pairs={{0,1},{1,0},{2,3},{3,2},{4,5},{5,4},{6,7},{7,6},{8,9},{9,8},{10,11... | collective-permute-start | bytes 1572872 | tf_op jit(solution)/shard_map/ppermute | solution.py:990
  9.3 17.0 %collective-permute-start.1 = (bf16[1,4736]{1,0:T(2,128)(2,1)S(1)}, bf16[1,4736]{1,0:T(2,128)(2,1)S(1)}, u32[]{:S(2)}, u32[]{:S(2)}) collective-permute-start(bf16[1,4736]{1,0:T(2,128)(2,1)S(1)} %broadcast_in_dim.36), channel_id=1, source_target_pairs={{0,1},{1,0},{2,3},{3,2},{4,5},{5,4},{6,7},{7,6},{8,9},{9,8},{10,11... | collective-permute-start | bytes 28424 | tf_op jit(solution)/shard_map/ppermute | solution.py:990
  10.8 13.8 %collective-permute-start.2 = (bf16[128,1536]{1,0:T(8,128)(2,1)S(1)}, bf16[128,1536]{1,0:T(8,128)(2,1)S(1)}, u32[]{:S(2)}, u32[]{:S(2)}) collective-permute-start(bf16[128,1536]{1,0:T(8,128)(2,1)S(1)} %pad_maximum_fusion.1), channel_id=1, source_target_pairs={{0,1},{1,0},{2,3},{3,2},{4,5},{5,4},{6,7},{7,6},{8,9},{9,8},{10,11... | collective-permute-start | bytes 1179656 | tf_op jit(solution)/shard_map/ppermute | solution.py:990
  24.7 10.3 %collective-permute-start.3 = (bf16[128,1536]{1,0:T(8,128)(2,1)S(1)}, bf16[128,1536]{1,0:T(8,128)(2,1)S(1)}, u32[]{:S(2)}, u32[]{:S(2)}) collective-permute-start(bf16[128,1536]{1,0:T(8,128)(2,1)S(1)} %collective-permute-done.2), channel_id=1, source_target_pairs={{0,4},{2,6},{4,0},{6,2},{8,12},{10,14},{12,8},{14,10},{16,20},{18,... | collective-permute-start | bytes 1179656 | tf_op jit(solution)/shard_map/ppermute | solution.py:993
  26.5 25.6 %collective-permute-start.5 = (bf16[256,2048]{1,0:T(8,128)(2,1)S(1)}, bf16[256,2048]{1,0:T(8,128)(2,1)}, u32[]{:S(2)}, u32[]{:S(2)}) collective-permute-start(bf16[256,2048]{1,0:T(8,128)(2,1)S(1)} %dynamic_slice.194), channel_id=1, source_target_pairs={{0,1},{1,0},{2,3},{3,2},{4,5},{5,4},{6,7},{7,6},{8,9},{9,8},{10,11... | collective-permute-start | bytes 3145736 | tf_op jit(solution)/shard_map/ppermute | solution.py:990
  36.3 2.5 collective-permute-start.4
  52.1 14.3 %collective-permute-start.6 = (bf16[256,1024]{1,0:T(8,128)(2,1)}, bf16[256,1024]{1,0:T(8,128)(2,1)}, u32[]{:S(2)}, u32[]{:S(2)}) collective-permute-start(bf16[256,1024]{1,0:T(8,128)(2,1)} %bitcast.8.c_ref), channel_id=1, source_target_pairs={{0,1},{1,0},{2,3},{3,2},{4,5},{5,4},{6,7},{7,6},{8,9},{9,8},{10,11... | collective-permute-start | bytes 1572872 | tf_op jit(solution)/shard_map/ppermute | solution.py:990
  53.6 15.1 %collective-permute-start.7 = (bf16[256,2048]{1,0:T(8,128)(2,1)}, bf16[256,2048]{1,0:T(8,128)(2,1)}, u32[]{:S(2)}, u32[]{:S(2)}) collective-permute-start(bf16[256,2048]{1,0:T(8,128)(2,1)} %collective-permute-done.5), channel_id=1, source_target_pairs={{0,2},{2,0},{4,6},{6,4},{8,10},{10,8},{12,14},{14,12},{16,18},{18,... | collective-permute-start | bytes 3145736 | tf_op jit(solution)/shard_map/ppermute | solution.py:993
  56.1 47.0 %all-to-all-start = ((bf16[16,192,256]{2,1,0:T(8,128)(2,1)}), bf16[16,192,256]{2,1,0:T(8,128)(2,1)S(1)}, u32[]{:S(2)}, u32[]{:S(2)}) async-start(bf16[16,192,256]{2,1,0:T(8,128)(2,1)} %bitcast.171), calls=%async_computation | async-start | bytes 3145728 | tf_op jit(solution)/shard_map/all_to_all | solution.py:1055
  87.6 15.6 %collective-permute-start.8 = (bf16[8,128,1024]{2,1,0:T(8,128)(2,1)}, bf16[8,128,1024]{2,1,0:T(8,128)(2,1)}, u32[]{:S(2)}, u32[]{:S(2)}) collective-permute-start(bf16[8,128,1024]{2,1,0:T(8,128)(2,1)} %get-tuple-element.81), channel_id=1, source_target_pairs={{0,2},{2,0},{4,6},{6,4},{8,10},{10,8},{12,14},{14,12},{16,18},{18,... | collective-permute-start | bytes 6291464 | tf_op jit(solution)/shard_map/ppermute | solution.py:993
  87.7 15.5 %collective-permute-start.9 = (bf16[8,128,1024]{2,1,0:T(8,128)(2,1)}, bf16[8,128,1024]{2,1,0:T(8,128)(2,1)}, u32[]{:S(2)}, u32[]{:S(2)}) collective-permute-start(bf16[8,128,1024]{2,1,0:T(8,128)(2,1)} %get-tuple-element.82), channel_id=1, source_target_pairs={{0,2},{2,0},{4,6},{6,4},{8,10},{10,8},{12,14},{14,12},{16,18},{18,... | collective-permute-start | bytes 6291464 | tf_op jit(solution)/shard_map/ppermute | solution.py:993
  103.2 6.6 %copy-start.15 = (bf16[8,128,1024]{2,1,0:T(8,128)(2,1)S(1)}, bf16[8,128,1024]{2,1,0:T(8,128)(2,1)}, u32[]{:S(2)}) copy-start(bf16[8,128,1024]{2,1,0:T(8,128)(2,1)} %get-tuple-element.87) | copy-start | bytes 6291460
  108.4 40.8 %collective-permute-start.10 = (bf16[4,128,1024]{2,1,0:T(8,128)(2,1)}, bf16[4,128,1024]{2,1,0:T(8,128)(2,1)}, u32[]{:S(2)}, u32[]{:S(2)}) collective-permute-start(bf16[4,128,1024]{2,1,0:T(8,128)(2,1)} %get-tuple-element.128), channel_id=1, source_target_pairs={{0,4},{2,6},{4,0},{6,2},{8,12},{10,14},{12,8},{14,10},{16,20},{18,... | collective-permute-start | bytes 3145736 | tf_op jit(solution)/shard_map/ppermute | solution.py:993
  109.8 5.5 %copy-start.10 = (bf16[512,1024]{1,0:T(8,128)(2,1)S(1)}, bf16[512,1024]{1,0:T(8,128)(2,1)}, u32[]{:S(2)}) copy-start(bf16[512,1024]{1,0:T(8,128)(2,1)} %pad_maximum_fusion.dy_ref) | copy-start | bytes 3145732
  113.7 35.5 %collective-permute-start.11 = (bf16[4,128,1024]{2,1,0:T(8,128)(2,1)}, bf16[4,128,1024]{2,1,0:T(8,128)(2,1)}, u32[]{:S(2)}, u32[]{:S(2)}) collective-permute-start(bf16[4,128,1024]{2,1,0:T(8,128)(2,1)} %get-tuple-element.126), channel_id=1, source_target_pairs={{0,8},{2,10},{4,12},{6,14},{8,0},{10,2},{12,4},{14,6},{16,24},{18,... | collective-permute-start | bytes 3145736 | tf_op jit(solution)/shard_map/ppermute | solution.py:993
  117.1 35.7 %copy-start.11 = (bf16[4,128,1024]{2,1,0:T(8,128)(2,1)S(1)}, bf16[4,128,1024]{2,1,0:T(8,128)(2,1)}, u32[]{:S(2)}) copy-start(bf16[4,128,1024]{2,1,0:T(8,128)(2,1)} %get-tuple-element.93) | copy-start | bytes 3145732
  117.1 32.1 %all-to-all-start.1 = ((bf16[16,64,256]{2,1,0:T(8,128)(2,1)}), bf16[16,64,256]{2,1,0:T(8,128)(2,1)S(1)}, u32[]{:S(2)}, u32[]{:S(2)}) async-start(bf16[16,64,256]{2,1,0:T(8,128)(2,1)} %bitcast.17), calls=%async_computation.1 | async-start | bytes 1048576 | tf_op jit(solution)/shard_map/all_to_all | solution.py:1055
  149.2 6.1 %copy-start.14 = (bf16[16,64,256]{2,1,0:T(8,128)(2,1)}, bf16[16,64,256]{2,1,0:T(8,128)(2,1)S(1)}, u32[]{:S(2)}) copy-start(bf16[16,64,256]{2,1,0:T(8,128)(2,1)S(1)} %all-to-all-done.1.a_3_) | copy-start | bytes 1572868
  149.2 49.8 %all-to-all-start.2 = ((bf16[16,64,256]{2,1,0:T(8,128)(2,1)}), bf16[16,64,256]{2,1,0:T(8,128)(2,1)S(1)}, u32[]{:S(2)}, u32[]{:S(2)}) async-start(bf16[16,64,256]{2,1,0:T(8,128)(2,1)} %get-tuple-element.90.a_2_), calls=%async_computation.2 | async-start | bytes 1048576 | tf_op jit(solution)/shard_map/all_to_all | solution.py:1055
  155.3 42.9 %collective-permute-start.12 = (bf16[2,128,1024]{2,1,0:T(8,128)(2,1)S(1)}, bf16[2,128,1024]{2,1,0:T(8,128)(2,1)S(1)}, u32[]{:S(2)}, u32[]{:S(2)}) collective-permute-start(bf16[2,128,1024]{2,1,0:T(8,128)(2,1)S(1)} %get-tuple-element.139), channel_id=1, source_target_pairs={{0,8},{2,10},{4,12},{6,14},{8,0},{10,2},{12,4},{14,6},{16,24},{18,... | collective-permute-start | bytes 1572872 | tf_op jit(solution)/shard_map/ppermute | solution.py:993
  159.5 39.5 %collective-permute-start.13 = (bf16[2,128,1024]{2,1,0:T(8,128)(2,1)S(1)}, bf16[2,128,1024]{2,1,0:T(8,128)(2,1)}, u32[]{:S(2)}, u32[]{:S(2)}) collective-permute-start(bf16[2,128,1024]{2,1,0:T(8,128)(2,1)S(1)} %get-tuple-element.137), channel_id=1, source_target_pairs={{0,16},{2,18},{4,20},{6,22},{8,24},{10,26},{12,28},{14,30},{16,0},... | collective-permute-start | bytes 1572872 | tf_op jit(solution)/shard_map/ppermute | solution.py:993
  199.0 9.6 %copy-start.6 = (bf16[16,64,256]{2,1,0:T(8,128)(2,1)}, bf16[16,64,256]{2,1,0:T(8,128)(2,1)S(1)}, u32[]{:S(2)}) copy-start(bf16[16,64,256]{2,1,0:T(8,128)(2,1)S(1)} %all-to-all-done.2) | copy-start | bytes 1572868
  199.0 67.0 %all-to-all-start.3 = ((bf16[16,192,256]{2,1,0:T(8,128)(2,1)}), bf16[16,192,256]{2,1,0:T(8,128)(2,1)S(1)}, u32[]{:S(2)}, u32[]{:S(2)}) async-start(bf16[16,192,256]{2,1,0:T(8,128)(2,1)} %attn_bwd.1), calls=%async_computation.3 | async-start | bytes 3145728 | tf_op jit(solution)/shard_map/all_to_all | solution.py:1055
  204.8 19.2 %collective-permute-start.16 = (bf16[1,128,1024]{2,1,0:T(8,128)(2,1)}, bf16[1,128,1024]{2,1,0:T(8,128)(2,1)S(1)}, u32[]{:S(2)}, u32[]{:S(2)}) collective-permute-start(bf16[1,128,1024]{2,1,0:T(8,128)(2,1)} %add_convert_fusion.17), channel_id=1, source_target_pairs={{0,4},{2,6},{4,0},{6,2},{8,12},{10,14},{12,8},{14,10},{16,20},{18,... | collective-permute-start | bytes 786440 | tf_op jit(solution)/shard_map/ppermute | solution.py:993
  208.7 43.1 %copy-start.17 = (bf16[2,128,1024]{2,1,0:T(8,128)(2,1)S(1)}, bf16[2,128,1024]{2,1,0:T(8,128)(2,1)}, u32[]{:S(2)}) copy-start(bf16[2,128,1024]{2,1,0:T(8,128)(2,1)} %get-tuple-element.98) | copy-start | bytes 1572868
  208.7 43.1 %copy-start.22 = (bf16[2,128,1024]{2,1,0:T(8,128)(2,1)S(1)}, bf16[2,128,1024]{2,1,0:T(8,128)(2,1)}, u32[]{:S(2)}) copy-start(bf16[2,128,1024]{2,1,0:T(8,128)(2,1)} %copy-done.21) | copy-start | bytes 1572868
  208.7 45.0 %copy-start.26 = (f32[1,1024]{1,0:T(1,128)S(1)}, f32[1,1024]{1,0:T(1,128)}, u32[]{:S(2)}) copy-start(f32[1,1024]{1,0:T(1,128)} %get-tuple-element.107) | copy-start | bytes 12292
  208.7 45.0 %copy-start.27 = (f32[1,1024]{1,0:T(1,128)S(1)}, f32[1,1024]{1,0:T(1,128)}, u32[]{:S(2)}) copy-start(f32[1,1024]{1,0:T(1,128)} %get-tuple-element.106) | copy-start | bytes 12292
  209.9 41.8 %collective-permute-start.14 = (bf16[1,128,1024]{2,1,0:T(8,128)(2,1)S(1)}, bf16[1,128,1024]{2,1,0:T(8,128)(2,1)S(1)}, u32[]{:S(2)}, u32[]{:S(2)}) collective-permute-start(bf16[1,128,1024]{2,1,0:T(8,128)(2,1)S(1)} %add_convert_fusion.20), channel_id=1, source_target_pairs={{0,16},{2,18},{4,20},{6,22},{8,24},{10,26},{12,28},{14,30},{16,0},... | collective-permute-start | bytes 786440 | tf_op jit(solution)/shard_map/ppermute | solution.py:993
  225.2 26.7 %collective-permute-start.17 = (bf16[1,1,64,1024]{3,2,1,0:T(8,128)(2,1)S(1)}, bf16[1,1,64,1024]{3,2,1,0:T(8,128)(2,1)S(1)}, u32[]{:S(2)}, u32[]{:S(2)}) collective-permute-start(bf16[1,1,64,1024]{3,2,1,0:T(8,128)(2,1)S(1)} %get-tuple-element.146), channel_id=1, source_target_pairs={{0,1},{1,0},{2,3},{3,2},{4,5},{5,4},{6,7},{7,6},{8,9},{9,8},{10,11... | collective-permute-start | bytes 393224 | tf_op jit(solution)/shard_map/ppermute | solution.py:990
  251.8 13.3 %collective-permute-start.15 = (bf16[1,128,1024]{2,1,0:T(8,128)(2,1)S(1)}, bf16[1,128,1024]{2,1,0:T(8,128)(2,1)S(1)}, u32[]{:S(2)}, u32[]{:S(2)}) collective-permute-start(bf16[1,128,1024]{2,1,0:T(8,128)(2,1)S(1)} %add_convert_fusion.19), channel_id=1, source_target_pairs={{0,16},{2,18},{4,20},{6,22},{8,24},{10,26},{12,28},{14,30},{16,0},... | collective-permute-start | bytes 786440 | tf_op jit(solution)/shard_map/ppermute | solution.py:993
  252.0 14.0 %collective-permute-start.18 = (bf16[1,2,64,1024]{3,2,1,0:T(8,128)(2,1)S(1)}, bf16[1,2,64,1024]{3,2,1,0:T(8,128)(2,1)S(1)}, u32[]{:S(2)}, u32[]{:S(2)}) collective-permute-start(bf16[1,2,64,1024]{3,2,1,0:T(8,128)(2,1)S(1)} %maximum_select_fusion.14), channel_id=1, source_target_pairs={{0,4},{2,6},{4,0},{6,2},{8,12},{10,14},{12,8},{14,10},{16,20},{18,... | collective-permute-start | bytes 786440 | tf_op jit(solution)/shard_map/ppermute | solution.py:993
  282.8 28.9 %collective-permute-start.19 = (bf16[8,128,512]{2,1,0:T(8,128)(2,1)}, bf16[8,128,512]{2,1,0:T(8,128)(2,1)}, u32[]{:S(2)}, u32[]{:S(2)}) collective-permute-start(bf16[8,128,512]{2,1,0:T(8,128)(2,1)} %get-tuple-element.109), channel_id=1, source_target_pairs={{0,2},{2,0},{4,6},{6,4},{8,10},{10,8},{12,14},{14,12},{16,18},{18,... | collective-permute-start | bytes 3145736 | tf_op jit(solution)/shard_map/ppermute | solution.py:993
  282.9 32.9 %collective-permute-start.27 = (bf16[8,136,512]{2,1,0:T(8,128)(2,1)}, bf16[8,136,512]{2,1,0:T(8,128)(2,1)}, u32[]{:S(2)}, u32[]{:S(2)}) collective-permute-start(bf16[8,136,512]{2,1,0:T(8,128)(2,1)} %get-tuple-element.111), channel_id=1, source_target_pairs={{0,2},{2,0},{4,6},{6,4},{8,10},{10,8},{12,14},{14,12},{16,18},{18,... | collective-permute-start | bytes 3342344 | tf_op jit(solution)/shard_map/ppermute | solution.py:993
  283.4 25.3 %collective-permute-start.37 = (bf16[2,128,1024]{2,1,0:T(8,128)(2,1)}, bf16[2,128,1024]{2,1,0:T(8,128)(2,1)S(1)}, u32[]{:S(2)}, u32[]{:S(2)}) collective-permute-start(bf16[2,128,1024]{2,1,0:T(8,128)(2,1)} %maximum_select_fusion.10), channel_id=1, source_target_pairs={{0,8},{2,10},{4,12},{6,14},{8,0},{10,2},{12,4},{14,6},{16,24},{18,... | collective-permute-start | bytes 1572872 | tf_op jit(solution)/shard_map/ppermute | solution.py:993
  283.4 30.9 %collective-permute-start.40 = (bf16[2,2,64,1024]{3,2,1,0:T(8,128)(2,1)S(1)}, bf16[2,2,64,1024]{3,2,1,0:T(8,128)(2,1)}, u32[]{:S(2)}, u32[]{:S(2)}) collective-permute-start(bf16[2,2,64,1024]{3,2,1,0:T(8,128)(2,1)S(1)} %maximum_select_fusion.11), channel_id=1, source_target_pairs={{0,16},{2,18},{4,20},{6,22},{8,24},{10,26},{12,28},{14,30},{16,0},... | collective-permute-start | bytes 1572872 | tf_op jit(solution)/shard_map/ppermute | solution.py:993
  310.2 5.5 %copy-start.8 = (bf16[4,128,1024]{2,1,0:T(8,128)(2,1)}, bf16[4,128,1024]{2,1,0:T(8,128)(2,1)S(1)}, u32[]{:S(2)}) copy-start(bf16[4,128,1024]{2,1,0:T(8,128)(2,1)S(1)} %maximum_select_fusion.6) | copy-start | bytes 3145732
  310.2 36.0 %collective-permute-start.38 = (bf16[4,128,1024]{2,1,0:T(8,128)(2,1)S(1)}, bf16[4,128,1024]{2,1,0:T(8,128)(2,1)}, u32[]{:S(2)}, u32[]{:S(2)}) collective-permute-start(bf16[4,128,1024]{2,1,0:T(8,128)(2,1)S(1)} %maximum_select_fusion.6), channel_id=1, source_target_pairs={{0,4},{2,6},{4,0},{6,2},{8,12},{10,14},{12,8},{14,10},{16,20},{18,... | collective-permute-start | bytes 3145736 | tf_op jit(solution)/shard_map/ppermute | solution.py:993
  313.7 32.4 %collective-permute-start.20 = (bf16[4,128,512]{2,1,0:T(8,128)(2,1)S(1)}, bf16[4,128,512]{2,1,0:T(8,128)(2,1)S(1)}, u32[]{:S(2)}, u32[]{:S(2)}) collective-permute-start(bf16[4,128,512]{2,1,0:T(8,128)(2,1)S(1)} %get-tuple-element.136), channel_id=1, source_target_pairs={{0,4},{2,6},{4,0},{6,2},{8,12},{10,14},{12,8},{14,10},{16,20},{18,... | collective-permute-start | bytes 1572872 | tf_op jit(solution)/shard_map/ppermute | solution.py:993
  315.7 44.7 %collective-permute-start.41 = (bf16[4,2,64,1024]{3,2,1,0:T(8,128)(2,1)S(1)}, bf16[4,2,64,1024]{3,2,1,0:T(8,128)(2,1)S(1)}, u32[]{:S(2)}, u32[]{:S(2)}) collective-permute-start(bf16[4,2,64,1024]{3,2,1,0:T(8,128)(2,1)S(1)} %maximum_select_fusion.7), channel_id=1, source_target_pairs={{0,8},{2,10},{4,12},{6,14},{8,0},{10,2},{12,4},{14,6},{16,24},{18,... | collective-permute-start | bytes 3145736 | tf_op jit(solution)/shard_map/ppermute | solution.py:993
  317.5 38.5 %collective-permute-start.28 = (bf16[4,136,512]{2,1,0:T(8,128)(2,1)S(1)}, bf16[4,136,512]{2,1,0:T(8,128)(2,1)S(1)}, u32[]{:S(2)}, u32[]{:S(2)}) collective-permute-start(bf16[4,136,512]{2,1,0:T(8,128)(2,1)S(1)} %get-tuple-element.134), channel_id=1, source_target_pairs={{0,8},{2,10},{4,12},{6,14},{8,0},{10,2},{12,4},{14,6},{16,24},{18,... | collective-permute-start | bytes 1671176 | tf_op jit(solution)/shard_map/ppermute | solution.py:993
  320.2 62.4 %copy-start.4 = (f32[2,256,1024]{2,1,0:T(8,128)}, f32[2,256,1024]{2,1,0:T(8,128)S(1)}, u32[]{:S(2)}) copy-start(f32[2,256,1024]{2,1,0:T(8,128)S(1)} %convolution_add_fusion) | copy-start | bytes 6291460
  320.2 26.1 %copy-start.9 = (bf16[4,128,1024]{2,1,0:T(8,128)(2,1)S(1)}, bf16[4,128,1024]{2,1,0:T(8,128)(2,1)}, u32[]{:S(2)}) copy-start(bf16[4,128,1024]{2,1,0:T(8,128)(2,1)} %copy-done.8) | copy-start | bytes 3145732
  346.2 14.1 %collective-permute-start.21 = (bf16[2,128,512]{2,1,0:T(8,128)(2,1)S(1)}, bf16[2,128,512]{2,1,0:T(8,128)(2,1)S(1)}, u32[]{:S(2)}, u32[]{:S(2)}) collective-permute-start(bf16[2,128,512]{2,1,0:T(8,128)(2,1)S(1)} %get-tuple-element.144), channel_id=1, source_target_pairs={{0,8},{2,10},{4,12},{6,14},{8,0},{10,2},{12,4},{14,6},{16,24},{18,... | collective-permute-start | bytes 786440 | tf_op jit(solution)/shard_map/ppermute | solution.py:993
  348.2 13.9 %copy-start.2 = (bf16[8,128,1024]{2,1,0:T(8,128)(2,1)}, bf16[8,128,1024]{2,1,0:T(8,128)(2,1)S(1)}, u32[]{:S(2)}) copy-start(bf16[8,128,1024]{2,1,0:T(8,128)(2,1)S(1)} %maximum_select_fusion.1.own_ref) | copy-start | bytes 6291460
  348.2 63.9 %collective-permute-start.39 = (bf16[8,128,1024]{2,1,0:T(8,128)(2,1)S(1)}, bf16[8,128,1024]{2,1,0:T(8,128)(2,1)}, u32[]{:S(2)}, u32[]{:S(2)}) collective-permute-start(bf16[8,128,1024]{2,1,0:T(8,128)(2,1)S(1)} %maximum_select_fusion.1.own_ref), channel_id=1, source_target_pairs={{0,2},{2,0},{4,6},{6,4},{8,10},{10,8},{12,14},{14,12},{16,18},{18,... | collective-permute-start | bytes 6291464 | tf_op jit(solution)/shard_map/ppermute | solution.py:993
  356.2 14.1 %collective-permute-start.29 = (bf16[2,136,512]{2,1,0:T(8,128)(2,1)S(1)}, bf16[2,136,512]{2,1,0:T(8,128)(2,1)S(1)}, u32[]{:S(2)}, u32[]{:S(2)}) collective-permute-start(bf16[2,136,512]{2,1,0:T(8,128)(2,1)S(1)} %get-tuple-element.142), channel_id=1, source_target_pairs={{0,16},{2,18},{4,20},{6,22},{8,24},{10,26},{12,28},{14,30},{16,0},... | collective-permute-start | bytes 835592 | tf_op jit(solution)/shard_map/ppermute | solution.py:993
  360.3 11.4 %collective-permute-start.22 = (bf16[1,128,512]{2,1,0:T(8,128)(2,1)S(1)}, bf16[1,128,512]{2,1,0:T(8,128)(2,1)S(1)}, u32[]{:S(2)}, u32[]{:S(2)}) collective-permute-start(bf16[1,128,512]{2,1,0:T(8,128)(2,1)S(1)} %fusion.23), channel_id=1, source_target_pairs={{0,16},{2,18},{4,20},{6,22},{8,24},{10,26},{12,28},{14,30},{16,0},... | collective-permute-start | bytes 393224 | tf_op jit(solution)/shard_map/ppermute | solution.py:993
  362.0 57.1 %collective-permute-start.42 = (bf16[8,2,64,1024]{3,2,1,0:T(8,128)(2,1)}, bf16[8,2,64,1024]{3,2,1,0:T(8,128)(2,1)}, u32[]{:S(2)}, u32[]{:S(2)}) collective-permute-start(bf16[8,2,64,1024]{3,2,1,0:T(8,128)(2,1)} %maximum_select_fusion.2.own_ref), channel_id=1, source_target_pairs={{0,2},{2,0},{4,6},{6,4},{8,10},{10,8},{12,14},{14,12},{16,18},{18,... | collective-permute-start | bytes 6291464 | tf_op jit(solution)/shard_map/ppermute | solution.py:993
  370.3 5.9 %collective-permute-start.30 = (bf16[1,136,512]{2,1,0:T(8,128)(2,1)S(1)}, bf16[1,136,512]{2,1,0:T(8,128)(2,1)S(1)}, u32[]{:S(2)}, u32[]{:S(2)}) collective-permute-start(bf16[1,136,512]{2,1,0:T(8,128)(2,1)S(1)} %fusion.20), channel_id=1, source_target_pairs={{0,4},{2,6},{4,0},{6,2},{8,12},{10,14},{12,8},{14,10},{16,20},{18,... | collective-permute-start | bytes 417800 | tf_op jit(solution)/shard_map/ppermute | solution.py:993
  371.8 4.2 collective-permute-start.23
  376.1 8.8 %collective-permute-start.24 = (bf16[1,128,512]{2,1,0:T(8,128)(2,1)S(1)}, bf16[1,128,512]{2,1,0:T(8,128)(2,1)S(1)}, u32[]{:S(2)}, u32[]{:S(2)}) collective-permute-start(bf16[1,128,512]{2,1,0:T(8,128)(2,1)S(1)} %maximum_bitcast_fusion.1), channel_id=1, source_target_pairs={{0,16},{2,18},{4,20},{6,22},{8,24},{10,26},{12,28},{14,30},{16,0},... | collective-permute-start | bytes 393224 | tf_op jit(solution)/shard_map/ppermute | solution.py:993
  376.3 4.2 collective-permute-start.31
  380.6 7.9 %collective-permute-start.32 = (bf16[1,136,512]{2,1,0:T(8,128)(2,1)S(1)}, bf16[1,136,512]{2,1,0:T(8,128)(2,1)S(1)}, u32[]{:S(2)}, u32[]{:S(2)}) collective-permute-start(bf16[1,136,512]{2,1,0:T(8,128)(2,1)S(1)} %maximum_bitcast_fusion), channel_id=1, source_target_pairs={{0,4},{2,6},{4,0},{6,2},{8,12},{10,14},{12,8},{14,10},{16,20},{18,... | collective-permute-start | bytes 417800 | tf_op jit(solution)/shard_map/ppermute | solution.py:993
  383.4 17.3 %collective-permute-start.36 = (bf16[256,1024]{1,0:T(8,128)(2,1)}, bf16[256,1024]{1,0:T(8,128)(2,1)}, u32[]{:S(2)}, u32[]{:S(2)}) collective-permute-start(bf16[256,1024]{1,0:T(8,128)(2,1)} %fusion.18), channel_id=1, source_target_pairs={{0,1},{1,0},{2,3},{3,2},{4,5},{5,4},{6,7},{7,6},{8,9},{9,8},{10,11... | collective-permute-start | bytes 1572872 | tf_op jit(solution)/shard_map/ppermute | solution.py:990
  385.7 10.4 %collective-permute-start.25 = (bf16[2,128,512]{2,1,0:T(8,128)(2,1)}, bf16[2,128,512]{2,1,0:T(8,128)(2,1)}, u32[]{:S(2)}, u32[]{:S(2)}) collective-permute-start(bf16[2,128,512]{2,1,0:T(8,128)(2,1)} %maximum_select_fusion.15), channel_id=1, source_target_pairs={{0,8},{2,10},{4,12},{6,14},{8,0},{10,2},{12,4},{14,6},{16,24},{18,... | collective-permute-start | bytes 786440 | tf_op jit(solution)/shard_map/ppermute | solution.py:993
  388.5 9.9 %collective-permute-start.33 = (bf16[2,136,512]{2,1,0:T(8,128)(2,1)S(1)}, bf16[2,136,512]{2,1,0:T(8,128)(2,1)}, u32[]{:S(2)}, u32[]{:S(2)}) collective-permute-start(bf16[2,136,512]{2,1,0:T(8,128)(2,1)S(1)} %maximum_select_fusion.13), channel_id=1, source_target_pairs={{0,16},{2,18},{4,20},{6,22},{8,24},{10,26},{12,28},{14,30},{16,0},... | collective-permute-start | bytes 835592 | tf_op jit(solution)/shard_map/ppermute | solution.py:993
  390.1 11.9 %copy-start.3 = (bf16[1,256,1024]{2,1,0:T(8,128)(2,1)S(1)}, bf16[1,256,1024]{2,1,0:T(8,128)(2,1)}, u32[]{:S(2)}) copy-start(bf16[1,256,1024]{2,1,0:T(8,128)(2,1)} %param.16) | copy-start | bytes 1572868
  396.1 9.4 %collective-permute-start.35 = (bf16[256,1024]{1,0:T(8,128)(2,1)}, bf16[256,1024]{1,0:T(8,128)(2,1)S(1)}, u32[]{:S(2)}, u32[]{:S(2)}) collective-permute-start(bf16[256,1024]{1,0:T(8,128)(2,1)} %get-tuple-element.113), channel_id=1, source_target_pairs={{0,1},{1,0},{2,3},{3,2},{4,5},{5,4},{6,7},{7,6},{8,9},{9,8},{10,11... | collective-permute-start | bytes 1572872 | tf_op jit(solution)/shard_map/ppermute | solution.py:990
  398.4 11.3 %collective-permute-start.26 = (bf16[4,128,512]{2,1,0:T(8,128)(2,1)S(1)}, bf16[4,128,512]{2,1,0:T(8,128)(2,1)S(1)}, u32[]{:S(2)}, u32[]{:S(2)}) collective-permute-start(bf16[4,128,512]{2,1,0:T(8,128)(2,1)S(1)} %maximum_select_fusion.12), channel_id=1, source_target_pairs={{0,4},{2,6},{4,0},{6,2},{8,12},{10,14},{12,8},{14,10},{16,20},{18,... | collective-permute-start | bytes 1572872 | tf_op jit(solution)/shard_map/ppermute | solution.py:993
  400.6 10.2 %collective-permute-start.34 = (bf16[4,136,512]{2,1,0:T(8,128)(2,1)S(1)}, bf16[4,136,512]{2,1,0:T(8,128)(2,1)S(1)}, u32[]{:S(2)}, u32[]{:S(2)}) collective-permute-start(bf16[4,136,512]{2,1,0:T(8,128)(2,1)S(1)} %maximum_select_fusion.9), channel_id=1, source_target_pairs={{0,8},{2,10},{4,12},{6,14},{8,0},{10,2},{12,4},{14,6},{16,24},{18,... | collective-permute-start | bytes 1671176 | tf_op jit(solution)/shard_map/ppermute | solution.py:993
  426.2 4.5 %collective-permute-start.44 = (bf16[8,136,512]{2,1,0:T(8,128)(2,1)}, bf16[8,136,512]{2,1,0:T(8,128)(2,1)S(1)}, u32[]{:S(2)}, u32[]{:S(2)}) collective-permute-start(bf16[8,136,512]{2,1,0:T(8,128)(2,1)} %maximum_select_fusion.4.bo_ref), channel_id=1, source_target_pairs={{0,2},{2,0},{4,6},{6,4},{8,10},{10,8},{12,14},{14,12},{16,18},{18,... | collective-permute-start | bytes 3342344 | tf_op jit(solution)/shard_map/ppermute | solution.py:993
  426.2 4.5 %collective-permute-start.43 = (bf16[8,128,512]{2,1,0:T(8,128)(2,1)}, bf16[8,128,512]{2,1,0:T(8,128)(2,1)S(1)}, u32[]{:S(2)}, u32[]{:S(2)}) collective-permute-start(bf16[8,128,512]{2,1,0:T(8,128)(2,1)} %maximum_select_fusion.5.ao_ref), channel_id=1, source_target_pairs={{0,2},{2,0},{4,6},{6,4},{8,10},{10,8},{12,14},{14,12},{16,18},{18,... | collective-permute-start | bytes 3145736 | tf_op jit(solution)/shard_map/ppermute | solution.py:993
  (13 other events, 30.6 us)

commit v4 on v3

--- a/solution.py
+++ b/solution.py
@@ -395,9 +395,9 @@
 def _nn(a,b): return lax.dot_general(a,b,(((1,),(0,)),((),())),preferred_element_type=f32)
 def _nt(a,b): return lax.dot_general(a,b,(((1,),(1,)),((),())),preferred_element_type=f32)
 
-def attn_fwd_kernel(bm, x_ref, o_ref, lse_ref, q_s, kt_s, v_s, *, nblk, bq, bk):
+def attn_fwd_kernel(bm, x_ref, o_ref, lse_ref, q_s, kt_s, v_s, *, nblk, per, bq, bk):
     def perm(i,_):
-        p=bm[i]; c=i//2; l=pl.multiple_of((i%2)*HB,HB); d=pl.multiple_of(p*HB,HB)
+        p=bm[i]; c=i//per; l=pl.multiple_of((i%per)*HB,HB); d=pl.multiple_of(p*HB,HB)
         q_s[:,pl.ds(d,HB)]=x_ref[c,0:64,pl.ds(l,HB)]*bf16(0.125)
         kt_s[pl.ds(d,HB),:]=x_ref[c,64:128,pl.ds(l,HB)].astype(f32).T.astype(bf16)
         v_s[:,pl.ds(d,HB)]=x_ref[c,128:192,pl.ds(l,HB)]
@@ -427,25 +427,25 @@
         return 0
     lax.fori_loop(0,nq,qloop,0)
     def unperm(i,_):
-        p=bm[i]; c=i//2; l=pl.multiple_of((i%2)*HB,HB); d=pl.multiple_of(p*HB,HB)
+        p=bm[i]; c=i//per; l=pl.multiple_of((i%per)*HB,HB); d=pl.multiple_of(p*HB,HB)
         o_ref[c,:,pl.ds(l,HB)]=q_s[:,pl.ds(d,HB)]
         return 0
     lax.fori_loop(0,nblk,unperm,0)
 
 def attn_fwd(bm,x,*,bq=512,bk=512):
-    n=x.shape[0]; S=n*256; nblk=2*n
+    n=x.shape[0]; S=n*x.shape[2]; nblk=S//HB
     bq=math.gcd(S,bq); bk=math.gcd(bq,bk)
     return pl.pallas_call(
-        lambda *a: attn_fwd_kernel(*a,nblk=nblk,bq=bq,bk=bk),
-        out_shape=(jax.ShapeDtypeStruct((n,64,256),bf16),jax.ShapeDtypeStruct((1,S),f32)),
+        lambda *a: attn_fwd_kernel(*a,nblk=nblk,per=x.shape[2]//HB,bq=bq,bk=bk),
+        out_shape=(jax.ShapeDtypeStruct((n,64,x.shape[2]),bf16),jax.ShapeDtypeStruct((1,S),f32)),
         in_specs=[pl.BlockSpec(memory_space=pltpu.SMEM),pl.BlockSpec(memory_space=pltpu.VMEM)],
         out_specs=(pl.BlockSpec(memory_space=pltpu.VMEM),pl.BlockSpec(memory_space=pltpu.VMEM)),
         scratch_shapes=[pltpu.VMEM((64,S),bf16),pltpu.VMEM((S,64),bf16),pltpu.VMEM((64,S),bf16)],
         compiler_params=pltpu.CompilerParams(vmem_limit_bytes=56<<20),name="attn_fwd")(bm,x)
 
-def attn_bwd_kernel(bm, x_ref, o_ref, do_ref, lse_ref, cs_ref, g_ref, q_s, kt_s, k_s, vt_s, do_s, dl_s, dq_s, dk_s, dv_s, *, nblk, bq, bk):
+def attn_bwd_kernel(bm, x_ref, o_ref, do_ref, lse_ref, cs_ref, g_ref, q_s, kt_s, k_s, vt_s, do_s, dl_s, dq_s, dk_s, dv_s, *, nblk, per, bq, bk):
     def perm(i,_):
-        p=bm[i]; c=i//2; l=pl.multiple_of((i%2)*HB,HB); d=pl.multiple_of(p*HB,HB)
+        p=bm[i]; c=i//per; l=pl.multiple_of((i%per)*HB,HB); d=pl.multiple_of(p*HB,HB)
         q_s[:,pl.ds(d,HB)]=x_ref[c,0:64,pl.ds(l,HB)]*bf16(0.125)
         k=x_ref[c,64:128,pl.ds(l,HB)]
         k_s[:,pl.ds(d,HB)]=k*bf16(0.125)
@@ -480,7 +480,7 @@
         return 0
     lax.fori_loop(0,nq,qloop,0)
     def unperm(i,_):
-        p=bm[i]; c=i//2; l=pl.multiple_of((i%2)*HB,HB); d=pl.multiple_of(p*HB,HB)
+        p=bm[i]; c=i//per; l=pl.multiple_of((i%per)*HB,HB); d=pl.multiple_of(p*HB,HB)
         cos=cs_ref[0:8,pl.ds(d,HB)]; sin=cs_ref[8:16,pl.ds(d,HB)]
         for n_,src in ((0,dq_s),(1,dk_s)):
             g=src[:,pl.ds(d,HB)]
@@ -492,12 +492,12 @@
     lax.fori_loop(0,nblk,unperm,0)
 
 def attn_bwd(bm,x,o,do,lse,cs,*,bq=512,bk=512):
-    n=x.shape[0]; S=n*256; nblk=2*n
+    n=x.shape[0]; S=n*x.shape[2]; nblk=S//HB
     bq=math.gcd(S,bq); bk=math.gcd(bq,bk)
     vm=pl.BlockSpec(memory_space=pltpu.VMEM)
     return pl.pallas_call(
-        lambda *a: attn_bwd_kernel(*a,nblk=nblk,bq=bq,bk=bk),
-        out_shape=jax.ShapeDtypeStruct((n,192,256),bf16),
+        lambda *a: attn_bwd_kernel(*a,nblk=nblk,per=x.shape[2]//HB,bq=bq,bk=bk),
+        out_shape=jax.ShapeDtypeStruct((n,192,x.shape[2]),bf16),
         in_specs=[pl.BlockSpec(memory_space=pltpu.SMEM)]+[vm]*5,
         out_specs=vm,
         scratch_shapes=[pltpu.VMEM((64,S),bf16),pltpu.VMEM((S,64),bf16),pltpu.VMEM((64,S),bf16),pltpu.VMEM((S,64),bf16),pltpu.VMEM((64,S),bf16),
@@ -523,25 +523,31 @@
     return cen * inv, inv
 
 
-def _pieces(ids):
-    me, core = ids[0], ids[1]
-    return me, core
+def _full(v):
+    return pl.BlockSpec(v.shape, lambda *a: (0,) * v.ndim)
+
+
+def _wq_specs(half, width, cols, quarter, at):
+    own = lambda p: pl.BlockSpec(
+        (half, cols),
+        lambda *a: (0, p * (width // cols) + a[-1][0] * (half // cols) + a[-1][1] * (quarter // cols) + at(*a)),
+    )
+    got = lambda p: pl.BlockSpec((half, cols), lambda *a: (0, p * (quarter // cols) + at(*a)))
+    return [own(p) for p in range(3)] + [got(p) for p in range(3)]
 
 
 def qkv_kernel(
-    ids, xo_ref, xg_ref, n_ref, wq_ref, wk_ref, wv_ref, gq_ref, gk_ref, gv_ref, bq_ref, bk_ref, bv_ref, cs_ref,
-    send_ref, ain_ref, min_ref
+    ids, x_ref, n_ref, wq_ref, wk_ref, wv_ref, gq_ref, gk_ref, gv_ref, bq_ref, bk_ref, bv_ref, cs_ref, send_ref,
+    ain_ref, min_ref
 ):
-    rows, width = xo_ref.shape
+    rows, width = x_ref.shape
     half = width // 2
 
-    @pl.when(pl.program_id(0) == 0)
+    @pl.when(pl.program_id(1) == 0)
     def _():
-        for s in range(2):
-            x = xo_ref[...] if s == 0 else xg_ref[...]
-            xhat, _ = _norm(x)
-            ain_ref[s * rows : (s + 1) * rows, :] = (xhat * n_ref[0:1, :] + n_ref[1:2, :]).astype(bf16)
-            min_ref[s * rows : (s + 1) * rows, :] = (xhat * n_ref[2:3, :] + n_ref[3:4, :]).astype(bf16)
+        xhat, _ = _norm(x_ref[...])
+        ain_ref[...] = (xhat * n_ref[0:1, :] + n_ref[1:2, :]).astype(bf16)
+        min_ref[...] = (xhat * n_ref[2:3, :] + n_ref[3:4, :]).astype(bf16)
 
     me = ids[0]
     a_own = ain_ref[:, pl.ds(pl.multiple_of(me * half, half), half)]
@@ -551,78 +557,67 @@
     for n, (w, g, b) in enumerate(((wq_ref, gq_ref, bq_ref), (wk_ref, gk_ref, bk_ref), (wv_ref, gv_ref, bv_ref))):
         t = _nn(a_own, w[...]) + _nn(a_got, g[...]) + b[...]
         t = t.T
-        for s in range(2):
-            for k in range(2):
-                v = t[k * HD : (k + 1) * HD, s * rows : (s + 1) * rows]
-                if n < 2:
-                    lead = v[0:8]
-                    trail = v[8:16]
-                    v = jnp.concatenate([lead * cos - trail * sin, trail * cos + lead * sin, v[16:]], axis=0)
-                send_ref[s, k, n * HD : (n + 1) * HD, :] = v.astype(bf16)
-
-
-def _wq_specs(half, width, cols):
-    own = lambda p: pl.BlockSpec((half, cols), lambda i, ids: (0, p * (width // cols) + ids[0] * (half // cols) + i))
-    got = lambda p: pl.BlockSpec((half, cols), lambda i, ids: (0, p * (half // cols) + i))
-    return [own(p) for p in range(3)] + [got(p) for p in range(3)]
-
-
-def qkv_forward(ids, xo, xg, norms, w_own, w_got, bias, cs):
-    rows, width = xo.shape
+        for k in range(send_ref.shape[1]):
+            v = t[k * HD : (k + 1) * HD]
+            if n < 2:
+                lead = v[0:8]
+                trail = v[8:16]
+                v = jnp.concatenate([lead * cos - trail * sin, trail * cos + lead * sin, v[16:]], axis=0)
+            send_ref[0, k, n * HD : (n + 1) * HD, :] = v.astype(bf16)
+
+
+def qkv_forward(ids, x2, norms, w_own, w_got, bias, cs, cols=128):
+    rows, width = x2.shape[0] // 2, x2.shape[1]
     half = width // 2
-    full = lambda a: pl.BlockSpec(a.shape, lambda i, ids: (0,) * a.ndim)
-    bsp = lambda p: pl.BlockSpec((1, 128), lambda i, ids: (0, p * (half // 128) + i))
-    heads = half // HD
-    res = lambda: pl.BlockSpec((2 * rows, width), lambda i, ids: (0, 0))
+    quarter = w_got.shape[1] // 3
+    bsp = lambda p: pl.BlockSpec((1, cols), lambda s, i, ids: (0, p * (quarter // cols) + i))
+    row = lambda: pl.BlockSpec((rows, width), lambda s, i, ids: (s, 0))
     return pl.pallas_call(
         qkv_kernel,
         grid_spec=pltpu.PrefetchScalarGridSpec(
             num_scalar_prefetch=1,
-            grid=(half // 128,),
-            in_specs=[full(xo), full(xg), full(norms)]
-            + _wq_specs(half, width, 128)
+            grid=(2, quarter // cols),
+            in_specs=[row(), _full(norms)]
+            + _wq_specs(half, width, cols, quarter, lambda s, i, ids: i)
             + [bsp(p) for p in range(3)]
-            + [full(cs)],
-            out_specs=(pl.BlockSpec((2, 2, 3 * HD, rows), lambda i, ids: (0, i, 0, 0)), res(), res()),
+            + [_full(cs)],
+            out_specs=(pl.BlockSpec((1, cols // HD, 3 * HD, rows), lambda s, i, ids: (s, i, 0, 0)), row(), row()),
         ),
         out_shape=(
-            jax.ShapeDtypeStruct((2, heads, 3 * HD, rows), bf16),
+            jax.ShapeDtypeStruct((2, quarter // HD, 3 * HD, rows), bf16),
             jax.ShapeDtypeStruct((2 * rows, width), bf16),
             jax.ShapeDtypeStruct((2 * rows, width), bf16),
         ),
         compiler_params=_params(),
         cost_estimate=pl.CostEstimate(flops=1 << 20, transcendentals=0, bytes_accessed=1 << 20),
         name="qkv_forward",
-    )(ids, xo, xg, norms, w_own, w_own, w_own, w_got, w_got, w_got, bias, bias, bias, cs)
-
-
-def mlp_kernel(
-    ids, x_ref, xt_ref, dy_ref, wo_ref, wg_ref, wd_ref, bu_ref, y0_ref, dx0_ref, y_ref, dx_ref, gu_ref,
-    gd_ref, gb_ref, *, resume
-):
+    )(ids, x2, norms, w_own, w_own, w_own, w_got, w_got, w_got, bias, bias, bias, cs)
+
+
+def mlp_kernel(ids, x_ref, xt_ref, dy_ref, wo_ref, wg_ref, wd_ref, bu_ref, y_ref, dx_ref, gu_ref, gd_ref, gb_ref):
     rows, width = x_ref.shape
     half = width // 2
     me = ids[0]
     spans = (
-        (pl.multiple_of(me * half, half), half, wo_ref),
-        (pl.multiple_of((1 - me) * half, half), half, wg_ref),
+        (pl.multiple_of(me * half, half), wo_ref),
+        (pl.multiple_of((1 - me) * half, half), wg_ref),
     )
 
     @pl.when(pl.program_id(0) == 0)
     def _():
-        y_ref[...] = y0_ref[...] if resume else jnp.zeros_like(y_ref)
-        dx_ref[...] = dx0_ref[...] if resume else jnp.zeros_like(dx_ref)
+        y_ref[...] = jnp.zeros_like(y_ref)
+        dx_ref[...] = jnp.zeros_like(dx_ref)
 
     dy = dy_ref[...]
     wd = wd_ref[...]
-    u = bu_ref[...] + sum(_nn(x_ref[:, pl.ds(o, n)], w[...]) for o, n, w in spans)
+    u = bu_ref[...] + sum(_nn(x_ref[:, pl.ds(o, half)], w[...]) for o, w in spans)
     cdf = 0.5 * (1.0 + lax.erf(u * (1.0 / math.sqrt(2.0))))
     pdf = jnp.exp(-0.5 * u * u) * (1.0 / math.sqrt(2.0 * math.pi))
     act = (u * cdf).astype(bf16)
     du = (_nt(dy, wd) * (cdf + u * pdf)).astype(bf16)
     y_ref[...] += _nn(act, wd)
-    for o, n, w in spans:
-        dx_ref[:, pl.ds(o, n)] += _nt(du, w[...])
+    for o, w in spans:
+        dx_ref[:, pl.ds(o, half)] += _nt(du, w[...])
     gd = lax.dot_general(act, dy, (((0,), (0,)), ((), ())), preferred_element_type=f32).astype(bf16)
     k, r, _ = gd_ref.shape
     for c in range(k):
@@ -636,22 +631,16 @@
     gb_ref[...] = jnp.sum(du.astype(f32), axis=0, keepdims=True)
 
 
-def mlp(ids, x, xt, dy, w_own, w_got, wd, bu, n, sibling, before=None, tile=256):
+def mlp(ids, x, xt, dy, w_own, w_got, wd, bu, n, tile=256):
     rows, width = x.shape
     half = width // 2
-    steps = w_got.shape[1] // (2 * tile)
-    hidden = steps * tile
-    part = lambda i, ids: (1 - ids[1] if sibling else ids[1]) * steps + i
+    hidden = w_got.shape[1]
+    steps = hidden // tile
     whole = pl.BlockSpec((rows, width), lambda i, ids: (0, 0))
-    sums = [jax.ShapeDtypeStruct((rows, width), f32)] * 2
-    if before is None:
-        before = (jnp.zeros((8, 128), f32),) * 2
-        start = pl.BlockSpec((8, 128), lambda i, ids: (0, 0))
-    else:
-        start = whole
     per = hidden // n
+    part = lambda i, ids: ids[1] * steps + i
     return pl.pallas_call(
-        partial(mlp_kernel, resume=start is whole),
+        mlp_kernel,
         grid_spec=pltpu.PrefetchScalarGridSpec(
             num_scalar_prefetch=1,
             grid=(steps,),
@@ -660,11 +649,9 @@
                 pl.BlockSpec((width, rows), lambda i, ids: (0, 0)),
                 whole,
                 pl.BlockSpec((half, tile), lambda i, ids: (0, ids[0] * 2 * steps + part(i, ids))),
-                pl.BlockSpec((half, tile), lambda i, ids: (0, part(i, ids))),
+                pl.BlockSpec((half, tile), lambda i, ids: (0, i)),
                 pl.BlockSpec((tile, width), lambda i, ids: (part(i, ids), 0)),
                 pl.BlockSpec((1, tile), lambda i, ids: (0, part(i, ids))),
-                start,
-                start,
             ],
             out_specs=(
                 whole,
@@ -675,7 +662,8 @@
             ),
         ),
         out_shape=(
-            *sums,
+            jax.ShapeDtypeStruct((rows, width), f32),
+            jax.ShapeDtypeStruct((rows, width), f32),
             jax.ShapeDtypeStruct((n, width // n, hidden), bf16),
             jax.ShapeDtypeStruct((n, per, width), bf16),
             jax.ShapeDtypeStruct((1, hidden), f32),
@@ -685,151 +673,133 @@
             flops=12 * rows * width * hidden, transcendentals=2 * rows * hidden, bytes_accessed=24 << 20
         ),
         name="mlp",
-    )(ids, x, xt, dy, w_own, w_got, wd, bu, *before)
+    )(ids, x, xt, dy, w_own, w_got, wd, bu)
 
 
 def qkv_back_kernel(
-    ids, d_ref, at_ref, xo_ref, xg_ref, n_ref, wq_ref, wk_ref, wv_ref, gq_ref, gk_ref, gv_ref, dm_ref,
-    ob_ref, dy_ref, gb_ref, ak_ref, as_ref, bk_ref, bs_ref, eo_ref, ex_ref, da_s, sum_s, g_s
+    ids, d_ref, at_ref, x_ref, n_ref, wq_ref, wk_ref, wv_ref, gq_ref, gk_ref, gv_ref, dm_ref, ob_ref, dy_ref, gb_ref,
+    a_ref, b_ref, e_ref, g_s, go_s, bias_s, sum_s
 ):
-    rows, width = xo_ref.shape
+    rows, width = x_ref.shape
     half = width // 2
-    q4 = half // 2
     me = ids[0]
     core = ids[1]
-    i = pl.program_id(0)
-    outs = ((ak_ref, bk_ref), (as_ref, bs_ref))
-    n = ak_ref.shape[0]
-    r = half // (4 * n)
+    s = pl.program_id(0)
+    outs = (a_ref, b_ref)
+    n = a_ref.shape[0]
     nh = d_ref.shape[1]
     cols = nh * HD
-    lanes = pl.ds(pl.multiple_of(i * cols, cols), cols)
+    r = half // (2 * n)
+
+    @pl.when(s == 0)
+    def _():
+        g_s[...] = jnp.zeros_like(g_s)
+        go_s[...] = jnp.zeros_like(go_s)
+        bias_s[...] = jnp.zeros_like(bias_s)
+        sum_s[...] = jnp.zeros_like(sum_s)
+
     ones = jnp.ones((8, rows), bf16)
-    dts = [[], []]
+    at = at_ref[...]
+    dts = []
     for p in range(3):
-        g = jnp.zeros((width, cols), f32)
-        b = jnp.zeros((8, cols), f32)
-        for s in range(2):
-            dp = jnp.concatenate([d_ref[s, k, p * HD : (p + 1) * HD, :] for k in range(nh)], axis=0)
-            g = g + _nt(at_ref[:, s * rows : (s + 1) * rows], dp)
-            b = b + _nt(ones, dp)
-            dts[s].append(dp.astype(f32).T.astype(bf16))
-        sum_s[p * 8 : (p + 1) * 8, lanes] = b
-        g_s[...] = g.astype(bf16)
-        for side in range(2):
-            which = core if side == 0 else 1 - core
+        dp = jnp.concatenate([d_ref[0, k, p * HD : (p + 1) * HD, :] for k in range(nh)], axis=0)
+        g_s[p] += _nt(at, dp)
+        bias_s[p * 8 : (p + 1) * 8, :] += _nt(ones, dp)
+        dts.append(dp.astype(f32).T.astype(bf16))
+    go_s[...] += _nn(ob_ref[0], dy_ref[...])
+    dt = jnp.concatenate(dts, axis=1)
+    w_own = jnp.concatenate([wq_ref[...], wk_ref[...], wv_ref[...]], axis=1)
+    w_got = jnp.concatenate([gq_ref[...], gk_ref[...], gv_ref[...]], axis=1)
+    d_own = _nt(dt, w_own)
+    d_got = _nt(dt, w_got)
+    first = me == 0
+    xhat, _ = _norm(x_ref[...])
+    for h in range(2):
+        lanes = slice(h * half, (h + 1) * half)
+        da = jnp.where(first, d_own, d_got) if h == 0 else jnp.where(first, d_got, d_own)
+        dm = dm_ref[:, lanes]
+        xh = xhat[:, lanes]
+        e_ref[0, :, lanes] = da * n_ref[0:1, lanes] + dm * n_ref[2:3, lanes]
+        for k, v in enumerate((da * xh, da, dm * xh, dm)):
+            sum_s[k : k + 1, lanes] += jnp.sum(v, axis=0, keepdims=True)
+
+    @pl.when(s == 0)
+    def _():
+        mine = dy_ref[pl.ds(pl.multiple_of(core * (rows // 2), rows // 2), rows // 2), :]
+        sum_s[4:5, :] = jnp.sum(mine.astype(f32), axis=0, keepdims=True)
+
+    @pl.when(s == pl.num_programs(0) - 1)
+    def _():
+        for p in range(3):
+            g = g_s[p].astype(bf16)
             for h in range(2):
                 for c in range(n):
                     for a in range(2):
-                        at = pl.multiple_of(h * half + which * q4 + (c * 2 + a) * r, r)
+                        row = h * half + (c * 2 + a) * r
                         u = (h * 3 + p) * r
-                        outs[side][a][c, u : u + r, lanes] = g_s[pl.ds(at, r), :]
-    for o, m, refs in (
-        (pl.multiple_of(me * half, half), half, (wq_ref, wk_ref, wv_ref)),
-        (pl.multiple_of((1 - me) * half, half), half, (gq_ref, gk_ref, gv_ref)),
-    ):
-        w = jnp.concatenate([v[...] for v in refs], axis=1)
-        for s in range(2):
-            v = _nt(jnp.concatenate(dts[s], axis=1), w)
-            at = slice(s * rows, (s + 1) * rows)
-
-            @pl.when(i == 0)
-            def _(v=v, at=at, o=o, m=m):
-                da_s[at, pl.ds(o, m)] = v
-
-            @pl.when(i > 0)
-            def _(v=v, at=at, o=o, m=m):
-                da_s[at, pl.ds(o, m)] += v
-
-    @pl.when(i == pl.num_programs(0) - 1)
-    def _():
-        sums = [jnp.zeros((1, width), f32) for _ in range(4)]
-        for s in range(2):
-            x = xo_ref[...] if s == 0 else xg_ref[...]
-            xhat, _ = _norm(x)
-            da = da_s[s * rows : (s + 1) * rows, :]
-            dm = dm_ref[s * rows : (s + 1) * rows, :]
-            e = da * n_ref[0:1, :] + dm * n_ref[2:3, :]
-            if s == 0:
-                eo_ref[...] = e
-            else:
-                ex_ref[...] = e.astype(bf16)
-            for k, v in enumerate((da * xhat, da, dm * xhat, dm)):
-                sums[k] = sums[k] + jnp.sum(v, axis=0, keepdims=True)
-        sums.append(jnp.sum(dy_ref[0:rows, :].astype(f32), axis=0, keepdims=True))
-        flat = [v[:, h * half : (h + 1) * half] for v in sums for h in range(2)]
-        zero = jnp.zeros((1, half), f32)
+                        outs[a][c, u : u + r, :] = g[row : row + r, :]
+        go = go_s[...].astype(bf16)
+        q = cols // (2 * n)
+        for c in range(n):
+            for a in range(2):
+                row = (c * 2 + a) * q
+                for k in range(width // cols):
+                    u = 6 * r + k * q
+                    outs[a][c, u : u + q, :] = go[row : row + q, k * cols : (k + 1) * cols]
+        flat = [sum_s[k : k + 1, t * cols : (t + 1) * cols] for k in range(5) for t in range(width // cols)]
+        zero = jnp.zeros((1, cols), f32)
         for p in range(3):
-            flat += [jnp.where(me == k, sum_s[p * 8 : p * 8 + 1, :], zero) for k in range(2)]
-        hid = gb_ref.shape[1] // half
+            flat += [
+                jnp.where((me == k) & (core == j), bias_s[p * 8 : p * 8 + 1, :], zero) for k in range(2) for j in range(2)
+            ]
         flat += [
-            jnp.where(me == k, gb_ref[:, t * half : (t + 1) * half], zero) for k in range(2) for t in range(hid)
+            jnp.where((me == k) & (core == j), gb_ref[:, t * cols : (t + 1) * cols], zero)
+            for k in range(2)
+            for j in range(2)
+            for t in range(gb_ref.shape[1] // cols)
         ]
-        flat += [zero] * (4 * n - len(flat))
-        pad = jnp.zeros((6, half), f32)
-        top = 8 * r
-        first = core == 0
+        top = 6 * r + (width // cols) * q
+        per = len(flat) // n
+        pad = [zero] * (8 - per)
         for c in range(n):
-            low = jnp.concatenate([flat[2 * c], flat[2 * c + 1], pad], axis=0).astype(bf16)
-            d = c + n
-            high = jnp.concatenate([flat[2 * d], flat[2 * d + 1], pad], axis=0).astype(bf16)
-            bk_ref[c, top : top + 8, :] = jnp.where(first, low, high)
-            bs_ref[c, top : top + 8, :] = jnp.where(first, high, low)
-
-    rows_o = ob_ref.shape[1]
-    go = sum(_nn(ob_ref[s], dy_ref[s * rows : (s + 1) * rows, :]) for s in range(2)).astype(bf16)
-    same = core == i
-    for k in range(rows_o // (2 * r)):
-        for a in range(2):
-            at = (k * 2 + a) * r
-            for h in range(2):
-                u = (6 + h) * r
-                v = go[at : at + r, h * half : (h + 1) * half]
-
-                @pl.when(same)
-                def _(v=v, a=a, k=k, u=u):
-                    outs[0][a][k, u : u + r, :] = v
-
-                @pl.when(jnp.logical_not(same))
-                def _(v=v, a=a, k=k, u=u):
-                    outs[1][a][k, u : u + r, :] = v
-
-
-def qkv_backward(ids, d, at, xo, xg, norms, w_own, w_got, d_mlp, ob, dy, gb_up, n):
-    rows, width = xo.shape
+            b_ref[c, top : top + 8, :] = jnp.concatenate(flat[c * per : (c + 1) * per] + pad, axis=0).astype(bf16)
+
+
+def qkv_backward(ids, d, at, x2, norms, w_own, w_got, d_mlp, ob, dy, gb_up, n):
+    rows, width = x2.shape[0] // 2, x2.shape[1]
     half = width // 2
-    r = half // (4 * n)
-    full = lambda v: pl.BlockSpec(v.shape, lambda i, ids: (0,) * v.ndim)
-    steps = 2
-    cols = half // steps
+    cols = w_got.shape[1] // 3
+    size = 6 * (half // (2 * n)) + width // (2 * n)
+    row = lambda: pl.BlockSpec((rows, width), lambda s, ids: (s, 0))
     out = [
-        jax.ShapeDtypeStruct((n, 8 * r, half), bf16),
-        jax.ShapeDtypeStruct((n, 8 * r, half), bf16),
-        jax.ShapeDtypeStruct((n, 8 * r + 8, half), bf16),
-        jax.ShapeDtypeStruct((n, 8 * r + 8, half), bf16),
-        jax.ShapeDtypeStruct((rows, width), f32),
-        jax.ShapeDtypeStruct((rows, width), bf16),
+        jax.ShapeDtypeStruct((n, size, cols), bf16),
+        jax.ShapeDtypeStruct((n, size + 8, cols), bf16),
     ]
     return pl.pallas_call(
         qkv_back_kernel,
         grid_spec=pltpu.PrefetchScalarGridSpec(
             num_scalar_prefetch=1,
-            grid=(steps,),
-            in_specs=[pl.BlockSpec((2, cols // HD, 3 * HD, rows), lambda i, ids: (0, i, 0, 0))]
-            + [full(at), full(xo), full(xg), full(norms)]
-            + _wq_specs(half, width, cols)
-            + [full(d_mlp), pl.BlockSpec((2, cols, rows), lambda i, ids: (0, i, 0)), full(dy), full(gb_up)],
-            out_specs=tuple(full(v) for v in out),
+            grid=(2,),
+            in_specs=[
+                pl.BlockSpec((1, cols // HD, 3 * HD, rows), lambda s, ids: (s, 0, 0, 0)),
+                pl.BlockSpec((width, rows), lambda s, ids: (0, s)),
+                row(),
+                _full(norms),
+            ]
+            + _wq_specs(half, width, cols, cols, lambda s, ids: 0)
+            + [row(), pl.BlockSpec((1, cols, rows), lambda s, ids: (s, 0, 0)), row(), _full(gb_up)],
+            out_specs=(*[_full(v) for v in out], pl.BlockSpec((1, rows, width), lambda s, ids: (s, 0, 0))),
             scratch_shapes=[
-                pltpu.VMEM((2 * rows, width), f32),
-                pltpu.VMEM((24, half), f32),
-                pltpu.VMEM((width, cols), bf16),
+                pltpu.VMEM((3, width, cols), f32),
+                pltpu.VMEM((cols, width), f32),
+                pltpu.VMEM((24, cols), f32),
+                pltpu.VMEM((8, width), f32),
             ],
         ),
-        out_shape=tuple(out),
+        out_shape=(*out, jax.ShapeDtypeStruct((2, rows, width), f32)),
         compiler_params=_params(),
         name="qkv_backward",
-    )(ids, d, at, xo, xg, norms, w_own, w_own, w_own, w_got, w_got, w_got, d_mlp, ob, dy, gb_up)
+    )(ids, d, at, x2, norms, w_own, w_own, w_own, w_got, w_got, w_got, d_mlp, ob, dy, gb_up)
 
 
 def _mine(ids):
@@ -892,46 +862,51 @@
 
 
 def unpack_kernel(ids, ao_ref, ag_ref, bo_ref, bg_ref, q_ref, o_ref, s_ref):
-    mine = _mine(ids)
-    k = ao_ref.shape[0]
-    r = ao_ref.shape[1] // 8
-    half = ao_ref.shape[2]
+    first = ids[1] == 0
+    k, _, cols = ao_ref.shape
+    r = q_ref.shape[0] // (2 * k)
+    q = o_ref.shape[1] // (2 * k)
     for a, (own, got) in enumerate(((ao_ref, ag_ref), (bo_ref, bg_ref))):
         for c in range(k):
-            v = jnp.where(mine, own[c].astype(f32), got[c].astype(f32))
+            x = own[c].astype(f32)
+            y = got[c].astype(f32)
             to = slice((c * 2 + a) * r, (c * 2 + a + 1) * r)
-            for w in range(2):
-                for p in range(3):
-                    u = (w * 3 + p) * r
-                    at = (p * 2 + w) * half
-                    q_ref[to, at : at + half] = v[u : u + r, :]
-                u = (6 + w) * r
-                o_ref[to, w * half : (w + 1) * half] = v[u : u + r, :]
+            tq = slice((c * 2 + a) * q, (c * 2 + a + 1) * q)
+            for j in range(2):
+                v = jnp.where(first, x, y) if j == 0 else jnp.where(first, y, x)
+                for w in range(2):
+                    for p in range(3):
+                        u = (w * 3 + p) * r
+                        at = ((p * 2 + w) * 2 + j) * cols
+                        q_ref[to, at : at + cols] = v[u : u + r, :]
+                for t in range(o_ref.shape[2] // cols):
+                    u = 6 * r + t * q
+                    o_ref[j, tq, t * cols : (t + 1) * cols] = v[u : u + q, :]
             if a == 1:
-                s_ref[c] = v[8 * r : 8 * r + 8, :]
-
-
-def unpack(ids, a_own, a_got, b_own, b_got):
-    n, ra, half = a_own.shape
-    r = ra // 8
-    k = n // 2
-    spec = lambda v, f: pl.BlockSpec((k,) + v.shape[1:], lambda i, ids: (f(i, ids), 0, 0))
+                s_ref[c] = (x + y)[-8:, :]
+
+
+def unpack(ids, a_own, a_got, b_own, b_got, width, steps=4):
+    n, _, cols = a_own.shape
+    half = width // 2
+    k = n // steps
+    spec = lambda v: pl.BlockSpec((k,) + v.shape[1:], lambda i, ids: (i, 0, 0))
     return pl.pallas_call(
         unpack_kernel,
         grid_spec=pltpu.PrefetchScalarGridSpec(
             num_scalar_prefetch=1,
-            grid=(4,),
-            in_specs=[spec(a_own, _own_block), spec(a_got, _got_block), spec(b_own, _own_block), spec(b_got, _got_block)],
+            grid=(steps,),
+            in_specs=[spec(v) for v in (a_own, a_got, b_own, b_got)],
             out_specs=(
-                pl.BlockSpec((2 * k * r, 6 * half), lambda i, ids: (i, 0)),
-                pl.BlockSpec((2 * k * r, 2 * half), lambda i, ids: (i, 0)),
-                pl.BlockSpec((k, 8, half), lambda i, ids: (i, 0, 0)),
+                pl.BlockSpec((half // steps, 3 * width), lambda i, ids: (i, 0)),
+                pl.BlockSpec((2, cols // steps, width), lambda i, ids: (0, i, 0)),
+                pl.BlockSpec((k, 8, cols), lambda i, ids: (i, 0, 0)),
             ),
         ),
         out_shape=(
-            jax.ShapeDtypeStruct((4 * n * r, 6 * half), f32),
-            jax.ShapeDtypeStruct((4 * n * r, 2 * half), f32),
-            jax.ShapeDtypeStruct((2 * n, 8, half), f32),
+            jax.ShapeDtypeStruct((half, 3 * width), f32),
+            jax.ShapeDtypeStruct((2, cols, width), f32),
+            jax.ShapeDtypeStruct((n, 8, cols), f32),
         ),
         compiler_params=_params(),
         name="unpack",
@@ -978,11 +953,14 @@
     me = lax.axis_index("wsh")
     core = ctx % 2
     n_ctx = lax.axis_size("ctx")
-    rows, width = tokens.shape[1:]
+    chips = n_ctx // 2
+    own_rows, width = tokens.shape[1:]
+    rows = 2 * own_rows
     half = width // 2
-    seq = rows * n_ctx
-    heads = H // 2
-    hid = w_up.shape[1] // 2
+    quarter = half // 2
+    seq = own_rows * n_ctx
+    heads = H // 4
+    hid = w_up.shape[1] // 4
     ids = jnp.stack([me, core]).astype(jnp.int32)
     CORE, X, ZN, ZF = 0, 1, 2, 3
 
@@ -995,15 +973,15 @@
     def bit_of(bit):
         return (ctx >> bit) & 1
 
-    def add(a, b):
-        return (a.astype(f32) + b.astype(f32)).astype(bf16)
-
-    def halve(pair, bit):
+    def add(*terms):
+        return sum(v.astype(f32) for v in terms).astype(bf16) if len(terms) > 1 else terms[0]
+
+    def halve(terms, bit):
         b = bit_of(bit)
 
         def part(k):
-            terms = [v.reshape((2, v.shape[0] // 2) + v.shape[1:]) for v in pair]
-            return add(*[lax.dynamic_index_in_dim(v, k, 0, keepdims=False) for v in terms])
+            cut = [v.reshape((2, v.shape[0] // 2) + v.shape[1:]) for v in terms]
+            return add(*[lax.dynamic_index_in_dim(v, k, 0, keepdims=False) for v in cut])
 
         return part(b), flip(part(1 - b), bit)
 
@@ -1012,6 +990,13 @@
 
     def double(v, bit):
         return ordered(bit_of(bit), v, flip(v, bit))
+
+    def exchange(v):
+        groups = [[2 * i + c for i in range(chips)] for c in range(2)]
+        return lax.all_to_all(v, "ctx", 0, 0, axis_index_groups=groups, tiled=False)
+
+    def rows_of(v, at, n, axis=0):
+        return lax.dynamic_slice_in_dim(v, at, n, axis)
 
     len_parts = jnp.stack([lengths[0] // 64, lengths[0] % 64]).astype(bf16)
     small = jnp.concatenate(
@@ -1020,69 +1005,64 @@
     small = ordered(me, small, swap(small))
     x_own = tokens[0]
     x_got = swap(x_own)
-    q4 = half // 4
-    rows_of = lambda v, at, n: lax.dynamic_slice_in_dim(v, at, n, 0)
-    wq_rows = rows_of(w_qkv, (2 * core + bit_of(X)) * q4, q4)
-    cols = [lax.dynamic_slice_in_dim(wq_rows, p * width + (1 - me) * half, half, 1) for p in range(3)]
-    wq_got = swap(jnp.concatenate(cols, axis=1))
-    wu_send = lax.dynamic_slice_in_dim(rows_of(w_up, core * 2 * q4, 2 * q4), (1 - me) * hid, hid, 1)
+    mine = me * half + core * quarter
+    other = (1 - me) * half + core * quarter
+    wq_rows = rows_of(w_qkv, bit_of(X) * quarter, quarter)
+    wq_got = swap(jnp.concatenate([rows_of(wq_rows, p * width + other, quarter, 1) for p in range(3)], axis=1))
+    wu_send = rows_of(w_up, ((1 - me) * 2 + core) * hid, hid, 1)
     wq_got, wu_send = lax.optimization_barrier((wq_got, wu_send))
-    wq_got = double(double(wq_got, X), CORE)
+    wq_got = double(wq_got, X)
     wu_got = swap(wu_send)
+    x_sib = flip(x_own, CORE)
+    x2 = jnp.concatenate([ordered(core, x_own, x_sib), double(x_got, CORE)])
     cot_own = cotangent[0]
+    cot_sib = flip(cot_own, CORE)
 
     vec = lambda i: small[:, i * half : (i + 1) * half].reshape(width).astype(f32)
     norms = jnp.stack([vec(i) for i in range(4)])
     bias_out = vec(4) + vec(5)
     qkv_bias = small[:, 6 * half : 9 * half].astype(f32).reshape(3, width)
-    qkv_bias = lax.dynamic_slice_in_dim(qkv_bias, me * half, half, 1).reshape(1, 3 * half)
+    qkv_bias = rows_of(qkv_bias, mine, quarter, 1).reshape(1, 3 * quarter)
     lens = small[:, 9 * half : 9 * half + 2].astype(jnp.int32)
     lens = lens[:, 0] * 64 + lens[:, 1]
     other_len = lens[1 - me]
 
-    own_blocks = lax.dynamic_slice_in_dim(block_map, 2 * ctx, 2)
+    blocks = rows_of(block_map, (rows // HB) * (ctx // 2), rows // HB)
     offs = jnp.arange(HB, dtype=jnp.int32)
-    positions = (own_blocks[:, None] * HB + offs[None, :]).reshape(rows)
-    live_own = (positions < lengths[0]).astype(f32)[:, None]
-    live_got = (positions < other_len).astype(f32)[:, None]
+    positions = (blocks[:, None] * HB + offs[None, :]).reshape(rows)
+    live2 = jnp.concatenate([positions < lengths[0], positions < other_len]).astype(f32)[:, None]
+    live_own = rows_of(live2, core * own_rows, own_rows)
     freq = 10000.0 ** (-jnp.arange(ROT // 2, dtype=f32) * 2.0 / ROT)
     ang = freq[:, None] * jnp.arange(seq, dtype=jnp.int32).astype(f32)[None, :]
     table = jnp.concatenate([jnp.cos(ang), jnp.sin(ang)])
     own_ang = freq[:, None] * positions.astype(f32)[None, :]
     own_table = jnp.concatenate([jnp.cos(own_ang), jnp.sin(own_ang)])
 
-    def exchange(v):
-        return lax.all_to_all(v, "ctx", 0, 0, tiled=False)
-
-    send, attn_in, mlp_in = qkv_forward(ids, x_own, x_got, norms, w_qkv, wq_got, qkv_bias, own_table)
+    send, attn_in, mlp_in = qkv_forward(ids, x2, norms, w_qkv, wq_got, qkv_bias, own_table)
     qkv_head = exchange(send.reshape(2 * heads, 3 * HD, rows))
     mlp_in, wu_got, cot_send = lax.optimization_barrier((mlp_in, wu_got, cot_own))
     cot_got = swap(cot_send)
-    wu_got = double(wu_got, CORE)
-    dy = jnp.concatenate(
-        [(live_own * cot_own.astype(f32)).astype(bf16), (live_got * cot_got.astype(f32)).astype(bf16)]
-    )
-    dctx = jnp.einsum("ed,std->set", w_out, dy.reshape(2, rows, width), preferred_element_type=f32).astype(bf16)
+    cot2 = jnp.concatenate([ordered(core, cot_own, cot_sib), double(cot_got, CORE)])
+    dy = (live2 * cot2.astype(f32)).astype(bf16)
+    dy2 = dy.reshape(2, rows, width)
+    w_out_mine = rows_of(w_out, core * quarter, quarter)
+    dctx = jnp.einsum("ed,std->set", w_out_mine, dy2, preferred_element_type=f32).astype(bf16)
     do_head = exchange(dctx.reshape(2 * heads, HD, rows))
 
-    mlp_t = mlp_in.T
     attn_t = attn_in.T
-    run = partial(mlp, ids, mlp_in, mlp_t, dy, w_up, wu_got, w_down, b_up.astype(f32)[None, :], n_ctx // 2)
-    y_mlp, d_mlp, u_send, v_send, gb_send = run(True)
-    u_got = flip(u_send, CORE)
-    v_got = flip(v_send, CORE)
-    y_mlp, d_mlp, u_keep, v_keep, gb_keep = run(False, (y_mlp, d_mlp))
-    gb_up = ordered(core, gb_keep, gb_send, axis=1)
+    y_mlp, d_mlp, g_up, g_down, gb_up = mlp(
+        ids, mlp_in, mlp_in.T, dy, w_up, wu_got, w_down, b_up.astype(f32)[None, :], chips
+    )
 
     chain_a = (X, ZN, ZF)
     chain_b = (ZN, ZF, X)
-    qkv_head, u_keep, v_keep, u_got, v_got = lax.optimization_barrier((qkv_head, u_keep, v_keep, u_got, v_got))
-    down = halve((v_keep, v_got), chain_a[0])
-    up = halve((u_keep, u_got), chain_b[0])
+    qkv_head, g_up, g_down = lax.optimization_barrier((qkv_head, g_up, g_down))
+    down = halve((g_down,), chain_a[0])
+    up = halve((g_up,), chain_b[0])
 
     o_head, lse = attn_fwd(block_map, qkv_head, bq=1024, bk=1024)
     qkv_head, o_head, do_head, down, up = lax.optimization_barrier((qkv_head, o_head, do_head, down, up))
-    ob = exchange(o_head).reshape(2, half, rows)
+    ob = exchange(o_head).reshape(2, quarter, rows)
     down = halve(down, chain_a[1])
     up = halve(up, chain_b[1])
     g_head = attn_bwd(block_map, qkv_head, o_head, do_head, lse, table)
@@ -1092,42 +1072,41 @@
     down = add(*halve(down, chain_a[2]))
     up = add(*halve(up, chain_b[2]))
     up = up.reshape(1, 2, up.shape[1] // 2, up.shape[2])
-    up_keep = lax.dynamic_slice_in_dim(up, me, 1, 1)
-    up_got = swap(lax.dynamic_slice_in_dim(up, 1 - me, 1, 1))
+    up_keep = rows_of(up, me, 1, 1)
+    up_got = swap(rows_of(up, 1 - me, 1, 1))
     up = ordered(me, up_keep, up_got, axis=1)
-    down = double(down, chain_a[2])
-    up = double(up, chain_b[2])
-    d_qkv, down, up = lax.optimization_barrier((d_qkv, down, up))
-    for a, b in zip(chain_a[1::-1], chain_b[1::-1]):
+    for a, b in zip(chain_a[::-1], chain_b[::-1]):
         down = double(down, a)
         up = double(up, b)
     tot_down = join_rows(ids, down, flip(down, CORE))
     tot_up = join_cols(ids, up, flip(up, CORE))
 
-    part = jnp.einsum("sct,cd->std", ob, w_out, preferred_element_type=f32) + y_mlp.reshape(
-        2, rows, width
-    )
-    y_got = swap(part[1].astype(bf16)).astype(f32)
-    output = (live_own * (x_own.astype(f32) + part[0] + y_got + bias_out)).astype(bf16)
-
-    a_keep, a_send, b_keep, b_send, e_own, e_send = qkv_backward(
-        ids, d_qkv, attn_t, x_own, x_got, norms, w_qkv, wq_got, d_mlp, ob, dy, gb_up, n_ctx // 2
-    )
-    v_a = (a_keep, flip(a_send, CORE))
-    v_b = (b_keep, flip(b_send, CORE))
+    def settle(v):
+        give = rows_of(v, (1 - core) * own_rows, own_rows, 1).astype(bf16)
+        v = rows_of(v, core * own_rows, own_rows, 1) + flip(give, CORE).astype(f32)
+        return v[0], swap(v[1].astype(bf16))
+
+    part = jnp.einsum("sct,cd->std", ob, w_out_mine, preferred_element_type=f32) + y_mlp.reshape(2, rows, width)
+    part, part_got = settle(part)
+    output = (live_own * (x_own.astype(f32) + part + part_got.astype(f32) + bias_out)).astype(bf16)
+
+    v_a, v_b, e = qkv_backward(
+        ids, d_qkv, attn_t, x2, norms, w_qkv, wq_got, d_mlp, ob, dy, gb_up, chips
+    )
+    v_a = (v_a,)
+    v_b = (v_b,)
     for a, b in zip(chain_a, chain_b):
         v_a = halve(v_a, a)
         v_b = halve(v_b, b)
-    e_got = swap(e_send)
-    n3 = 3 * half // (2 * n_ctx)
+    e_own, e_got = settle(e)
+    n3 = 3 * half // (2 * chips)
+    size = 2 * n3 + width // (2 * chips)
     mixed = []
     for v, chain in ((add(*v_a)[0], chain_a), (add(*v_b)[0], chain_b)):
-        extra = v[8 * n3 // 3 :]
-        keep = lax.dynamic_slice_in_dim(v, me * n3, n3, 0)
-        give = lax.dynamic_slice_in_dim(v, (1 - me) * n3, n3, 0)
-        back = swap(jnp.concatenate([give, extra]))
+        extra = v[size:]
+        back = swap(jnp.concatenate([rows_of(v, (1 - me) * n3, n3), extra]))
         extra = add(extra, back[n3:])
-        v = jnp.concatenate([ordered(me, keep, back[:n3]), v[2 * n3 : 8 * n3 // 3], extra])[None]
+        v = jnp.concatenate([ordered(me, rows_of(v, me * n3, n3), back[:n3]), v[2 * n3 : size], extra])[None]
         for a in chain[::-1]:
             v = double(v, a)
         mixed.append(v)
@@ -1135,8 +1114,8 @@
     mixed[0], mixed[1], grad_tokens, output, tot_down, tot_up = lax.optimization_barrier(
         (mixed[0], mixed[1], grad_tokens, output, tot_down, tot_up)
     )
-    tot_qkv, tot_out, flat = unpack(ids, mixed[0], flip(mixed[0], CORE), mixed[1], flip(mixed[1], CORE))
-    flat = flat[:, :2].reshape(2 * n_ctx * half)
+    tot_qkv, tot_out, flat = unpack(ids, mixed[0], flip(mixed[0], CORE), mixed[1], flip(mixed[1], CORE), width)
+    flat = flat[:, :6].reshape(12 * width)
 
     def own(start, size):
         return lax.dynamic_slice_in_dim(flat, start + me * size, size)
@@ -1151,10 +1130,10 @@
         own(3 * width, half),
         tot_qkv,
         own(5 * width, 3 * half),
-        tot_out,
+        tot_out.reshape(half, width),
         gb_out,
         tot_up,
-        own(8 * width, hid),
+        own(8 * width, 2 * hid),
         tot_down,
         gb_out,
     )

time: 445 us -> 424 us (0.953)
  waiting for transfers between devices: 156 us -> 144 us
  other arithmetic: 56.8 us -> 48.1 us
  local copies, waits for them, and re-layouts: 26.2 us -> 33.9 us
  Pallas kernels: 135 us -> 129 us
  starting transfers between devices: 65.7 us -> 59.7 us
    ppermute x35, waiting for transfers between devices: 135 us -> 116 us  [flip(): return lax.ppermute(v, 'ctx', [(i, i ^ 1 << bit) for i in range(n_ctx)])]
    convert_element_type x21 -> x18, other arithmetic: 27.8 us -> 13.4 us  [the longest x13 8.15 us: add(): sum((v.astype(f32) for v in terms)).astype(bf16)]
    ppermute x10, waiting for transfers between devices: 14.9 us -> 22.7 us  [swap(): return lax.ppermute(v, 'wsh', SWAP)]
    squeeze x0 -> x3, local copies, waits for them, and re-layouts: none -> 5.95 us  [the longest x2 4.86 us: part(): lax.dynamic_index_in_dim(v, k, 0, keepdims=False)]
    ppermute x10, starting transfers between devices: 14.8 us -> 10.3 us  [swap(): return lax.ppermute(v, 'wsh', SWAP)]
    pallas_call x4 -> x3, Pallas kernels: 85.3 us -> 80.9 us  [the longest x1 35 us: attn_bwd(): pl.pallas_call(lambda *a: attn_bwd_kernel(*a, nblk=nblk, per=x.shape[2] /...]
    select_n x20 -> x21, other arithmetic: 22.5 us -> 23 us  [ordered(): jnp.where(first == 0, jnp.concatenate([a, b], axis), jnp.concatenate([b,...]
  transfers between devices with their start and end apart: 49 -> 49, of which waited for: 19 -> 19; matrix products, arithmetic and copies ran while one was open for 16% -> 18% of each run, Pallas kernels for 24% -> 29%
where the time goes in v4:
time: 424 us; the launch traced here: 422 us
  waiting for transfers between devices  144 us (34%)
  Pallas kernels  129 us (30%)
  starting transfers between devices  59.7 us (14%)
  other arithmetic  48.1 us (11%)
  local copies, waits for them, and re-layouts  33.9 us (8%)
  matrix products  4.6 us (1%)
    ppermute x35, waiting for transfers between devices, flip(): return lax.ppermute(v, 'ctx', [(i, i ^ 1 << bit) for i in range(n_ctx)])  116 us
    pallas_call x1, Pallas kernels, attn_bwd(): pl.pallas_call(lambda *a: attn_bwd_kernel(*a, nblk=nblk, per=x.shape[2] /...  35 us
    ppermute x35, starting transfers between devices, flip(): return lax.ppermute(v, 'ctx', [(i, i ^ 1 << bit) for i in range(n_ctx)])  29.8 us
    pallas_call x1, Pallas kernels, mlp(): pl.pallas_call(mlp_kernel, grid_spec=pltpu.PrefetchScalarGridSpec(num_sca...  24.2 us
    select_n x21, other arithmetic, ordered(): jnp.where(first == 0, jnp.concatenate([a, b], axis), jnp.concatenate([b,...  23 us
    ppermute x10, waiting for transfers between devices, swap(): return lax.ppermute(v, 'wsh', SWAP)  22.7 us
    pallas_call x1, Pallas kernels, attn_fwd(): pl.pallas_call(lambda *a: attn_fwd_kernel(*a, nblk=nblk, per=x.shape[2] /...  21.7 us
    all_to_all x4, starting transfers between devices, exchange(): return lax.all_to_all(v, 'ctx', 0, 0, axis_index_groups=groups, tiled=False)  19.6 us
  transfers between devices with their start and end apart: 49, of which 19 were waited for; matrix products, arithmetic and copies ran while one was open for 18% of the time, Pallas kernels for 29%

profile of v4, /device:TPU:0, one launch (start us, length us, event | category | flops | bytes accessed | tf_op | source)
XLA Modules:
  0.0 421.7 jit_solution(5393074533999709594)
XLA Ops:
  0.7 3.0 collective-permute-start.1
  4.4 5.0 %concatenate.184 = bf16[4736]{0:T(1024)(128)(2,1)S(1)} concatenate(bf16[512]{0:T(512)(128)(2,1)} %param.17, bf16[512]{0:T(512)(128)(2,1)} %param.18, bf16[512]{0:T(512)(128)(2,1)} %param.19, bf16[512]{0:T(512)(128)(2,1)} %param.20, bf16[512]{0:T(512)(128)(2,1)} %param.24, bf16[512]{0:T(512)(128)(2,1)} %param.28, bf16[1536]{0:T(1024)(128)(2,1)} %param.22, bf16[1]{0:T(256)(128)(2,1)} %bitcast.4, ...), dimensions={0} | concatenate | bytes 18944 | tf_op jit(solution)/shard_map/concatenate | solution.py:1002
  11.6 1.9 collective-permute-start.4
  18.3 6.4 %collective-permute-done.4 = bf16[256,768]{1,0:T(8,128)(2,1)} collective-permute-done((bf16[256,768]{1,0:T(8,128)(2,1)S(1)}, bf16[256,768]{1,0:T(8,128)(2,1)}, u32[]{:S(2)}, u32[]{:S(2)}) %collective-permute-start.4) | collective-permute-done | bytes 393248 | tf_op jit(solution)/shard_map/ppermute | solution.py:968
  24.8 1.7 collective-permute-start.6
  33.1 1.7 maximum_select_fusion.3
  34.7 1.7 collective-permute-done.5
  36.4 2.2 maximum_select_fusion.10.gq_ref.gk_ref.gv_ref
  38.7 1.6 maximum_select_fusion.4
  41.8 10.3 %qkv_forward.1 = (bf16[2,4,192,512]{3,2,1,0:T(8,128)(2,1)}, bf16[1024,1024]{1,0:T(8,128)(2,1)}, bf16[1024,1024]{1,0:T(8,128)(2,1)}) custom-call(s32[2]{0:T(128)} %pad_add_fusion.ids, bf16[1024,1024]{1,0:T(8,128)(2,1)} %pad_maximum_fusion.x_ref, f32[4,1024]{1,0:T(4,128)} %maximum_convert_fusion.1.n_ref, bf16[512,3072]{1,0:T(8,128)(2,1)} %wv_ref.3, ...), custom_call_target="tpu_custom_call" | custom-call | flops 1048576 | bytes 1048576 | tf_op jit(solution)/shard_map/qkv_forward/pallas_call | solution.py:575
  54.1 5.7 %all-to-all-start = ((bf16[8,192,512]{2,1,0:T(8,128)(2,1)}), bf16[8,192,512]{2,1,0:T(8,128)(2,1)S(1)}, u32[]{:S(2)}, u32[]{:S(2)}) async-start(bf16[8,192,512]{2,1,0:T(8,128)(2,1)} %bitcast.184), calls=%async_computation | async-start | bytes 3145728 | tf_op jit(solution)/shard_map/all_to_all | solution.py:996
  60.4 4.6 %collective-permute-done.8 = bf16[256,1024]{1,0:T(8,128)(2,1)} collective-permute-done((bf16[256,1024]{1,0:T(8,128)(2,1)S(1)}, bf16[256,1024]{1,0:T(8,128)(2,1)}, u32[]{:S(2)}, u32[]{:S(2)}) %collective-permute-start.8) | collective-permute-done | bytes 524320 | tf_op jit(solution)/shard_map/ppermute | solution.py:968
  65.8 2.6 maximum_select_fusion.5
  68.4 3.9 copy.33
  72.3 2.0 maximum_select_fusion.6
  74.3 2.4 maximum_convert_fusion
  76.8 1.8 multiply_convert_fusion.1.dy_ref
  78.5 24.2 %mlp.1 = (f32[1024,1024]{1,0:T(8,128)}, f32[1024,1024]{1,0:T(8,128)}, bf16[8,128,1024]{2,1,0:T(8,128)(2,1)}, bf16[8,128,1024]{2,1,0:T(8,128)(2,1)}, f32[1,1024]{1,0:T(1,128)}) custom-call(s32[2]{0:T(128)} %pad_add_fusion.ids, bf16[1024,1024]{1,0:T(8,128)(2,1)} %get-tuple-element.61.x_ref, bf16[1024,1024]{1,0:T(8,128)(2,1)} %bitcast.178, ...), custom_call_target="tpu_custom_call" | custom-call | flops 12884901888 | bytes 25165824 | tf_op jit(solution)/shard_map/mlp/pallas_call | solution.py:642
  102.7 3.7 dynamic-slice_bitcast_fusion.2
  108.2 1.6 collective-permute-start.11
  109.7 1.7 fusion.2
  111.4 5.7 %all-to-all-start.1 = ((bf16[8,64,512]{2,1,0:T(8,128)(2,1)}), bf16[8,64,512]{2,1,0:T(8,128)(2,1)S(1)}, u32[]{:S(2)}, u32[]{:S(2)}) async-start(bf16[8,64,512]{2,1,0:T(8,128)(2,1)} %bitcast.17), calls=%async_computation.1 | async-start | bytes 1048576 | tf_op jit(solution)/shard_map/all_to_all | solution.py:996
  117.1 21.7 %attn_fwd.1 = (bf16[8,64,512]{2,1,0:T(8,128)(2,1)}, f32[1,4096]{1,0:T(1,128)}) custom-call(s32[32]{0:T(128)} %a_0_.3, bf16[8,192,512]{2,1,0:T(8,128)(2,1)} %copy-done.3), custom_call_target="tpu_custom_call" | custom-call | tf_op jit(solution)/shard_map/attn_fwd/pallas_call | solution.py:438
  138.8 5.6 %all-to-all-done.1.a_3_ = bf16[8,64,512]{2,1,0:T(8,128)(2,1)S(1)} async-done(((bf16[8,64,512]{2,1,0:T(8,128)(2,1)}), bf16[8,64,512]{2,1,0:T(8,128)(2,1)S(1)}, u32[]{:S(2)}, u32[]{:S(2)}) %all-to-all-start.1) | async-done | bytes 524320 | tf_op jit(solution)/shard_map/all_to_all | solution.py:996
  144.3 3.6 all-to-all-start.2
  147.9 3.0 fusion.9
  150.9 2.0 collective-permute-start.12
  152.9 2.4 fusion.11
  155.3 2.4 collective-permute-start.13
  158.9 35.0 %attn_bwd.1 = bf16[8,192,512]{2,1,0:T(8,128)(2,1)} custom-call(s32[32]{0:T(128)} %a_0_.3, bf16[8,192,512]{2,1,0:T(8,128)(2,1)} %copy-done.3, bf16[8,64,512]{2,1,0:T(8,128)(2,1)} %get-tuple-element.71.a_2_, bf16[8,64,512]{2,1,0:T(8,128)(2,1)} %copy-done.15, f32[1,4096]{1,0:T(1,128)} %get-tuple-element.73.a_4_, f32[16,4096]{1,0:T(8,128)} %pad_maximum_fusion.2.a_5_), custom_call_target="tpu_custom_call" | custom-call | tf_op jit(solution)/shard_map/attn_bwd/pallas_call | solution.py:498
  194.0 4.7 %all-to-all-start.3 = ((bf16[8,192,512]{2,1,0:T(8,128)(2,1)}), bf16[8,192,512]{2,1,0:T(8,128)(2,1)}, u32[]{:S(2)}, u32[]{:S(2)}) async-start(bf16[8,192,512]{2,1,0:T(8,128)(2,1)} %attn_bwd.1), calls=%async_computation.3 | async-start | bytes 3145728 | tf_op jit(solution)/shard_map/all_to_all | solution.py:996
  199.7 2.6 collective-permute-start.32
  204.0 2.9 convolution_add_fusion
  206.9 38.1 %collective-permute-done.32 = bf16[1,128,1024]{2,1,0:T(8,128)(2,1)S(1)} collective-permute-done((bf16[1,128,1024]{2,1,0:T(8,128)(2,1)S(1)}, bf16[1,128,1024]{2,1,0:T(8,128)(2,1)S(1)}, u32[]{:S(2)}, u32[]{:S(2)}) %collective-permute-start.32) | collective-permute-done | bytes 262176 | tf_op jit(solution)/shard_map/ppermute | solution.py:971
  247.2 4.2 collective-permute-done.38
  252.9 5.2 %collective-permute-done.33 = bf16[1,128,1024]{2,1,0:T(8,128)(2,1)S(1)} collective-permute-done((bf16[1,128,1024]{2,1,0:T(8,128)(2,1)S(1)}, bf16[1,128,1024]{2,1,0:T(8,128)(2,1)S(1)}, u32[]{:S(2)}, u32[]{:S(2)}) %collective-permute-start.33) | collective-permute-done | bytes 262176 | tf_op jit(solution)/shard_map/ppermute | solution.py:971
  258.4 2.5 collective-permute-start.40
  260.9 20.2 %collective-permute-done.34 = bf16[2,128,1024]{2,1,0:T(8,128)(2,1)} collective-permute-done((bf16[2,128,1024]{2,1,0:T(8,128)(2,1)S(1)}, bf16[2,128,1024]{2,1,0:T(8,128)(2,1)}, u32[]{:S(2)}, u32[]{:S(2)}) %collective-permute-start.34) | collective-permute-done | bytes 524320 | tf_op jit(solution)/shard_map/ppermute | solution.py:971
  281.1 2.4 maximum_select_fusion.8
  283.5 4.0 collective-permute-start.35
  289.1 3.9 copy.34
  293.3 2.2 convert_add_fusion
  295.5 14.0 %qkv_backward.1 = (bf16[8,256,256]{2,1,0:T(8,128)(2,1)}, bf16[8,264,256]{2,1,0:T(8,128)(2,1)}, f32[2,512,1024]{2,1,0:T(8,128)}) custom-call(s32[2]{0:T(128)} %pad_add_fusion.ids, bf16[2,4,192,512]{3,2,1,0:T(8,128)(2,1)} %bitcast.33.d_ref, bf16[1024,1024]{1,0:T(8,128)(2,1)} %bitcast.165, bf16[1024,1024]{1,0:T(8,128)(2,1)} %pad_maximum_fusion.x_ref, ...), custom_call_target="tpu_custom_call" | custom-call | tf_op jit(solution)/shard_map/qkv_backward/pallas_call | solution.py:778
  311.2 2.1 collective-permute-start.21
  313.9 2.6 maximum_select_fusion.own_ref
  316.6 7.1 %collective-permute-done.14 = bf16[4,256,256]{2,1,0:T(8,128)(2,1)S(1)} collective-permute-done((bf16[4,256,256]{2,1,0:T(8,128)(2,1)S(1)}, bf16[4,256,256]{2,1,0:T(8,128)(2,1)S(1)}, u32[]{:S(2)}, u32[]{:S(2)}) %collective-permute-start.14) | collective-permute-done | bytes 524320 | tf_op jit(solution)/shard_map/ppermute | solution.py:971
  323.9 1.8 collective-permute-start.15
  325.6 8.2 %collective-permute-done.21 = bf16[4,264,256]{2,1,0:T(8,128)(2,1)S(1)} collective-permute-done((bf16[4,264,256]{2,1,0:T(8,128)(2,1)S(1)}, bf16[4,264,256]{2,1,0:T(8,128)(2,1)S(1)}, u32[]{:S(2)}, u32[]{:S(2)}) %collective-permute-start.21) | collective-permute-done | bytes 540704 | tf_op jit(solution)/shard_map/ppermute | solution.py:971
  334.1 2.0 maximum_select_fusion.1.own_ref
  337.3 1.8 collective-permute-start.16
  339.2 8.7 %collective-permute-done.22 = bf16[2,264,256]{2,1,0:T(8,128)(2,1)S(1)} collective-permute-done((bf16[2,264,256]{2,1,0:T(8,128)(2,1)S(1)}, bf16[2,264,256]{2,1,0:T(8,128)(2,1)S(1)}, u32[]{:S(2)}, u32[]{:S(2)}) %collective-permute-start.22) | collective-permute-done | bytes 270368 | tf_op jit(solution)/shard_map/ppermute | solution.py:971
  349.5 4.9 %collective-permute-done.23 = bf16[1,264,256]{2,1,0:T(8,128)(2,1)S(1)} collective-permute-done((bf16[1,264,256]{2,1,0:T(8,128)(2,1)S(1)}, bf16[1,264,256]{2,1,0:T(8,128)(2,1)S(1)}, u32[]{:S(2)}, u32[]{:S(2)}) %collective-permute-start.23) | collective-permute-done | bytes 135200 | tf_op jit(solution)/shard_map/ppermute | solution.py:971
  355.0 3.9 collective-permute-done.17
  359.5 3.6 collective-permute-done.24
  363.6 6.8 %collective-permute-done.18 = bf16[1,256,256]{2,1,0:T(8,128)(2,1)S(1)} collective-permute-done((bf16[1,256,256]{2,1,0:T(8,128)(2,1)S(1)}, bf16[1,256,256]{2,1,0:T(8,128)(2,1)S(1)}, u32[]{:S(2)}, u32[]{:S(2)}) %collective-permute-start.18) | collective-permute-done | bytes 131104 | tf_op jit(solution)/shard_map/ppermute | solution.py:971
  370.5 2.6 collective-permute-start.26
  374.0 8.5 %collective-permute-done.19 = bf16[2,256,256]{2,1,0:T(8,128)(2,1)S(1)} collective-permute-done((bf16[2,256,256]{2,1,0:T(8,128)(2,1)S(1)}, bf16[2,256,256]{2,1,0:T(8,128)(2,1)S(1)}, u32[]{:S(2)}, u32[]{:S(2)}) %collective-permute-start.19) | collective-permute-done | bytes 262176 | tf_op jit(solution)/shard_map/ppermute | solution.py:971
  386.2 7.0 %join_rows.1 = f32[2048,1024]{1,0:T(8,128)} custom-call(s32[2]{0:T(128)} %pad_add_fusion.ids, bf16[8,128,1024]{2,1,0:T(8,128)(2,1)} %copy-done.6, bf16[8,128,1024]{2,1,0:T(8,128)(2,1)} %collective-permute-done.36.got_ref), custom_call_target="tpu_custom_call" | custom-call | tf_op jit(solution)/shard_map/join_rows/pallas_call | solution.py:833
  393.3 7.1 %join_cols.1 = f32[512,4096]{1,0:T(8,128)} custom-call(s32[2]{0:T(128)} %pad_add_fusion.ids, bf16[8,2,64,1024]{3,2,1,0:T(8,128)(2,1)} %copy-done.7, bf16[8,2,64,1024]{3,2,1,0:T(8,128)(2,1)} %collective-permute-done.42.got_ref), custom_call_target="tpu_custom_call" | custom-call | tf_op jit(solution)/shard_map/join_cols/pallas_call | solution.py:850
  400.4 3.4 token_grad.1
  403.8 1.7 maximum_select_fusion.7.ao_ref
  405.6 1.8 maximum_select_fusion.2.bo_ref
  407.9 3.8 collective-permute-done.43.ag_ref
  411.7 6.6 %unpack.1 = (f32[512,3072]{1,0:T(8,128)}, f32[2,256,1024]{2,1,0:T(8,128)}, f32[8,8,256]{2,1,0:T(8,128)}) custom-call(s32[2]{0:T(128)} %pad_add_fusion.ids, bf16[8,256,256]{2,1,0:T(8,128)(2,1)} %copy-done.12, bf16[8,256,256]{2,1,0:T(8,128)(2,1)} %collective-permute-done.43.ag_ref, bf16[8,264,256]{2,1,0:T(8,128)(2,1)} %copy-done.11, ...), custom_call_target="tpu_custom_call" | custom-call | tf_op jit(solution)/shard_map/unpack/pallas_call | solution.py:894
  (201 shorter events, 45.6 us)
Async XLA Ops:
  0.6 109.1 %copy-start = (bf16[512,1024]{1,0:T(8,128)(2,1)S(1)}, bf16[512,1024]{1,0:T(8,128)(2,1)}, u32[]{:S(2)}) copy-start(bf16[512,1024]{1,0:T(8,128)(2,1)} %param.23) | copy-start | bytes 3145732
  0.7 27.3 %collective-permute-start.1 = (bf16[256,1024]{1,0:T(8,128)(2,1)}, bf16[256,1024]{1,0:T(8,128)(2,1)S(1)}, u32[]{:S(2)}, u32[]{:S(2)}) collective-permute-start(bf16[256,1024]{1,0:T(8,128)(2,1)} %bitcast.168), channel_id=1, source_target_pairs={{0,1},{1,0},{2,3},{3,2},{4,5},{5,4},{6,7},{7,6},{8,9},{9,8},{10,11... | collective-permute-start | bytes 1572872 | tf_op jit(solution)/shard_map/ppermute | solution.py:968
  3.7 29.4 %collective-permute-start = (bf16[256,1024]{1,0:T(8,128)(2,1)}, bf16[256,1024]{1,0:T(8,128)(2,1)}, u32[]{:S(2)}, u32[]{:S(2)}) collective-permute-start(bf16[256,1024]{1,0:T(8,128)(2,1)} %bitcast.169), channel_id=1, source_target_pairs={{0,2},{2,0},{4,6},{6,4},{8,10},{10,8},{12,14},{14,12},{16,18},{18,... | collective-permute-start | bytes 1572872 | tf_op jit(solution)/shard_map/ppermute | solution.py:971
  4.4 28.7 %copy-start.9 = (bf16[1,256,1024]{2,1,0:T(8,128)(2,1)S(1)}, bf16[1,256,1024]{2,1,0:T(8,128)(2,1)}, u32[]{:S(2)}) copy-start(bf16[1,256,1024]{2,1,0:T(8,128)(2,1)} %param.16) | copy-start | bytes 1572868
  10.0 7.4 %collective-permute-start.3 = (bf16[1,4736]{1,0:T(2,128)(2,1)}, bf16[1,4736]{1,0:T(2,128)(2,1)}, u32[]{:S(2)}, u32[]{:S(2)}) collective-permute-start(bf16[1,4736]{1,0:T(2,128)(2,1)} %broadcast_in_dim.32), channel_id=1, source_target_pairs={{0,1},{1,0},{2,3},{3,2},{4,5},{5,4},{6,7},{7,6},{8,9},{9,8},{10,11... | collective-permute-start | bytes 28424 | tf_op jit(solution)/shard_map/ppermute | solution.py:968
  11.6 13.2 %collective-permute-start.4 = (bf16[256,768]{1,0:T(8,128)(2,1)S(1)}, bf16[256,768]{1,0:T(8,128)(2,1)}, u32[]{:S(2)}, u32[]{:S(2)}) collective-permute-start(bf16[256,768]{1,0:T(8,128)(2,1)S(1)} %pad_maximum_fusion.1), channel_id=1, source_target_pairs={{0,1},{1,0},{2,3},{3,2},{4,5},{5,4},{6,7},{7,6},{8,9},{9,8},{10,11... | collective-permute-start | bytes 1179656 | tf_op jit(solution)/shard_map/ppermute | solution.py:968
  13.5 11.2 %copy-start.22 = (f32[8]{0:T(128)}, f32[8]{0:T(128)S(1)}, u32[]{:S(2)}) copy-start(f32[8]{0:T(128)S(1)} %multiply_power_fusion) | copy-start | bytes 100
  18.3 9.7 %copy-start.19 = (bf16[2,4736]{1,0:T(2,128)(2,1)}, bf16[2,4736]{1,0:T(2,128)(2,1)S(1)}, u32[]{:S(2)}) copy-start(bf16[2,4736]{1,0:T(2,128)(2,1)S(1)} %broadcast_select_fusion) | copy-start | bytes 56836
  24.8 27.3 %collective-permute-start.6 = (bf16[512,1024]{1,0:T(8,128)(2,1)S(1)}, bf16[512,1024]{1,0:T(8,128)(2,1)}, u32[]{:S(2)}, u32[]{:S(2)}) collective-permute-start(bf16[512,1024]{1,0:T(8,128)(2,1)S(1)} %constant_dynamic-slice_fusion.6), channel_id=1, source_target_pairs={{0,1},{1,0},{2,3},{3,2},{4,5},{5,4},{6,7},{7,6},{8,9},{9,8},{10,11... | collective-permute-start | bytes 3145736 | tf_op jit(solution)/shard_map/ppermute | solution.py:968
  26.5 9.9 %collective-permute-start.5 = (bf16[256,768]{1,0:T(8,128)(2,1)}, bf16[256,768]{1,0:T(8,128)(2,1)S(1)}, u32[]{:S(2)}, u32[]{:S(2)}) collective-permute-start(bf16[256,768]{1,0:T(8,128)(2,1)} %collective-permute-done.4), channel_id=1, source_target_pairs={{0,4},{2,6},{4,0},{6,2},{8,12},{10,14},{12,8},{14,10},{16,20},{18,... | collective-permute-start | bytes 1179656 | tf_op jit(solution)/shard_map/ppermute | solution.py:971
  28.0 10.7 %collective-permute-start.2 = (bf16[256,1024]{1,0:T(8,128)(2,1)S(1)}, bf16[256,1024]{1,0:T(8,128)(2,1)}, u32[]{:S(2)}, u32[]{:S(2)}) collective-permute-start(bf16[256,1024]{1,0:T(8,128)(2,1)S(1)} %collective-permute-done.1), channel_id=1, source_target_pairs={{0,2},{2,0},{4,6},{6,4},{8,10},{10,8},{12,14},{14,12},{16,18},{18,... | collective-permute-start | bytes 1572872 | tf_op jit(solution)/shard_map/ppermute | solution.py:971
  41.8 10.3 %copy-start.16 = (bf16[1,256,1024]{2,1,0:T(8,128)(2,1)S(1)}, bf16[1,256,1024]{2,1,0:T(8,128)(2,1)}, u32[]{:S(2)}) copy-start(bf16[1,256,1024]{2,1,0:T(8,128)(2,1)} %param.31) | copy-start | bytes 1572868
  41.8 11.0 %copy-start.21 = (bf16[2048]{0:T(1024)(128)(2,1)S(1)}, bf16[2048]{0:T(1024)(128)(2,1)}, u32[]{:S(2)}) copy-start(bf16[2048]{0:T(1024)(128)(2,1)} %param.26) | copy-start | bytes 12292
  52.1 12.9 %copy-start.25 = (s32[4]{0:T(128)S(1)}, s32[4]{0:T(128)}, u32[]{:S(2)}) copy-start(s32[4]{0:T(128)} %copy-done.24) | copy-start | bytes 52
  52.1 12.8 %collective-permute-start.8 = (bf16[256,1024]{1,0:T(8,128)(2,1)S(1)}, bf16[256,1024]{1,0:T(8,128)(2,1)}, u32[]{:S(2)}, u32[]{:S(2)}) collective-permute-start(bf16[256,1024]{1,0:T(8,128)(2,1)S(1)} %bitcast.180), channel_id=1, source_target_pairs={{0,1},{1,0},{2,3},{3,2},{4,5},{5,4},{6,7},{7,6},{8,9},{9,8},{10,11... | collective-permute-start | bytes 1572872 | tf_op jit(solution)/shard_map/ppermute | solution.py:968
  52.8 13.0 %collective-permute-start.7 = (bf16[256,1024]{1,0:T(8,128)(2,1)S(1)}, bf16[256,1024]{1,0:T(8,128)(2,1)}, u32[]{:S(2)}, u32[]{:S(2)}) collective-permute-start(bf16[256,1024]{1,0:T(8,128)(2,1)S(1)} %bitcast.181), channel_id=1, source_target_pairs={{0,2},{2,0},{4,6},{6,4},{8,10},{10,8},{12,14},{14,12},{16,18},{18,... | collective-permute-start | bytes 1572872 | tf_op jit(solution)/shard_map/ppermute | solution.py:971
  54.1 48.6 %all-to-all-start = ((bf16[8,192,512]{2,1,0:T(8,128)(2,1)}), bf16[8,192,512]{2,1,0:T(8,128)(2,1)S(1)}, u32[]{:S(2)}, u32[]{:S(2)}) async-start(bf16[8,192,512]{2,1,0:T(8,128)(2,1)} %bitcast.184), calls=%async_computation | async-start | bytes 3145728 | tf_op jit(solution)/shard_map/all_to_all | solution.py:996
  65.0 7.3 %collective-permute-start.9 = (bf16[256,1024]{1,0:T(8,128)(2,1)}, bf16[256,1024]{1,0:T(8,128)(2,1)}, u32[]{:S(2)}, u32[]{:S(2)}) collective-permute-start(bf16[256,1024]{1,0:T(8,128)(2,1)} %collective-permute-done.8), channel_id=1, source_target_pairs={{0,2},{2,0},{4,6},{6,4},{8,10},{10,8},{12,14},{14,12},{16,18},{18,... | collective-permute-start | bytes 1572872 | tf_op jit(solution)/shard_map/ppermute | solution.py:971
  106.5 37.9 %collective-permute-start.10 = (bf16[4,128,1024]{2,1,0:T(8,128)(2,1)}, bf16[4,128,1024]{2,1,0:T(8,128)(2,1)}, u32[]{:S(2)}, u32[]{:S(2)}) collective-permute-start(bf16[4,128,1024]{2,1,0:T(8,128)(2,1)} %get-tuple-element.109), channel_id=1, source_target_pairs={{0,4},{2,6},{4,0},{6,2},{8,12},{10,14},{12,8},{14,10},{16,20},{18,... | collective-permute-start | bytes 3145736 | tf_op jit(solution)/shard_map/ppermute | solution.py:971
  108.2 36.2 %collective-permute-start.11 = (bf16[4,128,1024]{2,1,0:T(8,128)(2,1)}, bf16[4,128,1024]{2,1,0:T(8,128)(2,1)}, u32[]{:S(2)}, u32[]{:S(2)}) collective-permute-start(bf16[4,128,1024]{2,1,0:T(8,128)(2,1)} %get-tuple-element.107), channel_id=1, source_target_pairs={{0,8},{2,10},{4,12},{6,14},{8,0},{10,2},{12,4},{14,6},{16,24},{18,... | collective-permute-start | bytes 3145736 | tf_op jit(solution)/shard_map/ppermute | solution.py:971
  111.4 32.9 %all-to-all-start.1 = ((bf16[8,64,512]{2,1,0:T(8,128)(2,1)}), bf16[8,64,512]{2,1,0:T(8,128)(2,1)S(1)}, u32[]{:S(2)}, u32[]{:S(2)}) async-start(bf16[8,64,512]{2,1,0:T(8,128)(2,1)} %bitcast.17), calls=%async_computation.1 | async-start | bytes 1048576 | tf_op jit(solution)/shard_map/all_to_all | solution.py:996
  144.3 6.6 %copy-start.15 = (bf16[8,64,512]{2,1,0:T(8,128)(2,1)}, bf16[8,64,512]{2,1,0:T(8,128)(2,1)S(1)}, u32[]{:S(2)}) copy-start(bf16[8,64,512]{2,1,0:T(8,128)(2,1)S(1)} %all-to-all-done.1.a_3_) | copy-start | bytes 1572868
  144.3 49.7 %all-to-all-start.2 = ((bf16[8,64,512]{2,1,0:T(8,128)(2,1)}), bf16[8,64,512]{2,1,0:T(8,128)(2,1)S(1)}, u32[]{:S(2)}, u32[]{:S(2)}) async-start(bf16[8,64,512]{2,1,0:T(8,128)(2,1)} %get-tuple-element.71.a_2_), calls=%async_computation.2 | async-start | bytes 1048576 | tf_op jit(solution)/shard_map/all_to_all | solution.py:996
  150.9 6.8 %copy-start.23 = (f32[8]{0:T(128)S(1)}, f32[8]{0:T(128)}, u32[]{:S(2)}) copy-start(f32[8]{0:T(128)} %copy-done.22) | copy-start | bytes 100
  150.9 43.1 %collective-permute-start.12 = (bf16[2,128,1024]{2,1,0:T(8,128)(2,1)}, bf16[2,128,1024]{2,1,0:T(8,128)(2,1)}, u32[]{:S(2)}, u32[]{:S(2)}) collective-permute-start(bf16[2,128,1024]{2,1,0:T(8,128)(2,1)} %get-tuple-element.105), channel_id=1, source_target_pairs={{0,8},{2,10},{4,12},{6,14},{8,0},{10,2},{12,4},{14,6},{16,24},{18,... | collective-permute-start | bytes 1572872 | tf_op jit(solution)/shard_map/ppermute | solution.py:971
  155.3 38.7 %collective-permute-start.13 = (bf16[2,128,1024]{2,1,0:T(8,128)(2,1)}, bf16[2,128,1024]{2,1,0:T(8,128)(2,1)S(1)}, u32[]{:S(2)}, u32[]{:S(2)}) collective-permute-start(bf16[2,128,1024]{2,1,0:T(8,128)(2,1)} %get-tuple-element.103), channel_id=1, source_target_pairs={{0,16},{2,18},{4,20},{6,22},{8,24},{10,26},{12,28},{14,30},{16,0},... | collective-permute-start | bytes 1572872 | tf_op jit(solution)/shard_map/ppermute | solution.py:971
  194.0 10.0 %copy-start.8 = (bf16[8,64,512]{2,1,0:T(8,128)(2,1)}, bf16[8,64,512]{2,1,0:T(8,128)(2,1)S(1)}, u32[]{:S(2)}) copy-start(bf16[8,64,512]{2,1,0:T(8,128)(2,1)S(1)} %all-to-all-done.2) | copy-start | bytes 1572868
  194.0 101.5 %all-to-all-start.3 = ((bf16[8,192,512]{2,1,0:T(8,128)(2,1)}), bf16[8,192,512]{2,1,0:T(8,128)(2,1)}, u32[]{:S(2)}, u32[]{:S(2)}) async-start(bf16[8,192,512]{2,1,0:T(8,128)(2,1)} %attn_bwd.1), calls=%async_computation.3 | async-start | bytes 3145728 | tf_op jit(solution)/shard_map/all_to_all | solution.py:996
  199.7 45.3 %collective-permute-start.32 = (bf16[1,128,1024]{2,1,0:T(8,128)(2,1)S(1)}, bf16[1,128,1024]{2,1,0:T(8,128)(2,1)S(1)}, u32[]{:S(2)}, u32[]{:S(2)}) collective-permute-start(bf16[1,128,1024]{2,1,0:T(8,128)(2,1)S(1)} %add_convert_fusion.10), channel_id=1, source_target_pairs={{0,16},{2,18},{4,20},{6,22},{8,24},{10,26},{12,28},{14,30},{16,0},... | collective-permute-start | bytes 786440 | tf_op jit(solution)/shard_map/ppermute | solution.py:971
  202.4 43.7 %collective-permute-start.37 = (bf16[1,128,1024]{2,1,0:T(8,128)(2,1)S(1)}, bf16[1,128,1024]{2,1,0:T(8,128)(2,1)S(1)}, u32[]{:S(2)}, u32[]{:S(2)}) collective-permute-start(bf16[1,128,1024]{2,1,0:T(8,128)(2,1)S(1)} %add_convert_fusion.7), channel_id=1, source_target_pairs={{0,4},{2,6},{4,0},{6,2},{8,12},{10,14},{12,8},{14,10},{16,20},{18,... | collective-permute-start | bytes 786440 | tf_op jit(solution)/shard_map/ppermute | solution.py:971
  206.9 40.2 %copy-start.4 = (f32[2,512,1024]{2,1,0:T(8,128)}, f32[2,512,1024]{2,1,0:T(8,128)S(1)}, u32[]{:S(2)}) copy-start(f32[2,512,1024]{2,1,0:T(8,128)S(1)} %convolution_add_fusion) | copy-start | bytes 12582916
  246.1 12.0 %collective-permute-start.33 = (bf16[1,128,1024]{2,1,0:T(8,128)(2,1)S(1)}, bf16[1,128,1024]{2,1,0:T(8,128)(2,1)S(1)}, u32[]{:S(2)}, u32[]{:S(2)}) collective-permute-start(bf16[1,128,1024]{2,1,0:T(8,128)(2,1)S(1)} %add_convert_fusion.9), channel_id=1, source_target_pairs={{0,16},{2,18},{4,20},{6,22},{8,24},{10,26},{12,28},{14,30},{16,0},... | collective-permute-start | bytes 786440 | tf_op jit(solution)/shard_map/ppermute | solution.py:971
  246.3 5.0 %collective-permute-start.38 = (bf16[1,1,64,1024]{3,2,1,0:T(8,128)(2,1)S(1)}, bf16[1,1,64,1024]{3,2,1,0:T(8,128)(2,1)S(1)}, u32[]{:S(2)}, u32[]{:S(2)}) collective-permute-start(bf16[1,1,64,1024]{3,2,1,0:T(8,128)(2,1)S(1)} %get-tuple-element.120), channel_id=1, source_target_pairs={{0,1},{1,0},{2,3},{3,2},{4,5},{5,4},{6,7},{7,6},{8,9},{9,8},{10,11... | collective-permute-start | bytes 393224 | tf_op jit(solution)/shard_map/ppermute | solution.py:968
  247.1 46.1 %collective-permute-start.30 = (bf16[2,256,1024]{2,1,0:T(8,128)(2,1)S(1)}, bf16[2,256,1024]{2,1,0:T(8,128)(2,1)}, u32[]{:S(2)}, u32[]{:S(2)}) collective-permute-start(bf16[2,256,1024]{2,1,0:T(8,128)(2,1)S(1)} %dynamic-slice_convert_fusion), channel_id=1, source_target_pairs={{0,2},{2,0},{4,6},{6,4},{8,10},{10,8},{12,14},{14,12},{16,18},{18,... | collective-permute-start | bytes 3145736 | tf_op jit(solution)/shard_map/ppermute | solution.py:971
  251.4 6.8 %collective-permute-start.39 = (bf16[1,2,64,1024]{3,2,1,0:T(8,128)(2,1)S(1)}, bf16[1,2,64,1024]{3,2,1,0:T(8,128)(2,1)S(1)}, u32[]{:S(2)}, u32[]{:S(2)}) collective-permute-start(bf16[1,2,64,1024]{3,2,1,0:T(8,128)(2,1)S(1)} %maximum_select_fusion.17), channel_id=1, source_target_pairs={{0,4},{2,6},{4,0},{6,2},{8,12},{10,14},{12,8},{14,10},{16,20},{18,... | collective-permute-start | bytes 786440 | tf_op jit(solution)/shard_map/ppermute | solution.py:971
  258.2 22.9 %collective-permute-start.34 = (bf16[2,128,1024]{2,1,0:T(8,128)(2,1)S(1)}, bf16[2,128,1024]{2,1,0:T(8,128)(2,1)}, u32[]{:S(2)}, u32[]{:S(2)}) collective-permute-start(bf16[2,128,1024]{2,1,0:T(8,128)(2,1)S(1)} %maximum_select_fusion.13), channel_id=1, source_target_pairs={{0,8},{2,10},{4,12},{6,14},{8,0},{10,2},{12,4},{14,6},{16,24},{18,... | collective-permute-start | bytes 1572872 | tf_op jit(solution)/shard_map/ppermute | solution.py:971
  258.4 34.7 %collective-permute-start.40 = (bf16[2,2,64,1024]{3,2,1,0:T(8,128)(2,1)S(1)}, bf16[2,2,64,1024]{3,2,1,0:T(8,128)(2,1)S(1)}, u32[]{:S(2)}, u32[]{:S(2)}) collective-permute-start(bf16[2,2,64,1024]{3,2,1,0:T(8,128)(2,1)S(1)} %maximum_select_fusion.14), channel_id=1, source_target_pairs={{0,16},{2,18},{4,20},{6,22},{8,24},{10,26},{12,28},{14,30},{16,0},... | collective-permute-start | bytes 1572872 | tf_op jit(solution)/shard_map/ppermute | solution.py:971
  283.5 30.4 %collective-permute-start.35 = (bf16[4,128,1024]{2,1,0:T(8,128)(2,1)}, bf16[4,128,1024]{2,1,0:T(8,128)(2,1)}, u32[]{:S(2)}, u32[]{:S(2)}) collective-permute-start(bf16[4,128,1024]{2,1,0:T(8,128)(2,1)} %maximum_select_fusion.8), channel_id=1, source_target_pairs={{0,4},{2,6},{4,0},{6,2},{8,12},{10,14},{12,8},{14,10},{16,20},{18,... | collective-permute-start | bytes 3145736 | tf_op jit(solution)/shard_map/ppermute | solution.py:971
  293.2 40.9 %collective-permute-start.41 = (bf16[4,2,64,1024]{3,2,1,0:T(8,128)(2,1)S(1)}, bf16[4,2,64,1024]{3,2,1,0:T(8,128)(2,1)}, u32[]{:S(2)}, u32[]{:S(2)}) collective-permute-start(bf16[4,2,64,1024]{3,2,1,0:T(8,128)(2,1)S(1)} %maximum_select_fusion.9), channel_id=1, source_target_pairs={{0,8},{2,10},{4,12},{6,14},{8,0},{10,2},{12,4},{14,6},{16,24},{18,... | collective-permute-start | bytes 3145736 | tf_op jit(solution)/shard_map/ppermute | solution.py:971
  310.9 12.8 %collective-permute-start.14 = (bf16[4,256,256]{2,1,0:T(8,128)(2,1)S(1)}, bf16[4,256,256]{2,1,0:T(8,128)(2,1)S(1)}, u32[]{:S(2)}, u32[]{:S(2)}) collective-permute-start(bf16[4,256,256]{2,1,0:T(8,128)(2,1)S(1)} %get-tuple-element.118), channel_id=1, source_target_pairs={{0,4},{2,6},{4,0},{6,2},{8,12},{10,14},{12,8},{14,10},{16,20},{18,... | collective-permute-start | bytes 1572872 | tf_op jit(solution)/shard_map/ppermute | solution.py:971
  311.2 22.6 %collective-permute-start.21 = (bf16[4,264,256]{2,1,0:T(8,128)(2,1)S(1)}, bf16[4,264,256]{2,1,0:T(8,128)(2,1)S(1)}, u32[]{:S(2)}, u32[]{:S(2)}) collective-permute-start(bf16[4,264,256]{2,1,0:T(8,128)(2,1)S(1)} %get-tuple-element.114), channel_id=1, source_target_pairs={{0,8},{2,10},{4,12},{6,14},{8,0},{10,2},{12,4},{14,6},{16,24},{18,... | collective-permute-start | bytes 1622024 | tf_op jit(solution)/shard_map/ppermute | solution.py:971
  313.3 70.7 %collective-permute-start.31 = (bf16[256,1024]{1,0:T(8,128)(2,1)S(1)}, bf16[256,1024]{1,0:T(8,128)(2,1)S(1)}, u32[]{:S(2)}, u32[]{:S(2)}) collective-permute-start(bf16[256,1024]{1,0:T(8,128)(2,1)S(1)} %fusion.13), channel_id=1, source_target_pairs={{0,1},{1,0},{2,3},{3,2},{4,5},{5,4},{6,7},{7,6},{8,9},{9,8},{10,11... | collective-permute-start | bytes 1572872 | tf_op jit(solution)/shard_map/ppermute | solution.py:968
  316.5 19.6 %copy-start.6 = (bf16[8,128,1024]{2,1,0:T(8,128)(2,1)}, bf16[8,128,1024]{2,1,0:T(8,128)(2,1)S(1)}, u32[]{:S(2)}) copy-start(bf16[8,128,1024]{2,1,0:T(8,128)(2,1)S(1)} %maximum_select_fusion.own_ref) | copy-start | bytes 6291460
  316.6 69.7 %collective-permute-start.36 = (bf16[8,128,1024]{2,1,0:T(8,128)(2,1)S(1)}, bf16[8,128,1024]{2,1,0:T(8,128)(2,1)}, u32[]{:S(2)}, u32[]{:S(2)}) collective-permute-start(bf16[8,128,1024]{2,1,0:T(8,128)(2,1)S(1)} %maximum_select_fusion.own_ref), channel_id=1, source_target_pairs={{0,2},{2,0},{4,6},{6,4},{8,10},{10,8},{12,14},{14,12},{16,18},{18,... | collective-permute-start | bytes 6291464 | tf_op jit(solution)/shard_map/ppermute | solution.py:971
  323.9 13.4 %collective-permute-start.15 = (bf16[2,256,256]{2,1,0:T(8,128)(2,1)S(1)}, bf16[2,256,256]{2,1,0:T(8,128)(2,1)S(1)}, u32[]{:S(2)}, u32[]{:S(2)}) collective-permute-start(bf16[2,256,256]{2,1,0:T(8,128)(2,1)S(1)} %get-tuple-element.116), channel_id=1, source_target_pairs={{0,8},{2,10},{4,12},{6,14},{8,0},{10,2},{12,4},{14,6},{16,24},{18,... | collective-permute-start | bytes 786440 | tf_op jit(solution)/shard_map/ppermute | solution.py:971
  334.0 14.0 %collective-permute-start.22 = (bf16[2,264,256]{2,1,0:T(8,128)(2,1)S(1)}, bf16[2,264,256]{2,1,0:T(8,128)(2,1)S(1)}, u32[]{:S(2)}, u32[]{:S(2)}) collective-permute-start(bf16[2,264,256]{2,1,0:T(8,128)(2,1)S(1)} %get-tuple-element.112), channel_id=1, source_target_pairs={{0,16},{2,18},{4,20},{6,22},{8,24},{10,26},{12,28},{14,30},{16,0},... | collective-permute-start | bytes 811016 | tf_op jit(solution)/shard_map/ppermute | solution.py:971
  336.1 18.9 %copy-start.7 = (bf16[8,2,64,1024]{3,2,1,0:T(8,128)(2,1)}, bf16[8,2,64,1024]{3,2,1,0:T(8,128)(2,1)S(1)}, u32[]{:S(2)}) copy-start(bf16[8,2,64,1024]{3,2,1,0:T(8,128)(2,1)S(1)} %maximum_select_fusion.1.own_ref) | copy-start | bytes 6291460
  336.1 57.2 %collective-permute-start.42 = (bf16[8,2,64,1024]{3,2,1,0:T(8,128)(2,1)S(1)}, bf16[8,2,64,1024]{3,2,1,0:T(8,128)(2,1)}, u32[]{:S(2)}, u32[]{:S(2)}) collective-permute-start(bf16[8,2,64,1024]{3,2,1,0:T(8,128)(2,1)S(1)} %maximum_select_fusion.1.own_ref), channel_id=1, source_target_pairs={{0,2},{2,0},{4,6},{6,4},{8,10},{10,8},{12,14},{14,12},{16,18},{18,... | collective-permute-start | bytes 6291464 | tf_op jit(solution)/shard_map/ppermute | solution.py:971
  337.3 12.0 %collective-permute-start.16 = (bf16[1,256,256]{2,1,0:T(8,128)(2,1)S(1)}, bf16[1,256,256]{2,1,0:T(8,128)(2,1)S(1)}, u32[]{:S(2)}, u32[]{:S(2)}) collective-permute-start(bf16[1,256,256]{2,1,0:T(8,128)(2,1)S(1)} %fusion.22), channel_id=1, source_target_pairs={{0,16},{2,18},{4,20},{6,22},{8,24},{10,26},{12,28},{14,30},{16,0},... | collective-permute-start | bytes 393224 | tf_op jit(solution)/shard_map/ppermute | solution.py:971
  348.0 15.2 %collective-permute-start.28 = (bf16[2,256,1024]{2,1,0:T(8,128)(2,1)S(1)}, bf16[2,256,1024]{2,1,0:T(8,128)(2,1)S(1)}, u32[]{:S(2)}, u32[]{:S(2)}) collective-permute-start(bf16[2,256,1024]{2,1,0:T(8,128)(2,1)S(1)} %dynamic-slice_convert_fusion.1), channel_id=1, source_target_pairs={{0,2},{2,0},{4,6},{6,4},{8,10},{10,8},{12,14},{14,12},{16,18},{18,... | collective-permute-start | bytes 3145736 | tf_op jit(solution)/shard_map/ppermute | solution.py:971
  349.4 5.0 %collective-permute-start.23 = (bf16[1,264,256]{2,1,0:T(8,128)(2,1)S(1)}, bf16[1,264,256]{2,1,0:T(8,128)(2,1)S(1)}, u32[]{:S(2)}, u32[]{:S(2)}) collective-permute-start(bf16[1,264,256]{2,1,0:T(8,128)(2,1)S(1)} %fusion.19), channel_id=1, source_target_pairs={{0,4},{2,6},{4,0},{6,2},{8,12},{10,14},{12,8},{14,10},{16,20},{18,... | collective-permute-start | bytes 405512 | tf_op jit(solution)/shard_map/ppermute | solution.py:971
  354.4 4.6 %collective-permute-start.17 = (bf16[96,256]{1,0:T(8,128)(2,1)S(1)}, bf16[96,256]{1,0:T(8,128)(2,1)S(1)}, u32[]{:S(2)}, u32[]{:S(2)}) collective-permute-start(bf16[96,256]{1,0:T(8,128)(2,1)S(1)} %get-tuple-element.124), channel_id=1, source_target_pairs={{0,1},{1,0},{2,3},{3,2},{4,5},{5,4},{6,7},{7,6},{8,9},{9,8},{10,11... | collective-permute-start | bytes 147464 | tf_op jit(solution)/shard_map/ppermute | solution.py:968
  358.9 4.1 collective-permute-start.24
  363.1 7.3 %collective-permute-start.18 = (bf16[1,256,256]{2,1,0:T(8,128)(2,1)S(1)}, bf16[1,256,256]{2,1,0:T(8,128)(2,1)S(1)}, u32[]{:S(2)}, u32[]{:S(2)}) collective-permute-start(bf16[1,256,256]{2,1,0:T(8,128)(2,1)S(1)} %maximum_bitcast_fusion.1), channel_id=1, source_target_pairs={{0,16},{2,18},{4,20},{6,22},{8,24},{10,26},{12,28},{14,30},{16,0},... | collective-permute-start | bytes 393224 | tf_op jit(solution)/shard_map/ppermute | solution.py:971
  363.2 7.3 %collective-permute-start.25 = (bf16[1,264,256]{2,1,0:T(8,128)(2,1)S(1)}, bf16[1,264,256]{2,1,0:T(8,128)(2,1)S(1)}, u32[]{:S(2)}, u32[]{:S(2)}) collective-permute-start(bf16[1,264,256]{2,1,0:T(8,128)(2,1)S(1)} %maximum_bitcast_fusion), channel_id=1, source_target_pairs={{0,4},{2,6},{4,0},{6,2},{8,12},{10,14},{12,8},{14,10},{16,20},{18,... | collective-permute-start | bytes 405512 | tf_op jit(solution)/shard_map/ppermute | solution.py:971
  363.6 20.5 %copy-start.10 = (bf16[1,256,1024]{2,1,0:T(8,128)(2,1)S(1)}, bf16[1,256,1024]{2,1,0:T(8,128)(2,1)}, u32[]{:S(2)}) copy-start(bf16[1,256,1024]{2,1,0:T(8,128)(2,1)} %param.16) | copy-start | bytes 1572868
  370.4 12.1 %collective-permute-start.19 = (bf16[2,256,256]{2,1,0:T(8,128)(2,1)S(1)}, bf16[2,256,256]{2,1,0:T(8,128)(2,1)S(1)}, u32[]{:S(2)}, u32[]{:S(2)}) collective-permute-start(bf16[2,256,256]{2,1,0:T(8,128)(2,1)S(1)} %maximum_select_fusion.16), channel_id=1, source_target_pairs={{0,8},{2,10},{4,12},{6,14},{8,0},{10,2},{12,4},{14,6},{16,24},{18,... | collective-permute-start | bytes 786440 | tf_op jit(solution)/shard_map/ppermute | solution.py:971
  370.5 13.4 %collective-permute-start.26 = (bf16[2,264,256]{2,1,0:T(8,128)(2,1)S(1)}, bf16[2,264,256]{2,1,0:T(8,128)(2,1)S(1)}, u32[]{:S(2)}, u32[]{:S(2)}) collective-permute-start(bf16[2,264,256]{2,1,0:T(8,128)(2,1)S(1)} %maximum_select_fusion.15), channel_id=1, source_target_pairs={{0,16},{2,18},{4,20},{6,22},{8,24},{10,26},{12,28},{14,30},{16,0},... | collective-permute-start | bytes 811016 | tf_op jit(solution)/shard_map/ppermute | solution.py:971
  382.5 17.9 %collective-permute-start.29 = (bf16[256,1024]{1,0:T(8,128)(2,1)}, bf16[256,1024]{1,0:T(8,128)(2,1)}, u32[]{:S(2)}, u32[]{:S(2)}) collective-permute-start(bf16[256,1024]{1,0:T(8,128)(2,1)} %fusion.12), channel_id=1, source_target_pairs={{0,1},{1,0},{2,3},{3,2},{4,5},{5,4},{6,7},{7,6},{8,9},{9,8},{10,11... | collective-permute-start | bytes 1572872 | tf_op jit(solution)/shard_map/ppermute | solution.py:968
  383.9 19.9 %collective-permute-start.20 = (bf16[4,256,256]{2,1,0:T(8,128)(2,1)}, bf16[4,256,256]{2,1,0:T(8,128)(2,1)}, u32[]{:S(2)}, u32[]{:S(2)}) collective-permute-start(bf16[4,256,256]{2,1,0:T(8,128)(2,1)} %maximum_select_fusion.12), channel_id=1, source_target_pairs={{0,4},{2,6},{4,0},{6,2},{8,12},{10,14},{12,8},{14,10},{16,20},{18,... | collective-permute-start | bytes 1572872 | tf_op jit(solution)/shard_map/ppermute | solution.py:971
  384.0 21.5 %collective-permute-start.27 = (bf16[4,264,256]{2,1,0:T(8,128)(2,1)S(1)}, bf16[4,264,256]{2,1,0:T(8,128)(2,1)}, u32[]{:S(2)}, u32[]{:S(2)}) collective-permute-start(bf16[4,264,256]{2,1,0:T(8,128)(2,1)S(1)} %maximum_select_fusion.11), channel_id=1, source_target_pairs={{0,8},{2,10},{4,12},{6,14},{8,0},{10,2},{12,4},{14,6},{16,24},{18,... | collective-permute-start | bytes 1622024 | tf_op jit(solution)/shard_map/ppermute | solution.py:971
  407.3 4.4 %collective-permute-start.44 = (bf16[8,264,256]{2,1,0:T(8,128)(2,1)S(1)}, bf16[8,264,256]{2,1,0:T(8,128)(2,1)}, u32[]{:S(2)}, u32[]{:S(2)}) collective-permute-start(bf16[8,264,256]{2,1,0:T(8,128)(2,1)S(1)} %maximum_select_fusion.2.bo_ref), channel_id=1, source_target_pairs={{0,2},{2,0},{4,6},{6,4},{8,10},{10,8},{12,14},{14,12},{16,18},{18,... | collective-permute-start | bytes 3244040 | tf_op jit(solution)/shard_map/ppermute | solution.py:971
  407.4 4.3 %collective-permute-start.43 = (bf16[8,256,256]{2,1,0:T(8,128)(2,1)S(1)}, bf16[8,256,256]{2,1,0:T(8,128)(2,1)}, u32[]{:S(2)}, u32[]{:S(2)}) collective-permute-start(bf16[8,256,256]{2,1,0:T(8,128)(2,1)S(1)} %maximum_select_fusion.7.ao_ref), channel_id=1, source_target_pairs={{0,2},{2,0},{4,6},{6,4},{8,10},{10,8},{12,14},{14,12},{16,18},{18,... | collective-permute-start | bytes 3145736 | tf_op jit(solution)/shard_map/ppermute | solution.py:971
  407.9 13.8 %copy-start.1 = (bf16[512,1024]{1,0:T(8,128)(2,1)S(1)}, bf16[512,1024]{1,0:T(8,128)(2,1)}, u32[]{:S(2)}) copy-start(bf16[512,1024]{1,0:T(8,128)(2,1)} %param.23) | copy-start | bytes 3145732
  (11 other events, 35.9 us)

commit v5 on v4

--- a/solution.py
+++ b/solution.py
@@ -536,19 +536,68 @@
     return [own(p) for p in range(3)] + [got(p) for p in range(3)]
 
 
+def norm_kernel(ids, a_ref, b_ref, n_ref, *refs):
+    x_ref, ain_ref, min_ref = refs[-3:]
+    mine = pl.program_id(0) == ids[1]
+    x = jnp.where(mine, a_ref[...].astype(f32), b_ref[...].astype(f32))
+    x_ref[...] = x.astype(bf16)
+    xhat, _ = _norm(x)
+    ain_ref[...] = (xhat * n_ref[0:1, :] + n_ref[1:2, :]).astype(bf16)
+    min_ref[...] = (xhat * n_ref[2:3, :] + n_ref[3:4, :]).astype(bf16)
+
+
+def norm_rows(ids, a, b, norms, before=()):
+    rows, width = a.shape
+    slot = 2 if before else 0
+    out = jax.ShapeDtypeStruct((4 * rows, width), bf16)
+    return pl.pallas_call(
+        norm_kernel,
+        grid_spec=pltpu.PrefetchScalarGridSpec(
+            num_scalar_prefetch=1,
+            grid=(2,),
+            in_specs=[_full(a), _full(b), _full(norms)] + [pl.BlockSpec(memory_space=pl.ANY)] * len(before),
+            out_specs=(pl.BlockSpec((rows, width), lambda i, ids: (slot + i, 0)),) * 3,
+        ),
+        out_shape=(out,) * 3,
+        input_output_aliases={4 + k: k for k in range(len(before))},
+        compiler_params=_params(),
+        cost_estimate=pl.CostEstimate(flops=0, transcendentals=0, bytes_accessed=1 << 20),
+        name="norm_rows",
+    )(ids, a, b, norms, *before)
+
+
+def mask_kernel(ids, a_ref, b_ref, c_ref, d_ref, live_ref, o_ref):
+    i = pl.program_id(0)
+    mine = (i % 2) == ids[1]
+    for slot, (own, sib) in enumerate(((a_ref, b_ref), (c_ref, d_ref))):
+        @pl.when((i // 2) == slot)
+        def _(own=own, sib=sib):
+            v = jnp.where(mine, own[...].astype(f32), sib[...].astype(f32))
+            o_ref[...] = (live_ref[...] * v).astype(bf16)
+
+
+def mask_rows(ids, own, own_sib, got, got_sib, live):
+    rows, width = own.shape
+    return pl.pallas_call(
+        mask_kernel,
+        grid_spec=pltpu.PrefetchScalarGridSpec(
+            num_scalar_prefetch=1,
+            grid=(4,),
+            in_specs=[_full(v) for v in (own, own_sib, got, got_sib)] + [pl.BlockSpec((rows, 1), lambda i, ids: (i, 0))],
+            out_specs=pl.BlockSpec((rows, width), lambda i, ids: (i, 0)),
+        ),
+        out_shape=jax.ShapeDtypeStruct((4 * rows, width), bf16),
+        compiler_params=_params(),
+        cost_estimate=pl.CostEstimate(flops=0, transcendentals=0, bytes_accessed=1 << 20),
+        name="mask_rows",
+    )(ids, own, own_sib, got, got_sib, live)
+
+
 def qkv_kernel(
-    ids, x_ref, n_ref, wq_ref, wk_ref, wv_ref, gq_ref, gk_ref, gv_ref, bq_ref, bk_ref, bv_ref, cs_ref, send_ref,
-    ain_ref, min_ref
+    ids, ain_ref, wq_ref, wk_ref, wv_ref, gq_ref, gk_ref, gv_ref, bq_ref, bk_ref, bv_ref, cs_ref, send_ref
 ):
-    rows, width = x_ref.shape
+    width = ain_ref.shape[1]
     half = width // 2
-
-    @pl.when(pl.program_id(1) == 0)
-    def _():
-        xhat, _ = _norm(x_ref[...])
-        ain_ref[...] = (xhat * n_ref[0:1, :] + n_ref[1:2, :]).astype(bf16)
-        min_ref[...] = (xhat * n_ref[2:3, :] + n_ref[3:4, :]).astype(bf16)
-
     me = ids[0]
     a_own = ain_ref[:, pl.ds(pl.multiple_of(me * half, half), half)]
     a_got = ain_ref[:, pl.ds(pl.multiple_of((1 - me) * half, half), half)]
@@ -566,79 +615,111 @@
             send_ref[0, k, n * HD : (n + 1) * HD, :] = v.astype(bf16)
 
 
-def qkv_forward(ids, x2, norms, w_own, w_got, bias, cs, cols=128):
-    rows, width = x2.shape[0] // 2, x2.shape[1]
+def qkv_forward(ids, attn_in, w_own, w_got, bias, cs, cols=256):
+    rows, width = attn_in.shape[0] // 2, attn_in.shape[1]
     half = width // 2
     quarter = w_got.shape[1] // 3
     bsp = lambda p: pl.BlockSpec((1, cols), lambda s, i, ids: (0, p * (quarter // cols) + i))
-    row = lambda: pl.BlockSpec((rows, width), lambda s, i, ids: (s, 0))
     return pl.pallas_call(
         qkv_kernel,
         grid_spec=pltpu.PrefetchScalarGridSpec(
             num_scalar_prefetch=1,
             grid=(2, quarter // cols),
-            in_specs=[row(), _full(norms)]
+            in_specs=[pl.BlockSpec((rows, width), lambda s, i, ids: (s, 0))]
             + _wq_specs(half, width, cols, quarter, lambda s, i, ids: i)
             + [bsp(p) for p in range(3)]
             + [_full(cs)],
-            out_specs=(pl.BlockSpec((1, cols // HD, 3 * HD, rows), lambda s, i, ids: (s, i, 0, 0)), row(), row()),
+            out_specs=pl.BlockSpec((1, cols // HD, 3 * HD, rows), lambda s, i, ids: (s, i, 0, 0)),
         ),
-        out_shape=(
-            jax.ShapeDtypeStruct((2, quarter // HD, 3 * HD, rows), bf16),
-            jax.ShapeDtypeStruct((2 * rows, width), bf16),
-            jax.ShapeDtypeStruct((2 * rows, width), bf16),
-        ),
+        out_shape=jax.ShapeDtypeStruct((2, quarter // HD, 3 * HD, rows), bf16),
         compiler_params=_params(),
         cost_estimate=pl.CostEstimate(flops=1 << 20, transcendentals=0, bytes_accessed=1 << 20),
         name="qkv_forward",
-    )(ids, x2, norms, w_own, w_own, w_own, w_got, w_got, w_got, bias, bias, bias, cs)
-
-
-def mlp_kernel(ids, x_ref, xt_ref, dy_ref, wo_ref, wg_ref, wd_ref, bu_ref, y_ref, dx_ref, gu_ref, gd_ref, gb_ref):
+    )(ids, attn_in, w_own, w_own, w_own, w_got, w_got, w_got, bias, bias, bias, cs)
+
+
+MLP_CHUNKS = 2
+
+
+def mlp_kernel(ids, x_ref, xt_ref, dy_ref, wo_ref, wg_ref, wd_ref, bu_ref, y_ref, dx_ref, uk_ref, us_ref, dk_ref, ds_ref, gb_ref,
+    g_s, act_s, du_s, y_s, dx_s
+):
     rows, width = x_ref.shape
     half = width // 2
     me = ids[0]
     spans = (
-        (pl.multiple_of(me * half, half), wo_ref),
-        (pl.multiple_of((1 - me) * half, half), wg_ref),
+        (pl.multiple_of(me * half, half), wo_ref[...]),
+        (pl.multiple_of((1 - me) * half, half), wg_ref[...]),
     )
 
     @pl.when(pl.program_id(0) == 0)
     def _():
-        y_ref[...] = jnp.zeros_like(y_ref)
-        dx_ref[...] = jnp.zeros_like(dx_ref)
-
-    dy = dy_ref[...]
+        y_s[...] = jnp.zeros_like(y_s)
+        dx_s[...] = jnp.zeros_like(dx_s)
+
     wd = wd_ref[...]
-    u = bu_ref[...] + sum(_nn(x_ref[:, pl.ds(o, half)], w[...]) for o, w in spans)
-    cdf = 0.5 * (1.0 + lax.erf(u * (1.0 / math.sqrt(2.0))))
-    pdf = jnp.exp(-0.5 * u * u) * (1.0 / math.sqrt(2.0 * math.pi))
-    act = (u * cdf).astype(bf16)
-    du = (_nt(dy, wd) * (cdf + u * pdf)).astype(bf16)
-    y_ref[...] += _nn(act, wd)
-    for o, w in spans:
-        dx_ref[:, pl.ds(o, half)] += _nt(du, w[...])
-    gd = lax.dot_general(act, dy, (((0,), (0,)), ((), ())), preferred_element_type=f32).astype(bf16)
-    k, r, _ = gd_ref.shape
+    bias = bu_ref[...]
+    step = rows // MLP_CHUNKS
+    for c in range(MLP_CHUNKS):
+        at = slice(c * step, (c + 1) * step)
+        u = bias + sum(_nn(x_ref[at, pl.ds(o, half)], w) for o, w in spans)
+        cdf = 0.5 * (1.0 + lax.erf(u * (1.0 / math.sqrt(2.0))))
+        pdf = jnp.exp(-0.5 * u * u) * (1.0 / math.sqrt(2.0 * math.pi))
+        act = (u * cdf).astype(bf16)
+        du = (_nt(dy_ref[at, :], wd) * (cdf + u * pdf)).astype(bf16)
+        y_s[at, :] += _nn(act, wd)
+        for o, w in spans:
+            dx_s[at, pl.ds(o, half)] += _nt(du, w)
+        act_s[at, :] = act
+        du_s[at, :] = du
+    du = du_s[...]
+    gd = lax.dot_general(
+        act_s[...], dy_ref[...], (((0,), (0,)), ((), ())), preferred_element_type=f32
+    ).astype(bf16)
+    k, r, _ = dk_ref.shape
+    k = gd.shape[0] // r
+    early = pl.program_id(0) < pl.num_programs(0) // 2
     for c in range(k):
-        gd_ref[c] = gd[c * r : (c + 1) * r, :]
-    gu = _nn(xt_ref[...], du).astype(bf16)
-    n = gu_ref.shape[0]
-    r = half // n
-    for h in range(2):
-        for c in range(n):
-            gu_ref[c, h * r : (h + 1) * r, :] = gu[h * half + c * r : h * half + (c + 1) * r, :]
+        v = gd[c * r : (c + 1) * r, :]
+
+        @pl.when(early)
+        def _(v=v, c=c):
+            ds_ref[c] = v
+
+        @pl.when(jnp.logical_not(early))
+        def _(v=v, c=c):
+            dk_ref[c] = v
+
+    g_s[...] = _nn(xt_ref[...], du).astype(bf16)
+    n = uk_ref.shape[0]
+    r = uk_ref.shape[1] // 2
+    for ref, side in ((uk_ref, ids[3]), (us_ref, 1 - ids[3])):
+        for h in range(2):
+            for c in range(n):
+                at = pl.multiple_of(h * half + (side * n + c) * r, r)
+                ref[c, h * r : (h + 1) * r, :] = g_s[pl.ds(at, r), :]
     gb_ref[...] = jnp.sum(du.astype(f32), axis=0, keepdims=True)
 
-
-def mlp(ids, x, xt, dy, w_own, w_got, wd, bu, n, tile=256):
+    @pl.when(pl.program_id(0) == pl.num_programs(0) - 1)
+    def _():
+        y_ref[...] = y_s[...].astype(bf16)
+        dx_ref[...] = dx_s[...].astype(bf16)
+
+
+def mlp(ids, x, xt, dy, w_own, w_got, wd, bu, n, tile=512):
     rows, width = x.shape
     half = width // 2
     hidden = w_got.shape[1]
     steps = hidden // tile
+    mid = steps // 2
     whole = pl.BlockSpec((rows, width), lambda i, ids: (0, 0))
     per = hidden // n
-    part = lambda i, ids: ids[1] * steps + i
+    order = lambda i, ids: i % mid + mid * jnp.where(i < mid, 1 - ids[2], ids[2])
+    part = lambda i, ids: ids[1] * steps + order(i, ids)
+    up_spec = pl.BlockSpec((n // 2, width // n, tile), lambda i, ids: (0, 0, order(i, ids)))
+    down_spec = lambda f: pl.BlockSpec((tile // per, per, width), lambda i, ids: (f(i), 0, 0))
+    up_shape = jax.ShapeDtypeStruct((n // 2, width // n, hidden), bf16)
+    down_shape = jax.ShapeDtypeStruct((n // 2, per, width), bf16)
     return pl.pallas_call(
         mlp_kernel,
         grid_spec=pltpu.PrefetchScalarGridSpec(
@@ -649,23 +730,29 @@
                 pl.BlockSpec((width, rows), lambda i, ids: (0, 0)),
                 whole,
                 pl.BlockSpec((half, tile), lambda i, ids: (0, ids[0] * 2 * steps + part(i, ids))),
-                pl.BlockSpec((half, tile), lambda i, ids: (0, i)),
+                pl.BlockSpec((half, tile), lambda i, ids: (0, order(i, ids))),
                 pl.BlockSpec((tile, width), lambda i, ids: (part(i, ids), 0)),
                 pl.BlockSpec((1, tile), lambda i, ids: (0, part(i, ids))),
             ],
             out_specs=(
                 whole,
                 whole,
-                pl.BlockSpec((n, width // n, tile), lambda i, ids: (0, 0, i)),
-                pl.BlockSpec((tile // per, per, width), lambda i, ids: (i, 0, 0)),
-                pl.BlockSpec((1, tile), lambda i, ids: (0, i)),
+                up_spec,
+                up_spec,
+                down_spec(lambda i: jnp.maximum(i - mid, 0)),
+                down_spec(lambda i: jnp.minimum(i, mid - 1)),
+                pl.BlockSpec((1, tile), lambda i, ids: (0, order(i, ids))),
             ),
+            scratch_shapes=[pltpu.VMEM((width, tile), bf16), pltpu.VMEM((rows, tile), bf16), pltpu.VMEM((rows, tile), bf16)]
+            + [pltpu.VMEM((rows, width), f32)] * 2,
         ),
         out_shape=(
-            jax.ShapeDtypeStruct((rows, width), f32),
-            jax.ShapeDtypeStruct((rows, width), f32),
-            jax.ShapeDtypeStruct((n, width // n, hidden), bf16),
-            jax.ShapeDtypeStruct((n, per, width), bf16),
+            jax.ShapeDtypeStruct((rows, width), bf16),
+            jax.ShapeDtypeStruct((rows, width), bf16),
+            up_shape,
+            up_shape,
+            down_shape,
+            down_shape,
             jax.ShapeDtypeStruct((1, hidden), f32),
         ),
         compiler_params=_params(),
@@ -717,7 +804,7 @@
     for h in range(2):
         lanes = slice(h * half, (h + 1) * half)
         da = jnp.where(first, d_own, d_got) if h == 0 else jnp.where(first, d_got, d_own)
-        dm = dm_ref[:, lanes]
+        dm = dm_ref[:, lanes].astype(f32)
         xh = xhat[:, lanes]
         e_ref[0, :, lanes] = da * n_ref[0:1, lanes] + dm * n_ref[2:3, lanes]
         for k, v in enumerate((da * xh, da, dm * xh, dm)):
@@ -961,7 +1048,6 @@
     seq = own_rows * n_ctx
     heads = H // 4
     hid = w_up.shape[1] // 4
-    ids = jnp.stack([me, core]).astype(jnp.int32)
     CORE, X, ZN, ZF = 0, 1, 2, 3
 
     def swap(v):
@@ -973,17 +1059,16 @@
     def bit_of(bit):
         return (ctx >> bit) & 1
 
+    ids = jnp.stack([me, core, bit_of(X), bit_of(ZN)]).astype(jnp.int32)
+
     def add(*terms):
         return sum(v.astype(f32) for v in terms).astype(bf16) if len(terms) > 1 else terms[0]
 
     def halve(terms, bit):
         b = bit_of(bit)
-
-        def part(k):
-            cut = [v.reshape((2, v.shape[0] // 2) + v.shape[1:]) for v in terms]
-            return add(*[lax.dynamic_index_in_dim(v, k, 0, keepdims=False) for v in cut])
-
-        return part(b), flip(part(1 - b), bit)
+        cut = [v.reshape((2, v.shape[0] // 2) + v.shape[1:]) for v in terms]
+        part = lambda k: [lax.dynamic_index_in_dim(v, k, 0, keepdims=False) for v in cut]
+        return part(b) + [flip(add(*part(1 - b)), bit)]
 
     def ordered(first, a, b, axis=0):
         return jnp.where(first == 0, jnp.concatenate([a, b], axis), jnp.concatenate([b, a], axis))
@@ -998,34 +1083,37 @@
     def rows_of(v, at, n, axis=0):
         return lax.dynamic_slice_in_dim(v, at, n, axis)
 
-    len_parts = jnp.stack([lengths[0] // 64, lengths[0] % 64]).astype(bf16)
-    small = jnp.concatenate(
-        [ln1_gain, ln1_bias, ln2_gain, ln2_bias, b_out, b_down, b_qkv, len_parts, jnp.zeros((126,), bf16)]
-    )[None]
-    small = ordered(me, small, swap(small))
     x_own = tokens[0]
     x_got = swap(x_own)
+    x_sib = flip(x_own, CORE)
     mine = me * half + core * quarter
     other = (1 - me) * half + core * quarter
-    wq_rows = rows_of(w_qkv, bit_of(X) * quarter, quarter)
-    wq_got = swap(jnp.concatenate([rows_of(wq_rows, p * width + other, quarter, 1) for p in range(3)], axis=1))
-    wu_send = rows_of(w_up, ((1 - me) * 2 + core) * hid, hid, 1)
-    wq_got, wu_send = lax.optimization_barrier((wq_got, wu_send))
-    wq_got = double(wq_got, X)
-    wu_got = swap(wu_send)
-    x_sib = flip(x_own, CORE)
-    x2 = jnp.concatenate([ordered(core, x_own, x_sib), double(x_got, CORE)])
-    cot_own = cotangent[0]
-    cot_sib = flip(cot_own, CORE)
-
-    vec = lambda i: small[:, i * half : (i + 1) * half].reshape(width).astype(f32)
+    wq_send = jnp.concatenate([rows_of(w_qkv, p * width + other, quarter, 1) for p in range(3)], axis=1)
+    wq_send, ln1_gain = lax.optimization_barrier((wq_send, ln1_gain))
+    len_parts = jnp.stack([lengths[0] // 64, lengths[0] % 64]).astype(bf16)
+    parts = [ln1_gain, ln1_bias, ln2_gain, ln2_bias, b_out, b_down, b_qkv, jnp.pad(len_parts, (0, half - 2))]
+    small = jnp.concatenate([v.reshape(-1, half) for v in parts])
+    small = ordered(me, small[None], swap(small)[None])
+    wq_got = swap(wq_send)
+    vec = lambda i: small[:, i].reshape(width).astype(f32)
     norms = jnp.stack([vec(i) for i in range(4)])
     bias_out = vec(4) + vec(5)
-    qkv_bias = small[:, 6 * half : 9 * half].astype(f32).reshape(3, width)
+    qkv_bias = small[:, 6:9].astype(f32).reshape(3, width)
     qkv_bias = rows_of(qkv_bias, mine, quarter, 1).reshape(1, 3 * quarter)
-    lens = small[:, 9 * half : 9 * half + 2].astype(jnp.int32)
+    lens = small[:, 9, :2].astype(jnp.int32)
     lens = lens[:, 0] * 64 + lens[:, 1]
     other_len = lens[1 - me]
+
+    normed = norm_rows(ids, x_own, x_sib, norms)
+    cot_own = cotangent[0]
+    wu_send = rows_of(w_up, ((1 - me) * 2 + core) * hid, hid, 1)
+    wq_got, cot_send, normed = lax.optimization_barrier((wq_got, cot_own, normed))
+    cot_got = swap(cot_send)
+    cot_got, wu_send = lax.optimization_barrier((cot_got, wu_send))
+    wu_got = swap(wu_send)
+    normed = norm_rows(ids, x_got, flip(x_got, CORE), norms, normed)
+    x2, attn_in, mlp_in = normed
+    cot_sib = flip(cot_own, CORE)
 
     blocks = rows_of(block_map, (rows // HB) * (ctx // 2), rows // HB)
     offs = jnp.arange(HB, dtype=jnp.int32)
@@ -1038,35 +1126,32 @@
     own_ang = freq[:, None] * positions.astype(f32)[None, :]
     own_table = jnp.concatenate([jnp.cos(own_ang), jnp.sin(own_ang)])
 
-    send, attn_in, mlp_in = qkv_forward(ids, x2, norms, w_qkv, wq_got, qkv_bias, own_table)
+    attn_in, table = lax.optimization_barrier((attn_in, table))
+    send = qkv_forward(ids, attn_in, w_qkv, wq_got, qkv_bias, own_table)
     qkv_head = exchange(send.reshape(2 * heads, 3 * HD, rows))
-    mlp_in, wu_got, cot_send = lax.optimization_barrier((mlp_in, wu_got, cot_own))
-    cot_got = swap(cot_send)
-    cot2 = jnp.concatenate([ordered(core, cot_own, cot_sib), double(cot_got, CORE)])
-    dy = (live2 * cot2.astype(f32)).astype(bf16)
+    dy = mask_rows(ids, cot_own, cot_sib, cot_got, flip(cot_got, CORE), live2)
     dy2 = dy.reshape(2, rows, width)
     w_out_mine = rows_of(w_out, core * quarter, quarter)
     dctx = jnp.einsum("ed,std->set", w_out_mine, dy2, preferred_element_type=f32).astype(bf16)
+    attn_t = attn_in.T
     do_head = exchange(dctx.reshape(2 * heads, HD, rows))
-
-    attn_t = attn_in.T
-    y_mlp, d_mlp, g_up, g_down, gb_up = mlp(
+    y_mlp, d_mlp, up_keep, up_send, down_keep, down_send, gb_up = mlp(
         ids, mlp_in, mlp_in.T, dy, w_up, wu_got, w_down, b_up.astype(f32)[None, :], chips
     )
 
     chain_a = (X, ZN, ZF)
     chain_b = (ZN, ZF, X)
-    qkv_head, g_up, g_down = lax.optimization_barrier((qkv_head, g_up, g_down))
-    down = halve((g_down,), chain_a[0])
-    up = halve((g_up,), chain_b[0])
+    qkv_head, up_send, down_send = lax.optimization_barrier((qkv_head, up_send, down_send))
+    down = [down_keep, flip(down_send, chain_a[0])]
+    up = [up_keep, flip(up_send, chain_b[0])]
 
     o_head, lse = attn_fwd(block_map, qkv_head, bq=1024, bk=1024)
-    qkv_head, o_head, do_head, down, up = lax.optimization_barrier((qkv_head, o_head, do_head, down, up))
+    qkv_head, o_head, do_head, down[-1], up[-1] = lax.optimization_barrier((qkv_head, o_head, do_head, down[-1], up[-1]))
     ob = exchange(o_head).reshape(2, quarter, rows)
     down = halve(down, chain_a[1])
     up = halve(up, chain_b[1])
     g_head = attn_bwd(block_map, qkv_head, o_head, do_head, lse, table)
-    g_head, ob, down, up = lax.optimization_barrier((g_head, ob, down, up))
+    g_head, ob, down[-1], up[-1] = lax.optimization_barrier((g_head, ob, down[-1], up[-1]))
     d_qkv = exchange(g_head).reshape(2, heads, 3 * HD, rows)
 
     down = add(*halve(down, chain_a[2]))
@@ -1086,34 +1171,34 @@
         v = rows_of(v, core * own_rows, own_rows, 1) + flip(give, CORE).astype(f32)
         return v[0], swap(v[1].astype(bf16))
 
-    part = jnp.einsum("sct,cd->std", ob, w_out_mine, preferred_element_type=f32) + y_mlp.reshape(2, rows, width)
+    part = jnp.einsum("sct,cd->std", ob, w_out_mine, preferred_element_type=f32) + y_mlp.reshape(2, rows, width).astype(f32)
     part, part_got = settle(part)
     output = (live_own * (x_own.astype(f32) + part + part_got.astype(f32) + bias_out)).astype(bf16)
 
     v_a, v_b, e = qkv_backward(
         ids, d_qkv, attn_t, x2, norms, w_qkv, wq_got, d_mlp, ob, dy, gb_up, chips
     )
-    v_a = (v_a,)
-    v_b = (v_b,)
+    v_a = [v_a]
+    v_b = [v_b]
     for a, b in zip(chain_a, chain_b):
         v_a = halve(v_a, a)
         v_b = halve(v_b, b)
     e_own, e_got = settle(e)
     n3 = 3 * half // (2 * chips)
     size = 2 * n3 + width // (2 * chips)
-    mixed = []
-    for v, chain in ((add(*v_a)[0], chain_a), (add(*v_b)[0], chain_b)):
+    tail = []
+    for v in (add(*v_a)[0], add(*v_b)[0]):
         extra = v[size:]
         back = swap(jnp.concatenate([rows_of(v, (1 - me) * n3, n3), extra]))
         extra = add(extra, back[n3:])
-        v = jnp.concatenate([ordered(me, rows_of(v, me * n3, n3), back[:n3]), v[2 * n3 : size], extra])[None]
-        for a in chain[::-1]:
-            v = double(v, a)
-        mixed.append(v)
+        tail.append(jnp.concatenate([ordered(me, rows_of(v, me * n3, n3), back[:n3]), v[2 * n3 : size], extra])[None])
     grad_tokens = last(e_own, e_got, x_own, cot_own, live_own)
-    mixed[0], mixed[1], grad_tokens, output, tot_down, tot_up = lax.optimization_barrier(
-        (mixed[0], mixed[1], grad_tokens, output, tot_down, tot_up)
-    )
+    cover = [[tot_down], [tot_up], [grad_tokens, output]]
+    for k, (a, b) in enumerate(zip(chain_a[::-1], chain_b[::-1])):
+        tail = [double(tail[0], a), double(tail[1], b)]
+        tail, cover[k] = lax.optimization_barrier((tail, cover[k]))
+    mixed = tail
+    (tot_down,), (tot_up,), (grad_tokens, output) = cover
     tot_qkv, tot_out, flat = unpack(ids, mixed[0], flip(mixed[0], CORE), mixed[1], flip(mixed[1], CORE), width)
     flat = flat[:, :6].reshape(12 * width)
 

time: 424 us -> 394 us (0.929)
  other arithmetic: 48.1 us -> 29.8 us
  local copies, waits for them, and re-layouts: 33.9 us -> 22.4 us
  Pallas kernels: 129 us -> 136 us
    pallas_call x0 -> x3, Pallas kernels: none -> 12.9 us  [the longest x2 7.83 us: norm_rows(): pl.pallas_call(norm_kernel, grid_spec=pltpu.PrefetchScalarGridSpec(num_sc...]
    ppermute x10, waiting for transfers between devices: 22.7 us -> 35.2 us  [swap(): return lax.ppermute(v, 'wsh', SWAP)]
    select_n x21 -> x16, other arithmetic: 23 us -> 10.5 us  [ordered(): jnp.where(first == 0, jnp.concatenate([a, b], axis), jnp.concatenate([b,...]
    ppermute x35 -> x34, waiting for transfers between devices: 116 us -> 105 us  [flip(): return lax.ppermute(v, 'ctx', [(i, i ^ 1 << bit) for i in range(n_ctx)])]
    convert_element_type x3 -> x1, other arithmetic: 4.88 us -> 0.01 us  [fast_shards(): lens = small[:, 9, :2].astype(jnp.int32)]
    squeeze x2 -> x0, local copies, waits for them, and re-layouts: 4.86 us -> none  [part(): lax.dynamic_index_in_dim(v, k, 0, keepdims=False)]
    concatenate x1 -> x2, local copies, waits for them, and re-layouts: 4.98 us -> 0.16 us  [the longest x1 0.15 us: fast_shards(): small = jnp.concatenate([v.reshape(-1, half) for v in parts])]
    pallas_call x1, Pallas kernels: 10.3 us -> 5.6 us  [qkv_forward(): pl.pallas_call(qkv_kernel, grid_spec=pltpu.PrefetchScalarGridSpec(num_sca...]
  transfers between devices with their start and end apart: 49 -> 48, of which waited for: 19 -> 22; matrix products, arithmetic and copies ran while one was open for 18% -> 13% of each run, Pallas kernels for 29% -> 33%
where the time goes in v5:
time: 394 us; the launch traced here: 393 us
  waiting for transfers between devices  142 us (36%)
  Pallas kernels  136 us (35%)
  starting transfers between devices  57 us (14%)
  other arithmetic  29.8 us (8%)
  local copies, waits for them, and re-layouts  22.4 us (6%)
    ppermute x34, waiting for transfers between devices, flip(): return lax.ppermute(v, 'ctx', [(i, i ^ 1 << bit) for i in range(n_ctx)])  105 us
    ppermute x10, waiting for transfers between devices, swap(): return lax.ppermute(v, 'wsh', SWAP)  35.2 us
    pallas_call x1, Pallas kernels, attn_bwd(): pl.pallas_call(lambda *a: attn_bwd_kernel(*a, nblk=nblk, per=x.shape[2] /...  34.9 us
    ppermute x34, starting transfers between devices, flip(): return lax.ppermute(v, 'ctx', [(i, i ^ 1 << bit) for i in range(n_ctx)])  28 us
    pallas_call x1, Pallas kernels, mlp(): pl.pallas_call(mlp_kernel, grid_spec=pltpu.PrefetchScalarGridSpec(num_sca...  23.2 us
    pallas_call x1, Pallas kernels, attn_fwd(): pl.pallas_call(lambda *a: attn_fwd_kernel(*a, nblk=nblk, per=x.shape[2] /...  21.8 us
    all_to_all x4, starting transfers between devices, exchange(): return lax.all_to_all(v, 'ctx', 0, 0, axis_index_groups=groups, tiled=False)  18.4 us
    pallas_call x1, Pallas kernels, qkv_backward(): pl.pallas_call(qkv_back_kernel, grid_spec=pltpu.PrefetchScalarGridSpec(nu...  13.5 us
  transfers between devices with their start and end apart: 48, of which 22 were waited for; matrix products, arithmetic and copies ran while one was open for 13% of the time, Pallas kernels for 33%

profile of v5, /device:TPU:0, one launch (start us, length us, event | category | flops | bytes accessed | tf_op | source)
XLA Modules:
  0.0 392.9 jit_solution(13122426666971353479)
XLA Ops:
  0.7 3.0 collective-permute-start
  6.3 1.9 collective-permute-start.3
  11.1 6.0 %collective-permute-done.2 = bf16[10,512]{1,0:T(8,128)(2,1)S(1)} collective-permute-done((bf16[10,512]{1,0:T(8,128)(2,1)S(1)}, bf16[10,512]{1,0:T(8,128)(2,1)S(1)}, u32[]{:S(2)}, u32[]{:S(2)}) %collective-permute-start.2) | collective-permute-done | bytes 10272 | tf_op jit(solution)/shard_map/ppermute | solution.py:1054
  17.9 3.9 norm_rows.2
  21.8 11.3 %collective-permute-done.3.gq_ref.gk_ref.gv_ref = bf16[512,768]{1,0:T(8,128)(2,1)S(1)} collective-permute-done((bf16[512,768]{1,0:T(8,128)(2,1)S(1)}, bf16[512,768]{1,0:T(8,128)(2,1)S(1)}, u32[]{:S(2)}, u32[]{:S(2)}) %collective-permute-start.3) | collective-permute-done | bytes 786464 | tf_op jit(solution)/shard_map/ppermute | solution.py:1054
  33.1 1.7 collective-permute-start.6
  35.5 3.9 norm_rows.3
  39.4 5.6 %qkv_forward.1 = bf16[2,4,192,512]{3,2,1,0:T(8,128)(2,1)} custom-call(s32[4]{0:T(128)} %pad_add_fusion.ids, bf16[1024,1024]{1,0:T(8,128)(2,1)} %get-tuple-element.77.ain_ref, bf16[512,3072]{1,0:T(8,128)(2,1)} %wv_ref.3, bf16[512,3072]{1,0:T(8,128)(2,1)} %wv_ref.3, bf16[512,3072]{1,0:T(8,128)(2,1)} %wv_ref.3, bf16[512,768]{1,0:T(8,128)(2,1)} %copy-done.2, ...), custom_call_target="tpu_custom_call" | custom-call | flops 1048576 | bytes 1048576 | tf_op jit(solution)/shard_map/qkv_forward/pallas_call | solution.py:623
  45.0 5.9 %all-to-all-start = ((bf16[8,192,512]{2,1,0:T(8,128)(2,1)}), bf16[8,192,512]{2,1,0:T(8,128)(2,1)S(1)}, u32[]{:S(2)}, u32[]{:S(2)}) async-start(bf16[8,192,512]{2,1,0:T(8,128)(2,1)} %bitcast.173), calls=%async_computation | async-start | bytes 3145728 | tf_op jit(solution)/shard_map/all_to_all | solution.py:1081
  50.9 2.3 constant_dynamic-slice_fusion.5
  57.2 3.9 %copy.47 = bf16[1024,1024]{0,1:T(8,128)(2,1)} copy(bf16[1024,1024]{1,0:T(8,128)(2,1)} %get-tuple-element.79.x_ref) | data formatting | bytes 4194304 | tf_op jit(solution)/shard_map/norm_rows/pallas_call | solution.py:553
  61.1 5.1 %mask_rows.1.dy_ref = bf16[1024,1024]{1,0:T(8,128)(2,1)} custom-call(s32[4]{0:T(128)} %pad_add_fusion.ids, bf16[256,1024]{1,0:T(8,128)(2,1)} %bitcast.185, bf16[256,1024]{1,0:T(8,128)(2,1)} %collective-permute-done.5.b_ref, bf16[256,1024]{1,0:T(8,128)(2,1)} %collective-permute-done.6.c_ref, bf16[256,1024]{1,0:T(8,128)(2,1)} %collective-permute-done.7.d_ref, ...), custom_call_target="tpu_custom_call" | custom-call | bytes 1048576 | tf_op jit(solution)/shard_map/mask_rows/pallas_call | solution.py:581
  66.2 10.7 %collective-permute-done.8.wg_ref = bf16[512,1024]{1,0:T(8,128)(2,1)} collective-permute-done((bf16[512,1024]{1,0:T(8,128)(2,1)}, bf16[512,1024]{1,0:T(8,128)(2,1)}, u32[]{:S(2)}, u32[]{:S(2)}) %collective-permute-start.8) | collective-permute-done | bytes 1048608 | tf_op jit(solution)/shard_map/ppermute | solution.py:1054
  77.0 23.2 %mlp.1 = (bf16[1024,1024]{1,0:T(8,128)(2,1)}, bf16[1024,1024]{1,0:T(8,128)(2,1)}, bf16[4,128,1024]{2,1,0:T(8,128)(2,1)}, bf16[4,128,1024]{2,1,0:T(8,128)(2,1)}, ...) custom-call(s32[4]{0:T(128)} %pad_add_fusion.ids, ...), custom_call_target="tpu_custom_call" | custom-call | flops 12884901888 | bytes 25165824 | tf_op jit(solution)/shard_map/mlp/pallas_call | solution.py:723
  100.2 1.8 collective-permute-start.9
  102.0 1.5 collective-permute-start.10
  103.4 3.1 convolution_convert_fusion
  106.6 3.6 all-to-all-start.1
  110.2 21.8 %attn_fwd.1 = (bf16[8,64,512]{2,1,0:T(8,128)(2,1)}, f32[1,4096]{1,0:T(1,128)}) custom-call(s32[32]{0:T(128)} %a_0_.3, bf16[8,192,512]{2,1,0:T(8,128)(2,1)} %copy-done.4), custom_call_target="tpu_custom_call" | custom-call | tf_op jit(solution)/shard_map/attn_fwd/pallas_call | solution.py:438
  132.0 1.7 all-to-all-done.1.a_3_
  133.7 4.3 %all-to-all-start.2 = ((bf16[8,64,512]{2,1,0:T(8,128)(2,1)}), bf16[8,64,512]{2,1,0:T(8,128)(2,1)S(1)}, u32[]{:S(2)}, u32[]{:S(2)}) async-start(bf16[8,64,512]{2,1,0:T(8,128)(2,1)} %get-tuple-element.90.a_2_), calls=%async_computation.2 | async-start | bytes 1048576 | tf_op jit(solution)/shard_map/all_to_all | solution.py:1081
  138.0 2.0 fusion.5
  140.0 2.0 collective-permute-start.11
  142.1 2.2 fusion.6
  144.3 2.4 collective-permute-start.12
  146.6 34.9 %attn_bwd.1 = bf16[8,192,512]{2,1,0:T(8,128)(2,1)} custom-call(s32[32]{0:T(128)} %a_0_.3, bf16[8,192,512]{2,1,0:T(8,128)(2,1)} %copy-done.4, bf16[8,64,512]{2,1,0:T(8,128)(2,1)} %get-tuple-element.90.a_2_, bf16[8,64,512]{2,1,0:T(8,128)(2,1)} %copy-done.13, f32[1,4096]{1,0:T(1,128)} %get-tuple-element.92.a_4_, f32[16,4096]{1,0:T(8,128)} %pad_maximum_fusion.1.a_5_), custom_call_target="tpu_custom_call" | custom-call | tf_op jit(solution)/shard_map/attn_bwd/pallas_call | solution.py:498
  181.6 4.5 %all-to-all-start.3 = ((bf16[8,192,512]{2,1,0:T(8,128)(2,1)}), bf16[8,192,512]{2,1,0:T(8,128)(2,1)}, u32[]{:S(2)}, u32[]{:S(2)}) async-start(bf16[8,192,512]{2,1,0:T(8,128)(2,1)} %attn_bwd.1), calls=%async_computation.3 | async-start | bytes 3145728 | tf_op jit(solution)/shard_map/all_to_all | solution.py:1081
  186.1 1.3 fusion.12
  187.5 2.6 collective-permute-start.23
  191.3 1.5 collective-permute-start.30
  193.6 11.2 %collective-permute-done.30 = bf16[1,128,1024]{2,1,0:T(8,128)(2,1)S(1)} collective-permute-done((bf16[1,128,1024]{2,1,0:T(8,128)(2,1)S(1)}, bf16[1,128,1024]{2,1,0:T(8,128)(2,1)S(1)}, u32[]{:S(2)}, u32[]{:S(2)}) %collective-permute-start.30) | collective-permute-done | bytes 262176 | tf_op jit(solution)/shard_map/ppermute | solution.py:1057
  206.8 22.7 %collective-permute-done.23 = bf16[1,128,1024]{2,1,0:T(8,128)(2,1)S(1)} collective-permute-done((bf16[1,128,1024]{2,1,0:T(8,128)(2,1)S(1)}, bf16[1,128,1024]{2,1,0:T(8,128)(2,1)S(1)}, u32[]{:S(2)}, u32[]{:S(2)}) %collective-permute-start.23) | collective-permute-done | bytes 262176 | tf_op jit(solution)/shard_map/ppermute | solution.py:1057
  230.8 1.5 collective-permute-start.32
  233.5 8.4 %collective-permute-done.24 = bf16[1,128,1024]{2,1,0:T(8,128)(2,1)S(1)} collective-permute-done((bf16[1,128,1024]{2,1,0:T(8,128)(2,1)S(1)}, bf16[1,128,1024]{2,1,0:T(8,128)(2,1)S(1)}, u32[]{:S(2)}, u32[]{:S(2)}) %collective-permute-start.24) | collective-permute-done | bytes 262176 | tf_op jit(solution)/shard_map/ppermute | solution.py:1057
  243.2 1.8 collective-permute-start.33
  245.0 18.0 %collective-permute-done.25 = bf16[2,128,1024]{2,1,0:T(8,128)(2,1)} collective-permute-done((bf16[2,128,1024]{2,1,0:T(8,128)(2,1)S(1)}, bf16[2,128,1024]{2,1,0:T(8,128)(2,1)}, u32[]{:S(2)}, u32[]{:S(2)}) %collective-permute-start.25) | collective-permute-done | bytes 524320 | tf_op jit(solution)/shard_map/ppermute | solution.py:1057
  263.0 2.4 maximum_select_fusion.3
  265.4 3.2 collective-permute-start.26
  269.5 2.5 copy.49
  272.0 1.7 maximum_select_fusion.4
  273.8 2.2 convert_add_fusion.1
  276.0 13.5 %qkv_backward.1 = (bf16[8,256,256]{2,1,0:T(8,128)(2,1)}, bf16[8,264,256]{2,1,0:T(8,128)(2,1)}, f32[2,512,1024]{2,1,0:T(8,128)}) custom-call(s32[4]{0:T(128)} %pad_add_fusion.ids, bf16[2,4,192,512]{3,2,1,0:T(8,128)(2,1)} %bitcast.32.d_ref, bf16[1024,1024]{1,0:T(8,128)(2,1)} %bitcast.172, bf16[1024,1024]{1,0:T(8,128)(2,1)} %get-tuple-element.99.x_ref, ...), custom_call_target="tpu_custom_call" | custom-call | tf_op jit(solution)/shard_map/qkv_backward/pallas_call | solution.py:865
  289.5 1.4 constant_dynamic-slice_fusion.3
  291.2 2.1 collective-permute-start.18
  294.6 2.7 maximum_select_fusion.own_ref
  297.4 6.2 %collective-permute-done.13 = bf16[4,256,256]{2,1,0:T(8,128)(2,1)S(1)} collective-permute-done((bf16[4,256,256]{2,1,0:T(8,128)(2,1)S(1)}, bf16[4,256,256]{2,1,0:T(8,128)(2,1)S(1)}, u32[]{:S(2)}, u32[]{:S(2)}) %collective-permute-start.13) | collective-permute-done | bytes 524320 | tf_op jit(solution)/shard_map/ppermute | solution.py:1057
  303.6 1.8 collective-permute-start.14
  305.4 7.5 %collective-permute-done.18 = bf16[4,264,256]{2,1,0:T(8,128)(2,1)S(1)} collective-permute-done((bf16[4,264,256]{2,1,0:T(8,128)(2,1)S(1)}, bf16[4,264,256]{2,1,0:T(8,128)(2,1)S(1)}, u32[]{:S(2)}, u32[]{:S(2)}) %collective-permute-start.18) | collective-permute-done | bytes 540704 | tf_op jit(solution)/shard_map/ppermute | solution.py:1057
  314.3 1.9 maximum_select_fusion.1.own_ref
  316.3 1.7 collective-permute-done.14
  318.3 9.2 %collective-permute-done.19 = bf16[2,264,256]{2,1,0:T(8,128)(2,1)S(1)} collective-permute-done((bf16[2,264,256]{2,1,0:T(8,128)(2,1)S(1)}, bf16[2,264,256]{2,1,0:T(8,128)(2,1)S(1)}, u32[]{:S(2)}, u32[]{:S(2)}) %collective-permute-start.19) | collective-permute-done | bytes 270368 | tf_op jit(solution)/shard_map/ppermute | solution.py:1057
  327.6 1.3 collective-permute-done.15
  329.1 4.9 %collective-permute-done.20 = bf16[1,264,256]{2,1,0:T(8,128)(2,1)S(1)} collective-permute-done((bf16[1,264,256]{2,1,0:T(8,128)(2,1)S(1)}, bf16[1,264,256]{2,1,0:T(8,128)(2,1)S(1)}, u32[]{:S(2)}, u32[]{:S(2)}) %collective-permute-start.20) | collective-permute-done | bytes 135200 | tf_op jit(solution)/shard_map/ppermute | solution.py:1057
  334.8 3.7 collective-permute-done.16
  339.3 3.4 collective-permute-done.21
  343.2 6.0 %collective-permute-done.17 = bf16[1,256,256]{2,1,0:T(8,128)(2,1)S(1)} collective-permute-done((bf16[1,256,256]{2,1,0:T(8,128)(2,1)S(1)}, bf16[1,256,256]{2,1,0:T(8,128)(2,1)S(1)}, u32[]{:S(2)}, u32[]{:S(2)}) %collective-permute-start.17) | collective-permute-done | bytes 131104 | tf_op jit(solution)/shard_map/ppermute | solution.py:1057
  349.3 7.0 %join_rows.1 = f32[2048,1024]{1,0:T(8,128)} custom-call(s32[4]{0:T(128)} %pad_add_fusion.ids, bf16[8,128,1024]{2,1,0:T(8,128)(2,1)} %copy-done.6, bf16[8,128,1024]{2,1,0:T(8,128)(2,1)} %collective-permute-done.27.got_ref), custom_call_target="tpu_custom_call" | custom-call | tf_op jit(solution)/shard_map/join_rows/pallas_call | solution.py:920
  356.4 1.3 collective-permute-start.28
  360.1 7.1 %join_cols.1 = f32[512,4096]{1,0:T(8,128)} custom-call(s32[4]{0:T(128)} %pad_add_fusion.ids, bf16[8,2,64,1024]{3,2,1,0:T(8,128)(2,1)} %copy-done.7, bf16[8,2,64,1024]{3,2,1,0:T(8,128)(2,1)} %collective-permute-done.35.got_ref), custom_call_target="tpu_custom_call" | custom-call | tf_op jit(solution)/shard_map/join_cols/pallas_call | solution.py:937
  368.9 2.1 fusion.4
  372.0 3.4 token_grad.1
  375.4 2.0 collective-permute-done.36
  379.1 3.8 collective-permute-done.42.ag_ref
  382.9 6.6 %unpack.1 = (f32[512,3072]{1,0:T(8,128)}, f32[2,256,1024]{2,1,0:T(8,128)}, f32[8,8,256]{2,1,0:T(8,128)}) custom-call(s32[4]{0:T(128)} %pad_add_fusion.ids, bf16[8,256,256]{2,1,0:T(8,128)(2,1)} %copy-done.11, bf16[8,256,256]{2,1,0:T(8,128)(2,1)} %collective-permute-done.42.ag_ref, bf16[8,264,256]{2,1,0:T(8,128)(2,1)} %copy-done.10, ...), custom_call_target="tpu_custom_call" | custom-call | tf_op jit(solution)/shard_map/unpack/pallas_call | solution.py:981
  (200 shorter events, 34.3 us)
Async XLA Ops:
  0.6 102.8 %copy-start = (bf16[512,1024]{1,0:T(8,128)(2,1)S(1)}, bf16[512,1024]{1,0:T(8,128)(2,1)}, u32[]{:S(2)}) copy-start(bf16[512,1024]{1,0:T(8,128)(2,1)} %param.23) | copy-start | bytes 3145732
  0.7 7.5 %copy-start.22 = (s32[32]{0:T(128)S(1)}, s32[32]{0:T(128)}, u32[]{:S(2)}) copy-start(s32[32]{0:T(128)} %a_0_.3) | copy-start | bytes 388
  0.7 16.4 %collective-permute-start = (bf16[256,1024]{1,0:T(8,128)(2,1)}, bf16[256,1024]{1,0:T(8,128)(2,1)}, u32[]{:S(2)}, u32[]{:S(2)}) collective-permute-start(bf16[256,1024]{1,0:T(8,128)(2,1)} %bitcast.176), channel_id=1, source_target_pairs={{0,1},{1,0},{2,3},{3,2},{4,5},{5,4},{6,7},{7,6},{8,9},{9,8},{10,11... | collective-permute-start | bytes 1572872 | tf_op jit(solution)/shard_map/ppermute | solution.py:1054
  3.8 14.1 %collective-permute-start.4 = (bf16[256,1024]{1,0:T(8,128)(2,1)}, bf16[256,1024]{1,0:T(8,128)(2,1)}, u32[]{:S(2)}, u32[]{:S(2)}) collective-permute-start(bf16[256,1024]{1,0:T(8,128)(2,1)} %bitcast.177), channel_id=1, source_target_pairs={{0,2},{2,0},{4,6},{6,4},{8,10},{10,8},{12,14},{14,12},{16,18},{18,... | collective-permute-start | bytes 1572872 | tf_op jit(solution)/shard_map/ppermute | solution.py:1057
  5.7 27.5 %copy-start.16 = (bf16[1,256,1024]{2,1,0:T(8,128)(2,1)S(1)}, bf16[1,256,1024]{2,1,0:T(8,128)(2,1)}, u32[]{:S(2)}) copy-start(bf16[1,256,1024]{2,1,0:T(8,128)(2,1)} %param.31) | copy-start | bytes 1572868
  6.2 10.9 %collective-permute-start.2 = (bf16[10,512]{1,0:T(8,128)(2,1)S(1)}, bf16[10,512]{1,0:T(8,128)(2,1)S(1)}, u32[]{:S(2)}, u32[]{:S(2)}) collective-permute-start(bf16[10,512]{1,0:T(8,128)(2,1)S(1)} %concatenate.150), channel_id=1, source_target_pairs={{0,1},{1,0},{2,3},{3,2},{4,5},{5,4},{6,7},{7,6},{8,9},{9,8},{10,11... | collective-permute-start | bytes 30728 | tf_op jit(solution)/shard_map/ppermute | solution.py:1054
  6.3 26.8 %collective-permute-start.3 = (bf16[512,768]{1,0:T(8,128)(2,1)S(1)}, bf16[512,768]{1,0:T(8,128)(2,1)S(1)}, u32[]{:S(2)}, u32[]{:S(2)}) collective-permute-start(bf16[512,768]{1,0:T(8,128)(2,1)S(1)} %pad_maximum_fusion), channel_id=1, source_target_pairs={{0,1},{1,0},{2,3},{3,2},{4,5},{5,4},{6,7},{7,6},{8,9},{9,8},{10,11... | collective-permute-start | bytes 2359304 | tf_op jit(solution)/shard_map/ppermute | solution.py:1054
  17.1 18.3 %collective-permute-start.1 = (bf16[256,1024]{1,0:T(8,128)(2,1)}, bf16[256,1024]{1,0:T(8,128)(2,1)}, u32[]{:S(2)}, u32[]{:S(2)}) collective-permute-start(bf16[256,1024]{1,0:T(8,128)(2,1)} %collective-permute-done.a_ref), channel_id=1, source_target_pairs={{0,2},{2,0},{4,6},{6,4},{8,10},{10,8},{12,14},{14,12},{16,18},{18,... | collective-permute-start | bytes 1572872 | tf_op jit(solution)/shard_map/ppermute | solution.py:1057
  33.1 6.3 %copy-start.2 = (bf16[512,768]{1,0:T(8,128)(2,1)}, bf16[512,768]{1,0:T(8,128)(2,1)S(1)}, u32[]{:S(2)}) copy-start(bf16[512,768]{1,0:T(8,128)(2,1)S(1)} %collective-permute-done.3.gq_ref.gk_ref.gv_ref) | copy-start | bytes 2359300
  33.1 20.0 %collective-permute-start.6 = (bf16[256,1024]{1,0:T(8,128)(2,1)S(1)}, bf16[256,1024]{1,0:T(8,128)(2,1)}, u32[]{:S(2)}, u32[]{:S(2)}) collective-permute-start(bf16[256,1024]{1,0:T(8,128)(2,1)S(1)} %bitcast.187), channel_id=1, source_target_pairs={{0,1},{1,0},{2,3},{3,2},{4,5},{5,4},{6,7},{7,6},{8,9},{9,8},{10,11... | collective-permute-start | bytes 1572872 | tf_op jit(solution)/shard_map/ppermute | solution.py:1054
  45.0 8.7 %copy-start.20 = (bf16[2048]{0:T(1024)(128)(2,1)S(1)}, bf16[2048]{0:T(1024)(128)(2,1)}, u32[]{:S(2)}) copy-start(bf16[2048]{0:T(1024)(128)(2,1)} %param.26) | copy-start | bytes 12292
  45.0 55.2 %all-to-all-start = ((bf16[8,192,512]{2,1,0:T(8,128)(2,1)}), bf16[8,192,512]{2,1,0:T(8,128)(2,1)S(1)}, u32[]{:S(2)}, u32[]{:S(2)}) async-start(bf16[8,192,512]{2,1,0:T(8,128)(2,1)} %bitcast.173), calls=%async_computation | async-start | bytes 3145728 | tf_op jit(solution)/shard_map/all_to_all | solution.py:1081
  53.2 23.8 %collective-permute-start.8 = (bf16[512,1024]{1,0:T(8,128)(2,1)}, bf16[512,1024]{1,0:T(8,128)(2,1)}, u32[]{:S(2)}, u32[]{:S(2)}) collective-permute-start(bf16[512,1024]{1,0:T(8,128)(2,1)} %constant_dynamic-slice_fusion.5), channel_id=1, source_target_pairs={{0,1},{1,0},{2,3},{3,2},{4,5},{5,4},{6,7},{7,6},{8,9},{9,8},{10,11... | collective-permute-start | bytes 3145736 | tf_op jit(solution)/shard_map/ppermute | solution.py:1054
  53.7 7.4 %collective-permute-start.5 = (bf16[256,1024]{1,0:T(8,128)(2,1)S(1)}, bf16[256,1024]{1,0:T(8,128)(2,1)}, u32[]{:S(2)}, u32[]{:S(2)}) collective-permute-start(bf16[256,1024]{1,0:T(8,128)(2,1)S(1)} %bitcast.188), channel_id=1, source_target_pairs={{0,2},{2,0},{4,6},{6,4},{8,10},{10,8},{12,14},{14,12},{16,18},{18,... | collective-permute-start | bytes 1572872 | tf_op jit(solution)/shard_map/ppermute | solution.py:1057
  54.9 6.2 %collective-permute-start.7 = (bf16[256,1024]{1,0:T(8,128)(2,1)}, bf16[256,1024]{1,0:T(8,128)(2,1)}, u32[]{:S(2)}, u32[]{:S(2)}) collective-permute-start(bf16[256,1024]{1,0:T(8,128)(2,1)} %collective-permute-done.6.c_ref), channel_id=1, source_target_pairs={{0,2},{2,0},{4,6},{6,4},{8,10},{10,8},{12,14},{14,12},{16,18},{18,... | collective-permute-start | bytes 1572872 | tf_op jit(solution)/shard_map/ppermute | solution.py:1057
  100.1 6.4 %copy-start.4 = (bf16[8,192,512]{2,1,0:T(8,128)(2,1)}, bf16[8,192,512]{2,1,0:T(8,128)(2,1)S(1)}, u32[]{:S(2)}) copy-start(bf16[8,192,512]{2,1,0:T(8,128)(2,1)S(1)} %all-to-all-done.a_1_) | copy-start | bytes 4718596
  100.2 33.5 %collective-permute-start.9 = (bf16[4,128,1024]{2,1,0:T(8,128)(2,1)}, bf16[4,128,1024]{2,1,0:T(8,128)(2,1)}, u32[]{:S(2)}, u32[]{:S(2)}) collective-permute-start(bf16[4,128,1024]{2,1,0:T(8,128)(2,1)} %get-tuple-element.87), channel_id=1, source_target_pairs={{0,4},{2,6},{4,0},{6,2},{8,12},{10,14},{12,8},{14,10},{16,20},{18,... | collective-permute-start | bytes 3145736 | tf_op jit(solution)/shard_map/ppermute | solution.py:1057
  102.0 31.7 %collective-permute-start.10 = (bf16[4,128,1024]{2,1,0:T(8,128)(2,1)}, bf16[4,128,1024]{2,1,0:T(8,128)(2,1)}, u32[]{:S(2)}, u32[]{:S(2)}) collective-permute-start(bf16[4,128,1024]{2,1,0:T(8,128)(2,1)} %get-tuple-element.88), channel_id=1, source_target_pairs={{0,8},{2,10},{4,12},{6,14},{8,0},{10,2},{12,4},{14,6},{16,24},{18,... | collective-permute-start | bytes 3145736 | tf_op jit(solution)/shard_map/ppermute | solution.py:1057
  106.6 27.1 %all-to-all-start.1 = ((bf16[8,64,512]{2,1,0:T(8,128)(2,1)}), bf16[8,64,512]{2,1,0:T(8,128)(2,1)S(1)}, u32[]{:S(2)}, u32[]{:S(2)}) async-start(bf16[8,64,512]{2,1,0:T(8,128)(2,1)} %bitcast.206), calls=%async_computation.1 | async-start | bytes 1048576 | tf_op jit(solution)/shard_map/all_to_all | solution.py:1081
  110.2 27.8 %copy-start.18 = (bf16[4,128,1024]{2,1,0:T(8,128)(2,1)S(1)}, bf16[4,128,1024]{2,1,0:T(8,128)(2,1)}, u32[]{:S(2)}) copy-start(bf16[4,128,1024]{2,1,0:T(8,128)(2,1)} %get-tuple-element.94) | copy-start | bytes 3145732
  133.7 10.6 %copy-start.13 = (bf16[8,64,512]{2,1,0:T(8,128)(2,1)}, bf16[8,64,512]{2,1,0:T(8,128)(2,1)S(1)}, u32[]{:S(2)}) copy-start(bf16[8,64,512]{2,1,0:T(8,128)(2,1)S(1)} %all-to-all-done.1.a_3_) | copy-start | bytes 1572868
  133.7 47.9 %all-to-all-start.2 = ((bf16[8,64,512]{2,1,0:T(8,128)(2,1)}), bf16[8,64,512]{2,1,0:T(8,128)(2,1)S(1)}, u32[]{:S(2)}, u32[]{:S(2)}) async-start(bf16[8,64,512]{2,1,0:T(8,128)(2,1)} %get-tuple-element.90.a_2_), calls=%async_computation.2 | async-start | bytes 1048576 | tf_op jit(solution)/shard_map/all_to_all | solution.py:1081
  140.0 41.5 %collective-permute-start.11 = (bf16[2,128,1024]{2,1,0:T(8,128)(2,1)}, bf16[2,128,1024]{2,1,0:T(8,128)(2,1)}, u32[]{:S(2)}, u32[]{:S(2)}) collective-permute-start(bf16[2,128,1024]{2,1,0:T(8,128)(2,1)} %fusion.5), channel_id=1, source_target_pairs={{0,8},{2,10},{4,12},{6,14},{8,0},{10,2},{12,4},{14,6},{16,24},{18,... | collective-permute-start | bytes 1572872 | tf_op jit(solution)/shard_map/ppermute | solution.py:1057
  144.3 37.3 %collective-permute-start.12 = (bf16[2,128,1024]{2,1,0:T(8,128)(2,1)}, bf16[2,128,1024]{2,1,0:T(8,128)(2,1)}, u32[]{:S(2)}, u32[]{:S(2)}) collective-permute-start(bf16[2,128,1024]{2,1,0:T(8,128)(2,1)} %fusion.6), channel_id=1, source_target_pairs={{0,16},{2,18},{4,20},{6,22},{8,24},{10,26},{12,28},{14,30},{16,0},... | collective-permute-start | bytes 1572872 | tf_op jit(solution)/shard_map/ppermute | solution.py:1057
  181.6 11.3 %copy-start.8 = (bf16[8,64,512]{2,1,0:T(8,128)(2,1)}, bf16[8,64,512]{2,1,0:T(8,128)(2,1)S(1)}, u32[]{:S(2)}) copy-start(bf16[8,64,512]{2,1,0:T(8,128)(2,1)S(1)} %all-to-all-done.2) | copy-start | bytes 1572868
  181.6 94.4 %all-to-all-start.3 = ((bf16[8,192,512]{2,1,0:T(8,128)(2,1)}), bf16[8,192,512]{2,1,0:T(8,128)(2,1)}, u32[]{:S(2)}, u32[]{:S(2)}) async-start(bf16[8,192,512]{2,1,0:T(8,128)(2,1)} %attn_bwd.1), calls=%async_computation.3 | async-start | bytes 3145728 | tf_op jit(solution)/shard_map/all_to_all | solution.py:1081
  186.1 6.7 %copy-start.15 = (bf16[1024,1024]{1,0:T(8,128)(2,1)S(1)}, bf16[1024,1024]{1,0:T(8,128)(2,1)}, u32[]{:S(2)}) copy-start(bf16[1024,1024]{1,0:T(8,128)(2,1)} %get-tuple-element.112) | copy-start | bytes 6291460
  187.5 42.1 %collective-permute-start.23 = (bf16[1,128,1024]{2,1,0:T(8,128)(2,1)S(1)}, bf16[1,128,1024]{2,1,0:T(8,128)(2,1)S(1)}, u32[]{:S(2)}, u32[]{:S(2)}) collective-permute-start(bf16[1,128,1024]{2,1,0:T(8,128)(2,1)S(1)} %fusion.12), channel_id=1, source_target_pairs={{0,16},{2,18},{4,20},{6,22},{8,24},{10,26},{12,28},{14,30},{16,0},... | collective-permute-start | bytes 786440 | tf_op jit(solution)/shard_map/ppermute | solution.py:1057
  191.3 13.5 %collective-permute-start.30 = (bf16[1,128,1024]{2,1,0:T(8,128)(2,1)S(1)}, bf16[1,128,1024]{2,1,0:T(8,128)(2,1)S(1)}, u32[]{:S(2)}, u32[]{:S(2)}) collective-permute-start(bf16[1,128,1024]{2,1,0:T(8,128)(2,1)S(1)} %fusion.9), channel_id=1, source_target_pairs={{0,4},{2,6},{4,0},{6,2},{8,12},{10,14},{12,8},{14,10},{16,20},{18,... | collective-permute-start | bytes 786440 | tf_op jit(solution)/shard_map/ppermute | solution.py:1057
  193.6 39.9 %copy-start.5 = (f32[2,512,1024]{2,1,0:T(8,128)}, f32[2,512,1024]{2,1,0:T(8,128)S(1)}, u32[]{:S(2)}) copy-start(f32[2,512,1024]{2,1,0:T(8,128)S(1)} %convert_add_fusion) | copy-start | bytes 12582916
  206.2 24.6 %collective-permute-start.31 = (bf16[1,1,64,1024]{3,2,1,0:T(8,128)(2,1)S(1)}, bf16[1,1,64,1024]{3,2,1,0:T(8,128)(2,1)S(1)}, u32[]{:S(2)}, u32[]{:S(2)}) collective-permute-start(bf16[1,1,64,1024]{3,2,1,0:T(8,128)(2,1)S(1)} %get-tuple-element.130), channel_id=1, source_target_pairs={{0,1},{1,0},{2,3},{3,2},{4,5},{5,4},{6,7},{7,6},{8,9},{9,8},{10,11... | collective-permute-start | bytes 393224 | tf_op jit(solution)/shard_map/ppermute | solution.py:1054
  230.7 11.2 %collective-permute-start.24 = (bf16[1,128,1024]{2,1,0:T(8,128)(2,1)S(1)}, bf16[1,128,1024]{2,1,0:T(8,128)(2,1)S(1)}, u32[]{:S(2)}, u32[]{:S(2)}) collective-permute-start(bf16[1,128,1024]{2,1,0:T(8,128)(2,1)S(1)} %fusion.14), channel_id=1, source_target_pairs={{0,16},{2,18},{4,20},{6,22},{8,24},{10,26},{12,28},{14,30},{16,0},... | collective-permute-start | bytes 786440 | tf_op jit(solution)/shard_map/ppermute | solution.py:1057
  230.8 11.2 %collective-permute-start.32 = (bf16[1,2,64,1024]{3,2,1,0:T(8,128)(2,1)S(1)}, bf16[1,2,64,1024]{3,2,1,0:T(8,128)(2,1)}, u32[]{:S(2)}, u32[]{:S(2)}) collective-permute-start(bf16[1,2,64,1024]{3,2,1,0:T(8,128)(2,1)S(1)} %maximum_select_fusion.12), channel_id=1, source_target_pairs={{0,4},{2,6},{4,0},{6,2},{8,12},{10,14},{12,8},{14,10},{16,20},{18,... | collective-permute-start | bytes 786440 | tf_op jit(solution)/shard_map/ppermute | solution.py:1057
  233.5 40.3 %collective-permute-start.40 = (bf16[2,256,1024]{2,1,0:T(8,128)(2,1)}, bf16[2,256,1024]{2,1,0:T(8,128)(2,1)}, u32[]{:S(2)}, u32[]{:S(2)}) collective-permute-start(bf16[2,256,1024]{2,1,0:T(8,128)(2,1)} %dynamic-slice_convert_fusion), channel_id=1, source_target_pairs={{0,2},{2,0},{4,6},{6,4},{8,10},{10,8},{12,14},{14,12},{16,18},{18,... | collective-permute-start | bytes 3145736 | tf_op jit(solution)/shard_map/ppermute | solution.py:1057
  233.5 36.0 %copy-start.3 = (bf16[1024,1024]{1,0:T(8,128)(2,1)S(1)}, bf16[1024,1024]{1,0:T(8,128)(2,1)}, u32[]{:S(2)}) copy-start(bf16[1024,1024]{1,0:T(8,128)(2,1)} %get-tuple-element.77.ain_ref) | copy-start | bytes 6291460
  242.0 21.0 %collective-permute-start.25 = (bf16[2,128,1024]{2,1,0:T(8,128)(2,1)S(1)}, bf16[2,128,1024]{2,1,0:T(8,128)(2,1)}, u32[]{:S(2)}, u32[]{:S(2)}) collective-permute-start(bf16[2,128,1024]{2,1,0:T(8,128)(2,1)S(1)} %maximum_select_fusion.7), channel_id=1, source_target_pairs={{0,8},{2,10},{4,12},{6,14},{8,0},{10,2},{12,4},{14,6},{16,24},{18,... | collective-permute-start | bytes 1572872 | tf_op jit(solution)/shard_map/ppermute | solution.py:1057
  243.2 28.9 %copy-start.14 = (bf16[2,2,64,1024]{3,2,1,0:T(8,128)(2,1)}, bf16[2,2,64,1024]{3,2,1,0:T(8,128)(2,1)S(1)}, u32[]{:S(2)}) copy-start(bf16[2,2,64,1024]{3,2,1,0:T(8,128)(2,1)S(1)} %maximum_select_fusion.9) | copy-start | bytes 1572868
  243.2 28.8 %collective-permute-start.33 = (bf16[2,2,64,1024]{3,2,1,0:T(8,128)(2,1)S(1)}, bf16[2,2,64,1024]{3,2,1,0:T(8,128)(2,1)}, u32[]{:S(2)}, u32[]{:S(2)}) collective-permute-start(bf16[2,2,64,1024]{3,2,1,0:T(8,128)(2,1)S(1)} %maximum_select_fusion.9), channel_id=1, source_target_pairs={{0,16},{2,18},{4,20},{6,22},{8,24},{10,26},{12,28},{14,30},{16,0},... | collective-permute-start | bytes 1572872 | tf_op jit(solution)/shard_map/ppermute | solution.py:1057
  265.4 29.2 %collective-permute-start.26 = (bf16[4,128,1024]{2,1,0:T(8,128)(2,1)}, bf16[4,128,1024]{2,1,0:T(8,128)(2,1)}, u32[]{:S(2)}, u32[]{:S(2)}) collective-permute-start(bf16[4,128,1024]{2,1,0:T(8,128)(2,1)} %maximum_select_fusion.3), channel_id=1, source_target_pairs={{0,4},{2,6},{4,0},{6,2},{8,12},{10,14},{12,8},{14,10},{16,20},{18,... | collective-permute-start | bytes 3145736 | tf_op jit(solution)/shard_map/ppermute | solution.py:1057
  273.7 40.6 %collective-permute-start.34 = (bf16[4,2,64,1024]{3,2,1,0:T(8,128)(2,1)S(1)}, bf16[4,2,64,1024]{3,2,1,0:T(8,128)(2,1)}, u32[]{:S(2)}, u32[]{:S(2)}) collective-permute-start(bf16[4,2,64,1024]{3,2,1,0:T(8,128)(2,1)S(1)} %maximum_select_fusion.4), channel_id=1, source_target_pairs={{0,8},{2,10},{4,12},{6,14},{8,0},{10,2},{12,4},{14,6},{16,24},{18,... | collective-permute-start | bytes 3145736 | tf_op jit(solution)/shard_map/ppermute | solution.py:1057
  290.9 12.7 %collective-permute-start.13 = (bf16[4,256,256]{2,1,0:T(8,128)(2,1)S(1)}, bf16[4,256,256]{2,1,0:T(8,128)(2,1)S(1)}, u32[]{:S(2)}, u32[]{:S(2)}) collective-permute-start(bf16[4,256,256]{2,1,0:T(8,128)(2,1)S(1)} %get-tuple-element.128), channel_id=1, source_target_pairs={{0,4},{2,6},{4,0},{6,2},{8,12},{10,14},{12,8},{14,10},{16,20},{18,... | collective-permute-start | bytes 1572872 | tf_op jit(solution)/shard_map/ppermute | solution.py:1057
  291.2 21.8 %collective-permute-start.18 = (bf16[4,264,256]{2,1,0:T(8,128)(2,1)S(1)}, bf16[4,264,256]{2,1,0:T(8,128)(2,1)S(1)}, u32[]{:S(2)}, u32[]{:S(2)}) collective-permute-start(bf16[4,264,256]{2,1,0:T(8,128)(2,1)S(1)} %get-tuple-element.126), channel_id=1, source_target_pairs={{0,8},{2,10},{4,12},{6,14},{8,0},{10,2},{12,4},{14,6},{16,24},{18,... | collective-permute-start | bytes 1622024 | tf_op jit(solution)/shard_map/ppermute | solution.py:1057
  294.1 74.8 %collective-permute-start.41 = (bf16[256,1024]{1,0:T(8,128)(2,1)}, bf16[256,1024]{1,0:T(8,128)(2,1)}, u32[]{:S(2)}, u32[]{:S(2)}) collective-permute-start(bf16[256,1024]{1,0:T(8,128)(2,1)} %fusion.8), channel_id=1, source_target_pairs={{0,1},{1,0},{2,3},{3,2},{4,5},{5,4},{6,7},{7,6},{8,9},{9,8},{10,11... | collective-permute-start | bytes 1572872 | tf_op jit(solution)/shard_map/ppermute | solution.py:1054
  297.3 18.9 %copy-start.6 = (bf16[8,128,1024]{2,1,0:T(8,128)(2,1)}, bf16[8,128,1024]{2,1,0:T(8,128)(2,1)S(1)}, u32[]{:S(2)}) copy-start(bf16[8,128,1024]{2,1,0:T(8,128)(2,1)S(1)} %maximum_select_fusion.own_ref) | copy-start | bytes 6291460
  297.3 52.0 %collective-permute-start.27 = (bf16[8,128,1024]{2,1,0:T(8,128)(2,1)S(1)}, bf16[8,128,1024]{2,1,0:T(8,128)(2,1)}, u32[]{:S(2)}, u32[]{:S(2)}) collective-permute-start(bf16[8,128,1024]{2,1,0:T(8,128)(2,1)S(1)} %maximum_select_fusion.own_ref), channel_id=1, source_target_pairs={{0,2},{2,0},{4,6},{6,4},{8,10},{10,8},{12,14},{14,12},{16,18},{18,... | collective-permute-start | bytes 6291464 | tf_op jit(solution)/shard_map/ppermute | solution.py:1057
  303.6 14.4 %collective-permute-start.14 = (bf16[2,256,256]{2,1,0:T(8,128)(2,1)S(1)}, bf16[2,256,256]{2,1,0:T(8,128)(2,1)S(1)}, u32[]{:S(2)}, u32[]{:S(2)}) collective-permute-start(bf16[2,256,256]{2,1,0:T(8,128)(2,1)S(1)} %fusion.23), channel_id=1, source_target_pairs={{0,8},{2,10},{4,12},{6,14},{8,0},{10,2},{12,4},{14,6},{16,24},{18,... | collective-permute-start | bytes 786440 | tf_op jit(solution)/shard_map/ppermute | solution.py:1057
  313.0 14.5 %collective-permute-start.19 = (bf16[2,264,256]{2,1,0:T(8,128)(2,1)S(1)}, bf16[2,264,256]{2,1,0:T(8,128)(2,1)S(1)}, u32[]{:S(2)}, u32[]{:S(2)}) collective-permute-start(bf16[2,264,256]{2,1,0:T(8,128)(2,1)S(1)} %fusion.19), channel_id=1, source_target_pairs={{0,16},{2,18},{4,20},{6,22},{8,24},{10,26},{12,28},{14,30},{16,0},... | collective-permute-start | bytes 811016 | tf_op jit(solution)/shard_map/ppermute | solution.py:1057
  316.2 18.6 %copy-start.7 = (bf16[8,2,64,1024]{3,2,1,0:T(8,128)(2,1)}, bf16[8,2,64,1024]{3,2,1,0:T(8,128)(2,1)S(1)}, u32[]{:S(2)}) copy-start(bf16[8,2,64,1024]{3,2,1,0:T(8,128)(2,1)S(1)} %maximum_select_fusion.1.own_ref) | copy-start | bytes 6291460
  316.2 43.9 %collective-permute-start.35 = (bf16[8,2,64,1024]{3,2,1,0:T(8,128)(2,1)S(1)}, bf16[8,2,64,1024]{3,2,1,0:T(8,128)(2,1)}, u32[]{:S(2)}, u32[]{:S(2)}) collective-permute-start(bf16[8,2,64,1024]{3,2,1,0:T(8,128)(2,1)S(1)} %maximum_select_fusion.1.own_ref), channel_id=1, source_target_pairs={{0,2},{2,0},{4,6},{6,4},{8,10},{10,8},{12,14},{14,12},{16,18},{18,... | collective-permute-start | bytes 6291464 | tf_op jit(solution)/shard_map/ppermute | solution.py:1057
  318.1 10.9 %collective-permute-start.15 = (bf16[1,256,256]{2,1,0:T(8,128)(2,1)S(1)}, bf16[1,256,256]{2,1,0:T(8,128)(2,1)S(1)}, u32[]{:S(2)}, u32[]{:S(2)}) collective-permute-start(bf16[1,256,256]{2,1,0:T(8,128)(2,1)S(1)} %fusion.24), channel_id=1, source_target_pairs={{0,16},{2,18},{4,20},{6,22},{8,24},{10,26},{12,28},{14,30},{16,0},... | collective-permute-start | bytes 393224 | tf_op jit(solution)/shard_map/ppermute | solution.py:1057
  327.6 15.2 %collective-permute-start.38 = (bf16[2,256,1024]{2,1,0:T(8,128)(2,1)S(1)}, bf16[2,256,1024]{2,1,0:T(8,128)(2,1)S(1)}, u32[]{:S(2)}, u32[]{:S(2)}) collective-permute-start(bf16[2,256,1024]{2,1,0:T(8,128)(2,1)S(1)} %dynamic-slice_convert_fusion.1), channel_id=1, source_target_pairs={{0,2},{2,0},{4,6},{6,4},{8,10},{10,8},{12,14},{14,12},{16,18},{18,... | collective-permute-start | bytes 3145736 | tf_op jit(solution)/shard_map/ppermute | solution.py:1057
  329.0 5.0 %collective-permute-start.20 = (bf16[1,264,256]{2,1,0:T(8,128)(2,1)S(1)}, bf16[1,264,256]{2,1,0:T(8,128)(2,1)S(1)}, u32[]{:S(2)}, u32[]{:S(2)}) collective-permute-start(bf16[1,264,256]{2,1,0:T(8,128)(2,1)S(1)} %fusion.20), channel_id=1, source_target_pairs={{0,4},{2,6},{4,0},{6,2},{8,12},{10,14},{12,8},{14,10},{16,20},{18,... | collective-permute-start | bytes 405512 | tf_op jit(solution)/shard_map/ppermute | solution.py:1057
  334.0 4.6 %collective-permute-start.16 = (bf16[96,256]{1,0:T(8,128)(2,1)S(1)}, bf16[96,256]{1,0:T(8,128)(2,1)S(1)}, u32[]{:S(2)}, u32[]{:S(2)}) collective-permute-start(bf16[96,256]{1,0:T(8,128)(2,1)S(1)} %get-tuple-element.134), channel_id=1, source_target_pairs={{0,1},{1,0},{2,3},{3,2},{4,5},{5,4},{6,7},{7,6},{8,9},{9,8},{10,11... | collective-permute-start | bytes 147464 | tf_op jit(solution)/shard_map/ppermute | solution.py:1054
  338.5 4.1 %collective-permute-start.21 = (bf16[104,256]{1,0:T(8,128)(2,1)S(1)}, bf16[104,256]{1,0:T(8,128)(2,1)S(1)}, u32[]{:S(2)}, u32[]{:S(2)}) collective-permute-start(bf16[104,256]{1,0:T(8,128)(2,1)S(1)} %pad_maximum_fusion.2), channel_id=1, source_target_pairs={{0,1},{1,0},{2,3},{3,2},{4,5},{5,4},{6,7},{7,6},{8,9},{9,8},{10,11... | collective-permute-start | bytes 159752 | tf_op jit(solution)/shard_map/ppermute | solution.py:1054
  342.7 6.6 %collective-permute-start.17 = (bf16[1,256,256]{2,1,0:T(8,128)(2,1)S(1)}, bf16[1,256,256]{2,1,0:T(8,128)(2,1)S(1)}, u32[]{:S(2)}, u32[]{:S(2)}) collective-permute-start(bf16[1,256,256]{2,1,0:T(8,128)(2,1)S(1)} %maximum_bitcast_fusion.1), channel_id=1, source_target_pairs={{0,16},{2,18},{4,20},{6,22},{8,24},{10,26},{12,28},{14,30},{16,0},... | collective-permute-start | bytes 393224 | tf_op jit(solution)/shard_map/ppermute | solution.py:1057
  342.7 6.5 %collective-permute-start.22 = (bf16[1,264,256]{2,1,0:T(8,128)(2,1)S(1)}, bf16[1,264,256]{2,1,0:T(8,128)(2,1)S(1)}, u32[]{:S(2)}, u32[]{:S(2)}) collective-permute-start(bf16[1,264,256]{2,1,0:T(8,128)(2,1)S(1)} %maximum_bitcast_fusion), channel_id=1, source_target_pairs={{0,4},{2,6},{4,0},{6,2},{8,12},{10,14},{12,8},{14,10},{16,20},{18,... | collective-permute-start | bytes 405512 | tf_op jit(solution)/shard_map/ppermute | solution.py:1057
  356.4 10.9 %collective-permute-start.28 = (bf16[2,256,256]{2,1,0:T(8,128)(2,1)S(1)}, bf16[2,256,256]{2,1,0:T(8,128)(2,1)S(1)}, u32[]{:S(2)}, u32[]{:S(2)}) collective-permute-start(bf16[2,256,256]{2,1,0:T(8,128)(2,1)S(1)} %maximum_select_fusion.11), channel_id=1, source_target_pairs={{0,8},{2,10},{4,12},{6,14},{8,0},{10,2},{12,4},{14,6},{16,24},{18,... | collective-permute-start | bytes 786440 | tf_op jit(solution)/shard_map/ppermute | solution.py:1057
  357.7 10.4 %collective-permute-start.29 = (bf16[2,264,256]{2,1,0:T(8,128)(2,1)S(1)}, bf16[2,264,256]{2,1,0:T(8,128)(2,1)S(1)}, u32[]{:S(2)}, u32[]{:S(2)}) collective-permute-start(bf16[2,264,256]{2,1,0:T(8,128)(2,1)S(1)} %maximum_select_fusion.10), channel_id=1, source_target_pairs={{0,16},{2,18},{4,20},{6,22},{8,24},{10,26},{12,28},{14,30},{16,0},... | collective-permute-start | bytes 811016 | tf_op jit(solution)/shard_map/ppermute | solution.py:1057
  359.4 12.6 %collective-permute-start.39 = (bf16[256,1024]{1,0:T(8,128)(2,1)}, bf16[256,1024]{1,0:T(8,128)(2,1)}, u32[]{:S(2)}, u32[]{:S(2)}) collective-permute-start(bf16[256,1024]{1,0:T(8,128)(2,1)} %fusion.7), channel_id=1, source_target_pairs={{0,1},{1,0},{2,3},{3,2},{4,5},{5,4},{6,7},{7,6},{8,9},{9,8},{10,11... | collective-permute-start | bytes 1572872 | tf_op jit(solution)/shard_map/ppermute | solution.py:1054
  368.2 9.2 %collective-permute-start.36 = (bf16[4,256,256]{2,1,0:T(8,128)(2,1)S(1)}, bf16[4,256,256]{2,1,0:T(8,128)(2,1)S(1)}, u32[]{:S(2)}, u32[]{:S(2)}) collective-permute-start(bf16[4,256,256]{2,1,0:T(8,128)(2,1)S(1)} %maximum_select_fusion.8), channel_id=1, source_target_pairs={{0,4},{2,6},{4,0},{6,2},{8,12},{10,14},{12,8},{14,10},{16,20},{18,... | collective-permute-start | bytes 1572872 | tf_op jit(solution)/shard_map/ppermute | solution.py:1057
  368.6 9.8 %collective-permute-start.37 = (bf16[4,264,256]{2,1,0:T(8,128)(2,1)S(1)}, bf16[4,264,256]{2,1,0:T(8,128)(2,1)S(1)}, u32[]{:S(2)}, u32[]{:S(2)}) collective-permute-start(bf16[4,264,256]{2,1,0:T(8,128)(2,1)S(1)} %maximum_select_fusion.6), channel_id=1, source_target_pairs={{0,8},{2,10},{4,12},{6,14},{8,0},{10,2},{12,4},{14,6},{16,24},{18,... | collective-permute-start | bytes 1622024 | tf_op jit(solution)/shard_map/ppermute | solution.py:1057
  378.5 4.4 %collective-permute-start.43 = (bf16[8,264,256]{2,1,0:T(8,128)(2,1)S(1)}, bf16[8,264,256]{2,1,0:T(8,128)(2,1)}, u32[]{:S(2)}, u32[]{:S(2)}) collective-permute-start(bf16[8,264,256]{2,1,0:T(8,128)(2,1)S(1)} %maximum_select_fusion.2.bo_ref), channel_id=1, source_target_pairs={{0,2},{2,0},{4,6},{6,4},{8,10},{10,8},{12,14},{14,12},{16,18},{18,... | collective-permute-start | bytes 3244040 | tf_op jit(solution)/shard_map/ppermute | solution.py:1057
  378.6 4.3 %collective-permute-start.42 = (bf16[8,256,256]{2,1,0:T(8,128)(2,1)S(1)}, bf16[8,256,256]{2,1,0:T(8,128)(2,1)}, u32[]{:S(2)}, u32[]{:S(2)}) collective-permute-start(bf16[8,256,256]{2,1,0:T(8,128)(2,1)S(1)} %maximum_select_fusion.5.ao_ref), channel_id=1, source_target_pairs={{0,2},{2,0},{4,6},{6,4},{8,10},{10,8},{12,14},{14,12},{16,18},{18,... | collective-permute-start | bytes 3145736 | tf_op jit(solution)/shard_map/ppermute | solution.py:1057
  379.1 13.8 %copy-start.1 = (bf16[512,1024]{1,0:T(8,128)(2,1)S(1)}, bf16[512,1024]{1,0:T(8,128)(2,1)}, u32[]{:S(2)}) copy-start(bf16[512,1024]{1,0:T(8,128)(2,1)} %param.23) | copy-start | bytes 3145732
  (13 other events, 54.4 us)

commit v6 on v5

--- a/solution.py
+++ b/solution.py
@@ -402,7 +402,7 @@
         kt_s[pl.ds(d,HB),:]=x_ref[c,64:128,pl.ds(l,HB)].astype(f32).T.astype(bf16)
         v_s[:,pl.ds(d,HB)]=x_ref[c,128:192,pl.ds(l,HB)]
         return 0
-    lax.fori_loop(0,nblk,perm,0)
+    lax.fori_loop(0,nblk,perm,0,unroll=32)
     S=nblk*HB; nq=S//bq; r=bq//bk
     def step(q,qo,ko,carry,mask):
         m,l,acc=carry
@@ -430,7 +430,7 @@
         p=bm[i]; c=i//per; l=pl.multiple_of((i%per)*HB,HB); d=pl.multiple_of(p*HB,HB)
         o_ref[c,:,pl.ds(l,HB)]=q_s[:,pl.ds(d,HB)]
         return 0
-    lax.fori_loop(0,nblk,unperm,0)
+    lax.fori_loop(0,nblk,unperm,0,unroll=32)
 
 def attn_fwd(bm,x,*,bq=512,bk=512):
     n=x.shape[0]; S=n*x.shape[2]; nblk=S//HB
@@ -455,7 +455,7 @@
         do_s[:,pl.ds(d,HB)]=do
         dl_s[:,pl.ds(d,HB)]=jnp.sum(do.astype(f32)*o_ref[c,:,pl.ds(l,HB)].astype(f32),axis=0,keepdims=True)
         return 0
-    lax.fori_loop(0,nblk,perm,0)
+    lax.fori_loop(0,nblk,perm,0,unroll=32)
     S=nblk*HB; nq=S//bq; r=bq//bk
     dk_s[...]=jnp.zeros_like(dk_s); dv_s[...]=jnp.zeros_like(dv_s)
     def step(q,do,lse,dl,ko,dq,mask):
@@ -489,7 +489,7 @@
             g_ref[c,64*n_:64*n_+64,pl.ds(l,HB)]=full.astype(bf16)
         g_ref[c,128:192,pl.ds(l,HB)]=dv_s[:,pl.ds(d,HB)].astype(bf16)
         return 0
-    lax.fori_loop(0,nblk,unperm,0)
+    lax.fori_loop(0,nblk,unperm,0,unroll=32)
 
 def attn_bwd(bm,x,o,do,lse,cs,*,bq=512,bk=512):
     n=x.shape[0]; S=n*x.shape[2]; nblk=S//HB
@@ -564,6 +564,27 @@
         cost_estimate=pl.CostEstimate(flops=0, transcendentals=0, bytes_accessed=1 << 20),
         name="norm_rows",
     )(ids, a, b, norms, *before)
+
+
+def turn_kernel(a_ref, b_ref, at_ref, bt_ref):
+    at_ref[...] = a_ref[...].astype(f32).T.astype(bf16)
+    bt_ref[...] = b_ref[...].astype(f32).T.astype(bf16)
+
+
+def turn(a, b, steps=4):
+    rows, width = a.shape
+    src = pl.BlockSpec((rows // steps, width), lambda i: (i, 0))
+    dst = pl.BlockSpec((width, rows // steps), lambda i: (0, i))
+    return pl.pallas_call(
+        turn_kernel,
+        grid=(steps,),
+        in_specs=[src, src],
+        out_specs=(dst, dst),
+        out_shape=(jax.ShapeDtypeStruct((width, rows), a.dtype),) * 2,
+        compiler_params=_params(),
+        cost_estimate=pl.CostEstimate(flops=0, transcendentals=0, bytes_accessed=1 << 20),
+        name="turn",
+    )(a, b)
 
 
 def mask_kernel(ids, a_ref, b_ref, c_ref, d_ref, live_ref, o_ref):
@@ -1133,10 +1154,10 @@
     dy2 = dy.reshape(2, rows, width)
     w_out_mine = rows_of(w_out, core * quarter, quarter)
     dctx = jnp.einsum("ed,std->set", w_out_mine, dy2, preferred_element_type=f32).astype(bf16)
-    attn_t = attn_in.T
+    attn_t, mlp_t = turn(attn_in, mlp_in)
     do_head = exchange(dctx.reshape(2 * heads, HD, rows))
     y_mlp, d_mlp, up_keep, up_send, down_keep, down_send, gb_up = mlp(
-        ids, mlp_in, mlp_in.T, dy, w_up, wu_got, w_down, b_up.astype(f32)[None, :], chips
+        ids, mlp_in, mlp_t, dy, w_up, wu_got, w_down, b_up.astype(f32)[None, :], chips
     )
 
     chain_a = (X, ZN, ZF)

time: 394 us -> 387 us (0.982)
  local copies, waits for them, and re-layouts: 22.4 us -> 14.9 us
    pallas_call x0 -> x1, Pallas kernels: none -> 4.97 us  [turn(): pl.pallas_call(turn_kernel, grid=(steps,), in_specs=[src, src], out_specs...]
    ppermute x34, starting transfers between devices: 28 us -> 32.5 us  [flip(): return lax.ppermute(v, 'ctx', [(i, i ^ 1 << bit) for i in range(n_ctx)])]
  transfers between devices with their start and end apart: 48 -> 48, of which waited for: 22 -> 22; matrix products, arithmetic and copies ran while one was open for 13% -> 11% of each run, Pallas kernels for 33% -> 33%
where the time goes in v6:
time: 387 us; the launch traced here: 386 us
  waiting for transfers between devices  140 us (36%)
  Pallas kernels  135 us (35%)
  starting transfers between devices  60.6 us (16%)
  other arithmetic  28.4 us (7%)
  local copies, waits for them, and re-layouts  14.9 us (4%)
  matrix products  3.91 us (1%)
    ppermute x34, waiting for transfers between devices, flip(): return lax.ppermute(v, 'ctx', [(i, i ^ 1 << bit) for i in range(n_ctx)])  101 us
    ppermute x10, waiting for transfers between devices, swap(): return lax.ppermute(v, 'wsh', SWAP)  34.4 us
    ppermute x34, starting transfers between devices, flip(): return lax.ppermute(v, 'ctx', [(i, i ^ 1 << bit) for i in range(n_ctx)])  32.5 us
    pallas_call x1, Pallas kernels, attn_bwd(): pl.pallas_call(lambda *a: attn_bwd_kernel(*a, nblk=nblk, per=x.shape[2] /...  32.2 us
    pallas_call x1, Pallas kernels, mlp(): pl.pallas_call(mlp_kernel, grid_spec=pltpu.PrefetchScalarGridSpec(num_sca...  23.2 us
    pallas_call x1, Pallas kernels, attn_fwd(): pl.pallas_call(lambda *a: attn_fwd_kernel(*a, nblk=nblk, per=x.shape[2] /...  18.6 us
    all_to_all x4, starting transfers between devices, exchange(): return lax.all_to_all(v, 'ctx', 0, 0, axis_index_groups=groups, tiled=False)  17.9 us
    pallas_call x1, Pallas kernels, qkv_backward(): pl.pallas_call(qkv_back_kernel, grid_spec=pltpu.PrefetchScalarGridSpec(nu...  13.5 us
  transfers between devices with their start and end apart: 48, of which 22 were waited for; matrix products, arithmetic and copies ran while one was open for 11% of the time, Pallas kernels for 33%

profile of v6, /device:TPU:0, one launch (start us, length us, event | category | flops | bytes accessed | tf_op | source)
XLA Modules:
  0.0 385.6 jit_solution(4431827986079097552)
XLA Ops:
  0.7 3.0 collective-permute-start
  6.3 1.9 collective-permute-start.3
  11.1 6.0 %collective-permute-done.2 = bf16[10,512]{1,0:T(8,128)(2,1)S(1)} collective-permute-done((bf16[10,512]{1,0:T(8,128)(2,1)S(1)}, bf16[10,512]{1,0:T(8,128)(2,1)S(1)}, u32[]{:S(2)}, u32[]{:S(2)}) %collective-permute-start.2) | collective-permute-done | bytes 10272 | tf_op jit(solution)/shard_map/ppermute | solution.py:1075
  17.9 3.9 %norm_rows.2 = (bf16[1024,1024]{1,0:T(8,128)(2,1)}, bf16[1024,1024]{1,0:T(8,128)(2,1)}, bf16[1024,1024]{1,0:T(8,128)(2,1)}) custom-call(s32[4]{0:T(128)} %pad_add_fusion.ids, bf16[256,1024]{1,0:T(8,128)(2,1)} %bitcast.175, bf16[256,1024]{1,0:T(8,128)(2,1)} %collective-permute-done.4.b_ref, f32[4,1024]{1,0:T(4,128)} %maximum_convert_fusion.n_ref), custom_call_target="tpu_custom_call" | custom-call | bytes 1048576 | tf_op jit(solution)/shard_map/norm_rows/pallas_call | solution.py:553
  21.8 11.3 %collective-permute-done.3.gq_ref.gk_ref.gv_ref = bf16[512,768]{1,0:T(8,128)(2,1)S(1)} collective-permute-done((bf16[512,768]{1,0:T(8,128)(2,1)S(1)}, bf16[512,768]{1,0:T(8,128)(2,1)S(1)}, u32[]{:S(2)}, u32[]{:S(2)}) %collective-permute-start.3) | collective-permute-done | bytes 786464 | tf_op jit(solution)/shard_map/ppermute | solution.py:1075
  33.1 1.7 collective-permute-start.6
  35.5 3.9 %norm_rows.3 = (bf16[1024,1024]{1,0:T(8,128)(2,1)}, bf16[1024,1024]{1,0:T(8,128)(2,1)}, bf16[1024,1024]{1,0:T(8,128)(2,1)}) custom-call(s32[4]{0:T(128)} %pad_add_fusion.ids, bf16[256,1024]{1,0:T(8,128)(2,1)} %collective-permute-done.a_ref, ...), custom_call_target="tpu_custom_call", output_to_operand_aliasing={{0}: (4, {}), {1}: (5, {}), {2}: (6, {})} | custom-call | bytes 1048576 | tf_op jit(solution)/shard_map/norm_rows/pallas_call | solution.py:553
  39.4 5.6 %qkv_forward.1 = bf16[2,4,192,512]{3,2,1,0:T(8,128)(2,1)} custom-call(s32[4]{0:T(128)} %pad_add_fusion.ids, bf16[1024,1024]{1,0:T(8,128)(2,1)} %get-tuple-element.79.ain_ref.a_ref, bf16[512,3072]{1,0:T(8,128)(2,1)} %wv_ref.3, bf16[512,3072]{1,0:T(8,128)(2,1)} %wv_ref.3, bf16[512,3072]{1,0:T(8,128)(2,1)} %wv_ref.3, bf16[512,768]{1,0:T(8,128)(2,1)} %copy-done.2, ...), custom_call_target="tpu_custom_call" | custom-call | flops 1048576 | bytes 1048576 | tf_op jit(solution)/shard_map/qkv_forward/pallas_call | solution.py:644
  45.0 5.9 %all-to-all-start = ((bf16[8,192,512]{2,1,0:T(8,128)(2,1)}), bf16[8,192,512]{2,1,0:T(8,128)(2,1)S(1)}, u32[]{:S(2)}, u32[]{:S(2)}) async-start(bf16[8,192,512]{2,1,0:T(8,128)(2,1)} %bitcast.170), calls=%async_computation | async-start | bytes 3145728 | tf_op jit(solution)/shard_map/all_to_all | solution.py:1102
  51.0 2.3 constant_dynamic-slice_fusion.5
  57.2 5.0 %turn.1 = (bf16[1024,1024]{1,0:T(8,128)(2,1)}, bf16[1024,1024]{1,0:T(8,128)(2,1)}) custom-call(bf16[1024,1024]{1,0:T(8,128)(2,1)} %get-tuple-element.79.ain_ref.a_ref, bf16[1024,1024]{1,0:T(8,128)(2,1)} %get-tuple-element.81.b_ref.x_ref), custom_call_target="tpu_custom_call" | custom-call | bytes 1048576 | tf_op jit(solution)/shard_map/turn/pallas_call | solution.py:578
  62.2 5.1 %mask_rows.1.dy_ref = bf16[1024,1024]{1,0:T(8,128)(2,1)} custom-call(s32[4]{0:T(128)} %pad_add_fusion.ids, bf16[256,1024]{1,0:T(8,128)(2,1)} %bitcast.181, bf16[256,1024]{1,0:T(8,128)(2,1)} %collective-permute-done.5.b_ref, bf16[256,1024]{1,0:T(8,128)(2,1)} %collective-permute-done.6.c_ref, bf16[256,1024]{1,0:T(8,128)(2,1)} %collective-permute-done.7.d_ref, ...), custom_call_target="tpu_custom_call" | custom-call | bytes 1048576 | tf_op jit(solution)/shard_map/mask_rows/pallas_call | solution.py:602
  67.3 9.7 %collective-permute-done.8.wg_ref = bf16[512,1024]{1,0:T(8,128)(2,1)} collective-permute-done((bf16[512,1024]{1,0:T(8,128)(2,1)}, bf16[512,1024]{1,0:T(8,128)(2,1)}, u32[]{:S(2)}, u32[]{:S(2)}) %collective-permute-start.8) | collective-permute-done | bytes 1048608 | tf_op jit(solution)/shard_map/ppermute | solution.py:1075
  77.0 23.2 %mlp.1 = (bf16[1024,1024]{1,0:T(8,128)(2,1)}, bf16[1024,1024]{1,0:T(8,128)(2,1)}, bf16[4,128,1024]{2,1,0:T(8,128)(2,1)}, bf16[4,128,1024]{2,1,0:T(8,128)(2,1)}, ...) custom-call(s32[4]{0:T(128)} %pad_add_fusion.ids, ...), custom_call_target="tpu_custom_call" | custom-call | flops 12884901888 | bytes 25165824 | tf_op jit(solution)/shard_map/mlp/pallas_call | solution.py:744
  100.2 1.8 collective-permute-start.9
  102.0 1.5 collective-permute-start.10
  103.5 3.2 convolution_convert_fusion
  106.7 3.7 all-to-all-start.1
  110.4 18.6 %attn_fwd.1 = (bf16[8,64,512]{2,1,0:T(8,128)(2,1)}, f32[1,4096]{1,0:T(1,128)}) custom-call(s32[32]{0:T(128)} %a_0_.3, bf16[8,192,512]{2,1,0:T(8,128)(2,1)} %copy-done.3), custom_call_target="tpu_custom_call" | custom-call | tf_op jit(solution)/shard_map/attn_fwd/pallas_call | solution.py:438
  129.0 4.7 %all-to-all-done.1.a_3_ = bf16[8,64,512]{2,1,0:T(8,128)(2,1)S(1)} async-done(((bf16[8,64,512]{2,1,0:T(8,128)(2,1)}), bf16[8,64,512]{2,1,0:T(8,128)(2,1)S(1)}, u32[]{:S(2)}, u32[]{:S(2)}) %all-to-all-start.1) | async-done | bytes 524320 | tf_op jit(solution)/shard_map/all_to_all | solution.py:1102
  133.7 3.7 all-to-all-start.2
  137.4 2.1 fusion.5
  139.5 2.0 collective-permute-start.11
  141.5 2.2 fusion.6
  143.7 2.4 collective-permute-start.12
  146.0 32.2 %attn_bwd.1 = bf16[8,192,512]{2,1,0:T(8,128)(2,1)} custom-call(s32[32]{0:T(128)} %a_0_.3, bf16[8,192,512]{2,1,0:T(8,128)(2,1)} %copy-done.3, bf16[8,64,512]{2,1,0:T(8,128)(2,1)} %get-tuple-element.93.a_2_, bf16[8,64,512]{2,1,0:T(8,128)(2,1)} %copy-done.13, f32[1,4096]{1,0:T(1,128)} %get-tuple-element.95.a_4_, f32[16,4096]{1,0:T(8,128)} %pad_maximum_fusion.1.a_5_), custom_call_target="tpu_custom_call" | custom-call | tf_op jit(solution)/shard_map/attn_bwd/pallas_call | solution.py:498
  178.3 4.6 %all-to-all-start.3 = ((bf16[8,192,512]{2,1,0:T(8,128)(2,1)}), bf16[8,192,512]{2,1,0:T(8,128)(2,1)}, u32[]{:S(2)}, u32[]{:S(2)}) async-start(bf16[8,192,512]{2,1,0:T(8,128)(2,1)} %attn_bwd.1), calls=%async_computation.3 | async-start | bytes 3145728 | tf_op jit(solution)/shard_map/all_to_all | solution.py:1102
  182.9 1.3 fusion.12
  184.2 2.6 collective-permute-start.23
  188.0 1.5 collective-permute-start.30
  190.3 10.1 %collective-permute-done.30 = bf16[1,128,1024]{2,1,0:T(8,128)(2,1)S(1)} collective-permute-done((bf16[1,128,1024]{2,1,0:T(8,128)(2,1)S(1)}, bf16[1,128,1024]{2,1,0:T(8,128)(2,1)S(1)}, u32[]{:S(2)}, u32[]{:S(2)}) %collective-permute-start.30) | collective-permute-done | bytes 262176 | tf_op jit(solution)/shard_map/ppermute | solution.py:1078
  200.4 1.3 fusion.11
  202.4 23.0 %collective-permute-done.23 = bf16[1,128,1024]{2,1,0:T(8,128)(2,1)S(1)} collective-permute-done((bf16[1,128,1024]{2,1,0:T(8,128)(2,1)S(1)}, bf16[1,128,1024]{2,1,0:T(8,128)(2,1)S(1)}, u32[]{:S(2)}, u32[]{:S(2)}) %collective-permute-start.23) | collective-permute-done | bytes 262176 | tf_op jit(solution)/shard_map/ppermute | solution.py:1078
  228.2 8.6 %collective-permute-done.24 = bf16[1,128,1024]{2,1,0:T(8,128)(2,1)S(1)} collective-permute-done((bf16[1,128,1024]{2,1,0:T(8,128)(2,1)S(1)}, bf16[1,128,1024]{2,1,0:T(8,128)(2,1)S(1)}, u32[]{:S(2)}, u32[]{:S(2)}) %collective-permute-start.24) | collective-permute-done | bytes 262176 | tf_op jit(solution)/shard_map/ppermute | solution.py:1078
  237.1 2.8 collective-permute-start.33
  239.9 17.1 %collective-permute-done.25 = bf16[2,128,1024]{2,1,0:T(8,128)(2,1)} collective-permute-done((bf16[2,128,1024]{2,1,0:T(8,128)(2,1)S(1)}, bf16[2,128,1024]{2,1,0:T(8,128)(2,1)}, u32[]{:S(2)}, u32[]{:S(2)}) %collective-permute-start.25) | collective-permute-done | bytes 524320 | tf_op jit(solution)/shard_map/ppermute | solution.py:1078
  257.0 2.3 maximum_select_fusion.3
  259.3 5.6 %collective-permute-start.26 = (bf16[4,128,1024]{2,1,0:T(8,128)(2,1)}, bf16[4,128,1024]{2,1,0:T(8,128)(2,1)}, u32[]{:S(2)}, u32[]{:S(2)}) collective-permute-start(bf16[4,128,1024]{2,1,0:T(8,128)(2,1)} %maximum_select_fusion.3), channel_id=1, source_target_pairs={{0,4},{2,6},{4,0},{6,2},{8,12},{10,14},{12,8},{14,10},{16,20},{18,... | collective-permute-start | bytes 3145736 | tf_op jit(solution)/shard_map/ppermute | solution.py:1078
  266.0 2.2 convert_add_fusion.1
  268.3 13.5 %qkv_backward.1 = (bf16[8,256,256]{2,1,0:T(8,128)(2,1)}, bf16[8,264,256]{2,1,0:T(8,128)(2,1)}, f32[2,512,1024]{2,1,0:T(8,128)}) custom-call(s32[4]{0:T(128)} %pad_add_fusion.ids, bf16[2,4,192,512]{3,2,1,0:T(8,128)(2,1)} %bitcast.31.d_ref, bf16[1024,1024]{1,0:T(8,128)(2,1)} %get-tuple-element.102.at_ref, bf16[1024,1024]{1,0:T(8,128)(2,1)} %get-tuple-element.103.x_ref, ...), custom_call_target="tpu_custom_call" | custom-call | tf_op jit(solution)/shard_map/qkv_backward/pallas_call | solution.py:886
  281.8 1.4 constant_dynamic-slice_fusion.3
  283.4 2.1 collective-permute-start.18
  286.9 2.4 collective-permute-done.26
  289.3 2.5 maximum_select_fusion.own_ref
  291.9 6.9 %collective-permute-done.13 = bf16[4,256,256]{2,1,0:T(8,128)(2,1)S(1)} collective-permute-done((bf16[4,256,256]{2,1,0:T(8,128)(2,1)S(1)}, bf16[4,256,256]{2,1,0:T(8,128)(2,1)S(1)}, u32[]{:S(2)}, u32[]{:S(2)}) %collective-permute-start.13) | collective-permute-done | bytes 524320 | tf_op jit(solution)/shard_map/ppermute | solution.py:1078
  299.0 3.9 %collective-permute-done.18 = bf16[4,264,256]{2,1,0:T(8,128)(2,1)S(1)} collective-permute-done((bf16[4,264,256]{2,1,0:T(8,128)(2,1)S(1)}, bf16[4,264,256]{2,1,0:T(8,128)(2,1)S(1)}, u32[]{:S(2)}, u32[]{:S(2)}) %collective-permute-start.18) | collective-permute-done | bytes 540704 | tf_op jit(solution)/shard_map/ppermute | solution.py:1078
  302.9 3.3 collective-permute-start.19
  306.2 2.0 maximum_select_fusion.1.own_ref
  308.3 2.5 collective-permute-done.14
  311.1 7.9 %collective-permute-done.19 = bf16[2,264,256]{2,1,0:T(8,128)(2,1)S(1)} collective-permute-done((bf16[2,264,256]{2,1,0:T(8,128)(2,1)S(1)}, bf16[2,264,256]{2,1,0:T(8,128)(2,1)S(1)}, u32[]{:S(2)}, u32[]{:S(2)}) %collective-permute-start.19) | collective-permute-done | bytes 270368 | tf_op jit(solution)/shard_map/ppermute | solution.py:1078
  319.1 1.3 collective-permute-done.15
  321.2 4.2 %collective-permute-done.20 = bf16[1,264,256]{2,1,0:T(8,128)(2,1)S(1)} collective-permute-done((bf16[1,264,256]{2,1,0:T(8,128)(2,1)S(1)}, bf16[1,264,256]{2,1,0:T(8,128)(2,1)S(1)}, u32[]{:S(2)}, u32[]{:S(2)}) %collective-permute-start.20) | collective-permute-done | bytes 135200 | tf_op jit(solution)/shard_map/ppermute | solution.py:1078
  326.1 3.8 collective-permute-done.16
  330.6 3.5 collective-permute-done.21
  334.9 1.7 convert_add_fusion.2
  336.6 4.8 %collective-permute-done.17 = bf16[1,256,256]{2,1,0:T(8,128)(2,1)S(1)} collective-permute-done((bf16[1,256,256]{2,1,0:T(8,128)(2,1)S(1)}, bf16[1,256,256]{2,1,0:T(8,128)(2,1)S(1)}, u32[]{:S(2)}, u32[]{:S(2)}) %collective-permute-start.17) | collective-permute-done | bytes 131104 | tf_op jit(solution)/shard_map/ppermute | solution.py:1078
  341.5 7.2 %join_rows.1 = f32[2048,1024]{1,0:T(8,128)} custom-call(s32[4]{0:T(128)} %pad_add_fusion.ids, bf16[8,128,1024]{2,1,0:T(8,128)(2,1)} %copy-done.5, bf16[8,128,1024]{2,1,0:T(8,128)(2,1)} %collective-permute-done.27.got_ref), custom_call_target="tpu_custom_call" | custom-call | tf_op jit(solution)/shard_map/join_rows/pallas_call | solution.py:941
  348.7 1.5 collective-permute-start.28
  352.4 7.1 %join_cols.1 = f32[512,4096]{1,0:T(8,128)} custom-call(s32[4]{0:T(128)} %pad_add_fusion.ids, bf16[8,2,64,1024]{3,2,1,0:T(8,128)(2,1)} %copy-done.6, bf16[8,2,64,1024]{3,2,1,0:T(8,128)(2,1)} %collective-permute-done.35.got_ref), custom_call_target="tpu_custom_call" | custom-call | tf_op jit(solution)/shard_map/join_cols/pallas_call | solution.py:958
  360.9 2.1 fusion.4
  364.1 3.4 token_grad.1
  367.5 2.4 collective-permute-done.36
  371.8 3.8 collective-permute-done.42.ag_ref
  375.7 6.6 %unpack.1 = (f32[512,3072]{1,0:T(8,128)}, f32[2,256,1024]{2,1,0:T(8,128)}, f32[8,8,256]{2,1,0:T(8,128)}) custom-call(s32[4]{0:T(128)} %pad_add_fusion.ids, bf16[8,256,256]{2,1,0:T(8,128)(2,1)} %copy-done.11, bf16[8,256,256]{2,1,0:T(8,128)(2,1)} %collective-permute-done.42.ag_ref, bf16[8,264,256]{2,1,0:T(8,128)(2,1)} %copy-done.10, ...), custom_call_target="tpu_custom_call" | custom-call | tf_op jit(solution)/shard_map/unpack/pallas_call | solution.py:1002
  (197 shorter events, 31.9 us)
Async XLA Ops:
  0.6 102.8 %copy-start = (bf16[512,1024]{1,0:T(8,128)(2,1)S(1)}, bf16[512,1024]{1,0:T(8,128)(2,1)}, u32[]{:S(2)}) copy-start(bf16[512,1024]{1,0:T(8,128)(2,1)} %param.23) | copy-start | bytes 3145732
  0.7 7.5 %copy-start.21 = (s32[32]{0:T(128)S(1)}, s32[32]{0:T(128)}, u32[]{:S(2)}) copy-start(s32[32]{0:T(128)} %a_0_.3) | copy-start | bytes 388
  0.7 16.4 %collective-permute-start = (bf16[256,1024]{1,0:T(8,128)(2,1)}, bf16[256,1024]{1,0:T(8,128)(2,1)}, u32[]{:S(2)}, u32[]{:S(2)}) collective-permute-start(bf16[256,1024]{1,0:T(8,128)(2,1)} %bitcast.173), channel_id=1, source_target_pairs={{0,1},{1,0},{2,3},{3,2},{4,5},{5,4},{6,7},{7,6},{8,9},{9,8},{10,11... | collective-permute-start | bytes 1572872 | tf_op jit(solution)/shard_map/ppermute | solution.py:1075
  3.8 14.1 %collective-permute-start.4 = (bf16[256,1024]{1,0:T(8,128)(2,1)}, bf16[256,1024]{1,0:T(8,128)(2,1)}, u32[]{:S(2)}, u32[]{:S(2)}) collective-permute-start(bf16[256,1024]{1,0:T(8,128)(2,1)} %bitcast.174), channel_id=1, source_target_pairs={{0,2},{2,0},{4,6},{6,4},{8,10},{10,8},{12,14},{14,12},{16,18},{18,... | collective-permute-start | bytes 1572872 | tf_op jit(solution)/shard_map/ppermute | solution.py:1078
  5.7 27.5 %copy-start.15 = (bf16[1,256,1024]{2,1,0:T(8,128)(2,1)S(1)}, bf16[1,256,1024]{2,1,0:T(8,128)(2,1)}, u32[]{:S(2)}) copy-start(bf16[1,256,1024]{2,1,0:T(8,128)(2,1)} %param.31) | copy-start | bytes 1572868
  6.2 10.9 %collective-permute-start.2 = (bf16[10,512]{1,0:T(8,128)(2,1)S(1)}, bf16[10,512]{1,0:T(8,128)(2,1)S(1)}, u32[]{:S(2)}, u32[]{:S(2)}) collective-permute-start(bf16[10,512]{1,0:T(8,128)(2,1)S(1)} %concatenate.150), channel_id=1, source_target_pairs={{0,1},{1,0},{2,3},{3,2},{4,5},{5,4},{6,7},{7,6},{8,9},{9,8},{10,11... | collective-permute-start | bytes 30728 | tf_op jit(solution)/shard_map/ppermute | solution.py:1075
  6.3 26.8 %collective-permute-start.3 = (bf16[512,768]{1,0:T(8,128)(2,1)S(1)}, bf16[512,768]{1,0:T(8,128)(2,1)S(1)}, u32[]{:S(2)}, u32[]{:S(2)}) collective-permute-start(bf16[512,768]{1,0:T(8,128)(2,1)S(1)} %pad_maximum_fusion), channel_id=1, source_target_pairs={{0,1},{1,0},{2,3},{3,2},{4,5},{5,4},{6,7},{7,6},{8,9},{9,8},{10,11... | collective-permute-start | bytes 2359304 | tf_op jit(solution)/shard_map/ppermute | solution.py:1075
  17.1 18.3 %collective-permute-start.1 = (bf16[256,1024]{1,0:T(8,128)(2,1)}, bf16[256,1024]{1,0:T(8,128)(2,1)}, u32[]{:S(2)}, u32[]{:S(2)}) collective-permute-start(bf16[256,1024]{1,0:T(8,128)(2,1)} %collective-permute-done.a_ref), channel_id=1, source_target_pairs={{0,2},{2,0},{4,6},{6,4},{8,10},{10,8},{12,14},{14,12},{16,18},{18,... | collective-permute-start | bytes 1572872 | tf_op jit(solution)/shard_map/ppermute | solution.py:1078
  33.1 6.3 %copy-start.2 = (bf16[512,768]{1,0:T(8,128)(2,1)}, bf16[512,768]{1,0:T(8,128)(2,1)S(1)}, u32[]{:S(2)}) copy-start(bf16[512,768]{1,0:T(8,128)(2,1)S(1)} %collective-permute-done.3.gq_ref.gk_ref.gv_ref) | copy-start | bytes 2359300
  33.1 20.1 %collective-permute-start.6 = (bf16[256,1024]{1,0:T(8,128)(2,1)S(1)}, bf16[256,1024]{1,0:T(8,128)(2,1)}, u32[]{:S(2)}, u32[]{:S(2)}) collective-permute-start(bf16[256,1024]{1,0:T(8,128)(2,1)S(1)} %bitcast.183), channel_id=1, source_target_pairs={{0,1},{1,0},{2,3},{3,2},{4,5},{5,4},{6,7},{7,6},{8,9},{9,8},{10,11... | collective-permute-start | bytes 1572872 | tf_op jit(solution)/shard_map/ppermute | solution.py:1075
  45.0 8.7 %copy-start.19 = (bf16[2048]{0:T(1024)(128)(2,1)S(1)}, bf16[2048]{0:T(1024)(128)(2,1)}, u32[]{:S(2)}) copy-start(bf16[2048]{0:T(1024)(128)(2,1)} %param.26) | copy-start | bytes 12292
  45.0 55.2 %all-to-all-start = ((bf16[8,192,512]{2,1,0:T(8,128)(2,1)}), bf16[8,192,512]{2,1,0:T(8,128)(2,1)S(1)}, u32[]{:S(2)}, u32[]{:S(2)}) async-start(bf16[8,192,512]{2,1,0:T(8,128)(2,1)} %bitcast.170), calls=%async_computation | async-start | bytes 3145728 | tf_op jit(solution)/shard_map/all_to_all | solution.py:1102
  53.2 23.8 %collective-permute-start.8 = (bf16[512,1024]{1,0:T(8,128)(2,1)}, bf16[512,1024]{1,0:T(8,128)(2,1)}, u32[]{:S(2)}, u32[]{:S(2)}) collective-permute-start(bf16[512,1024]{1,0:T(8,128)(2,1)} %constant_dynamic-slice_fusion.5), channel_id=1, source_target_pairs={{0,1},{1,0},{2,3},{3,2},{4,5},{5,4},{6,7},{7,6},{8,9},{9,8},{10,11... | collective-permute-start | bytes 3145736 | tf_op jit(solution)/shard_map/ppermute | solution.py:1075
  53.7 8.5 %collective-permute-start.5 = (bf16[256,1024]{1,0:T(8,128)(2,1)S(1)}, bf16[256,1024]{1,0:T(8,128)(2,1)}, u32[]{:S(2)}, u32[]{:S(2)}) collective-permute-start(bf16[256,1024]{1,0:T(8,128)(2,1)S(1)} %bitcast.184), channel_id=1, source_target_pairs={{0,2},{2,0},{4,6},{6,4},{8,10},{10,8},{12,14},{14,12},{16,18},{18,... | collective-permute-start | bytes 1572872 | tf_op jit(solution)/shard_map/ppermute | solution.py:1078
  54.9 7.3 %collective-permute-start.7 = (bf16[256,1024]{1,0:T(8,128)(2,1)}, bf16[256,1024]{1,0:T(8,128)(2,1)}, u32[]{:S(2)}, u32[]{:S(2)}) collective-permute-start(bf16[256,1024]{1,0:T(8,128)(2,1)} %collective-permute-done.6.c_ref), channel_id=1, source_target_pairs={{0,2},{2,0},{4,6},{6,4},{8,10},{10,8},{12,14},{14,12},{16,18},{18,... | collective-permute-start | bytes 1572872 | tf_op jit(solution)/shard_map/ppermute | solution.py:1078
  100.2 6.5 %copy-start.3 = (bf16[8,192,512]{2,1,0:T(8,128)(2,1)}, bf16[8,192,512]{2,1,0:T(8,128)(2,1)S(1)}, u32[]{:S(2)}) copy-start(bf16[8,192,512]{2,1,0:T(8,128)(2,1)S(1)} %all-to-all-done.a_1_) | copy-start | bytes 4718596
  100.2 33.5 %collective-permute-start.9 = (bf16[4,128,1024]{2,1,0:T(8,128)(2,1)}, bf16[4,128,1024]{2,1,0:T(8,128)(2,1)}, u32[]{:S(2)}, u32[]{:S(2)}) collective-permute-start(bf16[4,128,1024]{2,1,0:T(8,128)(2,1)} %get-tuple-element.90), channel_id=1, source_target_pairs={{0,4},{2,6},{4,0},{6,2},{8,12},{10,14},{12,8},{14,10},{16,20},{18,... | collective-permute-start | bytes 3145736 | tf_op jit(solution)/shard_map/ppermute | solution.py:1078
  102.0 31.7 %collective-permute-start.10 = (bf16[4,128,1024]{2,1,0:T(8,128)(2,1)}, bf16[4,128,1024]{2,1,0:T(8,128)(2,1)}, u32[]{:S(2)}, u32[]{:S(2)}) collective-permute-start(bf16[4,128,1024]{2,1,0:T(8,128)(2,1)} %get-tuple-element.91), channel_id=1, source_target_pairs={{0,8},{2,10},{4,12},{6,14},{8,0},{10,2},{12,4},{14,6},{16,24},{18,... | collective-permute-start | bytes 3145736 | tf_op jit(solution)/shard_map/ppermute | solution.py:1078
  106.7 27.1 %all-to-all-start.1 = ((bf16[8,64,512]{2,1,0:T(8,128)(2,1)}), bf16[8,64,512]{2,1,0:T(8,128)(2,1)S(1)}, u32[]{:S(2)}, u32[]{:S(2)}) async-start(bf16[8,64,512]{2,1,0:T(8,128)(2,1)} %bitcast.202), calls=%async_computation.1 | async-start | bytes 1048576 | tf_op jit(solution)/shard_map/all_to_all | solution.py:1102
  110.4 27.0 %copy-start.17 = (bf16[4,128,1024]{2,1,0:T(8,128)(2,1)S(1)}, bf16[4,128,1024]{2,1,0:T(8,128)(2,1)}, u32[]{:S(2)}) copy-start(bf16[4,128,1024]{2,1,0:T(8,128)(2,1)} %get-tuple-element.97) | copy-start | bytes 3145732
  133.7 9.9 %copy-start.13 = (bf16[8,64,512]{2,1,0:T(8,128)(2,1)}, bf16[8,64,512]{2,1,0:T(8,128)(2,1)S(1)}, u32[]{:S(2)}) copy-start(bf16[8,64,512]{2,1,0:T(8,128)(2,1)S(1)} %all-to-all-done.1.a_3_) | copy-start | bytes 1572868
  133.7 44.5 %all-to-all-start.2 = ((bf16[8,64,512]{2,1,0:T(8,128)(2,1)}), bf16[8,64,512]{2,1,0:T(8,128)(2,1)S(1)}, u32[]{:S(2)}, u32[]{:S(2)}) async-start(bf16[8,64,512]{2,1,0:T(8,128)(2,1)} %get-tuple-element.93.a_2_), calls=%async_computation.2 | async-start | bytes 1048576 | tf_op jit(solution)/shard_map/all_to_all | solution.py:1102
  139.5 38.8 %collective-permute-start.11 = (bf16[2,128,1024]{2,1,0:T(8,128)(2,1)}, bf16[2,128,1024]{2,1,0:T(8,128)(2,1)}, u32[]{:S(2)}, u32[]{:S(2)}) collective-permute-start(bf16[2,128,1024]{2,1,0:T(8,128)(2,1)} %fusion.5), channel_id=1, source_target_pairs={{0,8},{2,10},{4,12},{6,14},{8,0},{10,2},{12,4},{14,6},{16,24},{18,... | collective-permute-start | bytes 1572872 | tf_op jit(solution)/shard_map/ppermute | solution.py:1078
  143.7 34.6 %collective-permute-start.12 = (bf16[2,128,1024]{2,1,0:T(8,128)(2,1)}, bf16[2,128,1024]{2,1,0:T(8,128)(2,1)}, u32[]{:S(2)}, u32[]{:S(2)}) collective-permute-start(bf16[2,128,1024]{2,1,0:T(8,128)(2,1)} %fusion.6), channel_id=1, source_target_pairs={{0,16},{2,18},{4,20},{6,22},{8,24},{10,26},{12,28},{14,30},{16,0},... | collective-permute-start | bytes 1572872 | tf_op jit(solution)/shard_map/ppermute | solution.py:1078
  178.3 11.3 %copy-start.8 = (bf16[8,64,512]{2,1,0:T(8,128)(2,1)}, bf16[8,64,512]{2,1,0:T(8,128)(2,1)S(1)}, u32[]{:S(2)}) copy-start(bf16[8,64,512]{2,1,0:T(8,128)(2,1)S(1)} %all-to-all-done.2) | copy-start | bytes 1572868
  178.3 90.0 %all-to-all-start.3 = ((bf16[8,192,512]{2,1,0:T(8,128)(2,1)}), bf16[8,192,512]{2,1,0:T(8,128)(2,1)}, u32[]{:S(2)}, u32[]{:S(2)}) async-start(bf16[8,192,512]{2,1,0:T(8,128)(2,1)} %attn_bwd.1), calls=%async_computation.3 | async-start | bytes 3145728 | tf_op jit(solution)/shard_map/all_to_all | solution.py:1102
  182.8 6.7 %copy-start.14 = (bf16[1024,1024]{1,0:T(8,128)(2,1)S(1)}, bf16[1024,1024]{1,0:T(8,128)(2,1)}, u32[]{:S(2)}) copy-start(bf16[1024,1024]{1,0:T(8,128)(2,1)} %get-tuple-element.116) | copy-start | bytes 6291460
  184.2 41.2 %collective-permute-start.23 = (bf16[1,128,1024]{2,1,0:T(8,128)(2,1)S(1)}, bf16[1,128,1024]{2,1,0:T(8,128)(2,1)S(1)}, u32[]{:S(2)}, u32[]{:S(2)}) collective-permute-start(bf16[1,128,1024]{2,1,0:T(8,128)(2,1)S(1)} %fusion.12), channel_id=1, source_target_pairs={{0,16},{2,18},{4,20},{6,22},{8,24},{10,26},{12,28},{14,30},{16,0},... | collective-permute-start | bytes 786440 | tf_op jit(solution)/shard_map/ppermute | solution.py:1078
  188.0 12.4 %collective-permute-start.30 = (bf16[1,128,1024]{2,1,0:T(8,128)(2,1)S(1)}, bf16[1,128,1024]{2,1,0:T(8,128)(2,1)S(1)}, u32[]{:S(2)}, u32[]{:S(2)}) collective-permute-start(bf16[1,128,1024]{2,1,0:T(8,128)(2,1)S(1)} %fusion.9), channel_id=1, source_target_pairs={{0,4},{2,6},{4,0},{6,2},{8,12},{10,14},{12,8},{14,10},{16,20},{18,... | collective-permute-start | bytes 786440 | tf_op jit(solution)/shard_map/ppermute | solution.py:1078
  190.3 37.8 %copy-start.4 = (f32[2,512,1024]{2,1,0:T(8,128)}, f32[2,512,1024]{2,1,0:T(8,128)S(1)}, u32[]{:S(2)}) copy-start(f32[2,512,1024]{2,1,0:T(8,128)S(1)} %convert_add_fusion) | copy-start | bytes 12582916
  201.8 24.9 %collective-permute-start.31 = (bf16[1,1,64,1024]{3,2,1,0:T(8,128)(2,1)S(1)}, bf16[1,1,64,1024]{3,2,1,0:T(8,128)(2,1)S(1)}, u32[]{:S(2)}, u32[]{:S(2)}) collective-permute-start(bf16[1,1,64,1024]{3,2,1,0:T(8,128)(2,1)S(1)} %get-tuple-element.134), channel_id=1, source_target_pairs={{0,1},{1,0},{2,3},{3,2},{4,5},{5,4},{6,7},{7,6},{8,9},{9,8},{10,11... | collective-permute-start | bytes 393224 | tf_op jit(solution)/shard_map/ppermute | solution.py:1075
  226.6 10.2 %collective-permute-start.24 = (bf16[1,128,1024]{2,1,0:T(8,128)(2,1)S(1)}, bf16[1,128,1024]{2,1,0:T(8,128)(2,1)S(1)}, u32[]{:S(2)}, u32[]{:S(2)}) collective-permute-start(bf16[1,128,1024]{2,1,0:T(8,128)(2,1)S(1)} %fusion.14), channel_id=1, source_target_pairs={{0,16},{2,18},{4,20},{6,22},{8,24},{10,26},{12,28},{14,30},{16,0},... | collective-permute-start | bytes 786440 | tf_op jit(solution)/shard_map/ppermute | solution.py:1078
  226.7 10.3 %collective-permute-start.32 = (bf16[1,2,64,1024]{3,2,1,0:T(8,128)(2,1)S(1)}, bf16[1,2,64,1024]{3,2,1,0:T(8,128)(2,1)S(1)}, u32[]{:S(2)}, u32[]{:S(2)}) collective-permute-start(bf16[1,2,64,1024]{3,2,1,0:T(8,128)(2,1)S(1)} %maximum_select_fusion.12), channel_id=1, source_target_pairs={{0,4},{2,6},{4,0},{6,2},{8,12},{10,14},{12,8},{14,10},{16,20},{18,... | collective-permute-start | bytes 786440 | tf_op jit(solution)/shard_map/ppermute | solution.py:1078
  228.1 37.9 %collective-permute-start.40 = (bf16[2,256,1024]{2,1,0:T(8,128)(2,1)S(1)}, bf16[2,256,1024]{2,1,0:T(8,128)(2,1)}, u32[]{:S(2)}, u32[]{:S(2)}) collective-permute-start(bf16[2,256,1024]{2,1,0:T(8,128)(2,1)S(1)} %dynamic-slice_convert_fusion), channel_id=1, source_target_pairs={{0,2},{2,0},{4,6},{6,4},{8,10},{10,8},{12,14},{14,12},{16,18},{18,... | collective-permute-start | bytes 3145736 | tf_op jit(solution)/shard_map/ppermute | solution.py:1078
  236.9 20.0 %collective-permute-start.25 = (bf16[2,128,1024]{2,1,0:T(8,128)(2,1)S(1)}, bf16[2,128,1024]{2,1,0:T(8,128)(2,1)}, u32[]{:S(2)}, u32[]{:S(2)}) collective-permute-start(bf16[2,128,1024]{2,1,0:T(8,128)(2,1)S(1)} %maximum_select_fusion.7), channel_id=1, source_target_pairs={{0,8},{2,10},{4,12},{6,14},{8,0},{10,2},{12,4},{14,6},{16,24},{18,... | collective-permute-start | bytes 1572872 | tf_op jit(solution)/shard_map/ppermute | solution.py:1078
  237.1 28.7 %collective-permute-start.33 = (bf16[2,2,64,1024]{3,2,1,0:T(8,128)(2,1)S(1)}, bf16[2,2,64,1024]{3,2,1,0:T(8,128)(2,1)S(1)}, u32[]{:S(2)}, u32[]{:S(2)}) collective-permute-start(bf16[2,2,64,1024]{3,2,1,0:T(8,128)(2,1)S(1)} %maximum_select_fusion.9), channel_id=1, source_target_pairs={{0,16},{2,18},{4,20},{6,22},{8,24},{10,26},{12,28},{14,30},{16,0},... | collective-permute-start | bytes 1572872 | tf_op jit(solution)/shard_map/ppermute | solution.py:1078
  259.3 30.0 %collective-permute-start.26 = (bf16[4,128,1024]{2,1,0:T(8,128)(2,1)}, bf16[4,128,1024]{2,1,0:T(8,128)(2,1)}, u32[]{:S(2)}, u32[]{:S(2)}) collective-permute-start(bf16[4,128,1024]{2,1,0:T(8,128)(2,1)} %maximum_select_fusion.3), channel_id=1, source_target_pairs={{0,4},{2,6},{4,0},{6,2},{8,12},{10,14},{12,8},{14,10},{16,20},{18,... | collective-permute-start | bytes 3145736 | tf_op jit(solution)/shard_map/ppermute | solution.py:1078
  265.9 40.3 %collective-permute-start.34 = (bf16[4,2,64,1024]{3,2,1,0:T(8,128)(2,1)S(1)}, bf16[4,2,64,1024]{3,2,1,0:T(8,128)(2,1)}, u32[]{:S(2)}, u32[]{:S(2)}) collective-permute-start(bf16[4,2,64,1024]{3,2,1,0:T(8,128)(2,1)S(1)} %maximum_select_fusion.4), channel_id=1, source_target_pairs={{0,8},{2,10},{4,12},{6,14},{8,0},{10,2},{12,4},{14,6},{16,24},{18,... | collective-permute-start | bytes 3145736 | tf_op jit(solution)/shard_map/ppermute | solution.py:1078
  283.1 15.7 %collective-permute-start.13 = (bf16[4,256,256]{2,1,0:T(8,128)(2,1)S(1)}, bf16[4,256,256]{2,1,0:T(8,128)(2,1)S(1)}, u32[]{:S(2)}, u32[]{:S(2)}) collective-permute-start(bf16[4,256,256]{2,1,0:T(8,128)(2,1)S(1)} %get-tuple-element.132), channel_id=1, source_target_pairs={{0,4},{2,6},{4,0},{6,2},{8,12},{10,14},{12,8},{14,10},{16,20},{18,... | collective-permute-start | bytes 1572872 | tf_op jit(solution)/shard_map/ppermute | solution.py:1078
  283.4 19.4 %collective-permute-start.18 = (bf16[4,264,256]{2,1,0:T(8,128)(2,1)S(1)}, bf16[4,264,256]{2,1,0:T(8,128)(2,1)S(1)}, u32[]{:S(2)}, u32[]{:S(2)}) collective-permute-start(bf16[4,264,256]{2,1,0:T(8,128)(2,1)S(1)} %get-tuple-element.130), channel_id=1, source_target_pairs={{0,8},{2,10},{4,12},{6,14},{8,0},{10,2},{12,4},{14,6},{16,24},{18,... | collective-permute-start | bytes 1622024 | tf_op jit(solution)/shard_map/ppermute | solution.py:1078
  286.3 74.6 %collective-permute-start.41 = (bf16[256,1024]{1,0:T(8,128)(2,1)}, bf16[256,1024]{1,0:T(8,128)(2,1)}, u32[]{:S(2)}, u32[]{:S(2)}) collective-permute-start(bf16[256,1024]{1,0:T(8,128)(2,1)} %fusion.8), channel_id=1, source_target_pairs={{0,1},{1,0},{2,3},{3,2},{4,5},{5,4},{6,7},{7,6},{8,9},{9,8},{10,11... | collective-permute-start | bytes 1572872 | tf_op jit(solution)/shard_map/ppermute | solution.py:1075
  291.8 16.4 %copy-start.5 = (bf16[8,128,1024]{2,1,0:T(8,128)(2,1)}, bf16[8,128,1024]{2,1,0:T(8,128)(2,1)S(1)}, u32[]{:S(2)}) copy-start(bf16[8,128,1024]{2,1,0:T(8,128)(2,1)S(1)} %maximum_select_fusion.own_ref) | copy-start | bytes 6291460
  291.8 49.7 %collective-permute-start.27 = (bf16[8,128,1024]{2,1,0:T(8,128)(2,1)S(1)}, bf16[8,128,1024]{2,1,0:T(8,128)(2,1)}, u32[]{:S(2)}, u32[]{:S(2)}) collective-permute-start(bf16[8,128,1024]{2,1,0:T(8,128)(2,1)S(1)} %maximum_select_fusion.own_ref), channel_id=1, source_target_pairs={{0,2},{2,0},{4,6},{6,4},{8,10},{10,8},{12,14},{14,12},{16,18},{18,... | collective-permute-start | bytes 6291464 | tf_op jit(solution)/shard_map/ppermute | solution.py:1078
  298.9 11.9 %collective-permute-start.14 = (bf16[2,256,256]{2,1,0:T(8,128)(2,1)S(1)}, bf16[2,256,256]{2,1,0:T(8,128)(2,1)S(1)}, u32[]{:S(2)}, u32[]{:S(2)}) collective-permute-start(bf16[2,256,256]{2,1,0:T(8,128)(2,1)S(1)} %fusion.23), channel_id=1, source_target_pairs={{0,8},{2,10},{4,12},{6,14},{8,0},{10,2},{12,4},{14,6},{16,24},{18,... | collective-permute-start | bytes 786440 | tf_op jit(solution)/shard_map/ppermute | solution.py:1078
  302.9 8.0 %copy-start.12 = (f32[2,512,1024]{2,1,0:T(8,128)S(1)}, f32[2,512,1024]{2,1,0:T(8,128)}, u32[]{:S(2)}) copy-start(f32[2,512,1024]{2,1,0:T(8,128)} %get-tuple-element.115) | copy-start | bytes 12582916
  302.9 16.1 %collective-permute-start.19 = (bf16[2,264,256]{2,1,0:T(8,128)(2,1)S(1)}, bf16[2,264,256]{2,1,0:T(8,128)(2,1)S(1)}, u32[]{:S(2)}, u32[]{:S(2)}) collective-permute-start(bf16[2,264,256]{2,1,0:T(8,128)(2,1)S(1)} %fusion.19), channel_id=1, source_target_pairs={{0,16},{2,18},{4,20},{6,22},{8,24},{10,26},{12,28},{14,30},{16,0},... | collective-permute-start | bytes 811016 | tf_op jit(solution)/shard_map/ppermute | solution.py:1078
  308.2 17.9 %copy-start.6 = (bf16[8,2,64,1024]{3,2,1,0:T(8,128)(2,1)}, bf16[8,2,64,1024]{3,2,1,0:T(8,128)(2,1)S(1)}, u32[]{:S(2)}) copy-start(bf16[8,2,64,1024]{3,2,1,0:T(8,128)(2,1)S(1)} %maximum_select_fusion.1.own_ref) | copy-start | bytes 6291460
  308.2 44.2 %collective-permute-start.35 = (bf16[8,2,64,1024]{3,2,1,0:T(8,128)(2,1)S(1)}, bf16[8,2,64,1024]{3,2,1,0:T(8,128)(2,1)}, u32[]{:S(2)}, u32[]{:S(2)}) collective-permute-start(bf16[8,2,64,1024]{3,2,1,0:T(8,128)(2,1)S(1)} %maximum_select_fusion.1.own_ref), channel_id=1, source_target_pairs={{0,2},{2,0},{4,6},{6,4},{8,10},{10,8},{12,14},{14,12},{16,18},{18,... | collective-permute-start | bytes 6291464 | tf_op jit(solution)/shard_map/ppermute | solution.py:1078
  310.8 9.6 %collective-permute-start.15 = (bf16[1,256,256]{2,1,0:T(8,128)(2,1)S(1)}, bf16[1,256,256]{2,1,0:T(8,128)(2,1)S(1)}, u32[]{:S(2)}, u32[]{:S(2)}) collective-permute-start(bf16[1,256,256]{2,1,0:T(8,128)(2,1)S(1)} %fusion.24), channel_id=1, source_target_pairs={{0,16},{2,18},{4,20},{6,22},{8,24},{10,26},{12,28},{14,30},{16,0},... | collective-permute-start | bytes 393224 | tf_op jit(solution)/shard_map/ppermute | solution.py:1078
  319.0 15.2 %collective-permute-start.38 = (bf16[2,256,1024]{2,1,0:T(8,128)(2,1)S(1)}, bf16[2,256,1024]{2,1,0:T(8,128)(2,1)S(1)}, u32[]{:S(2)}, u32[]{:S(2)}) collective-permute-start(bf16[2,256,1024]{2,1,0:T(8,128)(2,1)S(1)} %dynamic-slice_convert_fusion.1), channel_id=1, source_target_pairs={{0,2},{2,0},{4,6},{6,4},{8,10},{10,8},{12,14},{14,12},{16,18},{18,... | collective-permute-start | bytes 3145736 | tf_op jit(solution)/shard_map/ppermute | solution.py:1078
  320.4 5.0 %collective-permute-start.20 = (bf16[1,264,256]{2,1,0:T(8,128)(2,1)S(1)}, bf16[1,264,256]{2,1,0:T(8,128)(2,1)S(1)}, u32[]{:S(2)}, u32[]{:S(2)}) collective-permute-start(bf16[1,264,256]{2,1,0:T(8,128)(2,1)S(1)} %fusion.20), channel_id=1, source_target_pairs={{0,4},{2,6},{4,0},{6,2},{8,12},{10,14},{12,8},{14,10},{16,20},{18,... | collective-permute-start | bytes 405512 | tf_op jit(solution)/shard_map/ppermute | solution.py:1078
  325.4 4.6 %collective-permute-start.16 = (bf16[96,256]{1,0:T(8,128)(2,1)S(1)}, bf16[96,256]{1,0:T(8,128)(2,1)S(1)}, u32[]{:S(2)}, u32[]{:S(2)}) collective-permute-start(bf16[96,256]{1,0:T(8,128)(2,1)S(1)} %get-tuple-element.138), channel_id=1, source_target_pairs={{0,1},{1,0},{2,3},{3,2},{4,5},{5,4},{6,7},{7,6},{8,9},{9,8},{10,11... | collective-permute-start | bytes 147464 | tf_op jit(solution)/shard_map/ppermute | solution.py:1075
  330.0 4.1 %collective-permute-start.21 = (bf16[104,256]{1,0:T(8,128)(2,1)S(1)}, bf16[104,256]{1,0:T(8,128)(2,1)S(1)}, u32[]{:S(2)}, u32[]{:S(2)}) collective-permute-start(bf16[104,256]{1,0:T(8,128)(2,1)S(1)} %pad_maximum_fusion.2), channel_id=1, source_target_pairs={{0,1},{1,0},{2,3},{3,2},{4,5},{5,4},{6,7},{7,6},{8,9},{9,8},{10,11... | collective-permute-start | bytes 159752 | tf_op jit(solution)/shard_map/ppermute | solution.py:1075
  334.1 7.3 %collective-permute-start.17 = (bf16[1,256,256]{2,1,0:T(8,128)(2,1)S(1)}, bf16[1,256,256]{2,1,0:T(8,128)(2,1)S(1)}, u32[]{:S(2)}, u32[]{:S(2)}) collective-permute-start(bf16[1,256,256]{2,1,0:T(8,128)(2,1)S(1)} %maximum_bitcast_fusion.1), channel_id=1, source_target_pairs={{0,16},{2,18},{4,20},{6,22},{8,24},{10,26},{12,28},{14,30},{16,0},... | collective-permute-start | bytes 393224 | tf_op jit(solution)/shard_map/ppermute | solution.py:1078
  334.2 7.2 %collective-permute-start.22 = (bf16[1,264,256]{2,1,0:T(8,128)(2,1)S(1)}, bf16[1,264,256]{2,1,0:T(8,128)(2,1)S(1)}, u32[]{:S(2)}, u32[]{:S(2)}) collective-permute-start(bf16[1,264,256]{2,1,0:T(8,128)(2,1)S(1)} %maximum_bitcast_fusion), channel_id=1, source_target_pairs={{0,4},{2,6},{4,0},{6,2},{8,12},{10,14},{12,8},{14,10},{16,20},{18,... | collective-permute-start | bytes 405512 | tf_op jit(solution)/shard_map/ppermute | solution.py:1078
  341.5 9.5 %copy-start.7 = (f32[2,256,1024]{2,1,0:T(8,128)S(1)}, f32[2,256,1024]{2,1,0:T(8,128)}, u32[]{:S(2)}) copy-start(f32[2,256,1024]{2,1,0:T(8,128)} %convert_add_fusion.2) | copy-start | bytes 6291460
  348.7 10.8 %collective-permute-start.28 = (bf16[2,256,256]{2,1,0:T(8,128)(2,1)S(1)}, bf16[2,256,256]{2,1,0:T(8,128)(2,1)S(1)}, u32[]{:S(2)}, u32[]{:S(2)}) collective-permute-start(bf16[2,256,256]{2,1,0:T(8,128)(2,1)S(1)} %maximum_select_fusion.11), channel_id=1, source_target_pairs={{0,8},{2,10},{4,12},{6,14},{8,0},{10,2},{12,4},{14,6},{16,24},{18,... | collective-permute-start | bytes 786440 | tf_op jit(solution)/shard_map/ppermute | solution.py:1078
  350.2 10.4 %collective-permute-start.29 = (bf16[2,264,256]{2,1,0:T(8,128)(2,1)S(1)}, bf16[2,264,256]{2,1,0:T(8,128)(2,1)S(1)}, u32[]{:S(2)}, u32[]{:S(2)}) collective-permute-start(bf16[2,264,256]{2,1,0:T(8,128)(2,1)S(1)} %maximum_select_fusion.10), channel_id=1, source_target_pairs={{0,16},{2,18},{4,20},{6,22},{8,24},{10,26},{12,28},{14,30},{16,0},... | collective-permute-start | bytes 811016 | tf_op jit(solution)/shard_map/ppermute | solution.py:1078
  351.8 12.2 %collective-permute-start.39 = (bf16[256,1024]{1,0:T(8,128)(2,1)}, bf16[256,1024]{1,0:T(8,128)(2,1)}, u32[]{:S(2)}, u32[]{:S(2)}) collective-permute-start(bf16[256,1024]{1,0:T(8,128)(2,1)} %fusion.7), channel_id=1, source_target_pairs={{0,1},{1,0},{2,3},{3,2},{4,5},{5,4},{6,7},{7,6},{8,9},{9,8},{10,11... | collective-permute-start | bytes 1572872 | tf_op jit(solution)/shard_map/ppermute | solution.py:1075
  360.7 9.2 %collective-permute-start.36 = (bf16[4,256,256]{2,1,0:T(8,128)(2,1)S(1)}, bf16[4,256,256]{2,1,0:T(8,128)(2,1)S(1)}, u32[]{:S(2)}, u32[]{:S(2)}) collective-permute-start(bf16[4,256,256]{2,1,0:T(8,128)(2,1)S(1)} %maximum_select_fusion.8), channel_id=1, source_target_pairs={{0,4},{2,6},{4,0},{6,2},{8,12},{10,14},{12,8},{14,10},{16,20},{18,... | collective-permute-start | bytes 1572872 | tf_op jit(solution)/shard_map/ppermute | solution.py:1078
  360.8 10.3 %collective-permute-start.37 = (bf16[4,264,256]{2,1,0:T(8,128)(2,1)S(1)}, bf16[4,264,256]{2,1,0:T(8,128)(2,1)S(1)}, u32[]{:S(2)}, u32[]{:S(2)}) collective-permute-start(bf16[4,264,256]{2,1,0:T(8,128)(2,1)S(1)} %maximum_select_fusion.6), channel_id=1, source_target_pairs={{0,8},{2,10},{4,12},{6,14},{8,0},{10,2},{12,4},{14,6},{16,24},{18,... | collective-permute-start | bytes 1622024 | tf_op jit(solution)/shard_map/ppermute | solution.py:1078
  371.2 4.4 %collective-permute-start.43 = (bf16[8,264,256]{2,1,0:T(8,128)(2,1)S(1)}, bf16[8,264,256]{2,1,0:T(8,128)(2,1)}, u32[]{:S(2)}, u32[]{:S(2)}) collective-permute-start(bf16[8,264,256]{2,1,0:T(8,128)(2,1)S(1)} %maximum_select_fusion.2.bo_ref), channel_id=1, source_target_pairs={{0,2},{2,0},{4,6},{6,4},{8,10},{10,8},{12,14},{14,12},{16,18},{18,... | collective-permute-start | bytes 3244040 | tf_op jit(solution)/shard_map/ppermute | solution.py:1078
  371.3 4.3 %collective-permute-start.42 = (bf16[8,256,256]{2,1,0:T(8,128)(2,1)S(1)}, bf16[8,256,256]{2,1,0:T(8,128)(2,1)}, u32[]{:S(2)}, u32[]{:S(2)}) collective-permute-start(bf16[8,256,256]{2,1,0:T(8,128)(2,1)S(1)} %maximum_select_fusion.5.ao_ref), channel_id=1, source_target_pairs={{0,2},{2,0},{4,6},{6,4},{8,10},{10,8},{12,14},{14,12},{16,18},{18,... | collective-permute-start | bytes 3145736 | tf_op jit(solution)/shard_map/ppermute | solution.py:1078
  371.8 13.8 %copy-start.1 = (bf16[512,1024]{1,0:T(8,128)(2,1)S(1)}, bf16[512,1024]{1,0:T(8,128)(2,1)}, u32[]{:S(2)}) copy-start(bf16[512,1024]{1,0:T(8,128)(2,1)} %param.23) | copy-start | bytes 3145732
  (12 other events, 49.2 us)

commit v7 on v6

--- a/solution.py
+++ b/solution.py
@@ -587,7 +587,7 @@
     )(a, b)
 
 
-def mask_kernel(ids, a_ref, b_ref, c_ref, d_ref, live_ref, o_ref):
+def mask_kernel(ids, a_ref, b_ref, c_ref, d_ref, live_ref, w_ref, o_ref, f_ref):
     i = pl.program_id(0)
     mine = (i % 2) == ids[1]
     for slot, (own, sib) in enumerate(((a_ref, b_ref), (c_ref, d_ref))):
@@ -596,22 +596,37 @@
             v = jnp.where(mine, own[...].astype(f32), sib[...].astype(f32))
             o_ref[...] = (live_ref[...] * v).astype(bf16)
 
-
-def mask_rows(ids, own, own_sib, got, got_sib, live):
+    f = _nt(w_ref[...], o_ref[...]).astype(bf16)
+    for k in range(f_ref.shape[0]):
+        f_ref[k] = f[k * HD : (k + 1) * HD, :]
+
+
+def mask_rows(ids, own, own_sib, got, got_sib, live, w_out, quarter):
     rows, width = own.shape
+    heads = quarter // HD
     return pl.pallas_call(
         mask_kernel,
         grid_spec=pltpu.PrefetchScalarGridSpec(
             num_scalar_prefetch=1,
             grid=(4,),
-            in_specs=[_full(v) for v in (own, own_sib, got, got_sib)] + [pl.BlockSpec((rows, 1), lambda i, ids: (i, 0))],
-            out_specs=pl.BlockSpec((rows, width), lambda i, ids: (i, 0)),
+            in_specs=[_full(v) for v in (own, own_sib, got, got_sib)]
+            + [
+                pl.BlockSpec((rows, 1), lambda i, ids: (i, 0)),
+                pl.BlockSpec((quarter, width), lambda i, ids: (ids[1], 0)),
+            ],
+            out_specs=(
+                pl.BlockSpec((rows, width), lambda i, ids: (i, 0)),
+                pl.BlockSpec((heads, HD, rows), lambda i, ids: (i // 2, 0, i % 2)),
+            ),
         ),
-        out_shape=jax.ShapeDtypeStruct((4 * rows, width), bf16),
+        out_shape=(
+            jax.ShapeDtypeStruct((4 * rows, width), bf16),
+            jax.ShapeDtypeStruct((2 * heads, HD, 2 * rows), bf16),
+        ),
         compiler_params=_params(),
         cost_estimate=pl.CostEstimate(flops=0, transcendentals=0, bytes_accessed=1 << 20),
         name="mask_rows",
-    )(ids, own, own_sib, got, got_sib, live)
+    )(ids, own, own_sib, got, got_sib, live, w_out)
 
 
 def qkv_kernel(
@@ -1150,10 +1165,10 @@
     attn_in, table = lax.optimization_barrier((attn_in, table))
     send = qkv_forward(ids, attn_in, w_qkv, wq_got, qkv_bias, own_table)
     qkv_head = exchange(send.reshape(2 * heads, 3 * HD, rows))
-    dy = mask_rows(ids, cot_own, cot_sib, cot_got, flip(cot_got, CORE), live2)
-    dy2 = dy.reshape(2, rows, width)
+    dy, dctx = mask_rows(ids, cot_own, cot_sib, cot_got, flip(cot_got, CORE), live2, w_out, quarter)
     w_out_mine = rows_of(w_out, core * quarter, quarter)
-    dctx = jnp.einsum("ed,std->set", w_out_mine, dy2, preferred_element_type=f32).astype(bf16)
+    do_head = exchange(dctx)
+
     attn_t, mlp_t = turn(attn_in, mlp_in)
     do_head = exchange(dctx.reshape(2 * heads, HD, rows))
     y_mlp, d_mlp, up_keep, up_send, down_keep, down_send, gb_up = mlp(
@@ -1214,12 +1229,12 @@
         extra = add(extra, back[n3:])
         tail.append(jnp.concatenate([ordered(me, rows_of(v, me * n3, n3), back[:n3]), v[2 * n3 : size], extra])[None])
     grad_tokens = last(e_own, e_got, x_own, cot_own, live_own)
-    cover = [[tot_down], [tot_up], [grad_tokens, output]]
+    cover = [[grad_tokens, output], [tot_down], [tot_up]]
     for k, (a, b) in enumerate(zip(chain_a[::-1], chain_b[::-1])):
         tail = [double(tail[0], a), double(tail[1], b)]
         tail, cover[k] = lax.optimization_barrier((tail, cover[k]))
     mixed = tail
-    (tot_down,), (tot_up,), (grad_tokens, output) = cover
+    (grad_tokens, output), (tot_down,), (tot_up,) = cover
     tot_qkv, tot_out, flat = unpack(ids, mixed[0], flip(mixed[0], CORE), mixed[1], flip(mixed[1], CORE), width)
     flat = flat[:, :6].reshape(12 * width)
 

time: 387 us -> 381 us (0.984)
  waiting for transfers between devices: 140 us -> 130 us
  local copies, waits for them, and re-layouts: 14.9 us -> 21.5 us
  other arithmetic: 28.4 us -> 23.4 us
    ppermute x34, waiting for transfers between devices: 101 us -> 92.1 us  [flip(): return lax.ppermute(v, 'ctx', [(i, i ^ 1 << bit) for i in range(n_ctx)])]
    unnamed x59 -> x75, local copies, waits for them, and re-layouts: 1.4 us -> 9.76 us
    ppermute x10, starting transfers between devices: 10.2 us -> 15 us  [swap(): return lax.ppermute(v, 'wsh', SWAP)]
    ppermute x10, waiting for transfers between devices: 34.4 us -> 30.1 us  [swap(): return lax.ppermute(v, 'wsh', SWAP)]
  transfers between devices with their start and end apart: 48 -> 48, of which waited for: 22 -> 21; matrix products, arithmetic and copies ran while one was open for 11% -> 9% of each run, Pallas kernels for 33% -> 34%
where the time goes in v7:
time: 381 us; the launch traced here: 379 us
  Pallas kernels  136 us (36%)
  waiting for transfers between devices  130 us (34%)
  starting transfers between devices  63.7 us (17%)
  other arithmetic  23.4 us (6%)
  local copies, waits for them, and re-layouts  21.5 us (6%)
    ppermute x34, waiting for transfers between devices, flip(): return lax.ppermute(v, 'ctx', [(i, i ^ 1 << bit) for i in range(n_ctx)])  92.1 us
    pallas_call x1, Pallas kernels, attn_bwd(): pl.pallas_call(lambda *a: attn_bwd_kernel(*a, nblk=nblk, per=x.shape[2] /...  32.1 us
    ppermute x34, starting transfers between devices, flip(): return lax.ppermute(v, 'ctx', [(i, i ^ 1 << bit) for i in range(n_ctx)])  31 us
    ppermute x10, waiting for transfers between devices, swap(): return lax.ppermute(v, 'wsh', SWAP)  30.1 us
    pallas_call x1, Pallas kernels, mlp(): pl.pallas_call(mlp_kernel, grid_spec=pltpu.PrefetchScalarGridSpec(num_sca...  23.1 us
    pallas_call x1, Pallas kernels, attn_fwd(): pl.pallas_call(lambda *a: attn_fwd_kernel(*a, nblk=nblk, per=x.shape[2] /...  18.6 us
    all_to_all x4, starting transfers between devices, exchange(): return lax.all_to_all(v, 'ctx', 0, 0, axis_index_groups=groups, tiled=False)  17.7 us
    ppermute x10, starting transfers between devices, swap(): return lax.ppermute(v, 'wsh', SWAP)  15 us
  transfers between devices with their start and end apart: 48, of which 21 were waited for; matrix products, arithmetic and copies ran while one was open for 9% of the time, Pallas kernels for 34%

profile of v7, /device:TPU:0, one launch (start us, length us, event | category | flops | bytes accessed | tf_op | source)
XLA Modules:
  0.0 379.1 jit_solution(3748286268671034209)
XLA Ops:
  0.7 3.0 collective-permute-start
  6.3 1.9 collective-permute-start.3
  11.0 6.0 %collective-permute-done.2 = bf16[10,512]{1,0:T(8,128)(2,1)S(1)} collective-permute-done((bf16[10,512]{1,0:T(8,128)(2,1)S(1)}, bf16[10,512]{1,0:T(8,128)(2,1)S(1)}, u32[]{:S(2)}, u32[]{:S(2)}) %collective-permute-start.2) | collective-permute-done | bytes 10272 | tf_op jit(solution)/shard_map/ppermute | solution.py:1090
  18.7 3.9 %norm_rows.2 = (bf16[1024,1024]{1,0:T(8,128)(2,1)}, bf16[1024,1024]{1,0:T(8,128)(2,1)}, bf16[1024,1024]{1,0:T(8,128)(2,1)}) custom-call(s32[4]{0:T(128)} %pad_add_fusion.ids, bf16[256,1024]{1,0:T(8,128)(2,1)} %bitcast.167, bf16[256,1024]{1,0:T(8,128)(2,1)} %copy-done.23, f32[4,1024]{1,0:T(4,128)} %maximum_convert_fusion.n_ref), custom_call_target="tpu_custom_call" | custom-call | bytes 1048576 | tf_op jit(solution)/shard_map/norm_rows/pallas_call | solution.py:553
  22.6 10.5 %collective-permute-done.3.gq_ref.gk_ref.gv_ref = bf16[512,768]{1,0:T(8,128)(2,1)S(1)} collective-permute-done((bf16[512,768]{1,0:T(8,128)(2,1)S(1)}, bf16[512,768]{1,0:T(8,128)(2,1)S(1)}, u32[]{:S(2)}, u32[]{:S(2)}) %collective-permute-start.3) | collective-permute-done | bytes 786464 | tf_op jit(solution)/shard_map/ppermute | solution.py:1090
  33.1 1.7 collective-permute-start.6
  35.4 3.9 %norm_rows.3 = (bf16[1024,1024]{1,0:T(8,128)(2,1)}, bf16[1024,1024]{1,0:T(8,128)(2,1)}, bf16[1024,1024]{1,0:T(8,128)(2,1)}) custom-call(s32[4]{0:T(128)} %pad_add_fusion.ids, bf16[256,1024]{1,0:T(8,128)(2,1)} %copy-done.24, bf16[256,1024]{1,0:T(8,128)(2,1)} %collective-permute-done.1.b_ref, ...), custom_call_target="tpu_custom_call", output_to_operand_aliasing={{0}: (4, {}), {1}: (5, {}), {2}: (6, {})} | custom-call | bytes 1048576 | tf_op jit(solution)/shard_map/norm_rows/pallas_call | solution.py:553
  39.4 5.7 %qkv_forward.1 = bf16[2,4,192,512]{3,2,1,0:T(8,128)(2,1)} custom-call(s32[4]{0:T(128)} %pad_add_fusion.ids, bf16[1024,1024]{1,0:T(8,128)(2,1)} %get-tuple-element.81.ain_ref.a_ref, bf16[512,3072]{1,0:T(8,128)(2,1)} %wv_ref.3, bf16[512,3072]{1,0:T(8,128)(2,1)} %wv_ref.3, bf16[512,3072]{1,0:T(8,128)(2,1)} %wv_ref.3, bf16[512,768]{1,0:T(8,128)(2,1)} %copy-done, ...), custom_call_target="tpu_custom_call" | custom-call | flops 1048576 | bytes 1048576 | tf_op jit(solution)/shard_map/qkv_forward/pallas_call | solution.py:659
  45.1 5.9 %all-to-all-start = ((bf16[8,192,512]{2,1,0:T(8,128)(2,1)}), bf16[8,192,512]{2,1,0:T(8,128)(2,1)S(1)}, u32[]{:S(2)}, u32[]{:S(2)}) async-start(bf16[8,192,512]{2,1,0:T(8,128)(2,1)} %bitcast.162), calls=%async_computation | async-start | bytes 3145728 | tf_op jit(solution)/shard_map/all_to_all | solution.py:1117
  51.0 1.3 constant_dynamic-slice_fusion.5
  56.4 5.0 %turn.1 = (bf16[1024,1024]{1,0:T(8,128)(2,1)}, bf16[1024,1024]{1,0:T(8,128)(2,1)}) custom-call(bf16[1024,1024]{1,0:T(8,128)(2,1)} %get-tuple-element.81.ain_ref.a_ref, bf16[1024,1024]{1,0:T(8,128)(2,1)} %get-tuple-element.83.b_ref.x_ref), custom_call_target="tpu_custom_call" | custom-call | bytes 1048576 | tf_op jit(solution)/shard_map/turn/pallas_call | solution.py:578
  61.3 5.7 %mask_rows.1 = (bf16[1024,1024]{1,0:T(8,128)(2,1)}, bf16[8,64,512]{2,1,0:T(8,128)(2,1)}) custom-call(s32[4]{0:T(128)} %pad_add_fusion.ids, bf16[256,1024]{1,0:T(8,128)(2,1)} %bitcast.176, bf16[256,1024]{1,0:T(8,128)(2,1)} %collective-permute-done.5.b_ref, bf16[256,1024]{1,0:T(8,128)(2,1)} %collective-permute-done.6.c_ref, ...), custom_call_target="tpu_custom_call" | custom-call | bytes 1048576 | tf_op jit(solution)/shard_map/mask_rows/pallas_call | solution.py:607
  67.0 8.9 %collective-permute-done.8.wg_ref = bf16[512,1024]{1,0:T(8,128)(2,1)} collective-permute-done((bf16[512,1024]{1,0:T(8,128)(2,1)S(1)}, bf16[512,1024]{1,0:T(8,128)(2,1)}, u32[]{:S(2)}, u32[]{:S(2)}) %collective-permute-start.8) | collective-permute-done | bytes 1048608 | tf_op jit(solution)/shard_map/ppermute | solution.py:1090
  75.9 23.1 %mlp.1 = (bf16[1024,1024]{1,0:T(8,128)(2,1)}, bf16[1024,1024]{1,0:T(8,128)(2,1)}, bf16[4,128,1024]{2,1,0:T(8,128)(2,1)}, bf16[4,128,1024]{2,1,0:T(8,128)(2,1)}, ...) custom-call(s32[4]{0:T(128)} %pad_add_fusion.ids, ...), custom_call_target="tpu_custom_call" | custom-call | flops 12884901888 | bytes 25165824 | tf_op jit(solution)/shard_map/mlp/pallas_call | solution.py:759
  99.1 1.8 collective-permute-start.9
  100.9 1.5 collective-permute-start.10
  102.4 3.6 all-to-all-start.1
  106.0 18.6 %attn_fwd.1 = (bf16[8,64,512]{2,1,0:T(8,128)(2,1)}, f32[1,4096]{1,0:T(1,128)}) custom-call(s32[32]{0:T(128)} %a_0_.3, bf16[8,192,512]{2,1,0:T(8,128)(2,1)} %copy-done.1), custom_call_target="tpu_custom_call" | custom-call | tf_op jit(solution)/shard_map/attn_fwd/pallas_call | solution.py:438
  124.6 8.1 %all-to-all-done.1.a_3_ = bf16[8,64,512]{2,1,0:T(8,128)(2,1)S(1)} async-done(((bf16[8,64,512]{2,1,0:T(8,128)(2,1)}), bf16[8,64,512]{2,1,0:T(8,128)(2,1)S(1)}, u32[]{:S(2)}, u32[]{:S(2)}) %all-to-all-start.1) | async-done | bytes 524320 | tf_op jit(solution)/shard_map/all_to_all | solution.py:1117
  133.7 3.7 all-to-all-start.2
  137.4 2.2 fusion.5
  139.6 1.9 collective-permute-start.11
  141.5 2.1 fusion.6
  143.6 2.4 collective-permute-start.12
  146.0 32.1 %attn_bwd.1 = bf16[8,192,512]{2,1,0:T(8,128)(2,1)} custom-call(s32[32]{0:T(128)} %a_0_.3, bf16[8,192,512]{2,1,0:T(8,128)(2,1)} %copy-done.1, bf16[8,64,512]{2,1,0:T(8,128)(2,1)} %get-tuple-element.97.a_2_, bf16[8,64,512]{2,1,0:T(8,128)(2,1)} %copy-done.12, f32[1,4096]{1,0:T(1,128)} %get-tuple-element.99.a_4_, f32[16,4096]{1,0:T(8,128)} %pad_maximum_fusion.1.a_5_), custom_call_target="tpu_custom_call" | custom-call | tf_op jit(solution)/shard_map/attn_bwd/pallas_call | solution.py:498
  178.9 4.4 %all-to-all-start.3 = ((bf16[8,192,512]{2,1,0:T(8,128)(2,1)}), bf16[8,192,512]{2,1,0:T(8,128)(2,1)}, u32[]{:S(2)}, u32[]{:S(2)}) async-start(bf16[8,192,512]{2,1,0:T(8,128)(2,1)} %attn_bwd.1), calls=%async_computation.3 | async-start | bytes 3145728 | tf_op jit(solution)/shard_map/all_to_all | solution.py:1117
  184.5 1.9 collective-permute-start.36
  186.5 2.3 convert_add_fusion
  189.1 1.7 copy-done.16
  192.0 2.5 collective-permute-start.29
  194.4 5.8 %collective-permute-done.36 = bf16[1,128,1024]{2,1,0:T(8,128)(2,1)S(1)} collective-permute-done((bf16[1,128,1024]{2,1,0:T(8,128)(2,1)S(1)}, bf16[1,128,1024]{2,1,0:T(8,128)(2,1)S(1)}, u32[]{:S(2)}, u32[]{:S(2)}) %collective-permute-start.36) | collective-permute-done | bytes 262176 | tf_op jit(solution)/shard_map/ppermute | solution.py:1093
  202.1 24.7 %collective-permute-done.29 = bf16[1,128,1024]{2,1,0:T(8,128)(2,1)S(1)} collective-permute-done((bf16[1,128,1024]{2,1,0:T(8,128)(2,1)S(1)}, bf16[1,128,1024]{2,1,0:T(8,128)(2,1)S(1)}, u32[]{:S(2)}, u32[]{:S(2)}) %collective-permute-start.29) | collective-permute-done | bytes 262176 | tf_op jit(solution)/shard_map/ppermute | solution.py:1093
  227.8 9.6 %collective-permute-done.30 = bf16[1,128,1024]{2,1,0:T(8,128)(2,1)S(1)} collective-permute-done((bf16[1,128,1024]{2,1,0:T(8,128)(2,1)S(1)}, bf16[1,128,1024]{2,1,0:T(8,128)(2,1)S(1)}, u32[]{:S(2)}, u32[]{:S(2)}) %collective-permute-start.30) | collective-permute-done | bytes 262176 | tf_op jit(solution)/shard_map/ppermute | solution.py:1093
  237.7 2.9 collective-permute-start.39
  240.6 2.2 convert_add_fusion.1
  242.9 14.5 %collective-permute-done.31 = bf16[2,128,1024]{2,1,0:T(8,128)(2,1)S(1)} collective-permute-done((bf16[2,128,1024]{2,1,0:T(8,128)(2,1)S(1)}, bf16[2,128,1024]{2,1,0:T(8,128)(2,1)S(1)}, u32[]{:S(2)}, u32[]{:S(2)}) %collective-permute-start.31) | collective-permute-done | bytes 524320 | tf_op jit(solution)/shard_map/ppermute | solution.py:1093
  258.5 4.9 %collective-permute-start.32 = (bf16[4,128,1024]{2,1,0:T(8,128)(2,1)}, bf16[4,128,1024]{2,1,0:T(8,128)(2,1)}, u32[]{:S(2)}, u32[]{:S(2)}) collective-permute-start(bf16[4,128,1024]{2,1,0:T(8,128)(2,1)} %maximum_select_fusion.3), channel_id=1, source_target_pairs={{0,4},{2,6},{4,0},{6,2},{8,12},{10,14},{12,8},{14,10},{16,20},{18,... | collective-permute-start | bytes 3145736 | tf_op jit(solution)/shard_map/ppermute | solution.py:1093
  265.9 13.5 %qkv_backward.1 = (bf16[8,256,256]{2,1,0:T(8,128)(2,1)}, bf16[8,264,256]{2,1,0:T(8,128)(2,1)}, f32[2,512,1024]{2,1,0:T(8,128)}) custom-call(s32[4]{0:T(128)} %pad_add_fusion.ids, bf16[2,4,192,512]{3,2,1,0:T(8,128)(2,1)} %bitcast.27.d_ref, bf16[1024,1024]{1,0:T(8,128)(2,1)} %get-tuple-element.106.at_ref, bf16[1024,1024]{1,0:T(8,128)(2,1)} %get-tuple-element.107.x_ref, ...), custom_call_target="tpu_custom_call" | custom-call | tf_op jit(solution)/shard_map/qkv_backward/pallas_call | solution.py:901
  279.4 1.4 constant_dynamic-slice_fusion.3
  281.5 2.1 collective-permute-start.18
  283.6 2.1 fusion.4
  285.7 2.0 collective-permute-done.32
  287.7 2.6 maximum_select_fusion.own_ref
  290.4 6.8 %collective-permute-done.13 = bf16[4,256,256]{2,1,0:T(8,128)(2,1)S(1)} collective-permute-done((bf16[4,256,256]{2,1,0:T(8,128)(2,1)S(1)}, bf16[4,256,256]{2,1,0:T(8,128)(2,1)S(1)}, u32[]{:S(2)}, u32[]{:S(2)}) %collective-permute-start.13) | collective-permute-done | bytes 524320 | tf_op jit(solution)/shard_map/ppermute | solution.py:1093
  297.4 6.2 %collective-permute-done.18 = bf16[4,264,256]{2,1,0:T(8,128)(2,1)S(1)} collective-permute-done((bf16[4,264,256]{2,1,0:T(8,128)(2,1)S(1)}, bf16[4,264,256]{2,1,0:T(8,128)(2,1)S(1)}, u32[]{:S(2)}, u32[]{:S(2)}) %collective-permute-start.18) | collective-permute-done | bytes 540704 | tf_op jit(solution)/shard_map/ppermute | solution.py:1093
  303.7 1.8 collective-permute-start.19
  305.5 1.9 maximum_select_fusion.1.own_ref
  307.5 1.8 collective-permute-done.14
  309.6 8.9 %collective-permute-done.19 = bf16[2,264,256]{2,1,0:T(8,128)(2,1)S(1)} collective-permute-done((bf16[2,264,256]{2,1,0:T(8,128)(2,1)S(1)}, bf16[2,264,256]{2,1,0:T(8,128)(2,1)S(1)}, u32[]{:S(2)}, u32[]{:S(2)}) %collective-permute-start.19) | collective-permute-done | bytes 270368 | tf_op jit(solution)/shard_map/ppermute | solution.py:1093
  320.0 2.2 collective-permute-start.16
  322.2 1.5 collective-permute-done.20
  323.8 2.2 collective-permute-start.21
  326.1 2.6 collective-permute-done.21
  329.2 2.1 collective-permute-start.24
  332.5 3.9 %collective-permute-done.22 = bf16[1,264,256]{2,1,0:T(8,128)(2,1)S(1)} collective-permute-done((bf16[1,264,256]{2,1,0:T(8,128)(2,1)S(1)}, bf16[1,264,256]{2,1,0:T(8,128)(2,1)S(1)}, u32[]{:S(2)}, u32[]{:S(2)}) %collective-permute-start.22) | collective-permute-done | bytes 135200 | tf_op jit(solution)/shard_map/ppermute | solution.py:1093
  336.4 2.0 collective-permute-done.24.er_ref
  339.2 3.4 token_grad.1
  342.7 2.8 collective-permute-start.28
  345.5 1.3 copy-done.11
  346.9 7.0 %join_rows.1 = f32[2048,1024]{1,0:T(8,128)} custom-call(s32[4]{0:T(128)} %pad_add_fusion.ids, bf16[8,128,1024]{2,1,0:T(8,128)(2,1)} %copy-done.3, bf16[8,128,1024]{2,1,0:T(8,128)(2,1)} %copy-done.11), custom_call_target="tpu_custom_call" | custom-call | tf_op jit(solution)/shard_map/join_rows/pallas_call | solution.py:956
  354.6 7.1 %join_cols.1 = f32[512,4096]{1,0:T(8,128)} custom-call(s32[4]{0:T(128)} %pad_add_fusion.ids, bf16[8,2,64,1024]{3,2,1,0:T(8,128)(2,1)} %copy-done.4, bf16[8,2,64,1024]{3,2,1,0:T(8,128)(2,1)} %collective-permute-done.41.got_ref), custom_call_target="tpu_custom_call" | custom-call | tf_op jit(solution)/shard_map/join_cols/pallas_call | solution.py:973
  361.7 1.7 collective-permute-done.34
  364.4 3.8 %collective-permute-done.42.ag_ref = bf16[8,256,256]{2,1,0:T(8,128)(2,1)} collective-permute-done((bf16[8,256,256]{2,1,0:T(8,128)(2,1)S(1)}, bf16[8,256,256]{2,1,0:T(8,128)(2,1)}, u32[]{:S(2)}, u32[]{:S(2)}) %collective-permute-start.42) | collective-permute-done | bytes 1048608 | tf_op jit(solution)/shard_map/ppermute | solution.py:1093
  369.2 6.6 %unpack.1 = (f32[512,3072]{1,0:T(8,128)}, f32[2,256,1024]{2,1,0:T(8,128)}, f32[8,8,256]{2,1,0:T(8,128)}) custom-call(s32[4]{0:T(128)} %pad_add_fusion.ids, bf16[8,256,256]{2,1,0:T(8,128)(2,1)} %copy-done.8, bf16[8,256,256]{2,1,0:T(8,128)(2,1)} %collective-permute-done.42.ag_ref, bf16[8,264,256]{2,1,0:T(8,128)(2,1)} %copy-done.7, bf16[8,264,256]{2,1,0:T(8,128)(2,1)} %copy-done.14), custom_call_target="tpu_custom_call" | custom-call | tf_op jit(solution)/shard_map/unpack/pallas_call | solution.py:1017
  (212 shorter events, 33.4 us)
Async XLA Ops:
  0.7 7.5 %copy-start.29 = (s32[32]{0:T(128)S(1)}, s32[32]{0:T(128)}, u32[]{:S(2)}) copy-start(s32[32]{0:T(128)} %a_0_.3) | copy-start | bytes 388
  0.7 16.4 %collective-permute-start = (bf16[256,1024]{1,0:T(8,128)(2,1)}, bf16[256,1024]{1,0:T(8,128)(2,1)S(1)}, u32[]{:S(2)}, u32[]{:S(2)}) collective-permute-start(bf16[256,1024]{1,0:T(8,128)(2,1)} %bitcast.165), channel_id=1, source_target_pairs={{0,1},{1,0},{2,3},{3,2},{4,5},{5,4},{6,7},{7,6},{8,9},{9,8},{10,11... | collective-permute-start | bytes 1572872 | tf_op jit(solution)/shard_map/ppermute | solution.py:1090
  3.8 14.2 %collective-permute-start.4 = (bf16[256,1024]{1,0:T(8,128)(2,1)}, bf16[256,1024]{1,0:T(8,128)(2,1)S(1)}, u32[]{:S(2)}, u32[]{:S(2)}) collective-permute-start(bf16[256,1024]{1,0:T(8,128)(2,1)} %bitcast.166), channel_id=1, source_target_pairs={{0,2},{2,0},{4,6},{6,4},{8,10},{10,8},{12,14},{14,12},{16,18},{18,... | collective-permute-start | bytes 1572872 | tf_op jit(solution)/shard_map/ppermute | solution.py:1093
  5.6 27.5 %copy-start.13 = (bf16[1,256,1024]{2,1,0:T(8,128)(2,1)S(1)}, bf16[1,256,1024]{2,1,0:T(8,128)(2,1)}, u32[]{:S(2)}) copy-start(bf16[1,256,1024]{2,1,0:T(8,128)(2,1)} %param.31) | copy-start | bytes 1572868
  6.1 10.9 %collective-permute-start.2 = (bf16[10,512]{1,0:T(8,128)(2,1)S(1)}, bf16[10,512]{1,0:T(8,128)(2,1)S(1)}, u32[]{:S(2)}, u32[]{:S(2)}) collective-permute-start(bf16[10,512]{1,0:T(8,128)(2,1)S(1)} %concatenate.150), channel_id=1, source_target_pairs={{0,1},{1,0},{2,3},{3,2},{4,5},{5,4},{6,7},{7,6},{8,9},{9,8},{10,11... | collective-permute-start | bytes 30728 | tf_op jit(solution)/shard_map/ppermute | solution.py:1090
  6.3 26.8 %collective-permute-start.3 = (bf16[512,768]{1,0:T(8,128)(2,1)S(1)}, bf16[512,768]{1,0:T(8,128)(2,1)S(1)}, u32[]{:S(2)}, u32[]{:S(2)}) collective-permute-start(bf16[512,768]{1,0:T(8,128)(2,1)S(1)} %pad_maximum_fusion), channel_id=1, source_target_pairs={{0,1},{1,0},{2,3},{3,2},{4,5},{5,4},{6,7},{7,6},{8,9},{9,8},{10,11... | collective-permute-start | bytes 2359304 | tf_op jit(solution)/shard_map/ppermute | solution.py:1090
  17.1 18.3 %copy-start.24 = (bf16[256,1024]{1,0:T(8,128)(2,1)}, bf16[256,1024]{1,0:T(8,128)(2,1)S(1)}, u32[]{:S(2)}) copy-start(bf16[256,1024]{1,0:T(8,128)(2,1)S(1)} %collective-permute-done.a_ref) | copy-start | bytes 1572868
  17.1 18.3 %collective-permute-start.1 = (bf16[256,1024]{1,0:T(8,128)(2,1)S(1)}, bf16[256,1024]{1,0:T(8,128)(2,1)}, u32[]{:S(2)}, u32[]{:S(2)}) collective-permute-start(bf16[256,1024]{1,0:T(8,128)(2,1)S(1)} %collective-permute-done.a_ref), channel_id=1, source_target_pairs={{0,2},{2,0},{4,6},{6,4},{8,10},{10,8},{12,14},{14,12},{16,18},{18,... | collective-permute-start | bytes 1572872 | tf_op jit(solution)/shard_map/ppermute | solution.py:1093
  33.1 6.3 %copy-start = (bf16[512,768]{1,0:T(8,128)(2,1)}, bf16[512,768]{1,0:T(8,128)(2,1)S(1)}, u32[]{:S(2)}) copy-start(bf16[512,768]{1,0:T(8,128)(2,1)S(1)} %collective-permute-done.3.gq_ref.gk_ref.gv_ref) | copy-start | bytes 2359300
  33.1 19.2 %collective-permute-start.6 = (bf16[256,1024]{1,0:T(8,128)(2,1)S(1)}, bf16[256,1024]{1,0:T(8,128)(2,1)}, u32[]{:S(2)}, u32[]{:S(2)}) collective-permute-start(bf16[256,1024]{1,0:T(8,128)(2,1)S(1)} %bitcast.178), channel_id=1, source_target_pairs={{0,1},{1,0},{2,3},{3,2},{4,5},{5,4},{6,7},{7,6},{8,9},{9,8},{10,11... | collective-permute-start | bytes 1572872 | tf_op jit(solution)/shard_map/ppermute | solution.py:1090
  45.1 7.8 %copy-start.27 = (bf16[2048]{0:T(1024)(128)(2,1)S(1)}, bf16[2048]{0:T(1024)(128)(2,1)}, u32[]{:S(2)}) copy-start(bf16[2048]{0:T(1024)(128)(2,1)} %param.26) | copy-start | bytes 12292
  45.1 54.0 %all-to-all-start = ((bf16[8,192,512]{2,1,0:T(8,128)(2,1)}), bf16[8,192,512]{2,1,0:T(8,128)(2,1)S(1)}, u32[]{:S(2)}, u32[]{:S(2)}) async-start(bf16[8,192,512]{2,1,0:T(8,128)(2,1)} %bitcast.162), calls=%async_computation | async-start | bytes 3145728 | tf_op jit(solution)/shard_map/all_to_all | solution.py:1117
  52.3 23.6 %collective-permute-start.8 = (bf16[512,1024]{1,0:T(8,128)(2,1)S(1)}, bf16[512,1024]{1,0:T(8,128)(2,1)}, u32[]{:S(2)}, u32[]{:S(2)}) collective-permute-start(bf16[512,1024]{1,0:T(8,128)(2,1)S(1)} %constant_dynamic-slice_fusion.5), channel_id=1, source_target_pairs={{0,1},{1,0},{2,3},{3,2},{4,5},{5,4},{6,7},{7,6},{8,9},{9,8},{10,11... | collective-permute-start | bytes 3145736 | tf_op jit(solution)/shard_map/ppermute | solution.py:1090
  52.9 8.5 %collective-permute-start.5 = (bf16[256,1024]{1,0:T(8,128)(2,1)S(1)}, bf16[256,1024]{1,0:T(8,128)(2,1)}, u32[]{:S(2)}, u32[]{:S(2)}) collective-permute-start(bf16[256,1024]{1,0:T(8,128)(2,1)S(1)} %bitcast.179), channel_id=1, source_target_pairs={{0,2},{2,0},{4,6},{6,4},{8,10},{10,8},{12,14},{14,12},{16,18},{18,... | collective-permute-start | bytes 1572872 | tf_op jit(solution)/shard_map/ppermute | solution.py:1093
  54.1 7.2 %collective-permute-start.7 = (bf16[256,1024]{1,0:T(8,128)(2,1)}, bf16[256,1024]{1,0:T(8,128)(2,1)}, u32[]{:S(2)}, u32[]{:S(2)}) collective-permute-start(bf16[256,1024]{1,0:T(8,128)(2,1)} %collective-permute-done.6.c_ref), channel_id=1, source_target_pairs={{0,2},{2,0},{4,6},{6,4},{8,10},{10,8},{12,14},{14,12},{16,18},{18,... | collective-permute-start | bytes 1572872 | tf_op jit(solution)/shard_map/ppermute | solution.py:1093
  99.1 6.9 %copy-start.1 = (bf16[8,192,512]{2,1,0:T(8,128)(2,1)}, bf16[8,192,512]{2,1,0:T(8,128)(2,1)S(1)}, u32[]{:S(2)}) copy-start(bf16[8,192,512]{2,1,0:T(8,128)(2,1)S(1)} %all-to-all-done.a_1_) | copy-start | bytes 4718596
  99.1 33.5 %collective-permute-start.9 = (bf16[4,128,1024]{2,1,0:T(8,128)(2,1)}, bf16[4,128,1024]{2,1,0:T(8,128)(2,1)S(1)}, u32[]{:S(2)}, u32[]{:S(2)}) collective-permute-start(bf16[4,128,1024]{2,1,0:T(8,128)(2,1)} %get-tuple-element.94), channel_id=1, source_target_pairs={{0,4},{2,6},{4,0},{6,2},{8,12},{10,14},{12,8},{14,10},{16,20},{18,... | collective-permute-start | bytes 3145736 | tf_op jit(solution)/shard_map/ppermute | solution.py:1093
  100.9 31.7 %collective-permute-start.10 = (bf16[4,128,1024]{2,1,0:T(8,128)(2,1)}, bf16[4,128,1024]{2,1,0:T(8,128)(2,1)}, u32[]{:S(2)}, u32[]{:S(2)}) collective-permute-start(bf16[4,128,1024]{2,1,0:T(8,128)(2,1)} %get-tuple-element.95), channel_id=1, source_target_pairs={{0,8},{2,10},{4,12},{6,14},{8,0},{10,2},{12,4},{14,6},{16,24},{18,... | collective-permute-start | bytes 3145736 | tf_op jit(solution)/shard_map/ppermute | solution.py:1093
  102.4 30.3 %all-to-all-start.1 = ((bf16[8,64,512]{2,1,0:T(8,128)(2,1)}), bf16[8,64,512]{2,1,0:T(8,128)(2,1)S(1)}, u32[]{:S(2)}, u32[]{:S(2)}) async-start(bf16[8,64,512]{2,1,0:T(8,128)(2,1)} %get-tuple-element.93), calls=%async_computation.1 | async-start | bytes 1048576 | tf_op jit(solution)/shard_map/all_to_all | solution.py:1117
  124.6 17.0 %copy-start.19 = (bf16[4,128,1024]{2,1,0:T(8,128)(2,1)S(1)}, bf16[4,128,1024]{2,1,0:T(8,128)(2,1)}, u32[]{:S(2)}) copy-start(bf16[4,128,1024]{2,1,0:T(8,128)(2,1)} %get-tuple-element.103) | copy-start | bytes 3145732
  132.6 11.0 %copy-start.12 = (bf16[8,64,512]{2,1,0:T(8,128)(2,1)}, bf16[8,64,512]{2,1,0:T(8,128)(2,1)S(1)}, u32[]{:S(2)}) copy-start(bf16[8,64,512]{2,1,0:T(8,128)(2,1)S(1)} %all-to-all-done.1.a_3_) | copy-start | bytes 1572868
  133.7 44.5 %all-to-all-start.2 = ((bf16[8,64,512]{2,1,0:T(8,128)(2,1)}), bf16[8,64,512]{2,1,0:T(8,128)(2,1)S(1)}, u32[]{:S(2)}, u32[]{:S(2)}) async-start(bf16[8,64,512]{2,1,0:T(8,128)(2,1)} %get-tuple-element.97.a_2_), calls=%async_computation.2 | async-start | bytes 1048576 | tf_op jit(solution)/shard_map/all_to_all | solution.py:1117
  139.6 38.5 %collective-permute-start.11 = (bf16[2,128,1024]{2,1,0:T(8,128)(2,1)}, bf16[2,128,1024]{2,1,0:T(8,128)(2,1)S(1)}, u32[]{:S(2)}, u32[]{:S(2)}) collective-permute-start(bf16[2,128,1024]{2,1,0:T(8,128)(2,1)} %fusion.5), channel_id=1, source_target_pairs={{0,8},{2,10},{4,12},{6,14},{8,0},{10,2},{12,4},{14,6},{16,24},{18,... | collective-permute-start | bytes 1572872 | tf_op jit(solution)/shard_map/ppermute | solution.py:1093
  143.6 34.5 %collective-permute-start.12 = (bf16[2,128,1024]{2,1,0:T(8,128)(2,1)}, bf16[2,128,1024]{2,1,0:T(8,128)(2,1)S(1)}, u32[]{:S(2)}, u32[]{:S(2)}) collective-permute-start(bf16[2,128,1024]{2,1,0:T(8,128)(2,1)} %fusion.6), channel_id=1, source_target_pairs={{0,16},{2,18},{4,20},{6,22},{8,24},{10,26},{12,28},{14,30},{16,0},... | collective-permute-start | bytes 1572872 | tf_op jit(solution)/shard_map/ppermute | solution.py:1093
  178.1 5.2 %copy-start.20 = (bf16[4,128,1024]{2,1,0:T(8,128)(2,1)S(1)}, bf16[4,128,1024]{2,1,0:T(8,128)(2,1)}, u32[]{:S(2)}) copy-start(bf16[4,128,1024]{2,1,0:T(8,128)(2,1)} %get-tuple-element.103) | copy-start | bytes 3145732
  178.9 7.5 %copy-start.5 = (bf16[8,64,512]{2,1,0:T(8,128)(2,1)}, bf16[8,64,512]{2,1,0:T(8,128)(2,1)S(1)}, u32[]{:S(2)}) copy-start(bf16[8,64,512]{2,1,0:T(8,128)(2,1)S(1)} %all-to-all-done.2) | copy-start | bytes 1572868
  178.9 7.5 %copy-start.10 = (bf16[512,1024]{1,0:T(8,128)(2,1)S(1)}, bf16[512,1024]{1,0:T(8,128)(2,1)}, u32[]{:S(2)}) copy-start(bf16[512,1024]{1,0:T(8,128)(2,1)} %w_ref.1) | copy-start | bytes 3145732
  178.9 87.0 %all-to-all-start.3 = ((bf16[8,192,512]{2,1,0:T(8,128)(2,1)}), bf16[8,192,512]{2,1,0:T(8,128)(2,1)}, u32[]{:S(2)}, u32[]{:S(2)}) async-start(bf16[8,192,512]{2,1,0:T(8,128)(2,1)} %attn_bwd.1), calls=%async_computation.3 | async-start | bytes 3145728 | tf_op jit(solution)/shard_map/all_to_all | solution.py:1117
  184.5 15.8 %collective-permute-start.36 = (bf16[1,128,1024]{2,1,0:T(8,128)(2,1)S(1)}, bf16[1,128,1024]{2,1,0:T(8,128)(2,1)S(1)}, u32[]{:S(2)}, u32[]{:S(2)}) collective-permute-start(bf16[1,128,1024]{2,1,0:T(8,128)(2,1)S(1)} %fusion.9), channel_id=1, source_target_pairs={{0,4},{2,6},{4,0},{6,2},{8,12},{10,14},{12,8},{14,10},{16,20},{18,... | collective-permute-start | bytes 786440 | tf_op jit(solution)/shard_map/ppermute | solution.py:1093
  188.8 12.6 %copy-start.2 = (f32[2,512,1024]{2,1,0:T(8,128)}, f32[2,512,1024]{2,1,0:T(8,128)S(1)}, u32[]{:S(2)}) copy-start(f32[2,512,1024]{2,1,0:T(8,128)S(1)} %convert_add_fusion) | copy-start | bytes 12582916
  188.8 11.5 %copy-start.22 = (bf16[2,128,1024]{2,1,0:T(8,128)(2,1)S(1)}, bf16[2,128,1024]{2,1,0:T(8,128)(2,1)}, u32[]{:S(2)}) copy-start(bf16[2,128,1024]{2,1,0:T(8,128)(2,1)} %copy-done.21) | copy-start | bytes 1572868
  189.0 51.6 %collective-permute-start.25 = (bf16[2,256,1024]{2,1,0:T(8,128)(2,1)S(1)}, bf16[2,256,1024]{2,1,0:T(8,128)(2,1)}, u32[]{:S(2)}, u32[]{:S(2)}) collective-permute-start(bf16[2,256,1024]{2,1,0:T(8,128)(2,1)S(1)} %dynamic-slice_convert_fusion), channel_id=1, source_target_pairs={{0,2},{2,0},{4,6},{6,4},{8,10},{10,8},{12,14},{14,12},{16,18},{18,... | collective-permute-start | bytes 3145736 | tf_op jit(solution)/shard_map/ppermute | solution.py:1093
  192.0 34.8 %collective-permute-start.29 = (bf16[1,128,1024]{2,1,0:T(8,128)(2,1)S(1)}, bf16[1,128,1024]{2,1,0:T(8,128)(2,1)S(1)}, u32[]{:S(2)}, u32[]{:S(2)}) collective-permute-start(bf16[1,128,1024]{2,1,0:T(8,128)(2,1)S(1)} %fusion.12), channel_id=1, source_target_pairs={{0,16},{2,18},{4,20},{6,22},{8,24},{10,26},{12,28},{14,30},{16,0},... | collective-permute-start | bytes 786440 | tf_op jit(solution)/shard_map/ppermute | solution.py:1093
  201.5 25.6 %collective-permute-start.37 = (bf16[1,1,64,1024]{3,2,1,0:T(8,128)(2,1)S(1)}, bf16[1,1,64,1024]{3,2,1,0:T(8,128)(2,1)S(1)}, u32[]{:S(2)}, u32[]{:S(2)}) collective-permute-start(bf16[1,1,64,1024]{3,2,1,0:T(8,128)(2,1)S(1)} %get-tuple-element.138), channel_id=1, source_target_pairs={{0,1},{1,0},{2,3},{3,2},{4,5},{5,4},{6,7},{7,6},{8,9},{9,8},{10,11... | collective-permute-start | bytes 393224 | tf_op jit(solution)/shard_map/ppermute | solution.py:1090
  226.9 10.4 %collective-permute-start.30 = (bf16[1,128,1024]{2,1,0:T(8,128)(2,1)S(1)}, bf16[1,128,1024]{2,1,0:T(8,128)(2,1)S(1)}, u32[]{:S(2)}, u32[]{:S(2)}) collective-permute-start(bf16[1,128,1024]{2,1,0:T(8,128)(2,1)S(1)} %fusion.14), channel_id=1, source_target_pairs={{0,16},{2,18},{4,20},{6,22},{8,24},{10,26},{12,28},{14,30},{16,0},... | collective-permute-start | bytes 786440 | tf_op jit(solution)/shard_map/ppermute | solution.py:1093
  227.1 10.5 %collective-permute-start.38 = (bf16[1,2,64,1024]{3,2,1,0:T(8,128)(2,1)S(1)}, bf16[1,2,64,1024]{3,2,1,0:T(8,128)(2,1)S(1)}, u32[]{:S(2)}, u32[]{:S(2)}) collective-permute-start(bf16[1,2,64,1024]{3,2,1,0:T(8,128)(2,1)S(1)} %maximum_select_fusion.12), channel_id=1, source_target_pairs={{0,4},{2,6},{4,0},{6,2},{8,12},{10,14},{12,8},{14,10},{16,20},{18,... | collective-permute-start | bytes 786440 | tf_op jit(solution)/shard_map/ppermute | solution.py:1093
  237.5 19.9 %collective-permute-start.31 = (bf16[2,128,1024]{2,1,0:T(8,128)(2,1)S(1)}, bf16[2,128,1024]{2,1,0:T(8,128)(2,1)S(1)}, u32[]{:S(2)}, u32[]{:S(2)}) collective-permute-start(bf16[2,128,1024]{2,1,0:T(8,128)(2,1)S(1)} %maximum_select_fusion.8), channel_id=1, source_target_pairs={{0,8},{2,10},{4,12},{6,14},{8,0},{10,2},{12,4},{14,6},{16,24},{18,... | collective-permute-start | bytes 1572872 | tf_op jit(solution)/shard_map/ppermute | solution.py:1093
  237.7 27.1 %collective-permute-start.39 = (bf16[2,2,64,1024]{3,2,1,0:T(8,128)(2,1)S(1)}, bf16[2,2,64,1024]{3,2,1,0:T(8,128)(2,1)S(1)}, u32[]{:S(2)}, u32[]{:S(2)}) collective-permute-start(bf16[2,2,64,1024]{3,2,1,0:T(8,128)(2,1)S(1)} %maximum_select_fusion.9), channel_id=1, source_target_pairs={{0,16},{2,18},{4,20},{6,22},{8,24},{10,26},{12,28},{14,30},{16,0},... | collective-permute-start | bytes 1572872 | tf_op jit(solution)/shard_map/ppermute | solution.py:1093
  258.5 29.3 %collective-permute-start.32 = (bf16[4,128,1024]{2,1,0:T(8,128)(2,1)}, bf16[4,128,1024]{2,1,0:T(8,128)(2,1)}, u32[]{:S(2)}, u32[]{:S(2)}) collective-permute-start(bf16[4,128,1024]{2,1,0:T(8,128)(2,1)} %maximum_select_fusion.3), channel_id=1, source_target_pairs={{0,4},{2,6},{4,0},{6,2},{8,12},{10,14},{12,8},{14,10},{16,20},{18,... | collective-permute-start | bytes 3145736 | tf_op jit(solution)/shard_map/ppermute | solution.py:1093
  264.2 19.4 %collective-permute-start.26 = (bf16[256,1024]{1,0:T(8,128)(2,1)}, bf16[256,1024]{1,0:T(8,128)(2,1)}, u32[]{:S(2)}, u32[]{:S(2)}) collective-permute-start(bf16[256,1024]{1,0:T(8,128)(2,1)} %fusion.8), channel_id=1, source_target_pairs={{0,1},{1,0},{2,3},{3,2},{4,5},{5,4},{6,7},{7,6},{8,9},{9,8},{10,11... | collective-permute-start | bytes 1572872 | tf_op jit(solution)/shard_map/ppermute | solution.py:1090
  265.0 40.5 %collective-permute-start.40 = (bf16[4,2,64,1024]{3,2,1,0:T(8,128)(2,1)S(1)}, bf16[4,2,64,1024]{3,2,1,0:T(8,128)(2,1)}, u32[]{:S(2)}, u32[]{:S(2)}) collective-permute-start(bf16[4,2,64,1024]{3,2,1,0:T(8,128)(2,1)S(1)} %maximum_select_fusion.5), channel_id=1, source_target_pairs={{0,8},{2,10},{4,12},{6,14},{8,0},{10,2},{12,4},{14,6},{16,24},{18,... | collective-permute-start | bytes 3145736 | tf_op jit(solution)/shard_map/ppermute | solution.py:1093
  280.8 16.4 %collective-permute-start.13 = (bf16[4,256,256]{2,1,0:T(8,128)(2,1)S(1)}, bf16[4,256,256]{2,1,0:T(8,128)(2,1)S(1)}, u32[]{:S(2)}, u32[]{:S(2)}) collective-permute-start(bf16[4,256,256]{2,1,0:T(8,128)(2,1)S(1)} %get-tuple-element.136), channel_id=1, source_target_pairs={{0,4},{2,6},{4,0},{6,2},{8,12},{10,14},{12,8},{14,10},{16,20},{18,... | collective-permute-start | bytes 1572872 | tf_op jit(solution)/shard_map/ppermute | solution.py:1093
  281.5 22.1 %collective-permute-start.18 = (bf16[4,264,256]{2,1,0:T(8,128)(2,1)S(1)}, bf16[4,264,256]{2,1,0:T(8,128)(2,1)S(1)}, u32[]{:S(2)}, u32[]{:S(2)}) collective-permute-start(bf16[4,264,256]{2,1,0:T(8,128)(2,1)S(1)} %get-tuple-element.134), channel_id=1, source_target_pairs={{0,8},{2,10},{4,12},{6,14},{8,0},{10,2},{12,4},{14,6},{16,24},{18,... | collective-permute-start | bytes 1622024 | tf_op jit(solution)/shard_map/ppermute | solution.py:1093
  290.3 17.0 %copy-start.3 = (bf16[8,128,1024]{2,1,0:T(8,128)(2,1)}, bf16[8,128,1024]{2,1,0:T(8,128)(2,1)S(1)}, u32[]{:S(2)}) copy-start(bf16[8,128,1024]{2,1,0:T(8,128)(2,1)S(1)} %maximum_select_fusion.own_ref) | copy-start | bytes 6291460
  290.4 55.2 %collective-permute-start.33 = (bf16[8,128,1024]{2,1,0:T(8,128)(2,1)S(1)}, bf16[8,128,1024]{2,1,0:T(8,128)(2,1)S(1)}, u32[]{:S(2)}, u32[]{:S(2)}) collective-permute-start(bf16[8,128,1024]{2,1,0:T(8,128)(2,1)S(1)} %maximum_select_fusion.own_ref), channel_id=1, source_target_pairs={{0,2},{2,0},{4,6},{6,4},{8,10},{10,8},{12,14},{14,12},{16,18},{18,... | collective-permute-start | bytes 6291464 | tf_op jit(solution)/shard_map/ppermute | solution.py:1093
  297.3 11.9 %collective-permute-start.14 = (bf16[2,256,256]{2,1,0:T(8,128)(2,1)S(1)}, bf16[2,256,256]{2,1,0:T(8,128)(2,1)S(1)}, u32[]{:S(2)}, u32[]{:S(2)}) collective-permute-start(bf16[2,256,256]{2,1,0:T(8,128)(2,1)S(1)} %fusion.21), channel_id=1, source_target_pairs={{0,8},{2,10},{4,12},{6,14},{8,0},{10,2},{12,4},{14,6},{16,24},{18,... | collective-permute-start | bytes 786440 | tf_op jit(solution)/shard_map/ppermute | solution.py:1093
  303.7 5.7 %copy-start.9 = (f32[2,512,1024]{2,1,0:T(8,128)S(1)}, f32[2,512,1024]{2,1,0:T(8,128)}, u32[]{:S(2)}) copy-start(f32[2,512,1024]{2,1,0:T(8,128)} %get-tuple-element.113) | copy-start | bytes 12582916
  303.7 14.8 %collective-permute-start.19 = (bf16[2,264,256]{2,1,0:T(8,128)(2,1)S(1)}, bf16[2,264,256]{2,1,0:T(8,128)(2,1)S(1)}, u32[]{:S(2)}, u32[]{:S(2)}) collective-permute-start(bf16[2,264,256]{2,1,0:T(8,128)(2,1)S(1)} %fusion.17), channel_id=1, source_target_pairs={{0,16},{2,18},{4,20},{6,22},{8,24},{10,26},{12,28},{14,30},{16,0},... | collective-permute-start | bytes 811016 | tf_op jit(solution)/shard_map/ppermute | solution.py:1093
  307.4 16.4 %copy-start.4 = (bf16[8,2,64,1024]{3,2,1,0:T(8,128)(2,1)}, bf16[8,2,64,1024]{3,2,1,0:T(8,128)(2,1)S(1)}, u32[]{:S(2)}) copy-start(bf16[8,2,64,1024]{3,2,1,0:T(8,128)(2,1)S(1)} %maximum_select_fusion.1.own_ref) | copy-start | bytes 6291460
  307.4 47.2 %collective-permute-start.41 = (bf16[8,2,64,1024]{3,2,1,0:T(8,128)(2,1)S(1)}, bf16[8,2,64,1024]{3,2,1,0:T(8,128)(2,1)}, u32[]{:S(2)}, u32[]{:S(2)}) collective-permute-start(bf16[8,2,64,1024]{3,2,1,0:T(8,128)(2,1)S(1)} %maximum_select_fusion.1.own_ref), channel_id=1, source_target_pairs={{0,2},{2,0},{4,6},{6,4},{8,10},{10,8},{12,14},{14,12},{16,18},{18,... | collective-permute-start | bytes 6291464 | tf_op jit(solution)/shard_map/ppermute | solution.py:1093
  309.3 10.6 %collective-permute-start.15 = (bf16[1,256,256]{2,1,0:T(8,128)(2,1)S(1)}, bf16[1,256,256]{2,1,0:T(8,128)(2,1)S(1)}, u32[]{:S(2)}, u32[]{:S(2)}) collective-permute-start(bf16[1,256,256]{2,1,0:T(8,128)(2,1)S(1)} %fusion.22), channel_id=1, source_target_pairs={{0,16},{2,18},{4,20},{6,22},{8,24},{10,26},{12,28},{14,30},{16,0},... | collective-permute-start | bytes 393224 | tf_op jit(solution)/shard_map/ppermute | solution.py:1093
  309.6 19.2 %collective-permute-start.23 = (bf16[2,256,1024]{2,1,0:T(8,128)(2,1)S(1)}, bf16[2,256,1024]{2,1,0:T(8,128)(2,1)S(1)}, u32[]{:S(2)}, u32[]{:S(2)}) collective-permute-start(bf16[2,256,1024]{2,1,0:T(8,128)(2,1)S(1)} %dynamic-slice_convert_fusion.1), channel_id=1, source_target_pairs={{0,2},{2,0},{4,6},{6,4},{8,10},{10,8},{12,14},{14,12},{16,18},{18,... | collective-permute-start | bytes 3145736 | tf_op jit(solution)/shard_map/ppermute | solution.py:1093
  318.6 5.1 %collective-permute-start.20 = (bf16[1,264,256]{2,1,0:T(8,128)(2,1)S(1)}, bf16[1,264,256]{2,1,0:T(8,128)(2,1)S(1)}, u32[]{:S(2)}, u32[]{:S(2)}) collective-permute-start(bf16[1,264,256]{2,1,0:T(8,128)(2,1)S(1)} %fusion.18), channel_id=1, source_target_pairs={{0,4},{2,6},{4,0},{6,2},{8,12},{10,14},{12,8},{14,10},{16,20},{18,... | collective-permute-start | bytes 405512 | tf_op jit(solution)/shard_map/ppermute | solution.py:1093
  320.0 6.0 %collective-permute-start.16 = (bf16[96,256]{1,0:T(8,128)(2,1)S(1)}, bf16[96,256]{1,0:T(8,128)(2,1)S(1)}, u32[]{:S(2)}, u32[]{:S(2)}) collective-permute-start(bf16[96,256]{1,0:T(8,128)(2,1)S(1)} %get-tuple-element.142), channel_id=1, source_target_pairs={{0,1},{1,0},{2,3},{3,2},{4,5},{5,4},{6,7},{7,6},{8,9},{9,8},{10,11... | collective-permute-start | bytes 147464 | tf_op jit(solution)/shard_map/ppermute | solution.py:1090
  323.8 4.9 %collective-permute-start.21 = (bf16[104,256]{1,0:T(8,128)(2,1)S(1)}, bf16[104,256]{1,0:T(8,128)(2,1)S(1)}, u32[]{:S(2)}, u32[]{:S(2)}) collective-permute-start(bf16[104,256]{1,0:T(8,128)(2,1)S(1)} %pad_maximum_fusion.2), channel_id=1, source_target_pairs={{0,1},{1,0},{2,3},{3,2},{4,5},{5,4},{6,7},{7,6},{8,9},{9,8},{10,11... | collective-permute-start | bytes 159752 | tf_op jit(solution)/shard_map/ppermute | solution.py:1090
  326.0 6.4 %collective-permute-start.17 = (bf16[1,256,256]{2,1,0:T(8,128)(2,1)S(1)}, bf16[1,256,256]{2,1,0:T(8,128)(2,1)S(1)}, u32[]{:S(2)}, u32[]{:S(2)}) collective-permute-start(bf16[1,256,256]{2,1,0:T(8,128)(2,1)S(1)} %maximum_bitcast_fusion.1), channel_id=1, source_target_pairs={{0,16},{2,18},{4,20},{6,22},{8,24},{10,26},{12,28},{14,30},{16,0},... | collective-permute-start | bytes 393224 | tf_op jit(solution)/shard_map/ppermute | solution.py:1093
  329.2 9.2 %collective-permute-start.24 = (bf16[256,1024]{1,0:T(8,128)(2,1)S(1)}, bf16[256,1024]{1,0:T(8,128)(2,1)S(1)}, u32[]{:S(2)}, u32[]{:S(2)}) collective-permute-start(bf16[256,1024]{1,0:T(8,128)(2,1)S(1)} %fusion.7), channel_id=1, source_target_pairs={{0,1},{1,0},{2,3},{3,2},{4,5},{5,4},{6,7},{7,6},{8,9},{9,8},{10,11... | collective-permute-start | bytes 1572872 | tf_op jit(solution)/shard_map/ppermute | solution.py:1090
  331.3 5.1 %collective-permute-start.22 = (bf16[1,264,256]{2,1,0:T(8,128)(2,1)S(1)}, bf16[1,264,256]{2,1,0:T(8,128)(2,1)S(1)}, u32[]{:S(2)}, u32[]{:S(2)}) collective-permute-start(bf16[1,264,256]{2,1,0:T(8,128)(2,1)S(1)} %maximum_bitcast_fusion), channel_id=1, source_target_pairs={{0,4},{2,6},{4,0},{6,2},{8,12},{10,14},{12,8},{14,10},{16,20},{18,... | collective-permute-start | bytes 405512 | tf_op jit(solution)/shard_map/ppermute | solution.py:1093
  342.7 11.2 %collective-permute-start.27 = (bf16[2,256,256]{2,1,0:T(8,128)(2,1)S(1)}, bf16[2,256,256]{2,1,0:T(8,128)(2,1)S(1)}, u32[]{:S(2)}, u32[]{:S(2)}) collective-permute-start(bf16[2,256,256]{2,1,0:T(8,128)(2,1)S(1)} %maximum_select_fusion.11), channel_id=1, source_target_pairs={{0,8},{2,10},{4,12},{6,14},{8,0},{10,2},{12,4},{14,6},{16,24},{18,... | collective-permute-start | bytes 786440 | tf_op jit(solution)/shard_map/ppermute | solution.py:1093
  342.7 11.3 %collective-permute-start.28 = (bf16[2,264,256]{2,1,0:T(8,128)(2,1)S(1)}, bf16[2,264,256]{2,1,0:T(8,128)(2,1)S(1)}, u32[]{:S(2)}, u32[]{:S(2)}) collective-permute-start(bf16[2,264,256]{2,1,0:T(8,128)(2,1)S(1)} %maximum_select_fusion.10), channel_id=1, source_target_pairs={{0,16},{2,18},{4,20},{6,22},{8,24},{10,26},{12,28},{14,30},{16,0},... | collective-permute-start | bytes 811016 | tf_op jit(solution)/shard_map/ppermute | solution.py:1093
  354.1 9.2 %collective-permute-start.34 = (bf16[4,256,256]{2,1,0:T(8,128)(2,1)S(1)}, bf16[4,256,256]{2,1,0:T(8,128)(2,1)S(1)}, u32[]{:S(2)}, u32[]{:S(2)}) collective-permute-start(bf16[4,256,256]{2,1,0:T(8,128)(2,1)S(1)} %maximum_select_fusion.7), channel_id=1, source_target_pairs={{0,4},{2,6},{4,0},{6,2},{8,12},{10,14},{12,8},{14,10},{16,20},{18,... | collective-permute-start | bytes 1572872 | tf_op jit(solution)/shard_map/ppermute | solution.py:1093
  354.2 9.4 %collective-permute-start.35 = (bf16[4,264,256]{2,1,0:T(8,128)(2,1)S(1)}, bf16[4,264,256]{2,1,0:T(8,128)(2,1)S(1)}, u32[]{:S(2)}, u32[]{:S(2)}) collective-permute-start(bf16[4,264,256]{2,1,0:T(8,128)(2,1)S(1)} %maximum_select_fusion.6), channel_id=1, source_target_pairs={{0,8},{2,10},{4,12},{6,14},{8,0},{10,2},{12,4},{14,6},{16,24},{18,... | collective-permute-start | bytes 1622024 | tf_op jit(solution)/shard_map/ppermute | solution.py:1093
  363.8 4.4 %collective-permute-start.43 = (bf16[8,264,256]{2,1,0:T(8,128)(2,1)S(1)}, bf16[8,264,256]{2,1,0:T(8,128)(2,1)S(1)}, u32[]{:S(2)}, u32[]{:S(2)}) collective-permute-start(bf16[8,264,256]{2,1,0:T(8,128)(2,1)S(1)} %maximum_select_fusion.2.bo_ref), channel_id=1, source_target_pairs={{0,2},{2,0},{4,6},{6,4},{8,10},{10,8},{12,14},{14,12},{16,18},{18,... | collective-permute-start | bytes 3244040 | tf_op jit(solution)/shard_map/ppermute | solution.py:1093
  363.9 4.3 %collective-permute-start.42 = (bf16[8,256,256]{2,1,0:T(8,128)(2,1)S(1)}, bf16[8,256,256]{2,1,0:T(8,128)(2,1)}, u32[]{:S(2)}, u32[]{:S(2)}) collective-permute-start(bf16[8,256,256]{2,1,0:T(8,128)(2,1)S(1)} %maximum_select_fusion.4.ao_ref), channel_id=1, source_target_pairs={{0,2},{2,0},{4,6},{6,4},{8,10},{10,8},{12,14},{14,12},{16,18},{18,... | collective-permute-start | bytes 3145736 | tf_op jit(solution)/shard_map/ppermute | solution.py:1093
  (20 other events, 62.3 us)

commit v8 on v7

--- a/solution.py
+++ b/solution.py
@@ -1187,7 +1187,7 @@
     down = halve(down, chain_a[1])
     up = halve(up, chain_b[1])
     g_head = attn_bwd(block_map, qkv_head, o_head, do_head, lse, table)
-    g_head, ob, down[-1], up[-1] = lax.optimization_barrier((g_head, ob, down[-1], up[-1]))
+    g_head, ob = lax.optimization_barrier((g_head, ob))
     d_qkv = exchange(g_head).reshape(2, heads, 3 * HD, rows)
 
     down = add(*halve(down, chain_a[2]))

time: 381 us -> 369 us (0.969)
  waiting for transfers between devices: 130 us -> 122 us
  starting transfers between devices: 63.7 us -> 58.1 us
  other arithmetic: 23.4 us -> 28.5 us
    ppermute x34, waiting for transfers between devices: 92.1 us -> 81.1 us  [flip(): return lax.ppermute(v, 'ctx', [(i, i ^ 1 << bit) for i in range(n_ctx)])]
    ppermute x10, starting transfers between devices: 15 us -> 10.5 us  [swap(): return lax.ppermute(v, 'wsh', SWAP)]
    unnamed x75 -> x71, local copies, waits for them, and re-layouts: 9.76 us -> 8 us
  transfers between devices with their start and end apart: 48 -> 48, of which waited for: 21 -> 22; matrix products, arithmetic and copies ran while one was open for 9% -> 10% of each run, Pallas kernels for 34% -> 35%
where the time goes in v8:
time: 369 us; the launch traced here: 367 us
  Pallas kernels  136 us (37%)
  waiting for transfers between devices  122 us (33%)
  starting transfers between devices  58.1 us (16%)
  other arithmetic  28.5 us (8%)
  local copies, waits for them, and re-layouts  19.8 us (5%)
    ppermute x34, waiting for transfers between devices, flip(): return lax.ppermute(v, 'ctx', [(i, i ^ 1 << bit) for i in range(n_ctx)])  81.1 us
    ppermute x10, waiting for transfers between devices, swap(): return lax.ppermute(v, 'wsh', SWAP)  33 us
    pallas_call x1, Pallas kernels, attn_bwd(): pl.pallas_call(lambda *a: attn_bwd_kernel(*a, nblk=nblk, per=x.shape[2] /...  32.2 us
    ppermute x34, starting transfers between devices, flip(): return lax.ppermute(v, 'ctx', [(i, i ^ 1 << bit) for i in range(n_ctx)])  30 us
    pallas_call x1, Pallas kernels, mlp(): pl.pallas_call(mlp_kernel, grid_spec=pltpu.PrefetchScalarGridSpec(num_sca...  23.2 us
    pallas_call x1, Pallas kernels, attn_fwd(): pl.pallas_call(lambda *a: attn_fwd_kernel(*a, nblk=nblk, per=x.shape[2] /...  18.6 us
    all_to_all x4, starting transfers between devices, exchange(): return lax.all_to_all(v, 'ctx', 0, 0, axis_index_groups=groups, tiled=False)  17.6 us
    pallas_call x1, Pallas kernels, qkv_backward(): pl.pallas_call(qkv_back_kernel, grid_spec=pltpu.PrefetchScalarGridSpec(nu...  13.5 us
  transfers between devices with their start and end apart: 48, of which 22 were waited for; matrix products, arithmetic and copies ran while one was open for 10% of the time, Pallas kernels for 35%

profile of v8, /device:TPU:0, one launch (start us, length us, event | category | flops | bytes accessed | tf_op | source)
XLA Modules:
  0.0 367.2 jit_solution(10687877340952569983)
XLA Ops:
  0.7 3.0 collective-permute-start
  4.5 1.2 constant_dynamic-slice_fusion.9
  6.3 1.9 collective-permute-start.3
  11.0 6.0 %collective-permute-done.2 = bf16[10,512]{1,0:T(8,128)(2,1)S(1)} collective-permute-done((bf16[10,512]{1,0:T(8,128)(2,1)S(1)}, bf16[10,512]{1,0:T(8,128)(2,1)S(1)}, u32[]{:S(2)}, u32[]{:S(2)}) %collective-permute-start.2) | collective-permute-done | bytes 10272 | tf_op jit(solution)/shard_map/ppermute | solution.py:1090
  18.7 3.9 %norm_rows.2 = (bf16[1024,1024]{1,0:T(8,128)(2,1)}, bf16[1024,1024]{1,0:T(8,128)(2,1)}, bf16[1024,1024]{1,0:T(8,128)(2,1)}) custom-call(s32[4]{0:T(128)} %pad_add_fusion.ids, bf16[256,1024]{1,0:T(8,128)(2,1)} %bitcast.167, bf16[256,1024]{1,0:T(8,128)(2,1)} %copy-done.21, f32[4,1024]{1,0:T(4,128)} %maximum_convert_fusion.n_ref), custom_call_target="tpu_custom_call" | custom-call | bytes 1048576 | tf_op jit(solution)/shard_map/norm_rows/pallas_call | solution.py:553
  22.6 10.5 %collective-permute-done.3.gq_ref.gk_ref.gv_ref = bf16[512,768]{1,0:T(8,128)(2,1)S(1)} collective-permute-done((bf16[512,768]{1,0:T(8,128)(2,1)S(1)}, bf16[512,768]{1,0:T(8,128)(2,1)S(1)}, u32[]{:S(2)}, u32[]{:S(2)}) %collective-permute-start.3) | collective-permute-done | bytes 786464 | tf_op jit(solution)/shard_map/ppermute | solution.py:1090
  33.1 1.7 collective-permute-start.6
  35.4 3.9 %norm_rows.3 = (bf16[1024,1024]{1,0:T(8,128)(2,1)}, bf16[1024,1024]{1,0:T(8,128)(2,1)}, bf16[1024,1024]{1,0:T(8,128)(2,1)}) custom-call(s32[4]{0:T(128)} %pad_add_fusion.ids, bf16[256,1024]{1,0:T(8,128)(2,1)} %copy-done.22, bf16[256,1024]{1,0:T(8,128)(2,1)} %collective-permute-done.1.b_ref, ...), custom_call_target="tpu_custom_call", output_to_operand_aliasing={{0}: (4, {}), {1}: (5, {}), {2}: (6, {})} | custom-call | bytes 1048576 | tf_op jit(solution)/shard_map/norm_rows/pallas_call | solution.py:553
  39.4 5.7 %qkv_forward.1 = bf16[2,4,192,512]{3,2,1,0:T(8,128)(2,1)} custom-call(s32[4]{0:T(128)} %pad_add_fusion.ids, bf16[1024,1024]{1,0:T(8,128)(2,1)} %get-tuple-element.79.ain_ref.a_ref, bf16[512,3072]{1,0:T(8,128)(2,1)} %wv_ref.3, bf16[512,3072]{1,0:T(8,128)(2,1)} %wv_ref.3, bf16[512,3072]{1,0:T(8,128)(2,1)} %wv_ref.3, bf16[512,768]{1,0:T(8,128)(2,1)} %copy-done, ...), custom_call_target="tpu_custom_call" | custom-call | flops 1048576 | bytes 1048576 | tf_op jit(solution)/shard_map/qkv_forward/pallas_call | solution.py:659
  45.1 5.9 %all-to-all-start = ((bf16[8,192,512]{2,1,0:T(8,128)(2,1)}), bf16[8,192,512]{2,1,0:T(8,128)(2,1)S(1)}, u32[]{:S(2)}, u32[]{:S(2)}) async-start(bf16[8,192,512]{2,1,0:T(8,128)(2,1)} %bitcast.164), calls=%async_computation | async-start | bytes 3145728 | tf_op jit(solution)/shard_map/all_to_all | solution.py:1117
  51.0 1.3 constant_dynamic-slice_fusion.5
  56.4 5.0 %turn.1 = (bf16[1024,1024]{1,0:T(8,128)(2,1)}, bf16[1024,1024]{1,0:T(8,128)(2,1)}) custom-call(bf16[1024,1024]{1,0:T(8,128)(2,1)} %get-tuple-element.79.ain_ref.a_ref, bf16[1024,1024]{1,0:T(8,128)(2,1)} %get-tuple-element.81.b_ref.x_ref), custom_call_target="tpu_custom_call" | custom-call | bytes 1048576 | tf_op jit(solution)/shard_map/turn/pallas_call | solution.py:578
  61.3 5.7 %mask_rows.1 = (bf16[1024,1024]{1,0:T(8,128)(2,1)}, bf16[8,64,512]{2,1,0:T(8,128)(2,1)}) custom-call(s32[4]{0:T(128)} %pad_add_fusion.ids, bf16[256,1024]{1,0:T(8,128)(2,1)} %bitcast.176, bf16[256,1024]{1,0:T(8,128)(2,1)} %collective-permute-done.5.b_ref, bf16[256,1024]{1,0:T(8,128)(2,1)} %collective-permute-done.6.c_ref, ...), custom_call_target="tpu_custom_call" | custom-call | bytes 1048576 | tf_op jit(solution)/shard_map/mask_rows/pallas_call | solution.py:607
  67.0 8.9 %collective-permute-done.8.wg_ref = bf16[512,1024]{1,0:T(8,128)(2,1)} collective-permute-done((bf16[512,1024]{1,0:T(8,128)(2,1)S(1)}, bf16[512,1024]{1,0:T(8,128)(2,1)}, u32[]{:S(2)}, u32[]{:S(2)}) %collective-permute-start.8) | collective-permute-done | bytes 1048608 | tf_op jit(solution)/shard_map/ppermute | solution.py:1090
  75.9 23.2 %mlp.1 = (bf16[1024,1024]{1,0:T(8,128)(2,1)}, bf16[1024,1024]{1,0:T(8,128)(2,1)}, bf16[4,128,1024]{2,1,0:T(8,128)(2,1)}, bf16[4,128,1024]{2,1,0:T(8,128)(2,1)}, ...) custom-call(s32[4]{0:T(128)} %pad_add_fusion.ids, ...), custom_call_target="tpu_custom_call" | custom-call | flops 12884901888 | bytes 25165824 | tf_op jit(solution)/shard_map/mlp/pallas_call | solution.py:759
  99.1 1.8 collective-permute-start.9
  100.9 1.5 collective-permute-start.10
  102.4 3.6 all-to-all-start.1
  106.1 18.6 %attn_fwd.1 = (bf16[8,64,512]{2,1,0:T(8,128)(2,1)}, f32[1,4096]{1,0:T(1,128)}) custom-call(s32[32]{0:T(128)} %a_0_.3, bf16[8,192,512]{2,1,0:T(8,128)(2,1)} %copy-done.1), custom_call_target="tpu_custom_call" | custom-call | tf_op jit(solution)/shard_map/attn_fwd/pallas_call | solution.py:438
  124.7 8.0 %all-to-all-done.1.a_3_ = bf16[8,64,512]{2,1,0:T(8,128)(2,1)S(1)} async-done(((bf16[8,64,512]{2,1,0:T(8,128)(2,1)}), bf16[8,64,512]{2,1,0:T(8,128)(2,1)S(1)}, u32[]{:S(2)}, u32[]{:S(2)}) %all-to-all-start.1) | async-done | bytes 524320 | tf_op jit(solution)/shard_map/all_to_all | solution.py:1117
  132.7 2.4 fusion.5
  135.1 1.3 collective-permute-start.27
  136.3 3.7 %all-to-all-start.2 = ((bf16[8,64,512]{2,1,0:T(8,128)(2,1)}), bf16[8,64,512]{2,1,0:T(8,128)(2,1)S(1)}, u32[]{:S(2)}, u32[]{:S(2)}) async-start(bf16[8,64,512]{2,1,0:T(8,128)(2,1)} %get-tuple-element.95.a_2_), calls=%async_computation.2 | async-start | bytes 1048576 | tf_op jit(solution)/shard_map/all_to_all | solution.py:1117
  140.1 2.0 fusion.6
  142.1 2.6 collective-permute-start.35
  144.7 9.7 %collective-permute-done.27 = bf16[2,128,1024]{2,1,0:T(8,128)(2,1)S(1)} collective-permute-done((bf16[2,128,1024]{2,1,0:T(8,128)(2,1)}, bf16[2,128,1024]{2,1,0:T(8,128)(2,1)S(1)}, u32[]{:S(2)}, u32[]{:S(2)}) %collective-permute-start.27) | collective-permute-done | bytes 524320 | tf_op jit(solution)/shard_map/ppermute | solution.py:1093
  154.4 1.3 fusion.12
  155.9 32.2 %attn_bwd.1 = bf16[8,192,512]{2,1,0:T(8,128)(2,1)} custom-call(s32[32]{0:T(128)} %a_0_.3, bf16[8,192,512]{2,1,0:T(8,128)(2,1)} %copy-done.1, bf16[8,64,512]{2,1,0:T(8,128)(2,1)} %get-tuple-element.95.a_2_, bf16[8,64,512]{2,1,0:T(8,128)(2,1)} %copy-done.13, f32[1,4096]{1,0:T(1,128)} %get-tuple-element.97.a_4_, f32[16,4096]{1,0:T(8,128)} %pad_maximum_fusion.1.a_5_), custom_call_target="tpu_custom_call" | custom-call | tf_op jit(solution)/shard_map/attn_bwd/pallas_call | solution.py:498
  190.0 1.4 fusion.14
  191.5 2.9 collective-permute-start.29
  194.4 4.3 %all-to-all-start.3 = ((bf16[8,192,512]{2,1,0:T(8,128)(2,1)}), bf16[8,192,512]{2,1,0:T(8,128)(2,1)}, u32[]{:S(2)}, u32[]{:S(2)}) async-start(bf16[8,192,512]{2,1,0:T(8,128)(2,1)} %attn_bwd.1), calls=%async_computation.3 | async-start | bytes 3145728 | tf_op jit(solution)/shard_map/all_to_all | solution.py:1117
  201.7 1.2 copy-done.19
  202.8 1.4 fusion.11
  204.8 8.3 %collective-permute-done.29 = bf16[1,128,1024]{2,1,0:T(8,128)(2,1)} collective-permute-done((bf16[1,128,1024]{2,1,0:T(8,128)(2,1)S(1)}, bf16[1,128,1024]{2,1,0:T(8,128)(2,1)}, u32[]{:S(2)}, u32[]{:S(2)}) %collective-permute-start.29) | collective-permute-done | bytes 262176 | tf_op jit(solution)/shard_map/ppermute | solution.py:1093
  214.4 1.3 collective-permute-start.38
  215.6 6.4 %collective-permute-done.38 = bf16[1,2,64,1024]{3,2,1,0:T(8,128)(2,1)S(1)} collective-permute-done((bf16[1,2,64,1024]{3,2,1,0:T(8,128)(2,1)S(1)}, bf16[1,2,64,1024]{3,2,1,0:T(8,128)(2,1)S(1)}, u32[]{:S(2)}, u32[]{:S(2)}) %collective-permute-start.38) | collective-permute-done | bytes 262176 | tf_op jit(solution)/shard_map/ppermute | solution.py:1093
  222.1 2.5 collective-permute-start.39
  224.6 8.6 %collective-permute-done.30 = bf16[2,128,1024]{2,1,0:T(8,128)(2,1)S(1)} collective-permute-done((bf16[2,128,1024]{2,1,0:T(8,128)(2,1)S(1)}, bf16[2,128,1024]{2,1,0:T(8,128)(2,1)S(1)}, u32[]{:S(2)}, u32[]{:S(2)}) %collective-permute-start.30) | collective-permute-done | bytes 524320 | tf_op jit(solution)/shard_map/ppermute | solution.py:1093
  233.2 1.1 maximum_select_fusion.3
  235.0 2.2 convert_add_fusion.1
  238.7 13.9 %collective-permute-done.39 = bf16[2,2,64,1024]{3,2,1,0:T(8,128)(2,1)S(1)} collective-permute-done((bf16[2,2,64,1024]{3,2,1,0:T(8,128)(2,1)S(1)}, bf16[2,2,64,1024]{3,2,1,0:T(8,128)(2,1)S(1)}, u32[]{:S(2)}, u32[]{:S(2)}) %collective-permute-start.39) | collective-permute-done | bytes 524320 | tf_op jit(solution)/shard_map/ppermute | solution.py:1093
  253.7 13.5 %qkv_backward.1 = (bf16[8,256,256]{2,1,0:T(8,128)(2,1)}, bf16[8,264,256]{2,1,0:T(8,128)(2,1)}, f32[2,512,1024]{2,1,0:T(8,128)}) custom-call(s32[4]{0:T(128)} %pad_add_fusion.ids, bf16[2,4,192,512]{3,2,1,0:T(8,128)(2,1)} %bitcast.21.d_ref, bf16[1024,1024]{1,0:T(8,128)(2,1)} %get-tuple-element.100.at_ref, bf16[1024,1024]{1,0:T(8,128)(2,1)} %get-tuple-element.101.x_ref, ...), custom_call_target="tpu_custom_call" | custom-call | tf_op jit(solution)/shard_map/qkv_backward/pallas_call | solution.py:901
  267.2 1.4 constant_dynamic-slice_fusion.3
  269.7 2.1 collective-permute-start.16
  271.7 2.1 fusion.4
  273.8 2.7 maximum_select_fusion.own_ref
  276.6 1.3 collective-permute-done.11
  278.0 2.1 collective-permute-start.12
  280.0 12.2 %collective-permute-done.16 = bf16[4,264,256]{2,1,0:T(8,128)(2,1)S(1)} collective-permute-done((bf16[4,264,256]{2,1,0:T(8,128)(2,1)S(1)}, bf16[4,264,256]{2,1,0:T(8,128)(2,1)S(1)}, u32[]{:S(2)}, u32[]{:S(2)}) %collective-permute-start.16) | collective-permute-done | bytes 540704 | tf_op jit(solution)/shard_map/ppermute | solution.py:1093
  292.4 2.0 maximum_select_fusion.1.own_ref
  295.1 2.3 collective-permute-start.13
  297.9 8.0 %collective-permute-done.17 = bf16[2,264,256]{2,1,0:T(8,128)(2,1)S(1)} collective-permute-done((bf16[2,264,256]{2,1,0:T(8,128)(2,1)S(1)}, bf16[2,264,256]{2,1,0:T(8,128)(2,1)S(1)}, u32[]{:S(2)}, u32[]{:S(2)}) %collective-permute-start.17) | collective-permute-done | bytes 270368 | tf_op jit(solution)/shard_map/ppermute | solution.py:1093
  308.0 3.0 collective-permute-done.18
  311.9 4.1 %collective-permute-done.19 = bf16[104,256]{1,0:T(8,128)(2,1)S(1)} collective-permute-done((bf16[104,256]{1,0:T(8,128)(2,1)S(1)}, bf16[104,256]{1,0:T(8,128)(2,1)S(1)}, u32[]{:S(2)}, u32[]{:S(2)}) %collective-permute-start.19) | collective-permute-done | bytes 53280 | tf_op jit(solution)/shard_map/ppermute | solution.py:1090
  319.3 2.9 collective-permute-done.20
  322.2 3.5 collective-permute-done.22.er_ref
  326.5 3.4 token_grad.1
  330.0 2.5 collective-permute-start.26
  332.4 1.3 copy-done.11
  333.7 7.0 %join_rows.1 = f32[2048,1024]{1,0:T(8,128)} custom-call(s32[4]{0:T(128)} %pad_add_fusion.ids, bf16[8,128,1024]{2,1,0:T(8,128)(2,1)} %copy-done.3, bf16[8,128,1024]{2,1,0:T(8,128)(2,1)} %copy-done.11), custom_call_target="tpu_custom_call" | custom-call | tf_op jit(solution)/shard_map/join_rows/pallas_call | solution.py:956
  341.2 1.1 collective-permute-start.33
  342.5 7.1 %join_cols.1 = f32[512,4096]{1,0:T(8,128)} custom-call(s32[4]{0:T(128)} %pad_add_fusion.ids, bf16[8,2,64,1024]{3,2,1,0:T(8,128)(2,1)} %copy-done.4, bf16[8,2,64,1024]{3,2,1,0:T(8,128)(2,1)} %collective-permute-done.41.got_ref), custom_call_target="tpu_custom_call" | custom-call | tf_op jit(solution)/shard_map/join_cols/pallas_call | solution.py:973
  352.4 3.8 %collective-permute-done.42.ag_ref = bf16[8,256,256]{2,1,0:T(8,128)(2,1)} collective-permute-done((bf16[8,256,256]{2,1,0:T(8,128)(2,1)S(1)}, bf16[8,256,256]{2,1,0:T(8,128)(2,1)}, u32[]{:S(2)}, u32[]{:S(2)}) %collective-permute-start.42) | collective-permute-done | bytes 1048608 | tf_op jit(solution)/shard_map/ppermute | solution.py:1093
  357.3 6.6 %unpack.1 = (f32[512,3072]{1,0:T(8,128)}, f32[2,256,1024]{2,1,0:T(8,128)}, f32[8,8,256]{2,1,0:T(8,128)}) custom-call(s32[4]{0:T(128)} %pad_add_fusion.ids, bf16[8,256,256]{2,1,0:T(8,128)(2,1)} %copy-done.8, bf16[8,256,256]{2,1,0:T(8,128)(2,1)} %collective-permute-done.42.ag_ref, bf16[8,264,256]{2,1,0:T(8,128)(2,1)} %copy-done.7, bf16[8,264,256]{2,1,0:T(8,128)(2,1)} %copy-done.15), custom_call_target="tpu_custom_call" | custom-call | tf_op jit(solution)/shard_map/unpack/pallas_call | solution.py:1017
  (209 shorter events, 36.8 us)
Async XLA Ops:
  0.7 5.1 %copy-start.26 = (bf16[1536]{0:T(1024)(128)(2,1)S(1)}, bf16[1536]{0:T(1024)(128)(2,1)}, u32[]{:S(2)}) copy-start(bf16[1536]{0:T(1024)(128)(2,1)} %param.22) | copy-start | bytes 9220
  0.7 7.5 %copy-start.27 = (s32[32]{0:T(128)S(1)}, s32[32]{0:T(128)}, u32[]{:S(2)}) copy-start(s32[32]{0:T(128)} %a_0_.3) | copy-start | bytes 388
  0.7 16.4 %collective-permute-start = (bf16[256,1024]{1,0:T(8,128)(2,1)}, bf16[256,1024]{1,0:T(8,128)(2,1)S(1)}, u32[]{:S(2)}, u32[]{:S(2)}) collective-permute-start(bf16[256,1024]{1,0:T(8,128)(2,1)} %bitcast.165), channel_id=1, source_target_pairs={{0,1},{1,0},{2,3},{3,2},{4,5},{5,4},{6,7},{7,6},{8,9},{9,8},{10,11... | collective-permute-start | bytes 1572872 | tf_op jit(solution)/shard_map/ppermute | solution.py:1090
  3.8 14.1 %collective-permute-start.4 = (bf16[256,1024]{1,0:T(8,128)(2,1)}, bf16[256,1024]{1,0:T(8,128)(2,1)S(1)}, u32[]{:S(2)}, u32[]{:S(2)}) collective-permute-start(bf16[256,1024]{1,0:T(8,128)(2,1)} %bitcast.166), channel_id=1, source_target_pairs={{0,2},{2,0},{4,6},{6,4},{8,10},{10,8},{12,14},{14,12},{16,18},{18,... | collective-permute-start | bytes 1572872 | tf_op jit(solution)/shard_map/ppermute | solution.py:1093
  5.6 27.5 %copy-start.14 = (bf16[1,256,1024]{2,1,0:T(8,128)(2,1)S(1)}, bf16[1,256,1024]{2,1,0:T(8,128)(2,1)}, u32[]{:S(2)}) copy-start(bf16[1,256,1024]{2,1,0:T(8,128)(2,1)} %param.31) | copy-start | bytes 1572868
  6.1 10.9 %collective-permute-start.2 = (bf16[10,512]{1,0:T(8,128)(2,1)S(1)}, bf16[10,512]{1,0:T(8,128)(2,1)S(1)}, u32[]{:S(2)}, u32[]{:S(2)}) collective-permute-start(bf16[10,512]{1,0:T(8,128)(2,1)S(1)} %concatenate.150), channel_id=1, source_target_pairs={{0,1},{1,0},{2,3},{3,2},{4,5},{5,4},{6,7},{7,6},{8,9},{9,8},{10,11... | collective-permute-start | bytes 30728 | tf_op jit(solution)/shard_map/ppermute | solution.py:1090
  6.3 26.8 %collective-permute-start.3 = (bf16[512,768]{1,0:T(8,128)(2,1)S(1)}, bf16[512,768]{1,0:T(8,128)(2,1)S(1)}, u32[]{:S(2)}, u32[]{:S(2)}) collective-permute-start(bf16[512,768]{1,0:T(8,128)(2,1)S(1)} %pad_maximum_fusion), channel_id=1, source_target_pairs={{0,1},{1,0},{2,3},{3,2},{4,5},{5,4},{6,7},{7,6},{8,9},{9,8},{10,11... | collective-permute-start | bytes 2359304 | tf_op jit(solution)/shard_map/ppermute | solution.py:1090
  17.1 18.3 %copy-start.22 = (bf16[256,1024]{1,0:T(8,128)(2,1)}, bf16[256,1024]{1,0:T(8,128)(2,1)S(1)}, u32[]{:S(2)}) copy-start(bf16[256,1024]{1,0:T(8,128)(2,1)S(1)} %collective-permute-done.a_ref) | copy-start | bytes 1572868
  17.1 18.3 %collective-permute-start.1 = (bf16[256,1024]{1,0:T(8,128)(2,1)S(1)}, bf16[256,1024]{1,0:T(8,128)(2,1)}, u32[]{:S(2)}, u32[]{:S(2)}) collective-permute-start(bf16[256,1024]{1,0:T(8,128)(2,1)S(1)} %collective-permute-done.a_ref), channel_id=1, source_target_pairs={{0,2},{2,0},{4,6},{6,4},{8,10},{10,8},{12,14},{14,12},{16,18},{18,... | collective-permute-start | bytes 1572872 | tf_op jit(solution)/shard_map/ppermute | solution.py:1093
  33.1 6.3 %copy-start = (bf16[512,768]{1,0:T(8,128)(2,1)}, bf16[512,768]{1,0:T(8,128)(2,1)S(1)}, u32[]{:S(2)}) copy-start(bf16[512,768]{1,0:T(8,128)(2,1)S(1)} %collective-permute-done.3.gq_ref.gk_ref.gv_ref) | copy-start | bytes 2359300
  33.1 19.2 %collective-permute-start.6 = (bf16[256,1024]{1,0:T(8,128)(2,1)S(1)}, bf16[256,1024]{1,0:T(8,128)(2,1)}, u32[]{:S(2)}, u32[]{:S(2)}) collective-permute-start(bf16[256,1024]{1,0:T(8,128)(2,1)S(1)} %bitcast.178), channel_id=1, source_target_pairs={{0,1},{1,0},{2,3},{3,2},{4,5},{5,4},{6,7},{7,6},{8,9},{9,8},{10,11... | collective-permute-start | bytes 1572872 | tf_op jit(solution)/shard_map/ppermute | solution.py:1090
  45.1 7.8 %copy-start.25 = (bf16[2048]{0:T(1024)(128)(2,1)S(1)}, bf16[2048]{0:T(1024)(128)(2,1)}, u32[]{:S(2)}) copy-start(bf16[2048]{0:T(1024)(128)(2,1)} %param.26) | copy-start | bytes 12292
  45.1 54.1 %all-to-all-start = ((bf16[8,192,512]{2,1,0:T(8,128)(2,1)}), bf16[8,192,512]{2,1,0:T(8,128)(2,1)S(1)}, u32[]{:S(2)}, u32[]{:S(2)}) async-start(bf16[8,192,512]{2,1,0:T(8,128)(2,1)} %bitcast.164), calls=%async_computation | async-start | bytes 3145728 | tf_op jit(solution)/shard_map/all_to_all | solution.py:1117
  52.3 23.6 %collective-permute-start.8 = (bf16[512,1024]{1,0:T(8,128)(2,1)S(1)}, bf16[512,1024]{1,0:T(8,128)(2,1)}, u32[]{:S(2)}, u32[]{:S(2)}) collective-permute-start(bf16[512,1024]{1,0:T(8,128)(2,1)S(1)} %constant_dynamic-slice_fusion.5), channel_id=1, source_target_pairs={{0,1},{1,0},{2,3},{3,2},{4,5},{5,4},{6,7},{7,6},{8,9},{9,8},{10,11... | collective-permute-start | bytes 3145736 | tf_op jit(solution)/shard_map/ppermute | solution.py:1090
  52.9 8.5 %collective-permute-start.5 = (bf16[256,1024]{1,0:T(8,128)(2,1)S(1)}, bf16[256,1024]{1,0:T(8,128)(2,1)}, u32[]{:S(2)}, u32[]{:S(2)}) collective-permute-start(bf16[256,1024]{1,0:T(8,128)(2,1)S(1)} %bitcast.179), channel_id=1, source_target_pairs={{0,2},{2,0},{4,6},{6,4},{8,10},{10,8},{12,14},{14,12},{16,18},{18,... | collective-permute-start | bytes 1572872 | tf_op jit(solution)/shard_map/ppermute | solution.py:1093
  54.1 7.3 %collective-permute-start.7 = (bf16[256,1024]{1,0:T(8,128)(2,1)}, bf16[256,1024]{1,0:T(8,128)(2,1)}, u32[]{:S(2)}, u32[]{:S(2)}) collective-permute-start(bf16[256,1024]{1,0:T(8,128)(2,1)} %collective-permute-done.6.c_ref), channel_id=1, source_target_pairs={{0,2},{2,0},{4,6},{6,4},{8,10},{10,8},{12,14},{14,12},{16,18},{18,... | collective-permute-start | bytes 1572872 | tf_op jit(solution)/shard_map/ppermute | solution.py:1093
  99.1 6.9 %copy-start.1 = (bf16[8,192,512]{2,1,0:T(8,128)(2,1)}, bf16[8,192,512]{2,1,0:T(8,128)(2,1)S(1)}, u32[]{:S(2)}) copy-start(bf16[8,192,512]{2,1,0:T(8,128)(2,1)S(1)} %all-to-all-done.a_1_) | copy-start | bytes 4718596
  99.1 33.5 %collective-permute-start.9 = (bf16[4,128,1024]{2,1,0:T(8,128)(2,1)}, bf16[4,128,1024]{2,1,0:T(8,128)(2,1)}, u32[]{:S(2)}, u32[]{:S(2)}) collective-permute-start(bf16[4,128,1024]{2,1,0:T(8,128)(2,1)} %get-tuple-element.92), channel_id=1, source_target_pairs={{0,4},{2,6},{4,0},{6,2},{8,12},{10,14},{12,8},{14,10},{16,20},{18,... | collective-permute-start | bytes 3145736 | tf_op jit(solution)/shard_map/ppermute | solution.py:1093
  100.9 31.7 %collective-permute-start.10 = (bf16[4,128,1024]{2,1,0:T(8,128)(2,1)}, bf16[4,128,1024]{2,1,0:T(8,128)(2,1)}, u32[]{:S(2)}, u32[]{:S(2)}) collective-permute-start(bf16[4,128,1024]{2,1,0:T(8,128)(2,1)} %get-tuple-element.93), channel_id=1, source_target_pairs={{0,8},{2,10},{4,12},{6,14},{8,0},{10,2},{12,4},{14,6},{16,24},{18,... | collective-permute-start | bytes 3145736 | tf_op jit(solution)/shard_map/ppermute | solution.py:1093
  102.4 30.3 %all-to-all-start.1 = ((bf16[8,64,512]{2,1,0:T(8,128)(2,1)}), bf16[8,64,512]{2,1,0:T(8,128)(2,1)S(1)}, u32[]{:S(2)}, u32[]{:S(2)}) async-start(bf16[8,64,512]{2,1,0:T(8,128)(2,1)} %get-tuple-element.91), calls=%async_computation.1 | async-start | bytes 1048576 | tf_op jit(solution)/shard_map/all_to_all | solution.py:1117
  106.1 34.0 %copy-start.17 = (bf16[4,128,1024]{2,1,0:T(8,128)(2,1)S(1)}, bf16[4,128,1024]{2,1,0:T(8,128)(2,1)}, u32[]{:S(2)}) copy-start(bf16[4,128,1024]{2,1,0:T(8,128)(2,1)} %get-tuple-element.117) | copy-start | bytes 3145732
  132.7 9.4 %copy-start.13 = (bf16[8,64,512]{2,1,0:T(8,128)(2,1)}, bf16[8,64,512]{2,1,0:T(8,128)(2,1)S(1)}, u32[]{:S(2)}) copy-start(bf16[8,64,512]{2,1,0:T(8,128)(2,1)S(1)} %all-to-all-done.1.a_3_) | copy-start | bytes 1572868
  135.1 19.4 %collective-permute-start.27 = (bf16[2,128,1024]{2,1,0:T(8,128)(2,1)}, bf16[2,128,1024]{2,1,0:T(8,128)(2,1)S(1)}, u32[]{:S(2)}, u32[]{:S(2)}) collective-permute-start(bf16[2,128,1024]{2,1,0:T(8,128)(2,1)} %fusion.5), channel_id=1, source_target_pairs={{0,8},{2,10},{4,12},{6,14},{8,0},{10,2},{12,4},{14,6},{16,24},{18,... | collective-permute-start | bytes 1572872 | tf_op jit(solution)/shard_map/ppermute | solution.py:1093
  136.3 58.1 %all-to-all-start.2 = ((bf16[8,64,512]{2,1,0:T(8,128)(2,1)}), bf16[8,64,512]{2,1,0:T(8,128)(2,1)S(1)}, u32[]{:S(2)}, u32[]{:S(2)}) async-start(bf16[8,64,512]{2,1,0:T(8,128)(2,1)} %get-tuple-element.95.a_2_), calls=%async_computation.2 | async-start | bytes 1048576 | tf_op jit(solution)/shard_map/all_to_all | solution.py:1117
  142.1 46.0 %collective-permute-start.35 = (bf16[2,128,1024]{2,1,0:T(8,128)(2,1)}, bf16[2,128,1024]{2,1,0:T(8,128)(2,1)S(1)}, u32[]{:S(2)}, u32[]{:S(2)}) collective-permute-start(bf16[2,128,1024]{2,1,0:T(8,128)(2,1)} %fusion.6), channel_id=1, source_target_pairs={{0,16},{2,18},{4,20},{6,22},{8,24},{10,26},{12,28},{14,30},{16,0},... | collective-permute-start | bytes 1572872 | tf_op jit(solution)/shard_map/ppermute | solution.py:1093
  154.4 33.6 %copy-start.20 = (bf16[2,128,1024]{2,1,0:T(8,128)(2,1)}, bf16[2,128,1024]{2,1,0:T(8,128)(2,1)S(1)}, u32[]{:S(2)}) copy-start(bf16[2,128,1024]{2,1,0:T(8,128)(2,1)S(1)} %collective-permute-done.27) | copy-start | bytes 1572868
  155.8 34.3 %collective-permute-start.28 = (bf16[1,128,1024]{2,1,0:T(8,128)(2,1)S(1)}, bf16[1,128,1024]{2,1,0:T(8,128)(2,1)}, u32[]{:S(2)}, u32[]{:S(2)}) collective-permute-start(bf16[1,128,1024]{2,1,0:T(8,128)(2,1)S(1)} %fusion.12), channel_id=1, source_target_pairs={{0,16},{2,18},{4,20},{6,22},{8,24},{10,26},{12,28},{14,30},{16,0},... | collective-permute-start | bytes 786440 | tf_op jit(solution)/shard_map/ppermute | solution.py:1093
  189.9 8.8 %copy-start.10 = (bf16[512,1024]{1,0:T(8,128)(2,1)S(1)}, bf16[512,1024]{1,0:T(8,128)(2,1)}, u32[]{:S(2)}) copy-start(bf16[512,1024]{1,0:T(8,128)(2,1)} %w_ref.1) | copy-start | bytes 3145732
  189.9 11.7 %collective-permute-start.36 = (bf16[1,128,1024]{2,1,0:T(8,128)(2,1)S(1)}, bf16[1,128,1024]{2,1,0:T(8,128)(2,1)}, u32[]{:S(2)}, u32[]{:S(2)}) collective-permute-start(bf16[1,128,1024]{2,1,0:T(8,128)(2,1)S(1)} %fusion.9), channel_id=1, source_target_pairs={{0,4},{2,6},{4,0},{6,2},{8,12},{10,14},{12,8},{14,10},{16,20},{18,... | collective-permute-start | bytes 786440 | tf_op jit(solution)/shard_map/ppermute | solution.py:1093
  191.5 21.7 %collective-permute-start.29 = (bf16[1,128,1024]{2,1,0:T(8,128)(2,1)S(1)}, bf16[1,128,1024]{2,1,0:T(8,128)(2,1)}, u32[]{:S(2)}, u32[]{:S(2)}) collective-permute-start(bf16[1,128,1024]{2,1,0:T(8,128)(2,1)S(1)} %fusion.14), channel_id=1, source_target_pairs={{0,16},{2,18},{4,20},{6,22},{8,24},{10,26},{12,28},{14,30},{16,0},... | collective-permute-start | bytes 786440 | tf_op jit(solution)/shard_map/ppermute | solution.py:1093
  194.4 59.3 %all-to-all-start.3 = ((bf16[8,192,512]{2,1,0:T(8,128)(2,1)}), bf16[8,192,512]{2,1,0:T(8,128)(2,1)}, u32[]{:S(2)}, u32[]{:S(2)}) async-start(bf16[8,192,512]{2,1,0:T(8,128)(2,1)} %attn_bwd.1), calls=%async_computation.3 | async-start | bytes 3145728 | tf_op jit(solution)/shard_map/all_to_all | solution.py:1117
  201.4 12.9 %copy-start.2 = (f32[2,512,1024]{2,1,0:T(8,128)}, f32[2,512,1024]{2,1,0:T(8,128)S(1)}, u32[]{:S(2)}) copy-start(f32[2,512,1024]{2,1,0:T(8,128)S(1)} %convert_add_fusion) | copy-start | bytes 12582916
  201.6 33.5 %collective-permute-start.23 = (bf16[2,256,1024]{2,1,0:T(8,128)(2,1)S(1)}, bf16[2,256,1024]{2,1,0:T(8,128)(2,1)}, u32[]{:S(2)}, u32[]{:S(2)}) collective-permute-start(bf16[2,256,1024]{2,1,0:T(8,128)(2,1)S(1)} %dynamic-slice_convert_fusion), channel_id=1, source_target_pairs={{0,2},{2,0},{4,6},{6,4},{8,10},{10,8},{12,14},{14,12},{16,18},{18,... | collective-permute-start | bytes 3145736 | tf_op jit(solution)/shard_map/ppermute | solution.py:1093
  204.2 10.1 %collective-permute-start.37 = (bf16[1,1,64,1024]{3,2,1,0:T(8,128)(2,1)S(1)}, bf16[1,1,64,1024]{3,2,1,0:T(8,128)(2,1)S(1)}, u32[]{:S(2)}, u32[]{:S(2)}) collective-permute-start(bf16[1,1,64,1024]{3,2,1,0:T(8,128)(2,1)S(1)} %get-tuple-element.134), channel_id=1, source_target_pairs={{0,1},{1,0},{2,3},{3,2},{4,5},{5,4},{6,7},{7,6},{8,9},{9,8},{10,11... | collective-permute-start | bytes 393224 | tf_op jit(solution)/shard_map/ppermute | solution.py:1090
  214.2 19.0 %collective-permute-start.30 = (bf16[2,128,1024]{2,1,0:T(8,128)(2,1)S(1)}, bf16[2,128,1024]{2,1,0:T(8,128)(2,1)S(1)}, u32[]{:S(2)}, u32[]{:S(2)}) collective-permute-start(bf16[2,128,1024]{2,1,0:T(8,128)(2,1)S(1)} %maximum_select_fusion.8), channel_id=1, source_target_pairs={{0,8},{2,10},{4,12},{6,14},{8,0},{10,2},{12,4},{14,6},{16,24},{18,... | collective-permute-start | bytes 1572872 | tf_op jit(solution)/shard_map/ppermute | solution.py:1093
  214.4 7.6 %collective-permute-start.38 = (bf16[1,2,64,1024]{3,2,1,0:T(8,128)(2,1)S(1)}, bf16[1,2,64,1024]{3,2,1,0:T(8,128)(2,1)S(1)}, u32[]{:S(2)}, u32[]{:S(2)}) collective-permute-start(bf16[1,2,64,1024]{3,2,1,0:T(8,128)(2,1)S(1)} %maximum_select_fusion.12), channel_id=1, source_target_pairs={{0,4},{2,6},{4,0},{6,2},{8,12},{10,14},{12,8},{14,10},{16,20},{18,... | collective-permute-start | bytes 786440 | tf_op jit(solution)/shard_map/ppermute | solution.py:1093
  222.1 30.5 %collective-permute-start.39 = (bf16[2,2,64,1024]{3,2,1,0:T(8,128)(2,1)S(1)}, bf16[2,2,64,1024]{3,2,1,0:T(8,128)(2,1)S(1)}, u32[]{:S(2)}, u32[]{:S(2)}) collective-permute-start(bf16[2,2,64,1024]{3,2,1,0:T(8,128)(2,1)S(1)} %maximum_select_fusion.9), channel_id=1, source_target_pairs={{0,16},{2,18},{4,20},{6,22},{8,24},{10,26},{12,28},{14,30},{16,0},... | collective-permute-start | bytes 1572872 | tf_op jit(solution)/shard_map/ppermute | solution.py:1093
  234.4 39.4 %collective-permute-start.31 = (bf16[4,128,1024]{2,1,0:T(8,128)(2,1)}, bf16[4,128,1024]{2,1,0:T(8,128)(2,1)}, u32[]{:S(2)}, u32[]{:S(2)}) collective-permute-start(bf16[4,128,1024]{2,1,0:T(8,128)(2,1)} %maximum_select_fusion.3), channel_id=1, source_target_pairs={{0,4},{2,6},{4,0},{6,2},{8,12},{10,14},{12,8},{14,10},{16,20},{18,... | collective-permute-start | bytes 3145736 | tf_op jit(solution)/shard_map/ppermute | solution.py:1093
  238.1 33.6 %collective-permute-start.24 = (bf16[256,1024]{1,0:T(8,128)(2,1)}, bf16[256,1024]{1,0:T(8,128)(2,1)}, u32[]{:S(2)}, u32[]{:S(2)}) collective-permute-start(bf16[256,1024]{1,0:T(8,128)(2,1)} %fusion.8), channel_id=1, source_target_pairs={{0,1},{1,0},{2,3},{3,2},{4,5},{5,4},{6,7},{7,6},{8,9},{9,8},{10,11... | collective-permute-start | bytes 1572872 | tf_op jit(solution)/shard_map/ppermute | solution.py:1090
  252.8 39.7 %collective-permute-start.40 = (bf16[4,2,64,1024]{3,2,1,0:T(8,128)(2,1)S(1)}, bf16[4,2,64,1024]{3,2,1,0:T(8,128)(2,1)}, u32[]{:S(2)}, u32[]{:S(2)}) collective-permute-start(bf16[4,2,64,1024]{3,2,1,0:T(8,128)(2,1)S(1)} %maximum_select_fusion.5), channel_id=1, source_target_pairs={{0,8},{2,10},{4,12},{6,14},{8,0},{10,2},{12,4},{14,6},{16,24},{18,... | collective-permute-start | bytes 3145736 | tf_op jit(solution)/shard_map/ppermute | solution.py:1093
  268.6 9.2 %collective-permute-start.11 = (bf16[4,256,256]{2,1,0:T(8,128)(2,1)S(1)}, bf16[4,256,256]{2,1,0:T(8,128)(2,1)S(1)}, u32[]{:S(2)}, u32[]{:S(2)}) collective-permute-start(bf16[4,256,256]{2,1,0:T(8,128)(2,1)S(1)} %get-tuple-element.132), channel_id=1, source_target_pairs={{0,4},{2,6},{4,0},{6,2},{8,12},{10,14},{12,8},{14,10},{16,20},{18,... | collective-permute-start | bytes 1572872 | tf_op jit(solution)/shard_map/ppermute | solution.py:1093
  269.7 22.6 %collective-permute-start.16 = (bf16[4,264,256]{2,1,0:T(8,128)(2,1)S(1)}, bf16[4,264,256]{2,1,0:T(8,128)(2,1)S(1)}, u32[]{:S(2)}, u32[]{:S(2)}) collective-permute-start(bf16[4,264,256]{2,1,0:T(8,128)(2,1)S(1)} %get-tuple-element.130), channel_id=1, source_target_pairs={{0,8},{2,10},{4,12},{6,14},{8,0},{10,2},{12,4},{14,6},{16,24},{18,... | collective-permute-start | bytes 1622024 | tf_op jit(solution)/shard_map/ppermute | solution.py:1093
  276.5 18.0 %copy-start.3 = (bf16[8,128,1024]{2,1,0:T(8,128)(2,1)}, bf16[8,128,1024]{2,1,0:T(8,128)(2,1)S(1)}, u32[]{:S(2)}) copy-start(bf16[8,128,1024]{2,1,0:T(8,128)(2,1)S(1)} %maximum_select_fusion.own_ref) | copy-start | bytes 6291460
  276.5 55.9 %collective-permute-start.32 = (bf16[8,128,1024]{2,1,0:T(8,128)(2,1)S(1)}, bf16[8,128,1024]{2,1,0:T(8,128)(2,1)S(1)}, u32[]{:S(2)}, u32[]{:S(2)}) collective-permute-start(bf16[8,128,1024]{2,1,0:T(8,128)(2,1)S(1)} %maximum_select_fusion.own_ref), channel_id=1, source_target_pairs={{0,2},{2,0},{4,6},{6,4},{8,10},{10,8},{12,14},{14,12},{16,18},{18,... | collective-permute-start | bytes 6291464 | tf_op jit(solution)/shard_map/ppermute | solution.py:1093
  278.0 17.1 %collective-permute-start.12 = (bf16[2,256,256]{2,1,0:T(8,128)(2,1)S(1)}, bf16[2,256,256]{2,1,0:T(8,128)(2,1)S(1)}, u32[]{:S(2)}, u32[]{:S(2)}) collective-permute-start(bf16[2,256,256]{2,1,0:T(8,128)(2,1)S(1)} %fusion.22), channel_id=1, source_target_pairs={{0,8},{2,10},{4,12},{6,14},{8,0},{10,2},{12,4},{14,6},{16,24},{18,... | collective-permute-start | bytes 786440 | tf_op jit(solution)/shard_map/ppermute | solution.py:1093
  292.3 5.1 %copy-start.9 = (f32[2,512,1024]{2,1,0:T(8,128)S(1)}, f32[2,512,1024]{2,1,0:T(8,128)}, u32[]{:S(2)}) copy-start(f32[2,512,1024]{2,1,0:T(8,128)} %get-tuple-element.107) | copy-start | bytes 12582916
  292.3 13.5 %collective-permute-start.17 = (bf16[2,264,256]{2,1,0:T(8,128)(2,1)S(1)}, bf16[2,264,256]{2,1,0:T(8,128)(2,1)S(1)}, u32[]{:S(2)}, u32[]{:S(2)}) collective-permute-start(bf16[2,264,256]{2,1,0:T(8,128)(2,1)S(1)} %fusion.18), channel_id=1, source_target_pairs={{0,16},{2,18},{4,20},{6,22},{8,24},{10,26},{12,28},{14,30},{16,0},... | collective-permute-start | bytes 811016 | tf_op jit(solution)/shard_map/ppermute | solution.py:1093
  294.5 16.7 %copy-start.4 = (bf16[8,2,64,1024]{3,2,1,0:T(8,128)(2,1)}, bf16[8,2,64,1024]{3,2,1,0:T(8,128)(2,1)S(1)}, u32[]{:S(2)}) copy-start(bf16[8,2,64,1024]{3,2,1,0:T(8,128)(2,1)S(1)} %maximum_select_fusion.1.own_ref) | copy-start | bytes 6291460
  294.5 48.1 %collective-permute-start.41 = (bf16[8,2,64,1024]{3,2,1,0:T(8,128)(2,1)S(1)}, bf16[8,2,64,1024]{3,2,1,0:T(8,128)(2,1)}, u32[]{:S(2)}, u32[]{:S(2)}) collective-permute-start(bf16[8,2,64,1024]{3,2,1,0:T(8,128)(2,1)S(1)} %maximum_select_fusion.1.own_ref), channel_id=1, source_target_pairs={{0,2},{2,0},{4,6},{6,4},{8,10},{10,8},{12,14},{14,12},{16,18},{18,... | collective-permute-start | bytes 6291464 | tf_op jit(solution)/shard_map/ppermute | solution.py:1093
  295.1 12.2 %collective-permute-start.13 = (bf16[1,256,256]{2,1,0:T(8,128)(2,1)S(1)}, bf16[1,256,256]{2,1,0:T(8,128)(2,1)S(1)}, u32[]{:S(2)}, u32[]{:S(2)}) collective-permute-start(bf16[1,256,256]{2,1,0:T(8,128)(2,1)S(1)} %fusion.23), channel_id=1, source_target_pairs={{0,16},{2,18},{4,20},{6,22},{8,24},{10,26},{12,28},{14,30},{16,0},... | collective-permute-start | bytes 393224 | tf_op jit(solution)/shard_map/ppermute | solution.py:1093
  297.6 18.5 %collective-permute-start.21 = (bf16[2,256,1024]{2,1,0:T(8,128)(2,1)S(1)}, bf16[2,256,1024]{2,1,0:T(8,128)(2,1)S(1)}, u32[]{:S(2)}, u32[]{:S(2)}) collective-permute-start(bf16[2,256,1024]{2,1,0:T(8,128)(2,1)S(1)} %dynamic-slice_convert_fusion.1), channel_id=1, source_target_pairs={{0,2},{2,0},{4,6},{6,4},{8,10},{10,8},{12,14},{14,12},{16,18},{18,... | collective-permute-start | bytes 3145736 | tf_op jit(solution)/shard_map/ppermute | solution.py:1093
  305.9 5.1 %collective-permute-start.18 = (bf16[1,264,256]{2,1,0:T(8,128)(2,1)S(1)}, bf16[1,264,256]{2,1,0:T(8,128)(2,1)S(1)}, u32[]{:S(2)}, u32[]{:S(2)}) collective-permute-start(bf16[1,264,256]{2,1,0:T(8,128)(2,1)S(1)} %fusion.19), channel_id=1, source_target_pairs={{0,4},{2,6},{4,0},{6,2},{8,12},{10,14},{12,8},{14,10},{16,20},{18,... | collective-permute-start | bytes 405512 | tf_op jit(solution)/shard_map/ppermute | solution.py:1093
  307.4 4.4 %collective-permute-start.14 = (bf16[96,256]{1,0:T(8,128)(2,1)S(1)}, bf16[96,256]{1,0:T(8,128)(2,1)S(1)}, u32[]{:S(2)}, u32[]{:S(2)}) collective-permute-start(bf16[96,256]{1,0:T(8,128)(2,1)S(1)} %get-tuple-element.138), channel_id=1, source_target_pairs={{0,1},{1,0},{2,3},{3,2},{4,5},{5,4},{6,7},{7,6},{8,9},{9,8},{10,11... | collective-permute-start | bytes 147464 | tf_op jit(solution)/shard_map/ppermute | solution.py:1090
  311.2 4.8 %collective-permute-start.19 = (bf16[104,256]{1,0:T(8,128)(2,1)S(1)}, bf16[104,256]{1,0:T(8,128)(2,1)S(1)}, u32[]{:S(2)}, u32[]{:S(2)}) collective-permute-start(bf16[104,256]{1,0:T(8,128)(2,1)S(1)} %pad_maximum_fusion.2), channel_id=1, source_target_pairs={{0,1},{1,0},{2,3},{3,2},{4,5},{5,4},{6,7},{7,6},{8,9},{9,8},{10,11... | collective-permute-start | bytes 159752 | tf_op jit(solution)/shard_map/ppermute | solution.py:1090
  311.9 7.4 %collective-permute-start.15 = (bf16[1,256,256]{2,1,0:T(8,128)(2,1)S(1)}, bf16[1,256,256]{2,1,0:T(8,128)(2,1)S(1)}, u32[]{:S(2)}, u32[]{:S(2)}) collective-permute-start(bf16[1,256,256]{2,1,0:T(8,128)(2,1)S(1)} %maximum_bitcast_fusion.1), channel_id=1, source_target_pairs={{0,16},{2,18},{4,20},{6,22},{8,24},{10,26},{12,28},{14,30},{16,0},... | collective-permute-start | bytes 393224 | tf_op jit(solution)/shard_map/ppermute | solution.py:1093
  316.5 9.2 %collective-permute-start.22 = (bf16[256,1024]{1,0:T(8,128)(2,1)S(1)}, bf16[256,1024]{1,0:T(8,128)(2,1)S(1)}, u32[]{:S(2)}, u32[]{:S(2)}) collective-permute-start(bf16[256,1024]{1,0:T(8,128)(2,1)S(1)} %fusion.7), channel_id=1, source_target_pairs={{0,1},{1,0},{2,3},{3,2},{4,5},{5,4},{6,7},{7,6},{8,9},{9,8},{10,11... | collective-permute-start | bytes 1572872 | tf_op jit(solution)/shard_map/ppermute | solution.py:1090
  317.1 5.1 %collective-permute-start.20 = (bf16[1,264,256]{2,1,0:T(8,128)(2,1)S(1)}, bf16[1,264,256]{2,1,0:T(8,128)(2,1)S(1)}, u32[]{:S(2)}, u32[]{:S(2)}) collective-permute-start(bf16[1,264,256]{2,1,0:T(8,128)(2,1)S(1)} %maximum_bitcast_fusion), channel_id=1, source_target_pairs={{0,4},{2,6},{4,0},{6,2},{8,12},{10,14},{12,8},{14,10},{16,20},{18,... | collective-permute-start | bytes 405512 | tf_op jit(solution)/shard_map/ppermute | solution.py:1093
  330.0 11.0 %collective-permute-start.25 = (bf16[2,256,256]{2,1,0:T(8,128)(2,1)S(1)}, bf16[2,256,256]{2,1,0:T(8,128)(2,1)S(1)}, u32[]{:S(2)}, u32[]{:S(2)}) collective-permute-start(bf16[2,256,256]{2,1,0:T(8,128)(2,1)S(1)} %maximum_select_fusion.11), channel_id=1, source_target_pairs={{0,8},{2,10},{4,12},{6,14},{8,0},{10,2},{12,4},{14,6},{16,24},{18,... | collective-permute-start | bytes 786440 | tf_op jit(solution)/shard_map/ppermute | solution.py:1093
  330.0 11.1 %collective-permute-start.26 = (bf16[2,264,256]{2,1,0:T(8,128)(2,1)S(1)}, bf16[2,264,256]{2,1,0:T(8,128)(2,1)S(1)}, u32[]{:S(2)}, u32[]{:S(2)}) collective-permute-start(bf16[2,264,256]{2,1,0:T(8,128)(2,1)S(1)} %maximum_select_fusion.10), channel_id=1, source_target_pairs={{0,16},{2,18},{4,20},{6,22},{8,24},{10,26},{12,28},{14,30},{16,0},... | collective-permute-start | bytes 811016 | tf_op jit(solution)/shard_map/ppermute | solution.py:1093
  341.2 9.2 %collective-permute-start.33 = (bf16[4,256,256]{2,1,0:T(8,128)(2,1)S(1)}, bf16[4,256,256]{2,1,0:T(8,128)(2,1)S(1)}, u32[]{:S(2)}, u32[]{:S(2)}) collective-permute-start(bf16[4,256,256]{2,1,0:T(8,128)(2,1)S(1)} %maximum_select_fusion.7), channel_id=1, source_target_pairs={{0,4},{2,6},{4,0},{6,2},{8,12},{10,14},{12,8},{14,10},{16,20},{18,... | collective-permute-start | bytes 1572872 | tf_op jit(solution)/shard_map/ppermute | solution.py:1093
  342.3 9.4 %collective-permute-start.34 = (bf16[4,264,256]{2,1,0:T(8,128)(2,1)S(1)}, bf16[4,264,256]{2,1,0:T(8,128)(2,1)S(1)}, u32[]{:S(2)}, u32[]{:S(2)}) collective-permute-start(bf16[4,264,256]{2,1,0:T(8,128)(2,1)S(1)} %maximum_select_fusion.6), channel_id=1, source_target_pairs={{0,8},{2,10},{4,12},{6,14},{8,0},{10,2},{12,4},{14,6},{16,24},{18,... | collective-permute-start | bytes 1622024 | tf_op jit(solution)/shard_map/ppermute | solution.py:1093
  350.6 5.7 %copy-start.8 = (bf16[8,256,256]{2,1,0:T(8,128)(2,1)}, bf16[8,256,256]{2,1,0:T(8,128)(2,1)S(1)}, u32[]{:S(2)}) copy-start(bf16[8,256,256]{2,1,0:T(8,128)(2,1)S(1)} %maximum_select_fusion.4.ao_ref) | copy-start | bytes 3145732
  351.8 4.4 %collective-permute-start.43 = (bf16[8,264,256]{2,1,0:T(8,128)(2,1)S(1)}, bf16[8,264,256]{2,1,0:T(8,128)(2,1)S(1)}, u32[]{:S(2)}, u32[]{:S(2)}) collective-permute-start(bf16[8,264,256]{2,1,0:T(8,128)(2,1)S(1)} %maximum_select_fusion.2.bo_ref), channel_id=1, source_target_pairs={{0,2},{2,0},{4,6},{6,4},{8,10},{10,8},{12,14},{14,12},{16,18},{18,... | collective-permute-start | bytes 3244040 | tf_op jit(solution)/shard_map/ppermute | solution.py:1093
  351.9 4.3 %collective-permute-start.42 = (bf16[8,256,256]{2,1,0:T(8,128)(2,1)S(1)}, bf16[8,256,256]{2,1,0:T(8,128)(2,1)}, u32[]{:S(2)}, u32[]{:S(2)}) collective-permute-start(bf16[8,256,256]{2,1,0:T(8,128)(2,1)S(1)} %maximum_select_fusion.4.ao_ref), channel_id=1, source_target_pairs={{0,2},{2,0},{4,6},{6,4},{8,10},{10,8},{12,14},{14,12},{16,18},{18,... | collective-permute-start | bytes 3145736 | tf_op jit(solution)/shard_map/ppermute | solution.py:1093
  (18 other events, 55.2 us)

commit v9 on v8

--- a/solution.py
+++ b/solution.py
@@ -807,14 +807,14 @@
     half = width // 2
     me = ids[0]
     core = ids[1]
-    s = pl.program_id(0)
+    i = pl.program_id(0)
     outs = (a_ref, b_ref)
     n = a_ref.shape[0]
     nh = d_ref.shape[1]
     cols = nh * HD
     r = half // (2 * n)
 
-    @pl.when(s == 0)
+    @pl.when(i == 0)
     def _():
         g_s[...] = jnp.zeros_like(g_s)
         go_s[...] = jnp.zeros_like(go_s)
@@ -846,12 +846,11 @@
         for k, v in enumerate((da * xh, da, dm * xh, dm)):
             sum_s[k : k + 1, lanes] += jnp.sum(v, axis=0, keepdims=True)
 
-    @pl.when(s == 0)
+    @pl.when(i == core)
     def _():
-        mine = dy_ref[pl.ds(pl.multiple_of(core * (rows // 2), rows // 2), rows // 2), :]
-        sum_s[4:5, :] = jnp.sum(mine.astype(f32), axis=0, keepdims=True)
-
-    @pl.when(s == pl.num_programs(0) - 1)
+        sum_s[4:5, :] = jnp.sum(dy_ref[...].astype(f32), axis=0, keepdims=True)
+
+    @pl.when(i == pl.num_programs(0) - 1)
     def _():
         for p in range(3):
             g = g_s[p].astype(bf16)
@@ -889,7 +888,7 @@
 
 
 def qkv_backward(ids, d, at, x2, norms, w_own, w_got, d_mlp, ob, dy, gb_up, n):
-    rows, width = x2.shape[0] // 2, x2.shape[1]
+    rows, width = x2.shape[0] // 4, x2.shape[1]
     half = width // 2
     cols = w_got.shape[1] // 3
     size = 6 * (half // (2 * n)) + width // (2 * n)
@@ -902,16 +901,16 @@
         qkv_back_kernel,
         grid_spec=pltpu.PrefetchScalarGridSpec(
             num_scalar_prefetch=1,
-            grid=(2,),
+            grid=(4,),
             in_specs=[
-                pl.BlockSpec((1, cols // HD, 3 * HD, rows), lambda s, ids: (s, 0, 0, 0)),
+                pl.BlockSpec((1, cols // HD, 3 * HD, rows), lambda s, ids: (s // 2, 0, 0, s % 2)),
                 pl.BlockSpec((width, rows), lambda s, ids: (0, s)),
                 row(),
                 _full(norms),
             ]
             + _wq_specs(half, width, cols, cols, lambda s, ids: 0)
-            + [row(), pl.BlockSpec((1, cols, rows), lambda s, ids: (s, 0, 0)), row(), _full(gb_up)],
-            out_specs=(*[_full(v) for v in out], pl.BlockSpec((1, rows, width), lambda s, ids: (s, 0, 0))),
+            + [row(), pl.BlockSpec((1, cols, rows), lambda s, ids: (s // 2, 0, s % 2)), row(), _full(gb_up)],
+            out_specs=(*[_full(v) for v in out], pl.BlockSpec((1, rows, width), lambda s, ids: (s // 2, s % 2, 0))),
             scratch_shapes=[
                 pltpu.VMEM((3, width, cols), f32),
                 pltpu.VMEM((cols, width), f32),
@@ -919,7 +918,7 @@
                 pltpu.VMEM((8, width), f32),
             ],
         ),
-        out_shape=(*out, jax.ShapeDtypeStruct((2, rows, width), f32)),
+        out_shape=(*out, jax.ShapeDtypeStruct((2, 2 * rows, width), f32)),
         compiler_params=_params(),
         name="qkv_backward",
     )(ids, d, at, x2, norms, w_own, w_own, w_own, w_got, w_got, w_got, d_mlp, ob, dy, gb_up)
@@ -950,16 +949,27 @@
         o_ref[...] = got_ref[...].astype(f32).reshape(shape)
 
 
+def join_rows_kernel(ids, own_ref, got_ref, o_ref):
+    mine = pl.program_id(0) == ids[1]
+
+    @pl.when(mine)
+    def _():
+        o_ref[...] = own_ref[...].astype(f32).reshape(o_ref.shape)
+
+    @pl.when(jnp.logical_not(mine))
+    def _():
+        o_ref[...] = got_ref[...].astype(f32).reshape(o_ref.shape)
+
+
 def join_rows(ids, own, got):
     n, r, w = own.shape
-    src = lambda f: pl.BlockSpec((n // 2, r, w), lambda i, ids: (f(i, ids), 0, 0))
     return pl.pallas_call(
-        join_kernel,
+        join_rows_kernel,
         grid_spec=pltpu.PrefetchScalarGridSpec(
             num_scalar_prefetch=1,
-            grid=(4,),
-            in_specs=[src(_own_block), src(_got_block)],
-            out_specs=pl.BlockSpec((n * r // 2, w), lambda i, ids: (i, 0)),
+            grid=(2,),
+            in_specs=[_full(own), _full(got)],
+            out_specs=pl.BlockSpec((n * r, w), lambda i, ids: (i, 0)),
         ),
         out_shape=jax.ShapeDtypeStruct((2 * n * r, w), f32),
         compiler_params=_params(),

time: 369 us -> 369 us (level)
  no operation moved by 1% of the time
where the time goes in v9:
time: 369 us; the launch traced here: 367 us
  Pallas kernels  134 us (36%)
  waiting for transfers between devices  123 us (33%)
  starting transfers between devices  58.5 us (16%)
  other arithmetic  28.5 us (8%)
  local copies, waits for them, and re-layouts  19.8 us (5%)
    ppermute x34, waiting for transfers between devices, flip(): return lax.ppermute(v, 'ctx', [(i, i ^ 1 << bit) for i in range(n_ctx)])  82 us
    ppermute x10, waiting for transfers between devices, swap(): return lax.ppermute(v, 'wsh', SWAP)  33 us
    pallas_call x1, Pallas kernels, attn_bwd(): pl.pallas_call(lambda *a: attn_bwd_kernel(*a, nblk=nblk, per=x.shape[2] /...  32.1 us
    ppermute x34, starting transfers between devices, flip(): return lax.ppermute(v, 'ctx', [(i, i ^ 1 << bit) for i in range(n_ctx)])  30.4 us
    pallas_call x1, Pallas kernels, mlp(): pl.pallas_call(mlp_kernel, grid_spec=pltpu.PrefetchScalarGridSpec(num_sca...  23.2 us
    pallas_call x1, Pallas kernels, attn_fwd(): pl.pallas_call(lambda *a: attn_fwd_kernel(*a, nblk=nblk, per=x.shape[2] /...  18.6 us
    all_to_all x4, starting transfers between devices, exchange(): return lax.all_to_all(v, 'ctx', 0, 0, axis_index_groups=groups, tiled=False)  17.6 us
    pallas_call x1, Pallas kernels, qkv_backward(): pl.pallas_call(qkv_back_kernel, grid_spec=pltpu.PrefetchScalarGridSpec(nu...  12.6 us
  transfers between devices with their start and end apart: 48, of which 22 were waited for; matrix products, arithmetic and copies ran while one was open for 10% of the time, Pallas kernels for 35%

profile of v9, /device:TPU:0, one launch (start us, length us, event | category | flops | bytes accessed | tf_op | source)
XLA Modules:
  0.0 367.2 jit_solution(5297882104688377665)
XLA Ops:
  0.7 3.0 collective-permute-start
  4.5 1.2 constant_dynamic-slice_fusion.9
  6.3 1.9 collective-permute-start.3
  11.0 6.0 %collective-permute-done.2 = bf16[10,512]{1,0:T(8,128)(2,1)S(1)} collective-permute-done((bf16[10,512]{1,0:T(8,128)(2,1)S(1)}, bf16[10,512]{1,0:T(8,128)(2,1)S(1)}, u32[]{:S(2)}, u32[]{:S(2)}) %collective-permute-start.2) | collective-permute-done | bytes 10272 | tf_op jit(solution)/shard_map/ppermute | solution.py:1100
  18.7 3.9 %norm_rows.2 = (bf16[1024,1024]{1,0:T(8,128)(2,1)}, bf16[1024,1024]{1,0:T(8,128)(2,1)}, bf16[1024,1024]{1,0:T(8,128)(2,1)}) custom-call(s32[4]{0:T(128)} %pad_add_fusion.ids, bf16[256,1024]{1,0:T(8,128)(2,1)} %bitcast.167, bf16[256,1024]{1,0:T(8,128)(2,1)} %copy-done.21, f32[4,1024]{1,0:T(4,128)} %maximum_convert_fusion.n_ref), custom_call_target="tpu_custom_call" | custom-call | bytes 1048576 | tf_op jit(solution)/shard_map/norm_rows/pallas_call | solution.py:553
  22.6 10.5 %collective-permute-done.3.gq_ref.gk_ref.gv_ref = bf16[512,768]{1,0:T(8,128)(2,1)S(1)} collective-permute-done((bf16[512,768]{1,0:T(8,128)(2,1)S(1)}, bf16[512,768]{1,0:T(8,128)(2,1)S(1)}, u32[]{:S(2)}, u32[]{:S(2)}) %collective-permute-start.3) | collective-permute-done | bytes 786464 | tf_op jit(solution)/shard_map/ppermute | solution.py:1100
  33.1 1.7 collective-permute-start.6
  35.4 3.9 %norm_rows.3 = (bf16[1024,1024]{1,0:T(8,128)(2,1)}, bf16[1024,1024]{1,0:T(8,128)(2,1)}, bf16[1024,1024]{1,0:T(8,128)(2,1)}) custom-call(s32[4]{0:T(128)} %pad_add_fusion.ids, bf16[256,1024]{1,0:T(8,128)(2,1)} %copy-done.22, bf16[256,1024]{1,0:T(8,128)(2,1)} %collective-permute-done.1.b_ref, ...), custom_call_target="tpu_custom_call", output_to_operand_aliasing={{0}: (4, {}), {1}: (5, {}), {2}: (6, {})} | custom-call | bytes 1048576 | tf_op jit(solution)/shard_map/norm_rows/pallas_call | solution.py:553
  39.4 5.7 %qkv_forward.1 = bf16[2,4,192,512]{3,2,1,0:T(8,128)(2,1)} custom-call(s32[4]{0:T(128)} %pad_add_fusion.ids, bf16[1024,1024]{1,0:T(8,128)(2,1)} %get-tuple-element.79.ain_ref.a_ref, bf16[512,3072]{1,0:T(8,128)(2,1)} %wv_ref.3, bf16[512,3072]{1,0:T(8,128)(2,1)} %wv_ref.3, bf16[512,3072]{1,0:T(8,128)(2,1)} %wv_ref.3, bf16[512,768]{1,0:T(8,128)(2,1)} %copy-done, ...), custom_call_target="tpu_custom_call" | custom-call | flops 1048576 | bytes 1048576 | tf_op jit(solution)/shard_map/qkv_forward/pallas_call | solution.py:659
  45.1 5.9 %all-to-all-start = ((bf16[8,192,512]{2,1,0:T(8,128)(2,1)}), bf16[8,192,512]{2,1,0:T(8,128)(2,1)S(1)}, u32[]{:S(2)}, u32[]{:S(2)}) async-start(bf16[8,192,512]{2,1,0:T(8,128)(2,1)} %bitcast.164), calls=%async_computation | async-start | bytes 3145728 | tf_op jit(solution)/shard_map/all_to_all | solution.py:1127
  51.0 1.3 constant_dynamic-slice_fusion.5
  56.4 5.0 %turn.1 = (bf16[1024,1024]{1,0:T(8,128)(2,1)}, bf16[1024,1024]{1,0:T(8,128)(2,1)}) custom-call(bf16[1024,1024]{1,0:T(8,128)(2,1)} %get-tuple-element.79.ain_ref.a_ref, bf16[1024,1024]{1,0:T(8,128)(2,1)} %get-tuple-element.81.b_ref.x_ref), custom_call_target="tpu_custom_call" | custom-call | bytes 1048576 | tf_op jit(solution)/shard_map/turn/pallas_call | solution.py:578
  61.3 5.7 %mask_rows.1 = (bf16[1024,1024]{1,0:T(8,128)(2,1)}, bf16[8,64,512]{2,1,0:T(8,128)(2,1)}) custom-call(s32[4]{0:T(128)} %pad_add_fusion.ids, bf16[256,1024]{1,0:T(8,128)(2,1)} %bitcast.176, bf16[256,1024]{1,0:T(8,128)(2,1)} %collective-permute-done.5.b_ref, bf16[256,1024]{1,0:T(8,128)(2,1)} %collective-permute-done.6.c_ref, ...), custom_call_target="tpu_custom_call" | custom-call | bytes 1048576 | tf_op jit(solution)/shard_map/mask_rows/pallas_call | solution.py:607
  67.0 8.9 %collective-permute-done.8.wg_ref = bf16[512,1024]{1,0:T(8,128)(2,1)} collective-permute-done((bf16[512,1024]{1,0:T(8,128)(2,1)S(1)}, bf16[512,1024]{1,0:T(8,128)(2,1)}, u32[]{:S(2)}, u32[]{:S(2)}) %collective-permute-start.8) | collective-permute-done | bytes 1048608 | tf_op jit(solution)/shard_map/ppermute | solution.py:1100
  75.9 23.2 %mlp.1 = (bf16[1024,1024]{1,0:T(8,128)(2,1)}, bf16[1024,1024]{1,0:T(8,128)(2,1)}, bf16[4,128,1024]{2,1,0:T(8,128)(2,1)}, bf16[4,128,1024]{2,1,0:T(8,128)(2,1)}, ...) custom-call(s32[4]{0:T(128)} %pad_add_fusion.ids, ...), custom_call_target="tpu_custom_call" | custom-call | flops 12884901888 | bytes 25165824 | tf_op jit(solution)/shard_map/mlp/pallas_call | solution.py:759
  99.1 1.8 collective-permute-start.9
  100.9 1.5 collective-permute-start.10
  102.4 3.6 all-to-all-start.1
  106.1 18.6 %attn_fwd.1 = (bf16[8,64,512]{2,1,0:T(8,128)(2,1)}, f32[1,4096]{1,0:T(1,128)}) custom-call(s32[32]{0:T(128)} %a_0_.3, bf16[8,192,512]{2,1,0:T(8,128)(2,1)} %copy-done.1), custom_call_target="tpu_custom_call" | custom-call | tf_op jit(solution)/shard_map/attn_fwd/pallas_call | solution.py:438
  124.7 8.0 %all-to-all-done.1.a_3_ = bf16[8,64,512]{2,1,0:T(8,128)(2,1)S(1)} async-done(((bf16[8,64,512]{2,1,0:T(8,128)(2,1)}), bf16[8,64,512]{2,1,0:T(8,128)(2,1)S(1)}, u32[]{:S(2)}, u32[]{:S(2)}) %all-to-all-start.1) | async-done | bytes 524320 | tf_op jit(solution)/shard_map/all_to_all | solution.py:1127
  132.7 2.4 fusion.5
  135.1 1.3 collective-permute-start.27
  136.3 3.7 %all-to-all-start.2 = ((bf16[8,64,512]{2,1,0:T(8,128)(2,1)}), bf16[8,64,512]{2,1,0:T(8,128)(2,1)S(1)}, u32[]{:S(2)}, u32[]{:S(2)}) async-start(bf16[8,64,512]{2,1,0:T(8,128)(2,1)} %get-tuple-element.95.a_2_), calls=%async_computation.2 | async-start | bytes 1048576 | tf_op jit(solution)/shard_map/all_to_all | solution.py:1127
  140.1 2.0 fusion.6
  142.1 2.6 collective-permute-start.35
  144.7 9.7 %collective-permute-done.27 = bf16[2,128,1024]{2,1,0:T(8,128)(2,1)S(1)} collective-permute-done((bf16[2,128,1024]{2,1,0:T(8,128)(2,1)}, bf16[2,128,1024]{2,1,0:T(8,128)(2,1)S(1)}, u32[]{:S(2)}, u32[]{:S(2)}) %collective-permute-start.27) | collective-permute-done | bytes 524320 | tf_op jit(solution)/shard_map/ppermute | solution.py:1103
  154.4 1.3 fusion.12
  155.9 32.1 %attn_bwd.1 = bf16[8,192,512]{2,1,0:T(8,128)(2,1)} custom-call(s32[32]{0:T(128)} %a_0_.3, bf16[8,192,512]{2,1,0:T(8,128)(2,1)} %copy-done.1, bf16[8,64,512]{2,1,0:T(8,128)(2,1)} %get-tuple-element.95.a_2_, bf16[8,64,512]{2,1,0:T(8,128)(2,1)} %copy-done.13, f32[1,4096]{1,0:T(1,128)} %get-tuple-element.97.a_4_, f32[16,4096]{1,0:T(8,128)} %pad_maximum_fusion.1.a_5_), custom_call_target="tpu_custom_call" | custom-call | tf_op jit(solution)/shard_map/attn_bwd/pallas_call | solution.py:498
  190.0 1.4 fusion.14
  191.5 2.9 collective-permute-start.29
  194.4 4.3 %all-to-all-start.3 = ((bf16[8,192,512]{2,1,0:T(8,128)(2,1)}), bf16[8,192,512]{2,1,0:T(8,128)(2,1)}, u32[]{:S(2)}, u32[]{:S(2)}) async-start(bf16[8,192,512]{2,1,0:T(8,128)(2,1)} %attn_bwd.1), calls=%async_computation.3 | async-start | bytes 3145728 | tf_op jit(solution)/shard_map/all_to_all | solution.py:1127
  201.6 1.2 copy-done.19
  202.8 1.4 fusion.11
  204.8 8.3 %collective-permute-done.29 = bf16[1,128,1024]{2,1,0:T(8,128)(2,1)} collective-permute-done((bf16[1,128,1024]{2,1,0:T(8,128)(2,1)S(1)}, bf16[1,128,1024]{2,1,0:T(8,128)(2,1)}, u32[]{:S(2)}, u32[]{:S(2)}) %collective-permute-start.29) | collective-permute-done | bytes 262176 | tf_op jit(solution)/shard_map/ppermute | solution.py:1103
  214.3 1.3 collective-permute-start.38
  215.6 6.4 %collective-permute-done.38 = bf16[1,2,64,1024]{3,2,1,0:T(8,128)(2,1)S(1)} collective-permute-done((bf16[1,2,64,1024]{3,2,1,0:T(8,128)(2,1)S(1)}, bf16[1,2,64,1024]{3,2,1,0:T(8,128)(2,1)S(1)}, u32[]{:S(2)}, u32[]{:S(2)}) %collective-permute-start.38) | collective-permute-done | bytes 262176 | tf_op jit(solution)/shard_map/ppermute | solution.py:1103
  222.1 2.5 collective-permute-start.39
  224.6 8.7 %collective-permute-done.30 = bf16[2,128,1024]{2,1,0:T(8,128)(2,1)S(1)} collective-permute-done((bf16[2,128,1024]{2,1,0:T(8,128)(2,1)S(1)}, bf16[2,128,1024]{2,1,0:T(8,128)(2,1)S(1)}, u32[]{:S(2)}, u32[]{:S(2)}) %collective-permute-start.30) | collective-permute-done | bytes 524320 | tf_op jit(solution)/shard_map/ppermute | solution.py:1103
  233.2 1.1 maximum_select_fusion.3
  235.0 2.2 convert_add_fusion.1
  238.7 13.9 %collective-permute-done.39 = bf16[2,2,64,1024]{3,2,1,0:T(8,128)(2,1)S(1)} collective-permute-done((bf16[2,2,64,1024]{3,2,1,0:T(8,128)(2,1)S(1)}, bf16[2,2,64,1024]{3,2,1,0:T(8,128)(2,1)S(1)}, u32[]{:S(2)}, u32[]{:S(2)}) %collective-permute-start.39) | collective-permute-done | bytes 524320 | tf_op jit(solution)/shard_map/ppermute | solution.py:1103
  253.7 12.6 %qkv_backward.1 = (bf16[8,256,256]{2,1,0:T(8,128)(2,1)}, bf16[8,264,256]{2,1,0:T(8,128)(2,1)}, f32[2,512,1024]{2,1,0:T(8,128)}) custom-call(s32[4]{0:T(128)} %pad_add_fusion.ids, bf16[2,4,192,512]{3,2,1,0:T(8,128)(2,1)} %bitcast.21.d_ref, bf16[1024,1024]{1,0:T(8,128)(2,1)} %get-tuple-element.100.at_ref, bf16[1024,1024]{1,0:T(8,128)(2,1)} %get-tuple-element.101.x_ref, ...), custom_call_target="tpu_custom_call" | custom-call | tf_op jit(solution)/shard_map/qkv_backward/pallas_call | solution.py:900
  266.4 1.4 constant_dynamic-slice_fusion.3
  268.8 2.1 collective-permute-start.16
  270.9 2.1 fusion.4
  273.0 2.7 maximum_select_fusion.own_ref
  275.7 1.3 collective-permute-done.11
  277.1 2.1 collective-permute-start.12
  279.2 13.1 %collective-permute-done.16 = bf16[4,264,256]{2,1,0:T(8,128)(2,1)S(1)} collective-permute-done((bf16[4,264,256]{2,1,0:T(8,128)(2,1)S(1)}, bf16[4,264,256]{2,1,0:T(8,128)(2,1)S(1)}, u32[]{:S(2)}, u32[]{:S(2)}) %collective-permute-start.16) | collective-permute-done | bytes 540704 | tf_op jit(solution)/shard_map/ppermute | solution.py:1103
  292.4 2.0 maximum_select_fusion.1.own_ref
  295.1 2.3 collective-permute-start.13
  297.9 8.0 %collective-permute-done.17 = bf16[2,264,256]{2,1,0:T(8,128)(2,1)S(1)} collective-permute-done((bf16[2,264,256]{2,1,0:T(8,128)(2,1)S(1)}, bf16[2,264,256]{2,1,0:T(8,128)(2,1)S(1)}, u32[]{:S(2)}, u32[]{:S(2)}) %collective-permute-start.17) | collective-permute-done | bytes 270368 | tf_op jit(solution)/shard_map/ppermute | solution.py:1103
  308.0 3.0 collective-permute-done.18
  311.9 4.1 %collective-permute-done.19 = bf16[104,256]{1,0:T(8,128)(2,1)S(1)} collective-permute-done((bf16[104,256]{1,0:T(8,128)(2,1)S(1)}, bf16[104,256]{1,0:T(8,128)(2,1)S(1)}, u32[]{:S(2)}, u32[]{:S(2)}) %collective-permute-start.19) | collective-permute-done | bytes 53280 | tf_op jit(solution)/shard_map/ppermute | solution.py:1100
  319.3 2.9 collective-permute-done.20
  322.2 3.5 collective-permute-done.22.er_ref
  326.5 3.4 token_grad.1
  330.0 2.5 collective-permute-start.26
  332.4 1.3 copy-done.11
  333.7 6.6 %join_rows.1 = f32[2048,1024]{1,0:T(8,128)} custom-call(s32[4]{0:T(128)} %pad_add_fusion.ids, bf16[8,128,1024]{2,1,0:T(8,128)(2,1)} %copy-done.3, bf16[8,128,1024]{2,1,0:T(8,128)(2,1)} %copy-done.11), custom_call_target="tpu_custom_call" | custom-call | tf_op jit(solution)/shard_map/join_rows/pallas_call | solution.py:966
  341.2 1.1 collective-permute-start.33
  342.9 7.1 %join_cols.1 = f32[512,4096]{1,0:T(8,128)} custom-call(s32[4]{0:T(128)} %pad_add_fusion.ids, bf16[8,2,64,1024]{3,2,1,0:T(8,128)(2,1)} %copy-done.4, bf16[8,2,64,1024]{3,2,1,0:T(8,128)(2,1)} %collective-permute-done.41.got_ref), custom_call_target="tpu_custom_call" | custom-call | tf_op jit(solution)/shard_map/join_cols/pallas_call | solution.py:983
  352.4 3.8 %collective-permute-done.42.ag_ref = bf16[8,256,256]{2,1,0:T(8,128)(2,1)} collective-permute-done((bf16[8,256,256]{2,1,0:T(8,128)(2,1)S(1)}, bf16[8,256,256]{2,1,0:T(8,128)(2,1)}, u32[]{:S(2)}, u32[]{:S(2)}) %collective-permute-start.42) | collective-permute-done | bytes 1048608 | tf_op jit(solution)/shard_map/ppermute | solution.py:1103
  357.3 6.6 %unpack.1 = (f32[512,3072]{1,0:T(8,128)}, f32[2,256,1024]{2,1,0:T(8,128)}, f32[8,8,256]{2,1,0:T(8,128)}) custom-call(s32[4]{0:T(128)} %pad_add_fusion.ids, bf16[8,256,256]{2,1,0:T(8,128)(2,1)} %copy-done.8, bf16[8,256,256]{2,1,0:T(8,128)(2,1)} %collective-permute-done.42.ag_ref, bf16[8,264,256]{2,1,0:T(8,128)(2,1)} %copy-done.7, bf16[8,264,256]{2,1,0:T(8,128)(2,1)} %copy-done.15), custom_call_target="tpu_custom_call" | custom-call | tf_op jit(solution)/shard_map/unpack/pallas_call | solution.py:1027
  (209 shorter events, 37.2 us)
Async XLA Ops:
  0.7 5.1 %copy-start.26 = (bf16[1536]{0:T(1024)(128)(2,1)S(1)}, bf16[1536]{0:T(1024)(128)(2,1)}, u32[]{:S(2)}) copy-start(bf16[1536]{0:T(1024)(128)(2,1)} %param.22) | copy-start | bytes 9220
  0.7 7.5 %copy-start.27 = (s32[32]{0:T(128)S(1)}, s32[32]{0:T(128)}, u32[]{:S(2)}) copy-start(s32[32]{0:T(128)} %a_0_.3) | copy-start | bytes 388
  0.7 16.4 %collective-permute-start = (bf16[256,1024]{1,0:T(8,128)(2,1)}, bf16[256,1024]{1,0:T(8,128)(2,1)S(1)}, u32[]{:S(2)}, u32[]{:S(2)}) collective-permute-start(bf16[256,1024]{1,0:T(8,128)(2,1)} %bitcast.165), channel_id=1, source_target_pairs={{0,1},{1,0},{2,3},{3,2},{4,5},{5,4},{6,7},{7,6},{8,9},{9,8},{10,11... | collective-permute-start | bytes 1572872 | tf_op jit(solution)/shard_map/ppermute | solution.py:1100
  3.8 14.1 %collective-permute-start.4 = (bf16[256,1024]{1,0:T(8,128)(2,1)}, bf16[256,1024]{1,0:T(8,128)(2,1)S(1)}, u32[]{:S(2)}, u32[]{:S(2)}) collective-permute-start(bf16[256,1024]{1,0:T(8,128)(2,1)} %bitcast.166), channel_id=1, source_target_pairs={{0,2},{2,0},{4,6},{6,4},{8,10},{10,8},{12,14},{14,12},{16,18},{18,... | collective-permute-start | bytes 1572872 | tf_op jit(solution)/shard_map/ppermute | solution.py:1103
  5.6 27.5 %copy-start.14 = (bf16[1,256,1024]{2,1,0:T(8,128)(2,1)S(1)}, bf16[1,256,1024]{2,1,0:T(8,128)(2,1)}, u32[]{:S(2)}) copy-start(bf16[1,256,1024]{2,1,0:T(8,128)(2,1)} %param.31) | copy-start | bytes 1572868
  6.1 10.9 %collective-permute-start.2 = (bf16[10,512]{1,0:T(8,128)(2,1)S(1)}, bf16[10,512]{1,0:T(8,128)(2,1)S(1)}, u32[]{:S(2)}, u32[]{:S(2)}) collective-permute-start(bf16[10,512]{1,0:T(8,128)(2,1)S(1)} %concatenate.150), channel_id=1, source_target_pairs={{0,1},{1,0},{2,3},{3,2},{4,5},{5,4},{6,7},{7,6},{8,9},{9,8},{10,11... | collective-permute-start | bytes 30728 | tf_op jit(solution)/shard_map/ppermute | solution.py:1100
  6.3 26.8 %collective-permute-start.3 = (bf16[512,768]{1,0:T(8,128)(2,1)S(1)}, bf16[512,768]{1,0:T(8,128)(2,1)S(1)}, u32[]{:S(2)}, u32[]{:S(2)}) collective-permute-start(bf16[512,768]{1,0:T(8,128)(2,1)S(1)} %pad_maximum_fusion), channel_id=1, source_target_pairs={{0,1},{1,0},{2,3},{3,2},{4,5},{5,4},{6,7},{7,6},{8,9},{9,8},{10,11... | collective-permute-start | bytes 2359304 | tf_op jit(solution)/shard_map/ppermute | solution.py:1100
  17.1 18.3 %copy-start.22 = (bf16[256,1024]{1,0:T(8,128)(2,1)}, bf16[256,1024]{1,0:T(8,128)(2,1)S(1)}, u32[]{:S(2)}) copy-start(bf16[256,1024]{1,0:T(8,128)(2,1)S(1)} %collective-permute-done.a_ref) | copy-start | bytes 1572868
  17.1 18.3 %collective-permute-start.1 = (bf16[256,1024]{1,0:T(8,128)(2,1)S(1)}, bf16[256,1024]{1,0:T(8,128)(2,1)}, u32[]{:S(2)}, u32[]{:S(2)}) collective-permute-start(bf16[256,1024]{1,0:T(8,128)(2,1)S(1)} %collective-permute-done.a_ref), channel_id=1, source_target_pairs={{0,2},{2,0},{4,6},{6,4},{8,10},{10,8},{12,14},{14,12},{16,18},{18,... | collective-permute-start | bytes 1572872 | tf_op jit(solution)/shard_map/ppermute | solution.py:1103
  33.1 6.3 %copy-start = (bf16[512,768]{1,0:T(8,128)(2,1)}, bf16[512,768]{1,0:T(8,128)(2,1)S(1)}, u32[]{:S(2)}) copy-start(bf16[512,768]{1,0:T(8,128)(2,1)S(1)} %collective-permute-done.3.gq_ref.gk_ref.gv_ref) | copy-start | bytes 2359300
  33.1 19.2 %collective-permute-start.6 = (bf16[256,1024]{1,0:T(8,128)(2,1)S(1)}, bf16[256,1024]{1,0:T(8,128)(2,1)}, u32[]{:S(2)}, u32[]{:S(2)}) collective-permute-start(bf16[256,1024]{1,0:T(8,128)(2,1)S(1)} %bitcast.178), channel_id=1, source_target_pairs={{0,1},{1,0},{2,3},{3,2},{4,5},{5,4},{6,7},{7,6},{8,9},{9,8},{10,11... | collective-permute-start | bytes 1572872 | tf_op jit(solution)/shard_map/ppermute | solution.py:1100
  45.1 7.8 %copy-start.25 = (bf16[2048]{0:T(1024)(128)(2,1)S(1)}, bf16[2048]{0:T(1024)(128)(2,1)}, u32[]{:S(2)}) copy-start(bf16[2048]{0:T(1024)(128)(2,1)} %param.26) | copy-start | bytes 12292
  45.1 54.1 %all-to-all-start = ((bf16[8,192,512]{2,1,0:T(8,128)(2,1)}), bf16[8,192,512]{2,1,0:T(8,128)(2,1)S(1)}, u32[]{:S(2)}, u32[]{:S(2)}) async-start(bf16[8,192,512]{2,1,0:T(8,128)(2,1)} %bitcast.164), calls=%async_computation | async-start | bytes 3145728 | tf_op jit(solution)/shard_map/all_to_all | solution.py:1127
  52.3 23.6 %collective-permute-start.8 = (bf16[512,1024]{1,0:T(8,128)(2,1)S(1)}, bf16[512,1024]{1,0:T(8,128)(2,1)}, u32[]{:S(2)}, u32[]{:S(2)}) collective-permute-start(bf16[512,1024]{1,0:T(8,128)(2,1)S(1)} %constant_dynamic-slice_fusion.5), channel_id=1, source_target_pairs={{0,1},{1,0},{2,3},{3,2},{4,5},{5,4},{6,7},{7,6},{8,9},{9,8},{10,11... | collective-permute-start | bytes 3145736 | tf_op jit(solution)/shard_map/ppermute | solution.py:1100
  52.9 8.5 %collective-permute-start.5 = (bf16[256,1024]{1,0:T(8,128)(2,1)S(1)}, bf16[256,1024]{1,0:T(8,128)(2,1)}, u32[]{:S(2)}, u32[]{:S(2)}) collective-permute-start(bf16[256,1024]{1,0:T(8,128)(2,1)S(1)} %bitcast.179), channel_id=1, source_target_pairs={{0,2},{2,0},{4,6},{6,4},{8,10},{10,8},{12,14},{14,12},{16,18},{18,... | collective-permute-start | bytes 1572872 | tf_op jit(solution)/shard_map/ppermute | solution.py:1103
  54.1 7.3 %collective-permute-start.7 = (bf16[256,1024]{1,0:T(8,128)(2,1)}, bf16[256,1024]{1,0:T(8,128)(2,1)}, u32[]{:S(2)}, u32[]{:S(2)}) collective-permute-start(bf16[256,1024]{1,0:T(8,128)(2,1)} %collective-permute-done.6.c_ref), channel_id=1, source_target_pairs={{0,2},{2,0},{4,6},{6,4},{8,10},{10,8},{12,14},{14,12},{16,18},{18,... | collective-permute-start | bytes 1572872 | tf_op jit(solution)/shard_map/ppermute | solution.py:1103
  99.1 6.9 %copy-start.1 = (bf16[8,192,512]{2,1,0:T(8,128)(2,1)}, bf16[8,192,512]{2,1,0:T(8,128)(2,1)S(1)}, u32[]{:S(2)}) copy-start(bf16[8,192,512]{2,1,0:T(8,128)(2,1)S(1)} %all-to-all-done.a_1_) | copy-start | bytes 4718596
  99.1 33.5 %collective-permute-start.9 = (bf16[4,128,1024]{2,1,0:T(8,128)(2,1)}, bf16[4,128,1024]{2,1,0:T(8,128)(2,1)}, u32[]{:S(2)}, u32[]{:S(2)}) collective-permute-start(bf16[4,128,1024]{2,1,0:T(8,128)(2,1)} %get-tuple-element.92), channel_id=1, source_target_pairs={{0,4},{2,6},{4,0},{6,2},{8,12},{10,14},{12,8},{14,10},{16,20},{18,... | collective-permute-start | bytes 3145736 | tf_op jit(solution)/shard_map/ppermute | solution.py:1103
  100.9 31.7 %collective-permute-start.10 = (bf16[4,128,1024]{2,1,0:T(8,128)(2,1)}, bf16[4,128,1024]{2,1,0:T(8,128)(2,1)}, u32[]{:S(2)}, u32[]{:S(2)}) collective-permute-start(bf16[4,128,1024]{2,1,0:T(8,128)(2,1)} %get-tuple-element.93), channel_id=1, source_target_pairs={{0,8},{2,10},{4,12},{6,14},{8,0},{10,2},{12,4},{14,6},{16,24},{18,... | collective-permute-start | bytes 3145736 | tf_op jit(solution)/shard_map/ppermute | solution.py:1103
  102.4 30.3 %all-to-all-start.1 = ((bf16[8,64,512]{2,1,0:T(8,128)(2,1)}), bf16[8,64,512]{2,1,0:T(8,128)(2,1)S(1)}, u32[]{:S(2)}, u32[]{:S(2)}) async-start(bf16[8,64,512]{2,1,0:T(8,128)(2,1)} %get-tuple-element.91), calls=%async_computation.1 | async-start | bytes 1048576 | tf_op jit(solution)/shard_map/all_to_all | solution.py:1127
  106.1 34.0 %copy-start.17 = (bf16[4,128,1024]{2,1,0:T(8,128)(2,1)S(1)}, bf16[4,128,1024]{2,1,0:T(8,128)(2,1)}, u32[]{:S(2)}) copy-start(bf16[4,128,1024]{2,1,0:T(8,128)(2,1)} %get-tuple-element.117) | copy-start | bytes 3145732
  132.7 9.4 %copy-start.13 = (bf16[8,64,512]{2,1,0:T(8,128)(2,1)}, bf16[8,64,512]{2,1,0:T(8,128)(2,1)S(1)}, u32[]{:S(2)}) copy-start(bf16[8,64,512]{2,1,0:T(8,128)(2,1)S(1)} %all-to-all-done.1.a_3_) | copy-start | bytes 1572868
  135.1 19.4 %collective-permute-start.27 = (bf16[2,128,1024]{2,1,0:T(8,128)(2,1)}, bf16[2,128,1024]{2,1,0:T(8,128)(2,1)S(1)}, u32[]{:S(2)}, u32[]{:S(2)}) collective-permute-start(bf16[2,128,1024]{2,1,0:T(8,128)(2,1)} %fusion.5), channel_id=1, source_target_pairs={{0,8},{2,10},{4,12},{6,14},{8,0},{10,2},{12,4},{14,6},{16,24},{18,... | collective-permute-start | bytes 1572872 | tf_op jit(solution)/shard_map/ppermute | solution.py:1103
  136.3 58.1 %all-to-all-start.2 = ((bf16[8,64,512]{2,1,0:T(8,128)(2,1)}), bf16[8,64,512]{2,1,0:T(8,128)(2,1)S(1)}, u32[]{:S(2)}, u32[]{:S(2)}) async-start(bf16[8,64,512]{2,1,0:T(8,128)(2,1)} %get-tuple-element.95.a_2_), calls=%async_computation.2 | async-start | bytes 1048576 | tf_op jit(solution)/shard_map/all_to_all | solution.py:1127
  142.1 45.9 %collective-permute-start.35 = (bf16[2,128,1024]{2,1,0:T(8,128)(2,1)}, bf16[2,128,1024]{2,1,0:T(8,128)(2,1)S(1)}, u32[]{:S(2)}, u32[]{:S(2)}) collective-permute-start(bf16[2,128,1024]{2,1,0:T(8,128)(2,1)} %fusion.6), channel_id=1, source_target_pairs={{0,16},{2,18},{4,20},{6,22},{8,24},{10,26},{12,28},{14,30},{16,0},... | collective-permute-start | bytes 1572872 | tf_op jit(solution)/shard_map/ppermute | solution.py:1103
  154.4 33.6 %copy-start.20 = (bf16[2,128,1024]{2,1,0:T(8,128)(2,1)}, bf16[2,128,1024]{2,1,0:T(8,128)(2,1)S(1)}, u32[]{:S(2)}) copy-start(bf16[2,128,1024]{2,1,0:T(8,128)(2,1)S(1)} %collective-permute-done.27) | copy-start | bytes 1572868
  155.8 34.2 %collective-permute-start.28 = (bf16[1,128,1024]{2,1,0:T(8,128)(2,1)S(1)}, bf16[1,128,1024]{2,1,0:T(8,128)(2,1)}, u32[]{:S(2)}, u32[]{:S(2)}) collective-permute-start(bf16[1,128,1024]{2,1,0:T(8,128)(2,1)S(1)} %fusion.12), channel_id=1, source_target_pairs={{0,16},{2,18},{4,20},{6,22},{8,24},{10,26},{12,28},{14,30},{16,0},... | collective-permute-start | bytes 786440 | tf_op jit(solution)/shard_map/ppermute | solution.py:1103
  189.9 8.8 %copy-start.10 = (bf16[512,1024]{1,0:T(8,128)(2,1)S(1)}, bf16[512,1024]{1,0:T(8,128)(2,1)}, u32[]{:S(2)}) copy-start(bf16[512,1024]{1,0:T(8,128)(2,1)} %w_ref.1) | copy-start | bytes 3145732
  189.9 11.7 %collective-permute-start.36 = (bf16[1,128,1024]{2,1,0:T(8,128)(2,1)S(1)}, bf16[1,128,1024]{2,1,0:T(8,128)(2,1)}, u32[]{:S(2)}, u32[]{:S(2)}) collective-permute-start(bf16[1,128,1024]{2,1,0:T(8,128)(2,1)S(1)} %fusion.9), channel_id=1, source_target_pairs={{0,4},{2,6},{4,0},{6,2},{8,12},{10,14},{12,8},{14,10},{16,20},{18,... | collective-permute-start | bytes 786440 | tf_op jit(solution)/shard_map/ppermute | solution.py:1103
  191.5 21.6 %collective-permute-start.29 = (bf16[1,128,1024]{2,1,0:T(8,128)(2,1)S(1)}, bf16[1,128,1024]{2,1,0:T(8,128)(2,1)}, u32[]{:S(2)}, u32[]{:S(2)}) collective-permute-start(bf16[1,128,1024]{2,1,0:T(8,128)(2,1)S(1)} %fusion.14), channel_id=1, source_target_pairs={{0,16},{2,18},{4,20},{6,22},{8,24},{10,26},{12,28},{14,30},{16,0},... | collective-permute-start | bytes 786440 | tf_op jit(solution)/shard_map/ppermute | solution.py:1103
  194.4 59.3 %all-to-all-start.3 = ((bf16[8,192,512]{2,1,0:T(8,128)(2,1)}), bf16[8,192,512]{2,1,0:T(8,128)(2,1)}, u32[]{:S(2)}, u32[]{:S(2)}) async-start(bf16[8,192,512]{2,1,0:T(8,128)(2,1)} %attn_bwd.1), calls=%async_computation.3 | async-start | bytes 3145728 | tf_op jit(solution)/shard_map/all_to_all | solution.py:1127
  201.4 12.9 %copy-start.2 = (f32[2,512,1024]{2,1,0:T(8,128)}, f32[2,512,1024]{2,1,0:T(8,128)S(1)}, u32[]{:S(2)}) copy-start(f32[2,512,1024]{2,1,0:T(8,128)S(1)} %convert_add_fusion) | copy-start | bytes 12582916
  201.5 33.5 %collective-permute-start.23 = (bf16[2,256,1024]{2,1,0:T(8,128)(2,1)S(1)}, bf16[2,256,1024]{2,1,0:T(8,128)(2,1)}, u32[]{:S(2)}, u32[]{:S(2)}) collective-permute-start(bf16[2,256,1024]{2,1,0:T(8,128)(2,1)S(1)} %dynamic-slice_convert_fusion), channel_id=1, source_target_pairs={{0,2},{2,0},{4,6},{6,4},{8,10},{10,8},{12,14},{14,12},{16,18},{18,... | collective-permute-start | bytes 3145736 | tf_op jit(solution)/shard_map/ppermute | solution.py:1103
  204.2 10.1 %collective-permute-start.37 = (bf16[1,1,64,1024]{3,2,1,0:T(8,128)(2,1)S(1)}, bf16[1,1,64,1024]{3,2,1,0:T(8,128)(2,1)S(1)}, u32[]{:S(2)}, u32[]{:S(2)}) collective-permute-start(bf16[1,1,64,1024]{3,2,1,0:T(8,128)(2,1)S(1)} %get-tuple-element.134), channel_id=1, source_target_pairs={{0,1},{1,0},{2,3},{3,2},{4,5},{5,4},{6,7},{7,6},{8,9},{9,8},{10,11... | collective-permute-start | bytes 393224 | tf_op jit(solution)/shard_map/ppermute | solution.py:1100
  214.2 19.0 %collective-permute-start.30 = (bf16[2,128,1024]{2,1,0:T(8,128)(2,1)S(1)}, bf16[2,128,1024]{2,1,0:T(8,128)(2,1)S(1)}, u32[]{:S(2)}, u32[]{:S(2)}) collective-permute-start(bf16[2,128,1024]{2,1,0:T(8,128)(2,1)S(1)} %maximum_select_fusion.8), channel_id=1, source_target_pairs={{0,8},{2,10},{4,12},{6,14},{8,0},{10,2},{12,4},{14,6},{16,24},{18,... | collective-permute-start | bytes 1572872 | tf_op jit(solution)/shard_map/ppermute | solution.py:1103
  214.3 7.6 %collective-permute-start.38 = (bf16[1,2,64,1024]{3,2,1,0:T(8,128)(2,1)S(1)}, bf16[1,2,64,1024]{3,2,1,0:T(8,128)(2,1)S(1)}, u32[]{:S(2)}, u32[]{:S(2)}) collective-permute-start(bf16[1,2,64,1024]{3,2,1,0:T(8,128)(2,1)S(1)} %maximum_select_fusion.12), channel_id=1, source_target_pairs={{0,4},{2,6},{4,0},{6,2},{8,12},{10,14},{12,8},{14,10},{16,20},{18,... | collective-permute-start | bytes 786440 | tf_op jit(solution)/shard_map/ppermute | solution.py:1103
  222.1 30.5 %collective-permute-start.39 = (bf16[2,2,64,1024]{3,2,1,0:T(8,128)(2,1)S(1)}, bf16[2,2,64,1024]{3,2,1,0:T(8,128)(2,1)S(1)}, u32[]{:S(2)}, u32[]{:S(2)}) collective-permute-start(bf16[2,2,64,1024]{3,2,1,0:T(8,128)(2,1)S(1)} %maximum_select_fusion.9), channel_id=1, source_target_pairs={{0,16},{2,18},{4,20},{6,22},{8,24},{10,26},{12,28},{14,30},{16,0},... | collective-permute-start | bytes 1572872 | tf_op jit(solution)/shard_map/ppermute | solution.py:1103
  234.4 38.6 %collective-permute-start.31 = (bf16[4,128,1024]{2,1,0:T(8,128)(2,1)}, bf16[4,128,1024]{2,1,0:T(8,128)(2,1)}, u32[]{:S(2)}, u32[]{:S(2)}) collective-permute-start(bf16[4,128,1024]{2,1,0:T(8,128)(2,1)} %maximum_select_fusion.3), channel_id=1, source_target_pairs={{0,4},{2,6},{4,0},{6,2},{8,12},{10,14},{12,8},{14,10},{16,20},{18,... | collective-permute-start | bytes 3145736 | tf_op jit(solution)/shard_map/ppermute | solution.py:1103
  238.1 32.8 %collective-permute-start.24 = (bf16[256,1024]{1,0:T(8,128)(2,1)}, bf16[256,1024]{1,0:T(8,128)(2,1)}, u32[]{:S(2)}, u32[]{:S(2)}) collective-permute-start(bf16[256,1024]{1,0:T(8,128)(2,1)} %fusion.8), channel_id=1, source_target_pairs={{0,1},{1,0},{2,3},{3,2},{4,5},{5,4},{6,7},{7,6},{8,9},{9,8},{10,11... | collective-permute-start | bytes 1572872 | tf_op jit(solution)/shard_map/ppermute | solution.py:1100
  252.8 39.7 %collective-permute-start.40 = (bf16[4,2,64,1024]{3,2,1,0:T(8,128)(2,1)S(1)}, bf16[4,2,64,1024]{3,2,1,0:T(8,128)(2,1)}, u32[]{:S(2)}, u32[]{:S(2)}) collective-permute-start(bf16[4,2,64,1024]{3,2,1,0:T(8,128)(2,1)S(1)} %maximum_select_fusion.5), channel_id=1, source_target_pairs={{0,8},{2,10},{4,12},{6,14},{8,0},{10,2},{12,4},{14,6},{16,24},{18,... | collective-permute-start | bytes 3145736 | tf_op jit(solution)/shard_map/ppermute | solution.py:1103
  267.8 9.2 %collective-permute-start.11 = (bf16[4,256,256]{2,1,0:T(8,128)(2,1)S(1)}, bf16[4,256,256]{2,1,0:T(8,128)(2,1)S(1)}, u32[]{:S(2)}, u32[]{:S(2)}) collective-permute-start(bf16[4,256,256]{2,1,0:T(8,128)(2,1)S(1)} %get-tuple-element.132), channel_id=1, source_target_pairs={{0,4},{2,6},{4,0},{6,2},{8,12},{10,14},{12,8},{14,10},{16,20},{18,... | collective-permute-start | bytes 1572872 | tf_op jit(solution)/shard_map/ppermute | solution.py:1103
  268.8 23.4 %collective-permute-start.16 = (bf16[4,264,256]{2,1,0:T(8,128)(2,1)S(1)}, bf16[4,264,256]{2,1,0:T(8,128)(2,1)S(1)}, u32[]{:S(2)}, u32[]{:S(2)}) collective-permute-start(bf16[4,264,256]{2,1,0:T(8,128)(2,1)S(1)} %get-tuple-element.130), channel_id=1, source_target_pairs={{0,8},{2,10},{4,12},{6,14},{8,0},{10,2},{12,4},{14,6},{16,24},{18,... | collective-permute-start | bytes 1622024 | tf_op jit(solution)/shard_map/ppermute | solution.py:1103
  275.6 18.8 %copy-start.3 = (bf16[8,128,1024]{2,1,0:T(8,128)(2,1)}, bf16[8,128,1024]{2,1,0:T(8,128)(2,1)S(1)}, u32[]{:S(2)}) copy-start(bf16[8,128,1024]{2,1,0:T(8,128)(2,1)S(1)} %maximum_select_fusion.own_ref) | copy-start | bytes 6291460
  275.7 56.8 %collective-permute-start.32 = (bf16[8,128,1024]{2,1,0:T(8,128)(2,1)S(1)}, bf16[8,128,1024]{2,1,0:T(8,128)(2,1)S(1)}, u32[]{:S(2)}, u32[]{:S(2)}) collective-permute-start(bf16[8,128,1024]{2,1,0:T(8,128)(2,1)S(1)} %maximum_select_fusion.own_ref), channel_id=1, source_target_pairs={{0,2},{2,0},{4,6},{6,4},{8,10},{10,8},{12,14},{14,12},{16,18},{18,... | collective-permute-start | bytes 6291464 | tf_op jit(solution)/shard_map/ppermute | solution.py:1103
  277.1 17.9 %collective-permute-start.12 = (bf16[2,256,256]{2,1,0:T(8,128)(2,1)S(1)}, bf16[2,256,256]{2,1,0:T(8,128)(2,1)S(1)}, u32[]{:S(2)}, u32[]{:S(2)}) collective-permute-start(bf16[2,256,256]{2,1,0:T(8,128)(2,1)S(1)} %fusion.22), channel_id=1, source_target_pairs={{0,8},{2,10},{4,12},{6,14},{8,0},{10,2},{12,4},{14,6},{16,24},{18,... | collective-permute-start | bytes 786440 | tf_op jit(solution)/shard_map/ppermute | solution.py:1103
  292.3 5.1 %copy-start.9 = (f32[2,512,1024]{2,1,0:T(8,128)S(1)}, f32[2,512,1024]{2,1,0:T(8,128)}, u32[]{:S(2)}) copy-start(f32[2,512,1024]{2,1,0:T(8,128)} %get-tuple-element.107) | copy-start | bytes 12582916
  292.3 13.5 %collective-permute-start.17 = (bf16[2,264,256]{2,1,0:T(8,128)(2,1)S(1)}, bf16[2,264,256]{2,1,0:T(8,128)(2,1)S(1)}, u32[]{:S(2)}, u32[]{:S(2)}) collective-permute-start(bf16[2,264,256]{2,1,0:T(8,128)(2,1)S(1)} %fusion.18), channel_id=1, source_target_pairs={{0,16},{2,18},{4,20},{6,22},{8,24},{10,26},{12,28},{14,30},{16,0},... | collective-permute-start | bytes 811016 | tf_op jit(solution)/shard_map/ppermute | solution.py:1103
  294.5 16.7 %copy-start.4 = (bf16[8,2,64,1024]{3,2,1,0:T(8,128)(2,1)}, bf16[8,2,64,1024]{3,2,1,0:T(8,128)(2,1)S(1)}, u32[]{:S(2)}) copy-start(bf16[8,2,64,1024]{3,2,1,0:T(8,128)(2,1)S(1)} %maximum_select_fusion.1.own_ref) | copy-start | bytes 6291460
  294.5 48.5 %collective-permute-start.41 = (bf16[8,2,64,1024]{3,2,1,0:T(8,128)(2,1)S(1)}, bf16[8,2,64,1024]{3,2,1,0:T(8,128)(2,1)}, u32[]{:S(2)}, u32[]{:S(2)}) collective-permute-start(bf16[8,2,64,1024]{3,2,1,0:T(8,128)(2,1)S(1)} %maximum_select_fusion.1.own_ref), channel_id=1, source_target_pairs={{0,2},{2,0},{4,6},{6,4},{8,10},{10,8},{12,14},{14,12},{16,18},{18,... | collective-permute-start | bytes 6291464 | tf_op jit(solution)/shard_map/ppermute | solution.py:1103
  295.1 12.2 %collective-permute-start.13 = (bf16[1,256,256]{2,1,0:T(8,128)(2,1)S(1)}, bf16[1,256,256]{2,1,0:T(8,128)(2,1)S(1)}, u32[]{:S(2)}, u32[]{:S(2)}) collective-permute-start(bf16[1,256,256]{2,1,0:T(8,128)(2,1)S(1)} %fusion.23), channel_id=1, source_target_pairs={{0,16},{2,18},{4,20},{6,22},{8,24},{10,26},{12,28},{14,30},{16,0},... | collective-permute-start | bytes 393224 | tf_op jit(solution)/shard_map/ppermute | solution.py:1103
  297.6 18.5 %collective-permute-start.21 = (bf16[2,256,1024]{2,1,0:T(8,128)(2,1)S(1)}, bf16[2,256,1024]{2,1,0:T(8,128)(2,1)S(1)}, u32[]{:S(2)}, u32[]{:S(2)}) collective-permute-start(bf16[2,256,1024]{2,1,0:T(8,128)(2,1)S(1)} %dynamic-slice_convert_fusion.1), channel_id=1, source_target_pairs={{0,2},{2,0},{4,6},{6,4},{8,10},{10,8},{12,14},{14,12},{16,18},{18,... | collective-permute-start | bytes 3145736 | tf_op jit(solution)/shard_map/ppermute | solution.py:1103
  305.9 5.1 %collective-permute-start.18 = (bf16[1,264,256]{2,1,0:T(8,128)(2,1)S(1)}, bf16[1,264,256]{2,1,0:T(8,128)(2,1)S(1)}, u32[]{:S(2)}, u32[]{:S(2)}) collective-permute-start(bf16[1,264,256]{2,1,0:T(8,128)(2,1)S(1)} %fusion.19), channel_id=1, source_target_pairs={{0,4},{2,6},{4,0},{6,2},{8,12},{10,14},{12,8},{14,10},{16,20},{18,... | collective-permute-start | bytes 405512 | tf_op jit(solution)/shard_map/ppermute | solution.py:1103
  307.4 4.4 %collective-permute-start.14 = (bf16[96,256]{1,0:T(8,128)(2,1)S(1)}, bf16[96,256]{1,0:T(8,128)(2,1)S(1)}, u32[]{:S(2)}, u32[]{:S(2)}) collective-permute-start(bf16[96,256]{1,0:T(8,128)(2,1)S(1)} %get-tuple-element.138), channel_id=1, source_target_pairs={{0,1},{1,0},{2,3},{3,2},{4,5},{5,4},{6,7},{7,6},{8,9},{9,8},{10,11... | collective-permute-start | bytes 147464 | tf_op jit(solution)/shard_map/ppermute | solution.py:1100
  311.2 4.8 %collective-permute-start.19 = (bf16[104,256]{1,0:T(8,128)(2,1)S(1)}, bf16[104,256]{1,0:T(8,128)(2,1)S(1)}, u32[]{:S(2)}, u32[]{:S(2)}) collective-permute-start(bf16[104,256]{1,0:T(8,128)(2,1)S(1)} %pad_maximum_fusion.2), channel_id=1, source_target_pairs={{0,1},{1,0},{2,3},{3,2},{4,5},{5,4},{6,7},{7,6},{8,9},{9,8},{10,11... | collective-permute-start | bytes 159752 | tf_op jit(solution)/shard_map/ppermute | solution.py:1100
  311.9 7.4 %collective-permute-start.15 = (bf16[1,256,256]{2,1,0:T(8,128)(2,1)S(1)}, bf16[1,256,256]{2,1,0:T(8,128)(2,1)S(1)}, u32[]{:S(2)}, u32[]{:S(2)}) collective-permute-start(bf16[1,256,256]{2,1,0:T(8,128)(2,1)S(1)} %maximum_bitcast_fusion.1), channel_id=1, source_target_pairs={{0,16},{2,18},{4,20},{6,22},{8,24},{10,26},{12,28},{14,30},{16,0},... | collective-permute-start | bytes 393224 | tf_op jit(solution)/shard_map/ppermute | solution.py:1103
  316.5 9.2 %collective-permute-start.22 = (bf16[256,1024]{1,0:T(8,128)(2,1)S(1)}, bf16[256,1024]{1,0:T(8,128)(2,1)S(1)}, u32[]{:S(2)}, u32[]{:S(2)}) collective-permute-start(bf16[256,1024]{1,0:T(8,128)(2,1)S(1)} %fusion.7), channel_id=1, source_target_pairs={{0,1},{1,0},{2,3},{3,2},{4,5},{5,4},{6,7},{7,6},{8,9},{9,8},{10,11... | collective-permute-start | bytes 1572872 | tf_op jit(solution)/shard_map/ppermute | solution.py:1100
  317.1 5.1 %collective-permute-start.20 = (bf16[1,264,256]{2,1,0:T(8,128)(2,1)S(1)}, bf16[1,264,256]{2,1,0:T(8,128)(2,1)S(1)}, u32[]{:S(2)}, u32[]{:S(2)}) collective-permute-start(bf16[1,264,256]{2,1,0:T(8,128)(2,1)S(1)} %maximum_bitcast_fusion), channel_id=1, source_target_pairs={{0,4},{2,6},{4,0},{6,2},{8,12},{10,14},{12,8},{14,10},{16,20},{18,... | collective-permute-start | bytes 405512 | tf_op jit(solution)/shard_map/ppermute | solution.py:1103
  330.0 11.0 %collective-permute-start.25 = (bf16[2,256,256]{2,1,0:T(8,128)(2,1)S(1)}, bf16[2,256,256]{2,1,0:T(8,128)(2,1)S(1)}, u32[]{:S(2)}, u32[]{:S(2)}) collective-permute-start(bf16[2,256,256]{2,1,0:T(8,128)(2,1)S(1)} %maximum_select_fusion.11), channel_id=1, source_target_pairs={{0,8},{2,10},{4,12},{6,14},{8,0},{10,2},{12,4},{14,6},{16,24},{18,... | collective-permute-start | bytes 786440 | tf_op jit(solution)/shard_map/ppermute | solution.py:1103
  330.0 11.1 %collective-permute-start.26 = (bf16[2,264,256]{2,1,0:T(8,128)(2,1)S(1)}, bf16[2,264,256]{2,1,0:T(8,128)(2,1)S(1)}, u32[]{:S(2)}, u32[]{:S(2)}) collective-permute-start(bf16[2,264,256]{2,1,0:T(8,128)(2,1)S(1)} %maximum_select_fusion.10), channel_id=1, source_target_pairs={{0,16},{2,18},{4,20},{6,22},{8,24},{10,26},{12,28},{14,30},{16,0},... | collective-permute-start | bytes 811016 | tf_op jit(solution)/shard_map/ppermute | solution.py:1103
  341.2 9.2 %collective-permute-start.33 = (bf16[4,256,256]{2,1,0:T(8,128)(2,1)S(1)}, bf16[4,256,256]{2,1,0:T(8,128)(2,1)S(1)}, u32[]{:S(2)}, u32[]{:S(2)}) collective-permute-start(bf16[4,256,256]{2,1,0:T(8,128)(2,1)S(1)} %maximum_select_fusion.7), channel_id=1, source_target_pairs={{0,4},{2,6},{4,0},{6,2},{8,12},{10,14},{12,8},{14,10},{16,20},{18,... | collective-permute-start | bytes 1572872 | tf_op jit(solution)/shard_map/ppermute | solution.py:1103
  342.3 9.4 %collective-permute-start.34 = (bf16[4,264,256]{2,1,0:T(8,128)(2,1)S(1)}, bf16[4,264,256]{2,1,0:T(8,128)(2,1)S(1)}, u32[]{:S(2)}, u32[]{:S(2)}) collective-permute-start(bf16[4,264,256]{2,1,0:T(8,128)(2,1)S(1)} %maximum_select_fusion.6), channel_id=1, source_target_pairs={{0,8},{2,10},{4,12},{6,14},{8,0},{10,2},{12,4},{14,6},{16,24},{18,... | collective-permute-start | bytes 1622024 | tf_op jit(solution)/shard_map/ppermute | solution.py:1103
  350.6 5.7 %copy-start.8 = (bf16[8,256,256]{2,1,0:T(8,128)(2,1)}, bf16[8,256,256]{2,1,0:T(8,128)(2,1)S(1)}, u32[]{:S(2)}) copy-start(bf16[8,256,256]{2,1,0:T(8,128)(2,1)S(1)} %maximum_select_fusion.4.ao_ref) | copy-start | bytes 3145732
  351.8 4.4 %collective-permute-start.43 = (bf16[8,264,256]{2,1,0:T(8,128)(2,1)S(1)}, bf16[8,264,256]{2,1,0:T(8,128)(2,1)S(1)}, u32[]{:S(2)}, u32[]{:S(2)}) collective-permute-start(bf16[8,264,256]{2,1,0:T(8,128)(2,1)S(1)} %maximum_select_fusion.2.bo_ref), channel_id=1, source_target_pairs={{0,2},{2,0},{4,6},{6,4},{8,10},{10,8},{12,14},{14,12},{16,18},{18,... | collective-permute-start | bytes 3244040 | tf_op jit(solution)/shard_map/ppermute | solution.py:1103
  351.9 4.3 %collective-permute-start.42 = (bf16[8,256,256]{2,1,0:T(8,128)(2,1)S(1)}, bf16[8,256,256]{2,1,0:T(8,128)(2,1)}, u32[]{:S(2)}, u32[]{:S(2)}) collective-permute-start(bf16[8,256,256]{2,1,0:T(8,128)(2,1)S(1)} %maximum_select_fusion.4.ao_ref), channel_id=1, source_target_pairs={{0,2},{2,0},{4,6},{6,4},{8,10},{10,8},{12,14},{14,12},{16,18},{18,... | collective-permute-start | bytes 3145736 | tf_op jit(solution)/shard_map/ppermute | solution.py:1103
  (18 other events, 55.2 us)
